TPU v7x, 256 devices: a whole 4x4x8 slice. The times are simulated.
256 devices in a mesh: grp: 8 (over x, core), slab: 32 (over y, z).
Axes of the slice: x: 4, y: 4, z: 8, core: 2. Of those that a mesh axis runs over, the one named last changes fastest.
Arguments:
- images: bfloat16 [8192, 16384], P(('grp', 'slab')), may hold values from -40 to 40
- image_class: int32 [8192], P(('grp', 'slab')), may hold values from 0 to 31, as said below
- image_ctf: int32 [8192], P(('grp', 'slab')), may hold values from 0 to 63
- class_owner: int32 [32], replicated, may hold values from 0 to 31, as said below
- references: bfloat16 [32, 16384], P('slab'), may hold values from -4 to 4
- ctf_table: bfloat16 [64, 8192], replicated, may hold values from -1.01 to 1.01
- x_base: int32 [32, 64], replicated, may hold values from 0 to 254
- y_base: int32 [32, 64], replicated, may hold values from 0 to 254
- x_frac: float32 [32, 64], replicated, may hold values from 0 to 1
- y_frac: float32 [32, 64], replicated, may hold values from 0 to 1
- z_offset: int32 [32, 128], replicated, may hold values from -1 to 1
- z_frac: float32 [32, 128], replicated, may hold values from 0 to 1
Outputs:
- volume: float32 [3, 256, 256, 256], P(None, 'slab', 'grp')
Inputs may be any that keep to these rules, and one draw needn't show every extreme that they name: `image_class`: among the 32 images of one device (aligned blocks of rows) at most 4 name one class, and in every block some class is named by exactly 4. `class_owner`: every index of slab owns exactly one class.
All inputs are finite; a program needn't handle non-finite values.
Results may differ from a plain program's by a relative error of at most 0.014.
Values may be sent and summed in bfloat16 or wider, within the bound.
A program may use at most 128 MiB of HBM per device.

v0:
```python
import math

import jax
import jax.numpy as jnp
from jax import lax
from jax.sharding import PartitionSpec as P

SHIFTS = 128


def padded_2(x, sides, width):
    for axis, dim in sides:
        devices, length = (lax.axis_size(axis), x.shape[dim])
        up = [(i, (i + 1) % devices) for i in range(devices - 1)]
        down = [(j, i) for i, j in up]
        last = lax.slice_in_dim(x, length - width, length, axis=dim)
        first = lax.slice_in_dim(x, 0, width, axis=dim)
        before = lax.ppermute(last, axis, up)
        after = lax.ppermute(first, axis, down)
        x = jnp.concatenate([before, x, after], axis=dim)
    return x


def phase_table(row_count, half_cols):
    shift_ids = jnp.arange(SHIFTS)
    shift_rows = (shift_ids // 8 - SHIFTS // 16).astype(jnp.float32)
    shift_cols = (shift_ids % 8 - 4).astype(jnp.float32)
    freq_rows = (jnp.arange(row_count) - row_count // 2).astype(jnp.float32)
    freq_cols = jnp.arange(half_cols).astype(jnp.float32)
    angles = (
        freq_rows[None, :, None] * shift_rows[:, None, None]
        + freq_cols[None, None, :] * shift_cols[:, None, None]
    ) * (2.0 * math.pi / row_count)
    angles = angles.reshape(SHIFTS, row_count * half_cols)
    return jnp.concatenate([jnp.cos(angles), jnp.sin(angles)], axis=1).astype(jnp.bfloat16)


def align_frames(frames, ctf_rows, ref_rows, phase, score_scale):
    pixels = ctf_rows.shape[1]
    frame_re = frames[:, :pixels].astype(jnp.float32)
    frame_im = frames[:, pixels:].astype(jnp.float32)
    ref_re = ref_rows[:, :pixels].astype(jnp.float32)
    ref_im = ref_rows[:, pixels:].astype(jnp.float32)
    weight = ctf_rows.astype(jnp.float32)
    cross_terms = jnp.concatenate(
        [
            weight * (ref_re * frame_re + ref_im * frame_im),
            weight * (ref_re * frame_im - ref_im * frame_re),
        ],
        axis=1,
    ).astype(jnp.bfloat16)
    scores = score_scale * jnp.einsum(
        "np,sp->ns", cross_terms, phase, preferred_element_type=jnp.float32
    )
    shift_probs = jax.nn.softmax(scores, axis=1).astype(jnp.bfloat16)
    shift_mix = jnp.dot(shift_probs, phase, preferred_element_type=jnp.float32)
    mix_re = shift_mix[:, :pixels]
    mix_im = shift_mix[:, pixels:]
    return jnp.concatenate(
        [
            weight * (frame_re * mix_re + frame_im * mix_im),
            weight * (frame_im * mix_re - frame_re * mix_im),
            weight * weight,
        ],
        axis=1,
    )


def stencil_weights(base_cell, fraction, side_cells):
    cell_ids = jnp.arange(side_cells, dtype=jnp.int32)
    dense_weight = jnp.where(
        cell_ids[None, None, :] == base_cell[:, :, None], (1.0 - fraction)[:, :, None], 0.0
    )
    dense_weight = dense_weight + jnp.where(
        cell_ids[None, None, :] == base_cell[:, :, None] + 1, fraction[:, :, None], 0.0
    )
    return dense_weight.astype(jnp.bfloat16)


def local(
    images,
    image_class,
    image_ctf,
    class_owner,
    references,
    ctf_table,
    x_base,
    y_base,
    x_frac,
    y_frac,
    z_offset,
    z_frac,
):
    slab_count = lax.axis_size("slab")
    group_count = lax.axis_size("grp")
    frame_count = images.shape[0]
    pixels = ctf_table.shape[1]
    groups_ctf = ctf_table.shape[0]
    row_count = z_offset.shape[1]
    half_cols = x_base.shape[1]
    class_count = class_owner.shape[0]
    side_cells = 2 * row_count
    band_rows = row_count // slab_count
    plane_count = 2 * band_rows + 2
    phase = phase_table(row_count, half_cols)
    score_scale = 2.0 / math.sqrt(2.0 * pixels)
    channel_scale = jnp.array(
        [
            1.0 / math.sqrt(frame_count * group_count),
            1.0 / math.sqrt(frame_count * group_count),
            1.0 / (frame_count * group_count),
        ],
        jnp.float32,
    )
    class_ids = jnp.arange(class_count, dtype=jnp.int32)
    owner_of = jnp.sum(
        jnp.where(image_class[:, None] == class_ids[None, :], class_owner[None, :], 0), axis=1
    )
    capacity = max(4, 2 * frame_count // slab_count)
    frame_ids = jnp.arange(frame_count, dtype=jnp.int32)
    earlier = (owner_of[None, :] == owner_of[:, None]) & (frame_ids[None, :] < frame_ids[:, None])
    slot_rank = jnp.sum(earlier.astype(jnp.int32), axis=1)
    slot_index = owner_of * capacity + slot_rank
    placed = slot_index[None, :] == jnp.arange(slab_count * capacity, dtype=jnp.int32)[:, None]
    outgoing = jnp.dot(
        placed.astype(jnp.bfloat16), images, preferred_element_type=jnp.float32
    ).astype(jnp.bfloat16)
    outgoing = outgoing.reshape(slab_count, capacity, 2 * pixels)
    slot_ctf = jnp.sum(jnp.where(placed, image_ctf[None, :], 0), axis=1)
    slot_valid = jnp.sum(placed.astype(jnp.int32), axis=1)
    details = jnp.stack([slot_ctf, slot_valid], axis=1).reshape(slab_count, capacity, 2)
    own_ref = references[0]
    frames = lax.all_to_all(outgoing, "slab", split_axis=0, concat_axis=0, tiled=True)
    slot_info = lax.all_to_all(details, "slab", split_axis=0, concat_axis=0, tiled=True)
    sources = frames.shape[0]
    item_count = frames.shape[1]
    flat_frames = frames.reshape(sources * item_count, 2 * pixels)
    group_ids = slot_info[:, :, 0].reshape(sources * item_count)
    used_rows = slot_info[:, :, 1].reshape(sources * item_count).astype(jnp.float32)
    chosen = (group_ids[:, None] == jnp.arange(groups_ctf, dtype=jnp.int32)[None, :]).astype(
        jnp.bfloat16
    )
    ctf_rows = jnp.dot(chosen, ctf_table, preferred_element_type=jnp.float32).astype(jnp.bfloat16)
    ref_rows = jnp.broadcast_to(own_ref[None, :], flat_frames.shape)
    stacked = align_frames(flat_frames, ctf_rows, ref_rows, phase, score_scale) * used_rows[:, None]
    per_item = jnp.sum(stacked.reshape(sources, item_count, 3 * pixels), axis=0)
    totals = jnp.sum(per_item, axis=0).reshape(3, pixels) * channel_scale[:, None]
    outgoing_bands = totals.astype(jnp.bfloat16).reshape(1, 3, slab_count, band_rows, half_cols)
    arrived = lax.all_to_all(outgoing_bands, "slab", split_axis=2, concat_axis=0, tiled=True)
    owned_by = (class_owner[:, None] == jnp.arange(slab_count, dtype=jnp.int32)[None, :]).astype(
        jnp.bfloat16
    )
    class_bands = jnp.dot(
        owned_by,
        arrived.reshape(slab_count, 3 * band_rows * half_cols),
        preferred_element_type=jnp.float32,
    ).astype(jnp.bfloat16)
    class_bands = class_bands.reshape(class_count, 3, band_rows, half_cols)
    class_bands = lax.optimization_barrier(class_bands)
    slab_index = lax.axis_index("slab")
    local_offset = lax.dynamic_slice_in_dim(z_offset, slab_index * band_rows, band_rows, 1)
    local_frac = lax.dynamic_slice_in_dim(z_frac, slab_index * band_rows, band_rows, 1)
    target = 2 * jnp.arange(band_rows, dtype=jnp.int32)[None, :] + local_offset + 1
    plane_ids = jnp.arange(plane_count, dtype=jnp.int32)
    depth_weight = jnp.where(
        plane_ids[None, None, :] == target[:, :, None], (1.0 - local_frac)[:, :, None], 0.0
    )
    depth_weight = depth_weight + jnp.where(
        plane_ids[None, None, :] == target[:, :, None] + 1, local_frac[:, :, None], 0.0
    )
    sectioned = jnp.einsum(
        "ckra,crj->ckja",
        class_bands.astype(jnp.float32),
        depth_weight,
        precision=lax.Precision.HIGHEST,
    )
    row_weights = stencil_weights(y_base, y_frac, side_cells)
    col_weights = stencil_weights(x_base, x_frac, side_cells)
    class_block = 4
    blocks = class_count // class_block

    def add_block(running, pieces):
        sectioned_part, row_part, col_part = pieces
        lifted = (
            sectioned_part.transpose(1, 2, 0, 3)[:, :, None, :, :]
            * row_part.transpose(2, 0, 1)[None, None, :, :, :]
        )
        lifted = lifted.astype(jnp.bfloat16).reshape(
            3 * plane_count * side_cells, class_block * half_cols
        )
        return (
            running
            + jnp.dot(
                lifted,
                col_part.reshape(class_block * half_cols, side_cells),
                preferred_element_type=jnp.float32,
            ),
            None,
        )

    partial_volume, _ = lax.scan(
        add_block,
        jnp.zeros((3 * plane_count * side_cells, side_cells), jnp.float32),
        (
            sectioned.reshape(blocks, class_block, 3, plane_count, half_cols),
            row_weights.reshape(blocks, class_block, half_cols, side_cells),
            col_weights.reshape(blocks, class_block, half_cols, side_cells),
        ),
    )
    partial_volume = lax.optimization_barrier(
        partial_volume.astype(jnp.bfloat16).reshape(3, plane_count, side_cells, side_cells)
    )
    edge_planes = jnp.concatenate(
        [partial_volume[:, :1], partial_volume[:, plane_count - 1 :]], axis=1
    )
    padded = padded_2(edge_planes, (("slab", 1),), 1)
    inner_planes = partial_volume[:, 1 : plane_count - 1].astype(jnp.float32)
    inner_planes = inner_planes.at[:, 0].add(padded[:, 0].astype(jnp.float32))
    inner_planes = inner_planes.at[:, plane_count - 3].add(padded[:, 3].astype(jnp.float32))
    return lax.psum_scatter(
        inner_planes.astype(jnp.bfloat16), "grp", scatter_dimension=2, tiled=True
    ).astype(jnp.float32)


def solution(mesh):
    in_specs = (
        P(("grp", "slab"), None),
        P(("grp", "slab")),
        P(("grp", "slab")),
        P(),
        P("slab", None),
        P(),
        P(),
        P(),
        P(),
        P(),
        P(),
        P(),
    )
    out_specs = P(None, "slab", "grp", None)
    return jax.shard_map(local, mesh=mesh, in_specs=in_specs, out_specs=out_specs, check_vma=False)
```

profile of v0, /device:TPU:1, one launch (start us, length us, event | category | flops | bytes accessed | tf_op | source)
XLA Modules:
  0.0 444.4 jit_solution(1918789707309425942)
XLA Ops:
  9.3 12.0 %all-to-all-start = ((s32[32,4,2]{1,2,0:T(2,128)}), s32[32,4,2]{1,2,0:T(2,128)S(1)}, u32[]{:S(2)}, u32[]{:S(2)}) async-start(s32[32,4,2]{1,2,0:T(2,128)} %copy.41), calls=%async_computation | async-start | bytes 65536 | tf_op jit(solution)/shard_map/all_to_all | solution.py:134
  21.3 4.5 %convolution_convert_fusion = bf16[128,16384]{1,0:T(8,128)(2,1)} fusion(bf16[32,16384]{1,0:T(8,128)(2,1)} %param.19, s32[32]{0:T(128)S(1)} %multiply_add_fusion), kind=kOutput, calls=%fused_computation.5 | convolution fusion | flops 136318976 | bytes 5243008 | tf_op jit(solution)/shard_map/dot_general | solution.py:125
  25.9 7.2 %reshape.318 = bf16[32,4,16384]{2,1,0:T(4,128)(2,1)} reshape(bf16[128,16384]{1,0:T(8,128)(2,1)} %convolution_convert_fusion) | data formatting | bytes 8388608 | tf_op jit(solution)/shard_map/reshape | solution.py:128
  33.1 9.5 %all-to-all-start.1 = ((bf16[32,4,16384]{2,1,0:T(4,128)(2,1)}), bf16[32,4,16384]{2,1,0:T(4,128)(2,1)}, u32[]{:S(2)}, u32[]{:S(2)}) async-start(bf16[32,4,16384]{2,1,0:T(4,128)(2,1)} %reshape.318), calls=%async_computation.1 | async-start | bytes 8388608 | tf_op jit(solution)/shard_map/all_to_all | solution.py:133
  43.1 4.6 %add_convert_fusion = (bf16[8,4,64,256]{3,2,1,0:T(8,128)(2,1)}, bf16[8,4,64,256]{3,2,1,0:T(8,128)(2,1)}) fusion(f32[8,4,64]{2,1,0:T(4,128)S(1)} %bitcast.71, s32[8,4,64]{2,1,0:T(4,128)S(1)} %bitcast.78, f32[8,4,64]{2,1,0:T(4,128)S(1)} %bitcast.77, s32[8,4,64]{2,1,0:T(4,128)S(1)} %bitcast.72, f32[8,4,64]{2,1,0:T(4,128)S(1)} %bitcast.73, ...), kind=kLoop, calls=%fused_computation.38 | loop fusion | flops 6291456 | bytes 2162688 | tf_op jit(solution)/shard_map/convert_element_type | solution.py:77
  47.6 16.0 %cosine_convert_fusion = (bf16[128,128,64]{0,2,1:T(8,128)(2,1)S(1)}, bf16[128,128,64]{0,2,1:T(8,128)(2,1)}) fusion(f32[128,64]{0,1:T(8,128)S(1)} %broadcast_multiply_fusion.1, f32[128,128]{0,1:T(8,128)S(1)} %broadcast_multiply_fusion), kind=kLoop, calls=%fused_computation.34 | loop fusion | flops 4194304 | bytes 4292608 | tf_op jit(solution)/shard_map/convert.7
  64.0 72.5 %all-to-all-done.1 = bf16[32,4,16384]{2,1,0:T(4,128)(2,1)} async-done(((bf16[32,4,16384]{2,1,0:T(4,128)(2,1)}), bf16[32,4,16384]{2,1,0:T(4,128)(2,1)}, u32[]{:S(2)}, u32[]{:S(2)}) %all-to-all-start.1) | async-done | bytes 4194336 | tf_op jit(solution)/shard_map/all_to_all | solution.py:133
  136.6 7.0 %reshape.319 = bf16[128,16384]{1,0:T(8,128)(2,1)} reshape(bf16[32,4,16384]{2,1,0:T(4,128)(2,1)} %all-to-all-done.1) | data formatting | bytes 8388608 | tf_op jit(solution)/shard_map/reshape | solution.py:137
  143.5 3.8 fusion.4
  151.3 5.2 %fusion.9 = (f32[128,8192]{1,0:T(8,128)}, f32[128,8192]{1,0:T(8,128)}, f32[128,8192]{1,0:T(8,128)}) fusion(f32[128,8192]{1,0:T(8,128)S(1)} %get-tuple-element.129, f32[128,16384]{1,0:T(8,128)S(1)} %fusion.16, bf16[128,16384]{1,0:T(8,128)(2,1)S(1)} %copy-done.2), kind=kLoop, calls=%fused_computation.25 | loop fusion | flops 11534336 | bytes 29360128 | tf_op jit(solution)/shard_map/mul | solution.py:61
  156.5 5.2 %concatenate.25 = f32[32,4,8192]{2,1,0:T(4,128)} reshape(f32[128,8192]{1,0:T(8,128)} %get-tuple-element.114) | data formatting | bytes 8388608 | tf_op jit(solution)/shard_map/concatenate | solution.py:59
  161.7 5.2 %concatenate.26 = f32[32,4,8192]{2,1,0:T(4,128)} reshape(f32[128,8192]{1,0:T(8,128)} %get-tuple-element.115) | data formatting | bytes 8388608 | tf_op jit(solution)/shard_map/concatenate | solution.py:59
  166.9 5.2 %concatenate.27 = f32[32,4,8192]{2,1,0:T(4,128)} reshape(f32[128,8192]{1,0:T(8,128)} %get-tuple-element.118) | data formatting | bytes 8388608 | tf_op jit(solution)/shard_map/concatenate | solution.py:59
  172.1 6.8 %fusion = f32[24576]{0:T(1024)S(1)} fusion(f32[32,4,8192]{2,1,0:T(4,128)} %concatenate.27, f32[32,4,8192]{2,1,0:T(4,128)} %concatenate.26, f32[32,4,8192]{2,1,0:T(4,128)} %concatenate.25, f32[32,4]{1,0:T(8,128)S(1)} %copy.43), kind=kLoop, calls=%fused_computation.7 | loop fusion | flops 12558336 | bytes 12681728 | tf_op jit(solution)/shard_map/reduce_sum | solution.py:147
  179.9 8.3 %all-to-all-start.2 = ((bf16[32,2,384]{2,1,0:T(2,128)(2,1)}), bf16[32,2,384]{2,1,0:T(2,128)(2,1)S(1)}, u32[]{:S(2)}, u32[]{:S(2)}) async-start(bf16[32,2,384]{2,1,0:T(2,128)(2,1)} %reshape.338), calls=%async_computation.2 | async-start | bytes 98304 | tf_op jit(solution)/shard_map/all_to_all | solution.py:149
  188.3 8.7 %all-to-all-done.2 = bf16[32,2,384]{2,1,0:T(2,128)(2,1)S(1)} async-done(((bf16[32,2,384]{2,1,0:T(2,128)(2,1)}), bf16[32,2,384]{2,1,0:T(2,128)(2,1)S(1)}, u32[]{:S(2)}, u32[]{:S(2)}) %all-to-all-start.2) | async-done | bytes 49184 | tf_op jit(solution)/shard_map/all_to_all | solution.py:149
  198.8 180.8 %while.13 = (s32[]{:T(128)}, f32[7680,256]{1,0:T(8,128)}, f32[8,4,3,10,64]{4,1,3,2,0:T(4,128)S(1)}, bf16[8,4,64,256]{3,2,1,0:T(8,128)(2,1)}, bf16[8,4,64,256]{3,2,1,0:T(8,128)(2,1)}, /*index=5*/s32[]{:T(128)}, s32[]{:T(128)}) while((s32[]{:T(128)}, f32[7680,256]{1,0:T(8,128)}, f32[8,4,3,10,64]{4,1,3,2,0:T(4,128)S(1)}, ...), condition=%wide.region_8.9_spmd.clone, body=%wide.region_7.8_spmd.clone.sunk | while | flops 1014562816 | bytes 32659552 | solution.py:201
  200.0 4.0 multiply_convert_fusion.4
  204.0 8.0 %convert_element_type.253 = bf16[7680,256]{0,1:T(8,128)(2,1)} reshape(bf16[3,10,256,4,64]{2,1,0,4,3:T(8,128)(2,1)} %multiply_convert_fusion.4) | data formatting | bytes 7864320 | tf_op jit(solution)/shard_map/while/body/eval_jaxpr/convert_element_type | solution.py:188
  213.0 6.4 %convolution_add_fusion.2 = f32[7680,256]{1,0:T(8,128)} fusion(bf16[7680,256]{0,1:T(8,128)(2,1)} %convert_element_type.253, bf16[256,256]{1,0:T(8,128)(2,1)S(1)} %bitcast.65, f32[7680,256]{1,0:T(8,128)} %get-tuple-element.175, pred[]{:T(512)S(6)} %compare.19), kind=kOutput, calls=%fused_computation.1.clone.1 | convolution fusion | flops 1010565120 | bytes 19791872 | tf_op jit(solution)/shard_map/while/body/eval_jaxpr/dot_general | solution.py:193
  220.6 4.0 multiply_convert_fusion.4
  224.6 8.0 %convert_element_type.253 = bf16[7680,256]{0,1:T(8,128)(2,1)} reshape(bf16[3,10,256,4,64]{2,1,0,4,3:T(8,128)(2,1)} %multiply_convert_fusion.4) | data formatting | bytes 7864320 | tf_op jit(solution)/shard_map/while/body/eval_jaxpr/convert_element_type | solution.py:188
  233.5 8.7 %convolution_add_fusion.2 = f32[7680,256]{1,0:T(8,128)} fusion(bf16[7680,256]{0,1:T(8,128)(2,1)} %convert_element_type.253, bf16[256,256]{1,0:T(8,128)(2,1)S(1)} %bitcast.65, f32[7680,256]{1,0:T(8,128)} %get-tuple-element.175, pred[]{:T(512)S(6)} %compare.19), kind=kOutput, calls=%fused_computation.1.clone.1 | convolution fusion | flops 1010565120 | bytes 19791872 | tf_op jit(solution)/shard_map/while/body/eval_jaxpr/dot_general | solution.py:193
  243.5 4.0 multiply_convert_fusion.4
  247.5 8.0 %convert_element_type.253 = bf16[7680,256]{0,1:T(8,128)(2,1)} reshape(bf16[3,10,256,4,64]{2,1,0,4,3:T(8,128)(2,1)} %multiply_convert_fusion.4) | data formatting | bytes 7864320 | tf_op jit(solution)/shard_map/while/body/eval_jaxpr/convert_element_type | solution.py:188
  256.4 8.7 %convolution_add_fusion.2 = f32[7680,256]{1,0:T(8,128)} fusion(bf16[7680,256]{0,1:T(8,128)(2,1)} %convert_element_type.253, bf16[256,256]{1,0:T(8,128)(2,1)S(1)} %bitcast.65, f32[7680,256]{1,0:T(8,128)} %get-tuple-element.175, pred[]{:T(512)S(6)} %compare.19), kind=kOutput, calls=%fused_computation.1.clone.1 | convolution fusion | flops 1010565120 | bytes 19791872 | tf_op jit(solution)/shard_map/while/body/eval_jaxpr/dot_general | solution.py:193
  266.4 4.0 multiply_convert_fusion.4
  270.4 8.0 %convert_element_type.253 = bf16[7680,256]{0,1:T(8,128)(2,1)} reshape(bf16[3,10,256,4,64]{2,1,0,4,3:T(8,128)(2,1)} %multiply_convert_fusion.4) | data formatting | bytes 7864320 | tf_op jit(solution)/shard_map/while/body/eval_jaxpr/convert_element_type | solution.py:188
  279.3 8.7 %convolution_add_fusion.2 = f32[7680,256]{1,0:T(8,128)} fusion(bf16[7680,256]{0,1:T(8,128)(2,1)} %convert_element_type.253, bf16[256,256]{1,0:T(8,128)(2,1)S(1)} %bitcast.65, f32[7680,256]{1,0:T(8,128)} %get-tuple-element.175, pred[]{:T(512)S(6)} %compare.19), kind=kOutput, calls=%fused_computation.1.clone.1 | convolution fusion | flops 1010565120 | bytes 19791872 | tf_op jit(solution)/shard_map/while/body/eval_jaxpr/dot_general | solution.py:193
  289.3 4.0 multiply_convert_fusion.4
  293.3 8.0 %convert_element_type.253 = bf16[7680,256]{0,1:T(8,128)(2,1)} reshape(bf16[3,10,256,4,64]{2,1,0,4,3:T(8,128)(2,1)} %multiply_convert_fusion.4) | data formatting | bytes 7864320 | tf_op jit(solution)/shard_map/while/body/eval_jaxpr/convert_element_type | solution.py:188
  302.2 8.7 %convolution_add_fusion.2 = f32[7680,256]{1,0:T(8,128)} fusion(bf16[7680,256]{0,1:T(8,128)(2,1)} %convert_element_type.253, bf16[256,256]{1,0:T(8,128)(2,1)S(1)} %bitcast.65, f32[7680,256]{1,0:T(8,128)} %get-tuple-element.175, pred[]{:T(512)S(6)} %compare.19), kind=kOutput, calls=%fused_computation.1.clone.1 | convolution fusion | flops 1010565120 | bytes 19791872 | tf_op jit(solution)/shard_map/while/body/eval_jaxpr/dot_general | solution.py:193
  312.1 4.0 multiply_convert_fusion.4
  316.1 8.0 %convert_element_type.253 = bf16[7680,256]{0,1:T(8,128)(2,1)} reshape(bf16[3,10,256,4,64]{2,1,0,4,3:T(8,128)(2,1)} %multiply_convert_fusion.4) | data formatting | bytes 7864320 | tf_op jit(solution)/shard_map/while/body/eval_jaxpr/convert_element_type | solution.py:188
  325.1 8.7 %convolution_add_fusion.2 = f32[7680,256]{1,0:T(8,128)} fusion(bf16[7680,256]{0,1:T(8,128)(2,1)} %convert_element_type.253, bf16[256,256]{1,0:T(8,128)(2,1)S(1)} %bitcast.65, f32[7680,256]{1,0:T(8,128)} %get-tuple-element.175, pred[]{:T(512)S(6)} %compare.19), kind=kOutput, calls=%fused_computation.1.clone.1 | convolution fusion | flops 1010565120 | bytes 19791872 | tf_op jit(solution)/shard_map/while/body/eval_jaxpr/dot_general | solution.py:193
  335.0 4.0 multiply_convert_fusion.4
  339.0 8.0 %convert_element_type.253 = bf16[7680,256]{0,1:T(8,128)(2,1)} reshape(bf16[3,10,256,4,64]{2,1,0,4,3:T(8,128)(2,1)} %multiply_convert_fusion.4) | data formatting | bytes 7864320 | tf_op jit(solution)/shard_map/while/body/eval_jaxpr/convert_element_type | solution.py:188
  348.0 8.7 %convolution_add_fusion.2 = f32[7680,256]{1,0:T(8,128)} fusion(bf16[7680,256]{0,1:T(8,128)(2,1)} %convert_element_type.253, bf16[256,256]{1,0:T(8,128)(2,1)S(1)} %bitcast.65, f32[7680,256]{1,0:T(8,128)} %get-tuple-element.175, pred[]{:T(512)S(6)} %compare.19), kind=kOutput, calls=%fused_computation.1.clone.1 | convolution fusion | flops 1010565120 | bytes 19791872 | tf_op jit(solution)/shard_map/while/body/eval_jaxpr/dot_general | solution.py:193
  357.9 4.0 multiply_convert_fusion.4
  361.9 8.0 %convert_element_type.253 = bf16[7680,256]{0,1:T(8,128)(2,1)} reshape(bf16[3,10,256,4,64]{2,1,0,4,3:T(8,128)(2,1)} %multiply_convert_fusion.4) | data formatting | bytes 7864320 | tf_op jit(solution)/shard_map/while/body/eval_jaxpr/convert_element_type | solution.py:188
  370.8 8.7 %convolution_add_fusion.2 = f32[7680,256]{1,0:T(8,128)} fusion(bf16[7680,256]{0,1:T(8,128)(2,1)} %convert_element_type.253, bf16[256,256]{1,0:T(8,128)(2,1)S(1)} %bitcast.65, f32[7680,256]{1,0:T(8,128)} %get-tuple-element.175, pred[]{:T(512)S(6)} %compare.19), kind=kOutput, calls=%fused_computation.1.clone.1 | convolution fusion | flops 1010565120 | bytes 19791872 | tf_op jit(solution)/shard_map/while/body/eval_jaxpr/dot_general | solution.py:193
  379.6 3.6 convert_element_type.176
  383.3 2.7 collective-permute-start
  388.0 4.6 %collective-permute-done = bf16[3,1,256,256]{3,2,1,0:T(8,128)(2,1)S(1)} collective-permute-done((bf16[3,1,256,256]{3,2,1,0:T(8,128)(2,1)S(1)}, bf16[3,1,256,256]{3,2,1,0:T(8,128)(2,1)S(1)}, u32[]{:S(2)}, u32[]{:S(2)}) %collective-permute-start) | collective-permute-done | bytes 393248 | tf_op jit(solution)/shard_map/ppermute | solution.py:18
  392.8 3.7 collective-permute-done.1
  396.6 2.1 convert_element_type.180
  398.7 36.9 %reduce-scatter.2.cloned.1.call-done = bf16[3,8,32,256]{3,2,1,0:T(8,128)(2,1)} async-done(((bf16[3,8,256,256]{3,2,1,0:T(8,128)(2,1)}), bf16[3,8,32,256]{3,2,1,0:T(8,128)(2,1)}) %reduce-scatter.2.cloned.1.call-update) | async-done | bytes 393232 | tf_op jit(solution)/shard_map/reduce_scatter | solution.py:220
  435.6 2.0 convert_element_type.181
  (106 shorter events, 29.6 us)
Async XLA Ops:
  6.5 137.0 %copy-start = (bf16[64,8192]{1,0:T(8,128)(2,1)S(1)}, bf16[64,8192]{1,0:T(8,128)(2,1)}, u32[]{:S(2)}) copy-start(bf16[64,8192]{1,0:T(8,128)(2,1)} %param.24) | copy-start | bytes 3145732
  9.3 23.8 %all-to-all-start = ((s32[32,4,2]{1,2,0:T(2,128)}), s32[32,4,2]{1,2,0:T(2,128)S(1)}, u32[]{:S(2)}, u32[]{:S(2)}) async-start(s32[32,4,2]{1,2,0:T(2,128)} %copy.41), calls=%async_computation | async-start | bytes 65536 | tf_op jit(solution)/shard_map/all_to_all | solution.py:134
  33.1 9.6 %copy-start.6 = (f32[32,64]{1,0:T(8,128)S(1)}, f32[32,64]{1,0:T(8,128)}, u32[]{:S(2)}) copy-start(f32[32,64]{1,0:T(8,128)} %param.28) | copy-start | bytes 24580
  33.1 9.6 %copy-start.7 = (s32[32,64]{1,0:T(8,128)S(1)}, s32[32,64]{1,0:T(8,128)}, u32[]{:S(2)}) copy-start(s32[32,64]{1,0:T(8,128)} %param.26) | copy-start | bytes 24580
  33.1 9.7 %copy-start.4 = (f32[32,64]{1,0:T(8,128)S(1)}, f32[32,64]{1,0:T(8,128)}, u32[]{:S(2)}) copy-start(f32[32,64]{1,0:T(8,128)} %param.27) | copy-start | bytes 24580
  33.1 9.7 %copy-start.5 = (s32[32,64]{1,0:T(8,128)S(1)}, s32[32,64]{1,0:T(8,128)}, u32[]{:S(2)}) copy-start(s32[32,64]{1,0:T(8,128)} %param.25) | copy-start | bytes 24580
  33.1 9.7 %copy-start.9 = (s32[32,128]{1,0:T(8,128)S(1)}, s32[32,128]{1,0:T(8,128)}, u32[]{:S(2)}) copy-start(s32[32,128]{1,0:T(8,128)} %param.29) | copy-start | bytes 49156
  33.1 103.4 %all-to-all-start.1 = ((bf16[32,4,16384]{2,1,0:T(4,128)(2,1)}), bf16[32,4,16384]{2,1,0:T(4,128)(2,1)}, u32[]{:S(2)}, u32[]{:S(2)}) async-start(bf16[32,4,16384]{2,1,0:T(4,128)(2,1)} %reshape.318), calls=%async_computation.1 | async-start | bytes 8388608 | tf_op jit(solution)/shard_map/all_to_all | solution.py:133
  42.6 21.0 %copy-start.8 = (bf16[1,16384]{1,0:T(2,128)(2,1)S(1)}, bf16[1,16384]{1,0:T(2,128)(2,1)}, u32[]{:S(2)}) copy-start(bf16[1,16384]{1,0:T(2,128)(2,1)} %param.23) | copy-start | bytes 98308
  143.5 3.8 copy-start.3
  149.1 2.2 copy-start.2
  172.1 7.0 %copy-start.12 = (f32[3]{0:T(128)S(1)}, f32[3]{0:T(128)}, u32[]{:S(2)}) copy-start(f32[3]{0:T(128)} %constant.134.clone) | copy-start | bytes 40
  172.1 16.2 %copy-start.10 = (f32[32,128]{1,0:T(8,128)S(1)}, f32[32,128]{1,0:T(8,128)}, u32[]{:S(2)}) copy-start(f32[32,128]{1,0:T(8,128)} %param.30) | copy-start | bytes 49156
  172.1 25.2 %copy-start.11 = (s32[32]{0:T(128)S(1)}, s32[32]{0:T(128)}, u32[]{:S(2)}) copy-start(s32[32]{0:T(128)} %param.22) | copy-start | bytes 388
  179.9 17.1 %all-to-all-start.2 = ((bf16[32,2,384]{2,1,0:T(2,128)(2,1)}), bf16[32,2,384]{2,1,0:T(2,128)(2,1)S(1)}, u32[]{:S(2)}, u32[]{:S(2)}) async-start(bf16[32,2,384]{2,1,0:T(2,128)(2,1)} %reshape.338), calls=%async_computation.2 | async-start | bytes 98304 | tf_op jit(solution)/shard_map/all_to_all | solution.py:149
  188.2 247.4 %reduce-scatter.2.cloned.1.call-start = ((), (), s32[]{:S(2)}) async-start(), calls=%async_computation.4 | async-start | bytes 3538944 | tf_op jit(solution)/shard_map/reduce_scatter | solution.py:220
  383.3 9.3 %collective-permute-start = (bf16[3,1,256,256]{3,2,1,0:T(8,128)(2,1)S(1)}, bf16[3,1,256,256]{3,2,1,0:T(8,128)(2,1)S(1)}, u32[]{:S(2)}, u32[]{:S(2)}) collective-permute-start(bf16[3,1,256,256]{3,2,1,0:T(8,128)(2,1)S(1)} %get-tuple-element.120), channel_id=1, source_target_pairs={{0,1},{1,2},{2,3},{3,4},{4,5},{5,6},{6,7},{7,8},{8,9},{9,10},{10,1... | collective-permute-start | bytes 1179656 | tf_op jit(solution)/shard_map/ppermute | solution.py:18
  385.9 10.5 %collective-permute-start.1 = (bf16[3,1,256,256]{3,2,1,0:T(8,128)(2,1)S(1)}, bf16[3,1,256,256]{3,2,1,0:T(8,128)(2,1)S(1)}, u32[]{:S(2)}, u32[]{:S(2)}) collective-permute-start(bf16[3,1,256,256]{3,2,1,0:T(8,128)(2,1)S(1)} %get-tuple-element.119), channel_id=1, source_target_pairs={{1,0},{2,1},{3,2},{4,3},{5,4},{6,5},{7,6},{8,7},{9,8},{10,9},{11,1... | collective-permute-start | bytes 1179656 | tf_op jit(solution)/shard_map/ppermute | solution.py:19
  396.6 40.9 %copy-start.1 = (bf16[64,8192]{1,0:T(8,128)(2,1)S(1)}, bf16[64,8192]{1,0:T(8,128)(2,1)}, u32[]{:S(2)}) copy-start(bf16[64,8192]{1,0:T(8,128)(2,1)} %param.24) | copy-start | bytes 3145732
Sparse Core Ops, SparseCore 0:
  398.8 36.7 reduce-scatter.1
where the time goes:
time: 449 us; the launch traced here: 444 us
  waiting for transfers between devices  126 us (28%)
  local copies, waits for them, and re-layouts  107 us (24%)
  other arithmetic  83.2 us (19%)
  matrix products  80.1 us (18%)
  starting transfers between devices  33.8 us (8%)
  between operations  13.8 us (3%)
    all_to_all x1, waiting for transfers between devices, local(): lax.all_to_all(outgoing, 'slab', split_axis=0, concat_axis=0, tiled=True)  72.5 us
    dot_general x8, matrix products, add_block(): jnp.dot(lifted, col_part.reshape(class_block * half_cols, side_cells), pr...  67.6 us
    convert_element_type x8, local copies, waits for them, and re-layouts, add_block(): lifted.astype(jnp.bfloat16)  64.1 us
    reduce_scatter x1, waiting for transfers between devices, local(): lax.psum_scatter(inner_planes.astype(jnp.bfloat16), 'grp', scatter_dimens...  36.9 us
    convert_element_type x8, other arithmetic, add_block(): lifted.astype(jnp.bfloat16)  32 us
    another operation x1, other arithmetic  16 us
    concatenate x3, local copies, waits for them, and re-layouts, align_frames(): jnp.concatenate([weight * (frame_re * mix_re + frame_im * mix_im), weight...  15.6 us
    all_to_all x1, starting transfers between devices, local(): lax.all_to_all(details, 'slab', split_axis=0, concat_axis=0, tiled=True)  12 us
  transfers between devices with their start and end apart: 6, of which 5 were waited for; matrix products, arithmetic and copies ran while one was open for 8% of the time, Pallas kernels for 0%

commit v1 on v0

--- a/solution.py
+++ b/solution.py
@@ -3,6 +3,8 @@
 import jax
 import jax.numpy as jnp
 from jax import lax
+from jax.experimental import pallas as pl
+from jax.experimental.pallas import tpu as pltpu
 from jax.sharding import PartitionSpec as P
 
 SHIFTS = 128
@@ -145,23 +147,36 @@
     stacked = align_frames(flat_frames, ctf_rows, ref_rows, phase, score_scale) * used_rows[:, None]
     per_item = jnp.sum(stacked.reshape(sources, item_count, 3 * pixels), axis=0)
     totals = jnp.sum(per_item, axis=0).reshape(3, pixels) * channel_scale[:, None]
-    outgoing_bands = totals.astype(jnp.bfloat16).reshape(1, 3, slab_count, band_rows, half_cols)
-    arrived = lax.all_to_all(outgoing_bands, "slab", split_axis=2, concat_axis=0, tiled=True)
+    totals = lax.psum(totals, "grp")
+    padded_rows = jnp.pad(
+        totals.reshape(3, row_count, half_cols), ((0, 0), (band_rows, band_rows), (0, 0))
+    ).reshape(3, slab_count + 2, band_rows, half_cols)
+    outgoing_bands = jnp.stack(
+        [padded_rows[:, k : k + slab_count] for k in range(3)], axis=2
+    ).astype(jnp.bfloat16)
+    outgoing_bands = outgoing_bands.transpose(1, 0, 2, 3, 4).reshape(
+        slab_count, 3, 3 * band_rows, half_cols
+    )
+    arrived = lax.all_to_all(outgoing_bands, "slab", split_axis=0, concat_axis=0, tiled=True)
     owned_by = (class_owner[:, None] == jnp.arange(slab_count, dtype=jnp.int32)[None, :]).astype(
         jnp.bfloat16
     )
     class_bands = jnp.dot(
         owned_by,
-        arrived.reshape(slab_count, 3 * band_rows * half_cols),
+        arrived.reshape(slab_count, 3 * 3 * band_rows * half_cols),
         preferred_element_type=jnp.float32,
-    ).astype(jnp.bfloat16)
-    class_bands = class_bands.reshape(class_count, 3, band_rows, half_cols)
-    class_bands = lax.optimization_barrier(class_bands)
+    ).reshape(class_count, 3, 3 * band_rows, half_cols)
     slab_index = lax.axis_index("slab")
-    local_offset = lax.dynamic_slice_in_dim(z_offset, slab_index * band_rows, band_rows, 1)
-    local_frac = lax.dynamic_slice_in_dim(z_frac, slab_index * band_rows, band_rows, 1)
-    target = 2 * jnp.arange(band_rows, dtype=jnp.int32)[None, :] + local_offset + 1
-    plane_ids = jnp.arange(plane_count, dtype=jnp.int32)
+    group_index = lax.axis_index("grp")
+    z_dev = 2 * band_rows
+    offset_pad = jnp.pad(z_offset, ((0, 0), (band_rows, band_rows)))
+    frac_pad = jnp.pad(z_frac, ((0, 0), (band_rows, band_rows)))
+    local_offset = lax.dynamic_slice_in_dim(offset_pad, slab_index * band_rows, 3 * band_rows, 1)
+    local_frac = lax.dynamic_slice_in_dim(frac_pad, slab_index * band_rows, 3 * band_rows, 1)
+    row_ids = jnp.arange(3 * band_rows, dtype=jnp.int32)
+    band_shift = (row_ids // band_rows - 1) * z_dev - 1
+    target = 2 * (row_ids % band_rows)[None, :] + local_offset + 1 + band_shift[None, :]
+    plane_ids = jnp.arange(z_dev, dtype=jnp.int32)
     depth_weight = jnp.where(
         plane_ids[None, None, :] == target[:, :, None], (1.0 - local_frac)[:, :, None], 0.0
     )
@@ -169,57 +184,54 @@
         plane_ids[None, None, :] == target[:, :, None] + 1, local_frac[:, :, None], 0.0
     )
     sectioned = jnp.einsum(
-        "ckra,crj->ckja",
-        class_bands.astype(jnp.float32),
+        "ckra,crz->kzca",
+        class_bands,
         depth_weight,
         precision=lax.Precision.HIGHEST,
-    )
-    row_weights = stencil_weights(y_base, y_frac, side_cells)
-    col_weights = stencil_weights(x_base, x_frac, side_cells)
-    class_block = 4
-    blocks = class_count // class_block
-
-    def add_block(running, pieces):
-        sectioned_part, row_part, col_part = pieces
+    ).reshape(3 * z_dev, class_count * half_cols)
+    y_rows = side_cells // group_count
+    y_ids = group_index * y_rows + jnp.arange(y_rows, dtype=jnp.int32)
+    row_weights = jnp.where(
+        y_ids[:, None, None] == y_base[None, :, :], (1.0 - y_frac)[None, :, :], 0.0
+    )
+    row_weights = row_weights + jnp.where(
+        y_ids[:, None, None] == y_base[None, :, :] + 1, y_frac[None, :, :], 0.0
+    )
+    row_weights = row_weights.astype(jnp.bfloat16).reshape(y_rows, class_count * half_cols)
+    col_weights = stencil_weights(x_base, x_frac, side_cells).reshape(
+        class_count * half_cols, side_cells
+    )
+    inserted = insert_planes(row_weights, sectioned, col_weights)
+    return inserted.reshape(3, z_dev, y_rows, side_cells)
+
+
+def insert_kernel(rows_ref, sec_ref, cols_ref, out_ref):
+    def body(i, carry):
         lifted = (
-            sectioned_part.transpose(1, 2, 0, 3)[:, :, None, :, :]
-            * row_part.transpose(2, 0, 1)[None, None, :, :, :]
-        )
-        lifted = lifted.astype(jnp.bfloat16).reshape(
-            3 * plane_count * side_cells, class_block * half_cols
-        )
-        return (
-            running
-            + jnp.dot(
-                lifted,
-                col_part.reshape(class_block * half_cols, side_cells),
-                preferred_element_type=jnp.float32,
-            ),
-            None,
-        )
-
-    partial_volume, _ = lax.scan(
-        add_block,
-        jnp.zeros((3 * plane_count * side_cells, side_cells), jnp.float32),
-        (
-            sectioned.reshape(blocks, class_block, 3, plane_count, half_cols),
-            row_weights.reshape(blocks, class_block, half_cols, side_cells),
-            col_weights.reshape(blocks, class_block, half_cols, side_cells),
+            rows_ref[...].astype(jnp.float32) * sec_ref[pl.ds(i, 1), :]
+        ).astype(jnp.bfloat16)
+        out_ref[i] = jnp.dot(lifted, cols_ref[...], preferred_element_type=jnp.float32)
+        return carry
+
+    lax.fori_loop(0, sec_ref.shape[0], body, 0)
+
+
+def insert_planes(row_weights, sectioned, col_weights):
+    planes = sectioned.shape[0]
+    y_rows, depth = row_weights.shape
+    side = col_weights.shape[1]
+    return pl.pallas_call(
+        insert_kernel,
+        out_shape=jax.ShapeDtypeStruct((planes, y_rows, side), jnp.float32),
+        in_specs=[pl.BlockSpec(memory_space=pltpu.VMEM)] * 3,
+        out_specs=pl.BlockSpec(memory_space=pltpu.VMEM),
+        cost_estimate=pl.CostEstimate(
+            flops=2 * planes * y_rows * depth * side,
+            transcendentals=0,
+            bytes_accessed=2 * y_rows * depth + 4 * planes * depth + 2 * depth * side
+            + 4 * planes * y_rows * side,
         ),
-    )
-    partial_volume = lax.optimization_barrier(
-        partial_volume.astype(jnp.bfloat16).reshape(3, plane_count, side_cells, side_cells)
-    )
-    edge_planes = jnp.concatenate(
-        [partial_volume[:, :1], partial_volume[:, plane_count - 1 :]], axis=1
-    )
-    padded = padded_2(edge_planes, (("slab", 1),), 1)
-    inner_planes = partial_volume[:, 1 : plane_count - 1].astype(jnp.float32)
-    inner_planes = inner_planes.at[:, 0].add(padded[:, 0].astype(jnp.float32))
-    inner_planes = inner_planes.at[:, plane_count - 3].add(padded[:, 3].astype(jnp.float32))
-    return lax.psum_scatter(
-        inner_planes.astype(jnp.bfloat16), "grp", scatter_dimension=2, tiled=True
-    ).astype(jnp.float32)
+    )(row_weights, sectioned, col_weights)
 
 
 def solution(mesh):

time: 449 us -> 232 us (0.52)
  local copies, waits for them, and re-layouts: 107 us -> 35.4 us
  matrix products: 80.1 us -> 12.6 us
  other arithmetic: 83.2 us -> 34 us
  waiting for transfers between devices: 126 us -> 82.2 us
  blocking collectives: 0 us -> 26.4 us
  between operations: 13.8 us -> 0.37 us
  Pallas kernels: 0 us -> 9.23 us
  starting transfers between devices: 33.8 us -> 28.2 us
    dot_general x10 -> x2, matrix products: 68.8 us -> 1.28 us  [the longest x1 1 us: local(): jnp.einsum('ckra,crz->kzca', class_bands, depth_weight, precision=lax.Pre...]
    convert_element_type x8 -> x0, local copies, waits for them, and re-layouts: 64.1 us -> none  [add_block(): lifted.astype(jnp.bfloat16)]
    convert_element_type x20 -> x1, other arithmetic: 47.8 us -> 0.77 us  [local(): row_weights.astype(jnp.bfloat16).reshape(y_rows, class_count * half_cols)]
    reduce_scatter x1 -> x0, waiting for transfers between devices: 36.9 us -> none  [local(): lax.psum_scatter(inner_planes.astype(jnp.bfloat16), 'grp', scatter_dimens...]
    psum x0 -> x1, blocking collectives: none -> 26.4 us  [local(): totals = lax.psum(totals, 'grp')]
    pallas_call x0 -> x1, Pallas kernels: none -> 9.23 us  [insert_planes(): pl.pallas_call(insert_kernel, out_shape=jax.ShapeDtypeStruct((planes, y_r...]
    ppermute x2 -> x0, waiting for transfers between devices: 8.31 us -> none  [the longest x1 4.62 us: padded_2(): before = lax.ppermute(last, axis, up)]
    dynamic_slice x8 -> x0, local copies, waits for them, and re-layouts: 7.3 us -> none  [local(): lax.scan(add_block, jnp.zeros((3 * plane_count * side_cells, side_cells),...]
  transfers between devices with their start and end apart: 6 -> 3, of which waited for: 5 -> 2; matrix products, arithmetic and copies ran while one was open for 8% -> 14% of each run, Pallas kernels for 0% -> 0%
where the time goes in v1:
time: 232 us; the launch traced here: 228 us
  waiting for transfers between devices  82.2 us (35%)
  local copies, waits for them, and re-layouts  35.4 us (15%)
  other arithmetic  34 us (15%)
  starting transfers between devices  28.2 us (12%)
  blocking collectives  26.4 us (11%)
  matrix products  12.6 us (5%)
  Pallas kernels  9.23 us (4%)
    all_to_all x1, waiting for transfers between devices, local(): lax.all_to_all(outgoing, 'slab', split_axis=0, concat_axis=0, tiled=True)  73.1 us
    psum x1, blocking collectives, local(): totals = lax.psum(totals, 'grp')  26.4 us
    another operation x1, other arithmetic  16.1 us
    concatenate x3, local copies, waits for them, and re-layouts, align_frames(): jnp.concatenate([weight * (frame_re * mix_re + frame_im * mix_im), weight...  15.5 us
    all_to_all x1, starting transfers between devices, local(): lax.all_to_all(details, 'slab', split_axis=0, concat_axis=0, tiled=True)  12 us
    all_to_all x1, starting transfers between devices, local(): lax.all_to_all(outgoing, 'slab', split_axis=0, concat_axis=0, tiled=True)  9.5 us
    pallas_call x1, Pallas kernels, insert_planes(): pl.pallas_call(insert_kernel, out_shape=jax.ShapeDtypeStruct((planes, y_r...  9.23 us
    all_to_all x1, waiting for transfers between devices, local(): lax.all_to_all(outgoing_bands, 'slab', split_axis=0, concat_axis=0, tiled...  9.12 us
  transfers between devices with their start and end apart: 3, of which 2 were waited for; matrix products, arithmetic and copies ran while one was open for 14% of the time, Pallas kernels for 0%

profile of v1, /device:TPU:1, one launch (start us, length us, event | category | flops | bytes accessed | tf_op | source)
XLA Modules:
  0.0 228.4 jit_solution(16797297391524548456)
XLA Ops:
  0.0 0.9 select_reduce_fusion.1
  0.9 0.2 convert_reduce_fusion.1
  1.1 0.7 select_reduce_fusion
  1.9 0.1 stack.25
  2.0 0.1 stack.26
  2.1 0.6 copy.46
  2.8 12.0 %all-to-all-start = ((s32[32,4,2]{1,2,0:T(2,128)}), s32[32,4,2]{1,2,0:T(2,128)S(1)}, u32[]{:S(2)}, u32[]{:S(2)}) async-start(s32[32,4,2]{1,2,0:T(2,128)} %copy.46), calls=%async_computation | async-start | bytes 65536 | tf_op jit(solution)/shard_map/all_to_all | solution.py:136
  14.8 4.5 %convolution_convert_fusion = bf16[128,16384]{1,0:T(8,128)(2,1)} fusion(bf16[32,16384]{1,0:T(8,128)(2,1)} %param.13, s32[32]{0:T(128)S(1)} %multiply_add_fusion), kind=kOutput, calls=%fused_computation | convolution fusion | flops 136318976 | bytes 5243008 | tf_op jit(solution)/shard_map/dot_general | solution.py:127
  19.3 7.2 %reshape.242 = bf16[32,4,16384]{2,1,0:T(4,128)(2,1)} reshape(bf16[128,16384]{1,0:T(8,128)(2,1)} %convolution_convert_fusion) | data formatting | bytes 8388608 | tf_op jit(solution)/shard_map/reshape | solution.py:130
  26.6 9.5 %all-to-all-start.1 = ((bf16[32,4,16384]{2,1,0:T(4,128)(2,1)}), bf16[32,4,16384]{2,1,0:T(4,128)(2,1)}, u32[]{:S(2)}, u32[]{:S(2)}) async-start(bf16[32,4,16384]{2,1,0:T(4,128)(2,1)} %reshape.242), calls=%async_computation.1 | async-start | bytes 8388608 | tf_op jit(solution)/shard_map/all_to_all | solution.py:135
  36.2 0.1 broadcast_in_dim.134
  36.3 0.1 eq.165
  36.5 0.1 broadcast_in_dim.148
  36.8 0.1 broadcast_subtract_fusion
  36.9 0.1 broadcast_multiply_fusion.1
  37.0 16.1 %cosine_convert_fusion = (bf16[128,128,64]{0,2,1:T(8,128)(2,1)S(1)}, bf16[128,128,64]{0,2,1:T(8,128)(2,1)}) fusion(f32[128,64]{0,1:T(8,128)S(1)} %broadcast_multiply_fusion.2, f32[128,128]{0,1:T(8,128)S(1)} %broadcast_multiply_fusion.1), kind=kLoop, calls=%fused_computation.29 | loop fusion | flops 4194304 | bytes 4292608 | tf_op jit(solution)/shard_map/convert.14
  53.1 0.8 add_convert_fusion.1.rows_ref
  53.8 2.7 %add_convert_fusion.cols_ref = bf16[2048,256]{1,0:T(8,128)(2,1)} fusion(f32[2048]{0:T(1024)S(1)} %broadcast_in_dim.151, s32[2048]{0:T(1024)S(1)} %eq.196, f32[2048]{0:T(1024)S(1)} %broadcast_in_dim.148, s32[2048]{0:T(1024)S(1)} %eq.192), kind=kLoop, calls=%fused_computation.32 | loop fusion | flops 3145728 | bytes 1081344 | tf_op jit(solution)/shard_map/convert_element_type | solution.py:79
  56.6 0.1 eq.187
  56.7 0.1 copy.58
  56.8 0.1 copy.48
  56.9 73.1 %all-to-all-done.1 = bf16[32,4,16384]{2,1,0:T(4,128)(2,1)} async-done(((bf16[32,4,16384]{2,1,0:T(4,128)(2,1)}), bf16[32,4,16384]{2,1,0:T(4,128)(2,1)}, u32[]{:S(2)}, u32[]{:S(2)}) %all-to-all-start.1) | async-done | bytes 4194336 | tf_op jit(solution)/shard_map/all_to_all | solution.py:135
  130.0 6.9 %reshape.243 = bf16[128,16384]{1,0:T(8,128)(2,1)} reshape(bf16[32,4,16384]{2,1,0:T(4,128)(2,1)} %all-to-all-done.1) | data formatting | bytes 8388608 | tf_op jit(solution)/shard_map/reshape | solution.py:139
  137.0 3.8 %fusion.4 = (bf16[128,8192]{1,0:T(8,128)(2,1)S(1)}, bf16[128,8192]{1,0:T(8,128)(2,1)S(1)}, f32[128,8192]{1,0:T(8,128)S(1)}) fusion(f32[8192]{0:T(1024)S(1)} %bitcast.50, f32[8192]{0:T(1024)S(1)} %bitcast.49, bf16[128,16384]{1,0:T(8,128)(2,1)} %reshape.243, bf16[64,8192]{1,0:T(8,128)(2,1)S(1)} %copy-done, s32[128]{0:T(128)S(1)} %eq.187), kind=kOutput, calls=%fused_computation.15 | convolution fusion | flops 148905984 | bytes 13697536 | tf_op jit(solution)/shard_map/dot_general | solution.py:145
  140.8 1.7 fusion.58
  142.6 1.3 fusion.16
  143.9 0.9 copy-done.2
  144.8 5.1 %fusion.9 = (f32[128,8192]{1,0:T(8,128)}, f32[128,8192]{1,0:T(8,128)}, f32[128,8192]{1,0:T(8,128)}) fusion(f32[128,8192]{1,0:T(8,128)S(1)} %get-tuple-element.25, f32[128,16384]{1,0:T(8,128)S(1)} %fusion.16, bf16[128,16384]{1,0:T(8,128)(2,1)S(1)} %copy-done.2), kind=kLoop, calls=%fused_computation.20 | loop fusion | flops 11534336 | bytes 29360128 | tf_op jit(solution)/shard_map/mul | solution.py:63
  149.9 5.2 %concatenate.21 = f32[32,4,8192]{2,1,0:T(4,128)} reshape(f32[128,8192]{1,0:T(8,128)} %get-tuple-element.11) | data formatting | bytes 8388608 | tf_op jit(solution)/shard_map/concatenate | solution.py:61
  155.1 5.2 %concatenate.22 = f32[32,4,8192]{2,1,0:T(4,128)} reshape(f32[128,8192]{1,0:T(8,128)} %get-tuple-element.12) | data formatting | bytes 8388608 | tf_op jit(solution)/shard_map/concatenate | solution.py:61
  160.3 5.2 %concatenate.23 = f32[32,4,8192]{2,1,0:T(4,128)} reshape(f32[128,8192]{1,0:T(8,128)} %get-tuple-element.15) | data formatting | bytes 8388608 | tf_op jit(solution)/shard_map/concatenate | solution.py:61
  165.4 6.8 %fusion = f32[24576]{0:T(1024)S(1)} fusion(f32[32,4,8192]{2,1,0:T(4,128)} %concatenate.23, f32[32,4,8192]{2,1,0:T(4,128)} %concatenate.22, f32[32,4,8192]{2,1,0:T(4,128)} %concatenate.21, f32[32,4]{1,0:T(8,128)S(1)} %copy.48), kind=kLoop, calls=%fused_computation.2 | loop fusion | flops 12558336 | bytes 12681728 | tf_op jit(solution)/shard_map/reduce_sum | solution.py:149
  172.3 0.1 broadcast_multiply_fusion
  172.4 0.2 reshape.245
  172.6 26.4 %psum.7 = bf16[3,128,64]{2,1,0:T(8,128)(2,1)S(1)} all-reduce(f32[3,128,64]{2,1,0:T(8,128)S(1)} %reshape.245), channel_id=1, replica_groups=mesh['grp'=8,'slab'=32] {'grp'}, use_global_device_ids=true, to_apply=%region_7.8 | all-reduce | flops 24576 | bytes 147456 | tf_op jit(solution)/shard_map/psum | solution.py:150
  199.1 0.1 fusion.56
  199.3 0.1 copy.52
  199.5 0.9 reshape.263
  200.4 6.6 %all-to-all-start.2 = ((bf16[32,2,1152]{2,1,0:T(2,128)(2,1)}), bf16[32,2,1152]{2,1,0:T(2,128)(2,1)S(1)}, u32[]{:S(2)}, u32[]{:S(2)}) async-start(bf16[32,2,1152]{2,1,0:T(2,128)(2,1)} %reshape.263), calls=%async_computation.2 | async-start | bytes 294912 | tf_op jit(solution)/shard_map/all_to_all | solution.py:160
  207.0 0.1 broadcast_add_fusion
  207.1 9.1 %all-to-all-done.2 = bf16[32,2,1152]{2,1,0:T(2,128)(2,1)S(1)} async-done(((bf16[32,2,1152]{2,1,0:T(2,128)(2,1)}), bf16[32,2,1152]{2,1,0:T(2,128)(2,1)S(1)}, u32[]{:S(2)}, u32[]{:S(2)}) %all-to-all-start.2) | async-done | bytes 147488 | tf_op jit(solution)/shard_map/all_to_all | solution.py:160
  216.2 0.2 reshape.264
  216.5 0.2 reshape.248
  216.7 0.2 dot_general.27
  217.0 0.3 fusion.21
  217.3 1.0 convolution_bitcast_fusion
  218.3 0.8 reshape.249.sec_ref
  219.2 9.2 %shard_map.127 = f32[24,32,256]{2,1,0:T(8,128)} custom-call(bf16[32,2048]{1,0:T(8,128)(2,1)} %add_convert_fusion.1.rows_ref, f32[24,2048]{1,0:T(8,128)} %reshape.249.sec_ref, bf16[2048,256]{1,0:T(8,128)(2,1)} %add_convert_fusion.cols_ref), custom_call_target="tpu_custom_call" | custom-call | flops 805306368 | bytes 2162688 | tf_op jit(solution)/shard_map/pallas_call | solution.py:223
  (54 shorter events, 1.0 us)
Async XLA Ops:
  0.0 137.0 %copy-start = (bf16[64,8192]{1,0:T(8,128)(2,1)S(1)}, bf16[64,8192]{1,0:T(8,128)(2,1)}, u32[]{:S(2)}) copy-start(bf16[64,8192]{1,0:T(8,128)(2,1)} %param.18) | copy-start | bytes 3145732
  2.8 23.8 %all-to-all-start = ((s32[32,4,2]{1,2,0:T(2,128)}), s32[32,4,2]{1,2,0:T(2,128)S(1)}, u32[]{:S(2)}, u32[]{:S(2)}) async-start(s32[32,4,2]{1,2,0:T(2,128)} %copy.46), calls=%async_computation | async-start | bytes 65536 | tf_op jit(solution)/shard_map/all_to_all | solution.py:136
  26.5 9.6 %copy-start.5 = (f32[32,64]{1,0:T(8,128)S(1)}, f32[32,64]{1,0:T(8,128)}, u32[]{:S(2)}) copy-start(f32[32,64]{1,0:T(8,128)} %param.22) | copy-start | bytes 24580
  26.5 9.7 %copy-start.6 = (s32[32,64]{1,0:T(8,128)S(1)}, s32[32,64]{1,0:T(8,128)}, u32[]{:S(2)}) copy-start(s32[32,64]{1,0:T(8,128)} %param.20) | copy-start | bytes 24580
  26.5 9.9 %copy-start.7 = (f32[32,64]{1,0:T(8,128)S(1)}, f32[32,64]{1,0:T(8,128)}, u32[]{:S(2)}) copy-start(f32[32,64]{1,0:T(8,128)} %param.21) | copy-start | bytes 24580
  26.5 10.0 %copy-start.8 = (s32[32,64]{1,0:T(8,128)S(1)}, s32[32,64]{1,0:T(8,128)}, u32[]{:S(2)}) copy-start(s32[32,64]{1,0:T(8,128)} %param.19) | copy-start | bytes 24580
  26.6 10.2 %copy-start.9 = (f32[32,128]{1,0:T(8,128)S(1)}, f32[32,128]{1,0:T(8,128)}, u32[]{:S(2)}) copy-start(f32[32,128]{1,0:T(8,128)} %param.24) | copy-start | bytes 49156
  26.6 103.4 %all-to-all-start.1 = ((bf16[32,4,16384]{2,1,0:T(4,128)(2,1)}), bf16[32,4,16384]{2,1,0:T(4,128)(2,1)}, u32[]{:S(2)}, u32[]{:S(2)}) async-start(bf16[32,4,16384]{2,1,0:T(4,128)(2,1)} %reshape.242), calls=%async_computation.1 | async-start | bytes 8388608 | tf_op jit(solution)/shard_map/all_to_all | solution.py:135
  36.1 20.4 %copy-start.4 = (bf16[1,16384]{1,0:T(2,128)(2,1)S(1)}, bf16[1,16384]{1,0:T(2,128)(2,1)}, u32[]{:S(2)}) copy-start(bf16[1,16384]{1,0:T(2,128)(2,1)} %param.17) | copy-start | bytes 98308
  137.0 3.8 %copy-start.3 = (bf16[128,128,64]{0,2,1:T(8,128)(2,1)S(1)}, bf16[128,128,64]{0,2,1:T(8,128)(2,1)}, u32[]{:S(2)}) copy-start(bf16[128,128,64]{0,2,1:T(8,128)(2,1)} %get-tuple-element.20) | copy-start | bytes 6291460
  142.6 2.2 copy-start.2
  165.4 6.9 %copy-start.12 = (f32[3]{0:T(128)S(1)}, f32[3]{0:T(128)}, u32[]{:S(2)}) copy-start(f32[3]{0:T(128)} %constant.106.clone) | copy-start | bytes 40
  172.3 34.8 %copy-start.10 = (s32[32,128]{1,0:T(8,128)S(1)}, s32[32,128]{1,0:T(8,128)}, u32[]{:S(2)}) copy-start(s32[32,128]{1,0:T(8,128)} %param.23) | copy-start | bytes 49156
  172.3 44.7 %copy-start.11 = (s32[32]{0:T(128)S(1)}, s32[32]{0:T(128)}, u32[]{:S(2)}) copy-start(s32[32]{0:T(128)} %param.16) | copy-start | bytes 388
  199.5 28.9 %copy-start.1 = (bf16[64,8192]{1,0:T(8,128)(2,1)S(1)}, bf16[64,8192]{1,0:T(8,128)(2,1)}, u32[]{:S(2)}) copy-start(bf16[64,8192]{1,0:T(8,128)(2,1)} %param.18) | copy-start | bytes 3145732
  200.4 15.9 %all-to-all-start.2 = ((bf16[32,2,1152]{2,1,0:T(2,128)(2,1)}), bf16[32,2,1152]{2,1,0:T(2,128)(2,1)S(1)}, u32[]{:S(2)}, u32[]{:S(2)}) async-start(bf16[32,2,1152]{2,1,0:T(2,128)(2,1)} %reshape.263), calls=%async_computation.2 | async-start | bytes 294912 | tf_op jit(solution)/shard_map/all_to_all | solution.py:160

commit v2 on v1

v2 whole, which is shorter than its diff:
```python
import math

import jax
import jax.numpy as jnp
from jax import lax
from jax.experimental import pallas as pl
from jax.experimental.pallas import tpu as pltpu
from jax.sharding import PartitionSpec as P

SHIFTS = 128


def phase_table(row_count, half_cols):
    shift_ids = jnp.arange(SHIFTS)
    shift_rows = (shift_ids // 8 - SHIFTS // 16).astype(jnp.float32)
    shift_cols = (shift_ids % 8 - 4).astype(jnp.float32)
    freq_rows = (jnp.arange(row_count) - row_count // 2).astype(jnp.float32)
    freq_cols = jnp.arange(half_cols).astype(jnp.float32)
    step = 2.0 * math.pi / row_count
    row_angle = shift_rows[:, None] * freq_rows[None, :] * step
    col_angle = shift_cols[:, None] * freq_cols[None, :] * step
    cos_r, sin_r = jnp.cos(row_angle)[:, :, None], jnp.sin(row_angle)[:, :, None]
    cos_c, sin_c = jnp.cos(col_angle)[:, None, :], jnp.sin(col_angle)[:, None, :]
    cos_t = (cos_r * cos_c - sin_r * sin_c).reshape(SHIFTS, row_count * half_cols)
    sin_t = (sin_r * cos_c + cos_r * sin_c).reshape(SHIFTS, row_count * half_cols)
    return jnp.concatenate([cos_t, sin_t], axis=1).astype(jnp.bfloat16)


def align_frames(frames, ctf_rows, ref_rows, phase, score_scale):
    pixels = ctf_rows.shape[1]
    frame_re = frames[:, :pixels].astype(jnp.float32)
    frame_im = frames[:, pixels:].astype(jnp.float32)
    ref_re = ref_rows[:, :pixels].astype(jnp.float32)
    ref_im = ref_rows[:, pixels:].astype(jnp.float32)
    weight = ctf_rows.astype(jnp.float32)
    cross_terms = jnp.concatenate(
        [
            weight * (ref_re * frame_re + ref_im * frame_im),
            weight * (ref_re * frame_im - ref_im * frame_re),
        ],
        axis=1,
    ).astype(jnp.bfloat16)
    scores = score_scale * jnp.einsum(
        "np,sp->ns", cross_terms, phase, preferred_element_type=jnp.float32
    )
    shift_probs = jax.nn.softmax(scores, axis=1).astype(jnp.bfloat16)
    shift_mix = jnp.dot(shift_probs, phase, preferred_element_type=jnp.float32)
    mix_re = shift_mix[:, :pixels]
    mix_im = shift_mix[:, pixels:]
    return jnp.concatenate(
        [
            weight * (frame_re * mix_re + frame_im * mix_im),
            weight * (frame_im * mix_re - frame_re * mix_im),
            weight * weight,
        ],
        axis=1,
    )


def stencil_weights(base_cell, fraction, side_cells):
    cell_ids = jnp.arange(side_cells, dtype=jnp.int32)
    dense_weight = jnp.where(
        cell_ids[None, None, :] == base_cell[:, :, None], (1.0 - fraction)[:, :, None], 0.0
    )
    dense_weight = dense_weight + jnp.where(
        cell_ids[None, None, :] == base_cell[:, :, None] + 1, fraction[:, :, None], 0.0
    )
    return dense_weight.astype(jnp.bfloat16)


def local(
    images,
    image_class,
    image_ctf,
    class_owner,
    references,
    ctf_table,
    x_base,
    y_base,
    x_frac,
    y_frac,
    z_offset,
    z_frac,
):
    slab_count = lax.axis_size("slab")
    group_count = lax.axis_size("grp")
    frame_count = images.shape[0]
    pixels = ctf_table.shape[1]
    groups_ctf = ctf_table.shape[0]
    row_count = z_offset.shape[1]
    half_cols = x_base.shape[1]
    class_count = class_owner.shape[0]
    side_cells = 2 * row_count
    band_rows = row_count // slab_count
    band_pixels = band_rows * half_cols
    z_dev = 2 * band_rows
    phase = phase_table(row_count, half_cols)
    score_scale = 2.0 / math.sqrt(2.0 * pixels)
    channel_scale = jnp.array(
        [
            1.0 / math.sqrt(frame_count * group_count),
            1.0 / math.sqrt(frame_count * group_count),
            1.0 / (frame_count * group_count),
        ],
        jnp.float32,
    )
    all_refs = lax.all_gather(references, "slab", axis=0, tiled=True)
    class_ids = jnp.arange(class_count, dtype=jnp.int32)
    owner_of = jnp.sum(
        jnp.where(image_class[:, None] == class_ids[None, :], class_owner[None, :], 0), axis=1
    )
    pick_ref = (owner_of[:, None] == jnp.arange(slab_count, dtype=jnp.int32)[None, :]).astype(
        jnp.bfloat16
    )
    ref_rows = jnp.dot(pick_ref, all_refs, preferred_element_type=jnp.float32).astype(
        jnp.bfloat16
    )
    pick_ctf = (image_ctf[:, None] == jnp.arange(groups_ctf, dtype=jnp.int32)[None, :]).astype(
        jnp.bfloat16
    )
    ctf_rows = jnp.dot(pick_ctf, ctf_table, preferred_element_type=jnp.float32).astype(
        jnp.bfloat16
    )
    stacked = align_frames(images, ctf_rows, ref_rows, phase, score_scale)
    member = (class_ids[:, None] == image_class[None, :]).astype(jnp.float32)
    partial = jnp.dot(
        member, stacked, precision=lax.Precision.HIGHEST, preferred_element_type=jnp.float32
    ).reshape(class_count, 3, pixels) * channel_scale[None, :, None]
    pieces = slab_count * group_count
    partial = partial.reshape(class_count, 3, pieces, pixels // pieces)
    piece = lax.psum_scatter(partial, ("slab", "grp"), scatter_dimension=2, tiled=True)
    band = lax.all_gather(piece, "grp", axis=2, tiled=True).reshape(
        class_count, 3, band_rows, half_cols
    )
    up = [(i, i + 1) for i in range(slab_count - 1)]
    down = [(i + 1, i) for i in range(slab_count - 1)]
    from_below = lax.ppermute(band[:, :, band_rows - 1 :], "slab", up)
    from_above = lax.ppermute(band[:, :, :1], "slab", down)
    class_bands = jnp.concatenate([from_below, band, from_above], axis=2)
    slab_index = lax.axis_index("slab")
    group_index = lax.axis_index("grp")
    offset_pad = jnp.pad(z_offset, ((0, 0), (1, 1)))
    frac_pad = jnp.pad(z_frac, ((0, 0), (1, 1)))
    rows_held = band_rows + 2
    local_offset = lax.dynamic_slice_in_dim(offset_pad, slab_index * band_rows, rows_held, 1)
    local_frac = lax.dynamic_slice_in_dim(frac_pad, slab_index * band_rows, rows_held, 1)
    row_ids = jnp.arange(rows_held, dtype=jnp.int32) + (band_rows - 1)
    band_shift = (row_ids // band_rows - 1) * z_dev - 1
    target = 2 * (row_ids % band_rows)[None, :] + local_offset + 1 + band_shift[None, :]
    plane_ids = jnp.arange(z_dev, dtype=jnp.int32)
    depth_weight = jnp.where(
        plane_ids[None, None, :] == target[:, :, None], (1.0 - local_frac)[:, :, None], 0.0
    )
    depth_weight = depth_weight + jnp.where(
        plane_ids[None, None, :] == target[:, :, None] + 1, local_frac[:, :, None], 0.0
    )
    sectioned = jnp.einsum(
        "ckra,crz->kzca",
        class_bands,
        depth_weight,
        precision=lax.Precision.HIGHEST,
    ).reshape(3 * z_dev, class_count * half_cols)
    y_rows = side_cells // group_count
    y_ids = group_index * y_rows + jnp.arange(y_rows, dtype=jnp.int32)
    row_weights = jnp.where(
        y_ids[:, None, None] == y_base[None, :, :], (1.0 - y_frac)[None, :, :], 0.0
    )
    row_weights = row_weights + jnp.where(
        y_ids[:, None, None] == y_base[None, :, :] + 1, y_frac[None, :, :], 0.0
    )
    row_weights = row_weights.astype(jnp.bfloat16).reshape(y_rows, class_count * half_cols)
    col_weights = stencil_weights(x_base, x_frac, side_cells).reshape(
        class_count * half_cols, side_cells
    )
    inserted = insert_planes(row_weights, sectioned, col_weights)
    return inserted.reshape(3, z_dev, y_rows, side_cells)


def insert_kernel(rows_ref, sec_ref, cols_ref, out_ref, lifted_ref):
    y_rows = rows_ref.shape[0]

    def body(i, carry):
        start = pl.multiple_of(i * y_rows, y_rows)
        lifted_ref[pl.ds(start, y_rows), :] = (
            rows_ref[...].astype(jnp.float32) * sec_ref[pl.ds(i, 1), :]
        ).astype(jnp.bfloat16)
        return carry

    lax.fori_loop(0, sec_ref.shape[0], body, 0)
    out_ref[...] = jnp.dot(lifted_ref[...], cols_ref[...], preferred_element_type=jnp.float32)


def insert_planes(row_weights, sectioned, col_weights):
    planes = sectioned.shape[0]
    y_rows, depth = row_weights.shape
    side = col_weights.shape[1]
    return pl.pallas_call(
        insert_kernel,
        out_shape=jax.ShapeDtypeStruct((planes * y_rows, side), jnp.float32),
        in_specs=[pl.BlockSpec(memory_space=pltpu.VMEM)] * 3,
        out_specs=pl.BlockSpec(memory_space=pltpu.VMEM),
        scratch_shapes=[pltpu.VMEM((planes * y_rows, depth), jnp.bfloat16)],
        cost_estimate=pl.CostEstimate(
            flops=2 * planes * y_rows * depth * side,
            transcendentals=0,
            bytes_accessed=2 * y_rows * depth + 4 * planes * depth + 2 * depth * side
            + 4 * planes * y_rows * side,
        ),
    )(row_weights, sectioned, col_weights)


def solution(mesh):
    in_specs = (
        P(("grp", "slab"), None),
        P(("grp", "slab")),
        P(("grp", "slab")),
        P(),
        P("slab", None),
        P(),
        P(),
        P(),
        P(),
        P(),
        P(),
        P(),
    )
    out_specs = P(None, "slab", "grp", None)
    return jax.shard_map(local, mesh=mesh, in_specs=in_specs, out_specs=out_specs, check_vma=False)
```

time: 232 us -> 579 us (2.50)
  waiting for transfers between devices: 82.2 us -> 480 us
  starting transfers between devices: 28.2 us -> 3.61 us
  other arithmetic: 34 us -> 19.3 us
  between operations: 0.37 us -> 13.6 us
  blocking collectives: 26.4 us -> 18.1 us
  local copies, waits for them, and re-layouts: 35.4 us -> 27.5 us
    reduce_scatter x0 -> x1, waiting for transfers between devices: none -> 399 us  [local(): lax.psum_scatter(partial, ('slab', 'grp'), scatter_dimension=2, tiled=True)]
    all_to_all x3 -> x0, waiting for transfers between devices: 82.2 us -> none  [the longest x1 73.1 us: local(): lax.all_to_all(outgoing, 'slab', split_axis=0, concat_axis=0, tiled=True)]
    all_gather x0 -> x1, waiting for transfers between devices: none -> 76.7 us  [local(): all_refs = lax.all_gather(references, 'slab', axis=0, tiled=True)]
    all_to_all x3 -> x0, starting transfers between devices: 28.2 us -> none  [the longest x1 12 us: local(): lax.all_to_all(details, 'slab', split_axis=0, concat_axis=0, tiled=True)]
    psum x1 -> x0, blocking collectives: 26.4 us -> none  [local(): totals = lax.psum(totals, 'grp')]
    all_gather x0 -> x1, blocking collectives: none -> 18.1 us  [local(): lax.all_gather(piece, 'grp', axis=2, tiled=True)]
    mul x0 -> x1, local copies, waits for them, and re-layouts: none -> 16.4 us  [local(): jnp.dot(member, stacked, precision=lax.Precision.HIGHEST, preferred_eleme...]
    concatenate x3 -> x0, local copies, waits for them, and re-layouts: 15.5 us -> none  [align_frames(): jnp.concatenate([weight * (frame_re * mix_re + frame_im * mix_im), weight...]
  transfers between devices with their start and end apart: 3 -> 4, of which waited for: 2 -> 3; matrix products, arithmetic and copies ran while one was open for 14% -> 1% of each run, Pallas kernels for 0% -> 0%
where the time goes in v2:
time: 579 us; the launch traced here: 578 us
  waiting for transfers between devices  480 us (83%)
  local copies, waits for them, and re-layouts  27.5 us (5%)
  other arithmetic  19.3 us (3%)
  blocking collectives  18.1 us (3%)
  between operations  13.6 us (2%)
  matrix products  11.5 us (2%)
    reduce_scatter x1, waiting for transfers between devices, local(): lax.psum_scatter(partial, ('slab', 'grp'), scatter_dimension=2, tiled=True)  399 us
    all_gather x1, waiting for transfers between devices, local(): all_refs = lax.all_gather(references, 'slab', axis=0, tiled=True)  76.7 us
    all_gather x1, blocking collectives, local(): lax.all_gather(piece, 'grp', axis=2, tiled=True)  18.1 us
    mul x1, local copies, waits for them, and re-layouts, local(): jnp.dot(member, stacked, precision=lax.Precision.HIGHEST, preferred_eleme...  16.4 us
  transfers between devices with their start and end apart: 4, of which 3 were waited for; matrix products, arithmetic and copies ran while one was open for 1% of the time, Pallas kernels for 0%

profile of v2, /device:TPU:1, one launch (start us, length us, event | category | flops | bytes accessed | tf_op | source)
XLA Modules:
  0.0 577.9 jit_solution(7837078584049342204)
XLA Ops:
  6.5 0.7 all-gather.3.cloned.1.call-update
  7.3 0.0 reduce-scatter.2.cloned.1.call-start
  7.3 0.9 select_reduce_fusion
  8.2 0.2 fusion.42
  8.4 0.3 fusion.35
  8.7 0.0 copy-start.11
  8.7 2.4 subtract_convert_fusion
  11.1 76.7 %all-gather.3.cloned.1.call-done = bf16[32,1,16384]{2,1,0:T(2,128)(2,1)} async-done(((bf16[1,1,16384]{2,1,0:T(2,128)(2,1)}), bf16[32,1,16384]{2,1,0:T(2,128)(2,1)}) %all-gather.3.cloned.1.call-update) | async-done | bytes 1048592 | tf_op jit(solution)/shard_map/all_gather | solution.py:107
  87.8 3.2 convolution_convert_fusion
  91.1 1.9 fusion.12
  93.0 0.9 fusion.64
  93.8 0.2 fusion.46
  94.0 0.0 copy-start.2
  94.0 1.6 fusion.7
  95.6 0.0 copy-start.9
  95.6 0.4 fusion.17
  96.0 0.3 copy-done.9
  96.3 3.2 fusion.1
  99.5 8.2 %reshape.253 = f32[32,3,256,32]{3,2,1,0:T(8,128)} reshape(f32[32,24576]{1,0:T(8,128)} %fusion.1) | data formatting | bytes 6291456 | tf_op jit(solution)/shard_map/reshape | solution.py:128
  107.8 11.3 %broadcast_multiply_fusion = f32[32,3,256,32]{3,2,1,0:T(8,128)} fusion(f32[32,3,256,32]{3,2,1,0:T(8,128)} %reshape.253, f32[3]{0:T(128)S(1)} %copy-done.10), kind=kLoop, calls=%fused_computation.3 | loop fusion | flops 786432 | bytes 6291468 | tf_op jit(solution)/shard_map/mul | solution.py:126
  119.1 16.4 %copy.19 = f32[32,3,256,32]{3,0,1,2:T(8,128)} copy(f32[32,3,256,32]{3,2,1,0:T(8,128)} %broadcast_multiply_fusion) | data formatting | bytes 6291456 | tf_op jit(solution)/shard_map/mul | solution.py:126
  135.5 0.0 reduce-scatter.2.cloned.1.call-update
  135.5 0.0 copy-start.8
  135.5 0.7 copy-done.3
  136.2 0.1 broadcast_in_dim.117
  136.2 0.1 broadcast_in_dim.114
  136.3 0.1 eq.145
  136.4 0.1 eq.148
  136.5 0.1 broadcast_in_dim.127
  136.5 0.1 broadcast_in_dim.124
  136.6 0.1 eq.170
  136.7 0.1 eq.174
  136.8 0.1 broadcast_add_fusion
  136.9 0.8 add_convert_fusion.2.rows_ref
  137.6 2.7 add_convert_fusion.1.cols_ref
  140.3 399.2 %reduce-scatter.2.cloned.1.call-done = f32[32,3,1,32]{3,0,1,2:T(8,128)} async-done(((f32[32,3,256,32]{3,0,1,2:T(8,128)}), f32[32,3,1,32]{3,0,1,2:T(8,128)}) %reduce-scatter.2.cloned.1.call-update) | async-done | bytes 12304 | tf_op jit(solution)/shard_map/reduce_scatter | solution.py:131
  539.5 18.1 %all_gather.7 = f32[32,3,8,32]{3,0,1,2:T(8,128)S(1)} all-gather(f32[32,3,1,32]{3,0,1,2:T(8,128)} %reduce-scatter.2.cloned.1.call-done), channel_id=1, replica_groups=mesh['grp'=8,'slab'=32] {'grp'}, dimensions={2}, use_global_device_ids=true | all-gather | bytes 110592 | tf_op jit(solution)/shard_map/all_gather | solution.py:132
  557.6 0.2 copy.20
  557.9 0.1 reshape.254
  558.0 0.1 fusion.63
  558.1 2.3 collective-permute-start
  560.4 1.3 collective-permute-start.1
  561.7 0.1 broadcast_subtract_fusion
  561.8 3.7 collective-permute-done.1
  565.5 0.7 convolution_bitcast_fusion
  566.2 0.1 copy.21
  566.3 0.8 reshape.255.sec_ref
  567.1 3.9 shard_map.127
  (29 shorter events, 0.1 us)
Async XLA Ops:
  6.5 84.5 %copy-start = (bf16[64,8192]{1,0:T(8,128)(2,1)S(1)}, bf16[64,8192]{1,0:T(8,128)(2,1)}, u32[]{:S(2)}) copy-start(bf16[64,8192]{1,0:T(8,128)(2,1)} %param.18) | copy-start | bytes 3145732
  6.5 81.3 %all-gather.3.cloned.1.call-start = ((), (), s32[]{:S(2)}) async-start(), calls=%async_computation.2 | async-start | bytes 2162688 | tf_op jit(solution)/shard_map/all_gather | solution.py:107
  7.3 532.2 %reduce-scatter.2.cloned.1.call-start = ((), (), s32[]{:S(2)}) async-start(), calls=%async_computation.1 | async-start | bytes 12632064 | tf_op jit(solution)/shard_map/reduce_scatter | solution.py:131
  8.7 82.3 %copy-start.11 = (s32[32]{0:T(128)S(1)}, s32[32]{0:T(128)}, u32[]{:S(2)}) copy-start(s32[32]{0:T(128)} %param.15) | copy-start | bytes 388
  87.8 5.1 copy-start.1
  94.0 1.6 copy-start.2
  95.6 0.7 copy-start.9
  99.5 8.3 %copy-start.10 = (f32[3]{0:T(128)S(1)}, f32[3]{0:T(128)}, u32[]{:S(2)}) copy-start(f32[3]{0:T(128)} %constant.104.clone) | copy-start | bytes 40
  135.4 0.7 copy-start.3
  135.4 0.9 copy-start.4
  135.4 1.0 copy-start.5
  135.4 1.2 copy-start.6
  135.5 1.3 copy-start.7
  135.5 426.2 %copy-start.8 = (f32[32,128]{1,0:T(8,128)S(1)}, f32[32,128]{1,0:T(8,128)}, u32[]{:S(2)}) copy-start(f32[32,128]{1,0:T(8,128)} %param.24) | copy-start | bytes 49156
  558.1 3.7 collective-permute-start
  560.4 5.1 collective-permute-start.1
Sparse Core Ops, SparseCore 0:
  10.0 77.8 all-gather.2
  135.6 403.8 reduce-scatter.1

commit v3 on v2

--- a/solution.py
+++ b/solution.py
@@ -1,3 +1,4 @@
+import functools
 import math
 
 import jax
@@ -14,16 +15,80 @@
     shift_ids = jnp.arange(SHIFTS)
     shift_rows = (shift_ids // 8 - SHIFTS // 16).astype(jnp.float32)
     shift_cols = (shift_ids % 8 - 4).astype(jnp.float32)
-    freq_rows = (jnp.arange(row_count) - row_count // 2).astype(jnp.float32)
-    freq_cols = jnp.arange(half_cols).astype(jnp.float32)
+    lanes = 128
+    per_lane_row = lanes // half_cols
+    blocks = row_count * half_cols // lanes
+    block_rows = (jnp.arange(blocks) * per_lane_row - row_count // 2).astype(jnp.float32)
+    lane_ids = jnp.arange(lanes)
+    lane_rows = (lane_ids // half_cols).astype(jnp.float32)
+    lane_cols = (lane_ids % half_cols).astype(jnp.float32)
     step = 2.0 * math.pi / row_count
-    row_angle = shift_rows[:, None] * freq_rows[None, :] * step
-    col_angle = shift_cols[:, None] * freq_cols[None, :] * step
-    cos_r, sin_r = jnp.cos(row_angle)[:, :, None], jnp.sin(row_angle)[:, :, None]
-    cos_c, sin_c = jnp.cos(col_angle)[:, None, :], jnp.sin(col_angle)[:, None, :]
-    cos_t = (cos_r * cos_c - sin_r * sin_c).reshape(SHIFTS, row_count * half_cols)
-    sin_t = (sin_r * cos_c + cos_r * sin_c).reshape(SHIFTS, row_count * half_cols)
+    block_angle = shift_rows[:, None] * block_rows[None, :] * step
+    lane_angle = (
+        shift_rows[:, None] * lane_rows[None, :] + shift_cols[:, None] * lane_cols[None, :]
+    ) * step
+    cos_b, sin_b = jnp.cos(block_angle)[:, :, None], jnp.sin(block_angle)[:, :, None]
+    cos_l, sin_l = jnp.cos(lane_angle)[:, None, :], jnp.sin(lane_angle)[:, None, :]
+    cos_t = (cos_b * cos_l - sin_b * sin_l).reshape(SHIFTS, row_count * half_cols)
+    sin_t = (sin_b * cos_l + cos_b * sin_l).reshape(SHIFTS, row_count * half_cols)
     return jnp.concatenate([cos_t, sin_t], axis=1).astype(jnp.bfloat16)
+
+
+def exchange_kernel(count, axis, other, same, x_ref, out_ref, local_sem, send_sems, recv_sems):
+    me = lax.axis_index(axis)
+    fixed = lax.axis_index(other)
+
+    def device(peer):
+        return (fixed, peer) if axis == "slab" else (peer, fixed)
+
+    def block(peer):
+        return x_ref.at[0] if same else x_ref.at[peer]
+
+    barrier = pltpu.get_barrier_semaphore()
+    for k in range(1, count):
+        pl.semaphore_signal(
+            barrier,
+            1,
+            device_id=device(lax.rem(me + k, count)),
+            device_id_type=pl.DeviceIdType.MESH,
+        )
+    pl.semaphore_wait(barrier, count - 1)
+    own = pltpu.make_async_copy(block(me), out_ref.at[me], local_sem)
+    own.start()
+    copies = []
+    for k in range(1, count):
+        peer = lax.rem(me + k, count)
+        copy = pltpu.make_async_remote_copy(
+            src_ref=block(peer),
+            dst_ref=out_ref.at[me],
+            send_sem=send_sems.at[k],
+            recv_sem=recv_sems.at[k],
+            device_id=device(peer),
+            device_id_type=pl.DeviceIdType.MESH,
+        )
+        copy.start()
+        copies.append(copy)
+    own.wait()
+    for copy in copies:
+        copy.wait_send()
+        copy.wait_recv()
+
+
+def exchange(x, axis, other, same, collective_id):
+    count = lax.axis_size(axis)
+    shape = (count,) + x.shape[1:]
+    return pl.pallas_call(
+        functools.partial(exchange_kernel, count, axis, other, same),
+        out_shape=jax.ShapeDtypeStruct(shape, x.dtype),
+        in_specs=[pl.BlockSpec(memory_space=pltpu.VMEM)],
+        out_specs=pl.BlockSpec(memory_space=pltpu.VMEM),
+        scratch_shapes=[
+            pltpu.SemaphoreType.DMA(()),
+            pltpu.SemaphoreType.DMA((count,)),
+            pltpu.SemaphoreType.DMA((count,)),
+        ],
+        compiler_params=pltpu.CompilerParams(collective_id=collective_id, has_side_effects=True),
+    )(x)
 
 
 def align_frames(frames, ctf_rows, ref_rows, phase, score_scale):
@@ -104,7 +169,10 @@
         ],
         jnp.float32,
     )
-    all_refs = lax.all_gather(references, "slab", axis=0, tiled=True)
+    lanes = 128
+    all_refs = exchange(
+        references.reshape(1, -1, lanes), "slab", "grp", True, 0
+    ).reshape(slab_count, 2 * pixels)
     class_ids = jnp.arange(class_count, dtype=jnp.int32)
     owner_of = jnp.sum(
         jnp.where(image_class[:, None] == class_ids[None, :], class_owner[None, :], 0), axis=1
@@ -126,10 +194,12 @@
     partial = jnp.dot(
         member, stacked, precision=lax.Precision.HIGHEST, preferred_element_type=jnp.float32
     ).reshape(class_count, 3, pixels) * channel_scale[None, :, None]
-    pieces = slab_count * group_count
-    partial = partial.reshape(class_count, 3, pieces, pixels // pieces)
-    piece = lax.psum_scatter(partial, ("slab", "grp"), scatter_dimension=2, tiled=True)
-    band = lax.all_gather(piece, "grp", axis=2, tiled=True).reshape(
+    by_band = partial.reshape(class_count, 3, slab_count, band_pixels).transpose(2, 0, 1, 3)
+    by_band = by_band.astype(jnp.bfloat16).reshape(slab_count, -1, lanes)
+    arrived = exchange(by_band, "slab", "grp", False, 1)
+    group_band = jnp.sum(arrived.astype(jnp.float32), axis=0).astype(jnp.bfloat16)
+    grouped = exchange(group_band[None], "grp", "slab", True, 2)
+    band = jnp.sum(grouped.astype(jnp.float32), axis=0).reshape(
         class_count, 3, band_rows, half_cols
     )
     up = [(i, i + 1) for i in range(slab_count - 1)]

time: 579 us -> 134 us (0.23)
  waiting for transfers between devices: 480 us -> 0.01 us
  Pallas kernels: 3.91 us -> 95.6 us
  blocking collectives: 18.1 us -> 0 us
  local copies, waits for them, and re-layouts: 27.5 us -> 13.4 us
  between operations: 13.6 us -> 0.31 us
  other arithmetic: 19.3 us -> 12.2 us
    reduce_scatter x1 -> x0, waiting for transfers between devices: 399 us -> none  [local(): lax.psum_scatter(partial, ('slab', 'grp'), scatter_dimension=2, tiled=True)]
    pallas_call x0 -> x3, Pallas kernels: none -> 91.7 us  [exchange(): pl.pallas_call(functools.partial(exchange_kernel, count, axis, other, sam...]
    all_gather x1 -> x0, waiting for transfers between devices: 76.7 us -> none  [local(): all_refs = lax.all_gather(references, 'slab', axis=0, tiled=True)]
    all_gather x1 -> x0, blocking collectives: 18.1 us -> none  [local(): lax.all_gather(piece, 'grp', axis=2, tiled=True)]
    mul x1 -> x0, local copies, waits for them, and re-layouts: 16.4 us -> none  [local(): jnp.dot(member, stacked, precision=lax.Precision.HIGHEST, preferred_eleme...]
    mul x1 -> x0, other arithmetic: 11.3 us -> none  [local(): jnp.dot(member, stacked, precision=lax.Precision.HIGHEST, preferred_eleme...]
  transfers between devices with their start and end apart: 4 -> 2, of which waited for: 3 -> 0; matrix products, arithmetic and copies ran while one was open for 1% -> 3% of each run, Pallas kernels for 0% -> 0%
where the time goes in v3:
time: 134 us; the launch traced here: 132 us
  Pallas kernels  95.6 us (71%)
  local copies, waits for them, and re-layouts  13.4 us (10%)
  other arithmetic  12.2 us (9%)
  matrix products  6.21 us (5%)
  starting transfers between devices  3.85 us (3%)
    pallas_call x3, Pallas kernels, exchange(): pl.pallas_call(functools.partial(exchange_kernel, count, axis, other, sam...  91.7 us
    unnamed x32, local copies, waits for them, and re-layouts  4.8 us
    pallas_call x1, Pallas kernels, insert_planes(): pl.pallas_call(insert_kernel, out_shape=jax.ShapeDtypeStruct((planes * y_...  3.91 us
    concatenate x1, local copies, waits for them, and re-layouts, phase_table(): return jnp.concatenate([cos_t, sin_t], axis=1).astype(jnp.bfloat16)  3.08 us
  transfers between devices with their start and end apart: 2, of which 0 were waited for; matrix products, arithmetic and copies ran while one was open for 3% of the time, Pallas kernels for 0%

profile of v3, /device:TPU:1, one launch (start us, length us, event | category | flops | bytes accessed | tf_op | source)
XLA Modules:
  0.0 131.6 jit_solution(11102016990314267361)
XLA Ops:
  0.0 0.3 fusion.35
  0.3 0.3 fusion.33
  0.7 2.5 %add_convert_fusion = (bf16[128,64,128]{2,1,0:T(8,128)(2,1)S(1)}, bf16[128,64,128]{2,1,0:T(8,128)(2,1)S(1)}) fusion(f32[128,128]{1,0:T(8,128)S(1)} %get-tuple-element.19, f32[128,64]{1,0:T(8,128)S(1)} %get-tuple-element.21, f32[128,128]{1,0:T(8,128)S(1)} %get-tuple-element.18, f32[128,64]{1,0:T(8,128)S(1)} %get-tuple-element.20), kind=kLoop, calls=%fused_computation.3 | loop fusion | flops 8388608 | bytes 4390912 | tf_op jit(solution)/shard_map/convert.3
  3.2 0.0 copy-start.4
  3.2 3.0 %bitcast_dynamic-update-slice_fusion.1 = bf16[128,16384]{1,0:T(8,128)(2,1)} fusion(bf16[16,8,64,128]{3,2,1,0:T(8,128)(2,1)S(1)} %bitcast.33), kind=kLoop, calls=%fused_computation.13 | loop fusion | bytes 4194304
  6.3 0.8 reduce.1
  7.1 36.0 %shard_map.127 = bf16[32,128,128]{2,1,0:T(8,128)(2,1)} custom-call(bf16[1,128,128]{2,1,0:T(8,128)(2,1)} %bitcast.36), custom_call_target="tpu_custom_call" | custom-call | tf_op jit(solution)/shard_map/pallas_call | solution.py:80
  43.1 0.0 copy-start.3
  43.1 3.1 %bitcast_dynamic-update-slice_fusion = bf16[128,16384]{1,0:T(8,128)(2,1)} fusion(bf16[128,16384]{1,0:T(8,128)(2,1)} %bitcast_dynamic-update-slice_fusion.1, bf16[16,8,64,128]{3,2,1,0:T(8,128)(2,1)S(1)} %bitcast.32), kind=kLoop, calls=%fused_computation.12 | loop fusion | bytes 4194304 | tf_op jit(solution)/shard_map/concatenate | solution.py:34
  46.2 0.2 select_reduce_fusion
  46.4 0.7 convolution_convert_fusion
  47.2 0.7 fusion.10
  47.9 0.7 copy-done.1
  48.6 1.6 %fusion.64 = (f32[32]{0:T(128)S(1)}, f32[32,128]{1,0:T(8,128)S(1)}) fusion(bf16[128,16384]{1,0:T(8,128)(2,1)S(1)} %copy-done.1, bf16[32,8192]{1,0:T(8,128)(2,1)S(1)} %get-tuple-element.12, bf16[32,8192]{1,0:T(8,128)(2,1)S(1)} %get-tuple-element.11), kind=kOutput, calls=%fused_computation.122 | convolution fusion | flops 136323040 | bytes 5259392 | tf_op jit(solution)/shard_map/np,sp->ns/dot_general | solution.py:108
  50.2 0.2 fusion.44
  50.4 0.7 fusion.45
  51.2 0.4 fusion.15
  51.6 1.7 %fusion.1 = f32[32,24576]{1,0:T(8,128)S(1)} fusion(f32[32,8192]{1,0:T(8,128)S(1)} %get-tuple-element.13, f32[32,8192]{1,0:T(8,128)S(1)} %get-tuple-element.10, f32[32,8192]{1,0:T(8,128)S(1)} %get-tuple-element.9, s32[32]{0:T(128)S(1)} %copy-done.11), kind=kOutput, calls=%fused_computation.5 | convolution fusion | flops 303563776 | bytes 6291584 | tf_op jit(solution)/shard_map/dot_general | solution.py:194
  53.3 0.0 copy-start.12
  53.3 1.0 copy.26
  54.3 0.5 fusion.7
  54.8 1.4 %copy.20 = bf16[32,32,3,256]{3,2,1,0:T(4,128)(2,1)S(1)} copy(bf16[32,32,3,256]{3,0,2,1:T(8,128)(2,1)S(1)} %fusion.7) | data formatting | bytes 3145728 | tf_op jit(solution)/shard_map/convert_element_type | solution.py:198
  56.1 2.5 %reshape.334.x_ref = bf16[32,192,128]{2,1,0:T(8,128)(2,1)} reshape(bf16[32,32,3,256]{3,2,1,0:T(4,128)(2,1)S(1)} %copy.20) | data formatting | bytes 3145728 | tf_op jit(solution)/shard_map/reshape | solution.py:198
  58.7 0.0 copy-start.9
  58.7 43.2 %shard_map.128 = bf16[32,192,128]{2,1,0:T(8,128)(2,1)} custom-call(bf16[32,192,128]{2,1,0:T(8,128)(2,1)} %reshape.334.x_ref), custom_call_target="tpu_custom_call" | custom-call | tf_op jit(solution)/shard_map/pallas_call | solution.py:80
  101.9 2.3 %reduce_sum.41 = bf16[192,128]{1,0:T(8,128)(2,1)} reduce(bf16[32,192,128]{2,1,0:T(8,128)(2,1)} %shard_map.128, bf16[]{:T(256)} %constant.129.clone.1), dimensions={0}, to_apply=%region_3.4 | reduce | flops 761856 | bytes 1622018 | tf_op jit(solution)/shard_map/reduce_sum | solution.py:200
  104.2 12.5 %shard_map.129 = bf16[8,192,128]{2,1,0:T(8,128)(2,1)} custom-call(bf16[1,192,128]{2,1,0:T(8,128)(2,1)} %bitcast.35), custom_call_target="tpu_custom_call" | custom-call | tf_op jit(solution)/shard_map/pallas_call | solution.py:80
  116.7 1.1 convert_reduce_fusion
  117.8 0.1 reshape.335
  117.9 0.1 fusion.63
  118.0 2.6 %collective-permute-start = (f32[32,3,1,64]{3,2,1,0:T(1,128)S(1)}, f32[32,3,1,64]{3,2,1,0:T(1,128)S(1)}, u32[]{:S(2)}, u32[]{:S(2)}) collective-permute-start(f32[32,3,1,64]{3,2,1,0:T(1,128)S(1)} %get-tuple-element.16), channel_id=1, source_target_pairs={{0,1},{1,2},{2,3},{3,4},{4,5},{5,6},{6,7},{7,8},{8,9},{9,10},{10,1... | collective-permute-start | bytes 73736 | tf_op jit(solution)/shard_map/ppermute | solution.py:207
  120.5 1.3 collective-permute-start.1
  121.9 0.1 broadcast_in_dim.122
  122.0 0.1 eq.146
  122.0 0.1 broadcast_in_dim.133
  122.1 0.1 eq.171
  122.2 0.1 broadcast_in_dim.119
  122.3 0.1 eq.149
  122.3 0.1 broadcast_in_dim.130
  122.4 0.1 eq.175
  122.5 0.1 broadcast_add_fusion
  122.6 2.7 %add_convert_fusion.1.cols_ref = bf16[2048,256]{1,0:T(8,128)(2,1)} fusion(f32[2048]{0:T(1024)S(1)} %broadcast_in_dim.133, s32[2048]{0:T(1024)S(1)} %eq.175, f32[2048]{0:T(1024)S(1)} %broadcast_in_dim.130, s32[2048]{0:T(1024)S(1)} %eq.171), kind=kLoop, calls=%fused_computation.14 | loop fusion | flops 3145728 | bytes 1081344 | tf_op jit(solution)/shard_map/convert_element_type | solution.py:133
  125.2 0.8 add_convert_fusion.2.rows_ref
  126.0 0.1 broadcast_subtract_fusion
  126.1 0.7 convolution_bitcast_fusion
  126.8 0.1 copy.21
  126.9 0.8 reshape.336.sec_ref
  127.7 3.9 %shard_map.130 = f32[768,256]{1,0:T(8,128)} custom-call(bf16[32,2048]{1,0:T(8,128)(2,1)} %add_convert_fusion.2.rows_ref, f32[24,2048]{1,0:T(8,128)} %reshape.336.sec_ref, bf16[2048,256]{1,0:T(8,128)(2,1)} %add_convert_fusion.1.cols_ref), custom_call_target="tpu_custom_call" | custom-call | flops 805306368 | bytes 2162688 | tf_op jit(solution)/shard_map/pallas_call | solution.py:267
  (36 shorter events, 0.1 us)
Async XLA Ops:
  0.0 47.2 %copy-start = (bf16[64,8192]{1,0:T(8,128)(2,1)S(1)}, bf16[64,8192]{1,0:T(8,128)(2,1)}, u32[]{:S(2)}) copy-start(bf16[64,8192]{1,0:T(8,128)(2,1)} %param.18) | copy-start | bytes 3145732
  3.2 3.1 %copy-start.4 = (bf16[1,16384]{1,0:T(2,128)(2,1)S(1)}, bf16[1,16384]{1,0:T(2,128)(2,1)}, u32[]{:S(2)}) copy-start(bf16[1,16384]{1,0:T(2,128)(2,1)} %param.17) | copy-start | bytes 98308
  6.3 40.0 %copy-start.11 = (s32[32]{0:T(128)S(1)}, s32[32]{0:T(128)}, u32[]{:S(2)}) copy-start(s32[32]{0:T(128)} %param.14) | copy-start | bytes 388
  6.3 40.0 %copy-start.13 = (s32[32]{0:T(128)S(1)}, s32[32]{0:T(128)}, u32[]{:S(2)}) copy-start(s32[32]{0:T(128)} %param.16) | copy-start | bytes 388
  43.1 3.3 %copy-start.2 = (bf16[32,128,128]{2,1,0:T(8,128)(2,1)S(1)}, bf16[32,128,128]{2,1,0:T(8,128)(2,1)}, u32[]{:S(2)}) copy-start(bf16[32,128,128]{2,1,0:T(8,128)(2,1)} %shard_map.127) | copy-start | bytes 3145732
  43.1 4.1 %copy-start.3 = (bf16[32,16384]{1,0:T(8,128)(2,1)S(1)}, bf16[32,16384]{1,0:T(8,128)(2,1)}, u32[]{:S(2)}) copy-start(bf16[32,16384]{1,0:T(8,128)(2,1)} %param.13) | copy-start | bytes 3145732
  43.1 4.0 %copy-start.14 = (s32[32]{0:T(128)S(1)}, s32[32]{0:T(128)}, u32[]{:S(2)}) copy-start(s32[32]{0:T(128)} %param.15) | copy-start | bytes 388
  46.4 2.2 %copy-start.1 = (bf16[128,16384]{1,0:T(8,128)(2,1)S(1)}, bf16[128,16384]{1,0:T(8,128)(2,1)}, u32[]{:S(2)}) copy-start(bf16[128,16384]{1,0:T(8,128)(2,1)} %bitcast_dynamic-update-slice_fusion) | copy-start | bytes 12582916
  53.3 1.0 copy-start.12
  58.7 63.2 %copy-start.5 = (f32[32,64]{1,0:T(8,128)S(1)}, f32[32,64]{1,0:T(8,128)}, u32[]{:S(2)}) copy-start(f32[32,64]{1,0:T(8,128)} %param.22) | copy-start | bytes 24580
  58.7 63.3 %copy-start.6 = (s32[32,64]{1,0:T(8,128)S(1)}, s32[32,64]{1,0:T(8,128)}, u32[]{:S(2)}) copy-start(s32[32,64]{1,0:T(8,128)} %param.20) | copy-start | bytes 24580
  58.7 63.3 %copy-start.7 = (f32[32,64]{1,0:T(8,128)S(1)}, f32[32,64]{1,0:T(8,128)}, u32[]{:S(2)}) copy-start(f32[32,64]{1,0:T(8,128)} %param.21) | copy-start | bytes 24580
  58.7 63.4 %copy-start.8 = (s32[32,64]{1,0:T(8,128)S(1)}, s32[32,64]{1,0:T(8,128)}, u32[]{:S(2)}) copy-start(s32[32,64]{1,0:T(8,128)} %param.19) | copy-start | bytes 24580
  58.7 63.8 %copy-start.9 = (s32[32,128]{1,0:T(8,128)S(1)}, s32[32,128]{1,0:T(8,128)}, u32[]{:S(2)}) copy-start(s32[32,128]{1,0:T(8,128)} %param.23) | copy-start | bytes 49156
  58.7 67.3 %copy-start.10 = (f32[32,128]{1,0:T(8,128)S(1)}, f32[32,128]{1,0:T(8,128)}, u32[]{:S(2)}) copy-start(f32[32,128]{1,0:T(8,128)} %param.24) | copy-start | bytes 49156
  118.0 8.1 %collective-permute-start = (f32[32,3,1,64]{3,2,1,0:T(1,128)S(1)}, f32[32,3,1,64]{3,2,1,0:T(1,128)S(1)}, u32[]{:S(2)}, u32[]{:S(2)}) collective-permute-start(f32[32,3,1,64]{3,2,1,0:T(1,128)S(1)} %get-tuple-element.16), channel_id=1, source_target_pairs={{0,1},{1,2},{2,3},{3,4},{4,5},{5,6},{6,7},{7,8},{8,9},{9,10},{10,1... | collective-permute-start | bytes 73736 | tf_op jit(solution)/shard_map/ppermute | solution.py:207
  120.5 5.5 %collective-permute-start.1 = (f32[32,3,1,64]{3,2,1,0:T(1,128)S(1)}, f32[32,3,1,64]{3,2,1,0:T(1,128)S(1)}, u32[]{:S(2)}, u32[]{:S(2)}) collective-permute-start(f32[32,3,1,64]{3,2,1,0:T(1,128)S(1)} %get-tuple-element.17), channel_id=1, source_target_pairs={{1,0},{2,1},{3,2},{4,3},{5,4},{6,5},{7,6},{8,7},{9,8},{10,9},{11,1... | collective-permute-start | bytes 73736 | tf_op jit(solution)/shard_map/ppermute | solution.py:208

commit v4 on v3

--- a/solution.py
+++ b/solution.py
@@ -34,16 +34,8 @@
     return jnp.concatenate([cos_t, sin_t], axis=1).astype(jnp.bfloat16)
 
 
-def exchange_kernel(count, axis, other, same, x_ref, out_ref, local_sem, send_sems, recv_sems):
-    me = lax.axis_index(axis)
-    fixed = lax.axis_index(other)
-
-    def device(peer):
-        return (fixed, peer) if axis == "slab" else (peer, fixed)
-
-    def block(peer):
-        return x_ref.at[0] if same else x_ref.at[peer]
-
+def exchange_kernel(count, place, same, x_ref, out_ref, local_sem, send_sems, recv_sems):
+    me, device = place()
     barrier = pltpu.get_barrier_semaphore()
     for k in range(1, count):
         pl.semaphore_signal(
@@ -53,6 +45,10 @@
             device_id_type=pl.DeviceIdType.MESH,
         )
     pl.semaphore_wait(barrier, count - 1)
+
+    def block(peer):
+        return x_ref.at[0] if same else x_ref.at[peer]
+
     own = pltpu.make_async_copy(block(me), out_ref.at[me], local_sem)
     own.start()
     copies = []
@@ -74,11 +70,25 @@
         copy.wait_recv()
 
 
-def exchange(x, axis, other, same, collective_id):
-    count = lax.axis_size(axis)
+def slab_place():
+    group = lax.axis_index("grp")
+    return lax.axis_index("slab"), lambda peer: (group, peer)
+
+
+def core_place():
+    group, slab = lax.axis_index("grp"), lax.axis_index("slab")
+    return lax.rem(group, 2), lambda peer: (group - lax.rem(group, 2) + peer, slab)
+
+
+def chip_place():
+    group, slab = lax.axis_index("grp"), lax.axis_index("slab")
+    return group // 2, lambda peer: (2 * peer + lax.rem(group, 2), slab)
+
+
+def exchange(x, count, place, same, collective_id):
     shape = (count,) + x.shape[1:]
     return pl.pallas_call(
-        functools.partial(exchange_kernel, count, axis, other, same),
+        functools.partial(exchange_kernel, count, place, same),
         out_shape=jax.ShapeDtypeStruct(shape, x.dtype),
         in_specs=[pl.BlockSpec(memory_space=pltpu.VMEM)],
         out_specs=pl.BlockSpec(memory_space=pltpu.VMEM),
@@ -170,9 +180,14 @@
         jnp.float32,
     )
     lanes = 128
-    all_refs = exchange(
-        references.reshape(1, -1, lanes), "slab", "grp", True, 0
-    ).reshape(slab_count, 2 * pixels)
+    core = lax.rem(lax.axis_index("grp"), 2)
+    ref_halves = references.reshape(2, -1, lanes)
+    my_half = lax.dynamic_slice_in_dim(ref_halves, core, 1, 0)
+    half_refs = exchange(my_half, slab_count, slab_place, True, 0)
+    both_halves = exchange(half_refs.reshape(1, -1, lanes), 2, core_place, True, 1)
+    all_refs = both_halves.reshape(2, slab_count, pixels).transpose(1, 0, 2).reshape(
+        slab_count, 2 * pixels
+    )
     class_ids = jnp.arange(class_count, dtype=jnp.int32)
     owner_of = jnp.sum(
         jnp.where(image_class[:, None] == class_ids[None, :], class_owner[None, :], 0), axis=1
@@ -194,12 +209,17 @@
     partial = jnp.dot(
         member, stacked, precision=lax.Precision.HIGHEST, preferred_element_type=jnp.float32
     ).reshape(class_count, 3, pixels) * channel_scale[None, :, None]
-    by_band = partial.reshape(class_count, 3, slab_count, band_pixels).transpose(2, 0, 1, 3)
-    by_band = by_band.astype(jnp.bfloat16).reshape(slab_count, -1, lanes)
-    arrived = exchange(by_band, "slab", "grp", False, 1)
-    group_band = jnp.sum(arrived.astype(jnp.float32), axis=0).astype(jnp.bfloat16)
-    grouped = exchange(group_band[None], "grp", "slab", True, 2)
-    band = jnp.sum(grouped.astype(jnp.float32), axis=0).reshape(
+    by_half = partial.reshape(class_count, 3, slab_count, 2, band_pixels // 2).transpose(
+        3, 2, 0, 1, 4
+    ).reshape(2, -1, lanes)
+    paired = exchange(by_half, 2, core_place, False, 2)
+    pair_sum = (paired[0] + paired[1]).astype(jnp.bfloat16).reshape(slab_count, -1, lanes)
+    arrived = exchange(pair_sum, slab_count, slab_place, False, 3)
+    chip_band = jnp.sum(arrived.astype(jnp.float32), axis=0).astype(jnp.bfloat16)
+    chips = exchange(chip_band[None], group_count // 2, chip_place, True, 4)
+    half_band = jnp.sum(chips.astype(jnp.float32), axis=0)
+    full = exchange(half_band[None], 2, core_place, True, 5)
+    band = full.reshape(2, class_count, 3, band_pixels // 2).transpose(1, 2, 0, 3).reshape(
         class_count, 3, band_rows, half_cols
     )
     up = [(i, i + 1) for i in range(slab_count - 1)]

time: 134 us -> 131 us (0.978)
  the two profiles are of different devices: /device:TPU:1 before, /device:TPU:8 now
where the time goes in v4:
time: 131 us
  Pallas kernels  77.6 us (59%)
  local copies, waits for them, and re-layouts  19.6 us (15%)
  other arithmetic  17.6 us (13%)
  starting transfers between devices  7.95 us (6%)
  matrix products  7.5 us (6%)
    pallas_call x6, Pallas kernels, exchange(): pl.pallas_call(functools.partial(exchange_kernel, count, place, same), ou...  73.7 us
    reshape x1, local copies, waits for them, and re-layouts, local(): partial = jnp.dot(member, stacked, precision=lax.Precision.HIGHEST, prefe...  5.27 us
    ppermute x1, starting transfers between devices, local(): from_above = lax.ppermute(band[:, :, :1], 'slab', down)  5.21 us
    pallas_call x1, Pallas kernels, insert_planes(): pl.pallas_call(insert_kernel, out_shape=jax.ShapeDtypeStruct((planes * y_...  3.91 us
    dot_general x1, matrix products, local(): jnp.dot(member, stacked, precision=lax.Precision.HIGHEST, preferred_eleme...  3.25 us
    convert_element_type x1, other arithmetic, local(): (paired[0] + paired[1]).astype(jnp.bfloat16).reshape(slab_count, -1, lanes)  2.94 us
    ppermute x1, starting transfers between devices, local(): from_below = lax.ppermute(band[:, :, band_rows - 1:], 'slab', up)  2.74 us
    another operation x1, other arithmetic  2.7 us
  transfers between devices with their start and end apart: 2, of which 0 were waited for; matrix products, arithmetic and copies ran while one was open for 3% of the time, Pallas kernels for 0%

profile of v4, /device:TPU:8, one launch (start us, length us, event | category | flops | bytes accessed | tf_op | source)
XLA Modules:
  0.0 130.6 jit_solution(2132878152153662388)
XLA Ops:
  0.0 1.1 reduce.1
  1.1 0.6 constant_dynamic-slice_fusion.x_ref
  1.8 23.8 %shard_map.127 = bf16[32,64,128]{2,1,0:T(8,128)(2,1)} custom-call(bf16[1,64,128]{2,1,0:T(8,128)(2,1)} %constant_dynamic-slice_fusion.x_ref), custom_call_target="tpu_custom_call" | custom-call | tf_op jit(solution)/shard_map/pallas_call | solution.py:90
  25.6 4.1 %shard_map.128 = bf16[2,2048,128]{2,1,0:T(8,128)(2,1)} custom-call(bf16[1,2048,128]{2,1,0:T(8,128)(2,1)} %bitcast.40), custom_call_target="tpu_custom_call" | custom-call | tf_op jit(solution)/shard_map/pallas_call | solution.py:90
  29.7 1.5 %reshape.347 = bf16[2,32,8192]{2,1,0:T(8,128)(2,1)S(1)} reshape(bf16[2,2048,128]{2,1,0:T(8,128)(2,1)} %shard_map.128) | data formatting | bytes 2097152 | tf_op jit(solution)/shard_map/reshape | solution.py:188
  31.2 1.1 copy.32
  32.3 0.6 copy.39
  32.9 0.3 fusion.33
  33.2 0.3 fusion.31
  33.6 2.7 %add_convert_fusion = (bf16[128,64,128]{2,1,0:T(8,128)(2,1)S(1)}, bf16[128,64,128]{2,1,0:T(8,128)(2,1)S(1)}) fusion(f32[128,128]{1,0:T(8,128)S(1)} %get-tuple-element.19, f32[128,64]{1,0:T(8,128)S(1)} %get-tuple-element.21, f32[128,128]{1,0:T(8,128)S(1)} %get-tuple-element.18, f32[128,64]{1,0:T(8,128)S(1)} %get-tuple-element.20), kind=kLoop, calls=%fused_computation.3 | loop fusion | flops 8388608 | bytes 4390912 | tf_op jit(solution)/shard_map/convert.3
  36.3 1.7 %bitcast_dynamic-update-slice_fusion.1 = bf16[128,16384]{1,0:T(8,128)(2,1)S(1)} fusion(bf16[16,8,64,128]{3,2,1,0:T(8,128)(2,1)S(1)} %bitcast.36), kind=kLoop, calls=%fused_computation.14 | loop fusion | bytes 4194304
  38.1 0.2 select_reduce_fusion
  38.3 0.5 convolution_convert_fusion
  38.7 1.7 %bitcast_dynamic-update-slice_fusion = bf16[128,16384]{1,0:T(8,128)(2,1)S(1)} fusion(bf16[128,16384]{1,0:T(8,128)(2,1)S(1)} %bitcast_dynamic-update-slice_fusion.1, bf16[16,8,64,128]{3,2,1,0:T(8,128)(2,1)S(1)} %bitcast.35), kind=kLoop, calls=%fused_computation.13 | loop fusion | bytes 4194304 | tf_op jit(solution)/shard_map/concatenate | solution.py:34
  40.5 0.7 fusion.10
  41.2 1.6 %fusion.62 = (f32[32]{0:T(128)S(1)}, f32[32,128]{1,0:T(8,128)S(1)}) fusion(bf16[128,16384]{1,0:T(8,128)(2,1)S(1)} %bitcast_dynamic-update-slice_fusion, bf16[32,8192]{1,0:T(8,128)(2,1)S(1)} %get-tuple-element.12, bf16[32,8192]{1,0:T(8,128)(2,1)S(1)} %get-tuple-element.11), kind=kOutput, calls=%fused_computation.122 | convolution fusion | flops 136323040 | bytes 5259392 | tf_op jit(solution)/shard_map/np,sp->ns/dot_general | solution.py:118
  42.8 0.2 fusion.42
  43.0 0.8 fusion.43
  43.8 0.4 fusion.15
  44.2 3.3 %fusion.1 = f32[32,24576]{1,0:T(8,128)} fusion(f32[32,8192]{1,0:T(8,128)S(1)} %get-tuple-element.13, f32[32,8192]{1,0:T(8,128)S(1)} %get-tuple-element.10, f32[32,8192]{1,0:T(8,128)S(1)} %get-tuple-element.9, s32[32]{0:T(128)S(1)} %copy-done.8), kind=kOutput, calls=%fused_computation.5 | convolution fusion | flops 303563776 | bytes 6291584 | tf_op jit(solution)/shard_map/dot_general | solution.py:209
  47.4 5.3 %reshape.349 = f32[32,3,32,2,128]{4,3,2,1,0:T(2,128)} reshape(f32[32,24576]{1,0:T(8,128)} %fusion.1) | data formatting | bytes 6291456 | tf_op jit(solution)/shard_map/reshape | solution.py:211
  52.7 2.4 %fusion.7 = f32[2,32,32,3,128]{4,1,0,3,2:T(8,128)S(1)} fusion(f32[32,3,32,2,128]{4,3,2,1,0:T(2,128)} %reshape.349, f32[3]{0:T(128)S(1)} %copy-done.9), kind=kLoop, calls=%fused_computation.12 | loop fusion | flops 786432 | bytes 6291468 | tf_op jit(solution)/shard_map/transpose | solution.py:212
  55.1 2.4 %copy.34 = f32[2,32,32,3,128]{4,0,3,2,1:T(2,128)S(1)} copy(f32[2,32,32,3,128]{4,1,0,3,2:T(8,128)S(1)} %fusion.7) | data formatting | bytes 6291456 | tf_op jit(solution)/shard_map/transpose | solution.py:212
  57.6 1.8 %copy.35.x_ref = f32[2,3072,128]{2,1,0:T(8,128)} copy(f32[2,3072,128]{2,0,1:T(2,128)S(1)} %bitcast.34) | data formatting | bytes 6291456 | tf_op jit(solution)/shard_map/reshape | solution.py:214
  59.4 7.1 %shard_map.129 = f32[2,3072,128]{2,1,0:T(8,128)} custom-call(f32[2,3072,128]{2,1,0:T(8,128)} %copy.35.x_ref), custom_call_target="tpu_custom_call" | custom-call | tf_op jit(solution)/shard_map/pallas_call | solution.py:90
  66.6 2.9 %add_convert_fusion.2 = bf16[1,3072,128]{2,1,0:T(8,128)(2,1)} fusion(f32[2,3072,128]{2,1,0:T(8,128)} %shard_map.129), kind=kLoop, calls=%fused_computation.26 | loop fusion | flops 786432 | bytes 3932160 | tf_op jit(solution)/shard_map/convert_element_type | solution.py:216
  69.6 28.1 %shard_map.130 = bf16[32,96,128]{2,1,0:T(8,128)(2,1)} custom-call(bf16[32,96,128]{2,1,0:T(8,128)(2,1)} %bitcast.39), custom_call_target="tpu_custom_call" | custom-call | tf_op jit(solution)/shard_map/pallas_call | solution.py:90
  97.7 1.9 %reduce_sum.41 = bf16[96,128]{1,0:T(8,128)(2,1)} reduce(bf16[32,96,128]{2,1,0:T(8,128)(2,1)} %shard_map.130, bf16[]{:T(256)} %constant.132.clone.1), dimensions={0}, to_apply=%region_3.4 | reduce | flops 380928 | bytes 811010 | tf_op jit(solution)/shard_map/reduce_sum | solution.py:218
  99.6 7.7 %shard_map.131 = bf16[4,96,128]{2,1,0:T(8,128)(2,1)} custom-call(bf16[1,96,128]{2,1,0:T(8,128)(2,1)} %bitcast.43), custom_call_target="tpu_custom_call" | custom-call | tf_op jit(solution)/shard_map/pallas_call | solution.py:90
  107.3 1.5 %convert_reduce_fusion = f32[96,128]{1,0:T(8,128)} fusion(bf16[4,96,128]{2,1,0:T(8,128)(2,1)} %shard_map.131), kind=kLoop, calls=%fused_computation.48 | loop fusion | flops 86016 | bytes 147456 | tf_op jit(solution)/shard_map/reduce_sum | solution.py:220
  108.9 2.7 %shard_map.132 = f32[2,96,128]{2,1,0:T(8,128)} custom-call(f32[1,96,128]{2,1,0:T(8,128)} %bitcast.42), custom_call_target="tpu_custom_call" | custom-call | tf_op jit(solution)/shard_map/pallas_call | solution.py:90
  111.6 1.0 copy.36
  112.6 0.2 reshape.352
  112.7 0.1 fusion.61
  112.8 2.7 %collective-permute-start = (f32[32,3,1,64]{3,2,1,0:T(1,128)S(1)}, f32[32,3,1,64]{3,2,1,0:T(1,128)S(1)}, u32[]{:S(2)}, u32[]{:S(2)}) collective-permute-start(f32[32,3,1,64]{3,2,1,0:T(1,128)S(1)} %get-tuple-element.16), channel_id=1, source_target_pairs={{0,1},{1,2},{2,3},{3,4},{4,5},{5,6},{6,7},{7,8},{8,9},{9,10},{10,1... | collective-permute-start | bytes 73736 | tf_op jit(solution)/shard_map/ppermute | solution.py:227
  115.6 5.2 %collective-permute-start.1 = (f32[32,3,1,64]{3,2,1,0:T(1,128)S(1)}, f32[32,3,1,64]{3,2,1,0:T(1,128)S(1)}, u32[]{:S(2)}, u32[]{:S(2)}) collective-permute-start(f32[32,3,1,64]{3,2,1,0:T(1,128)S(1)} %get-tuple-element.17), channel_id=1, source_target_pairs={{1,0},{2,1},{3,2},{4,3},{5,4},{6,5},{7,6},{8,7},{9,8},{10,9},{11,1... | collective-permute-start | bytes 73736 | tf_op jit(solution)/shard_map/ppermute | solution.py:228
  120.8 0.1 broadcast_in_dim.125
  120.9 0.1 eq.146
  121.0 0.1 broadcast_in_dim.137
  121.1 0.1 eq.171
  121.4 0.1 broadcast_add_fusion
  121.5 2.7 %add_convert_fusion.1.cols_ref = bf16[2048,256]{1,0:T(8,128)(2,1)} fusion(f32[2048]{0:T(1024)S(1)} %broadcast_in_dim.137, s32[2048]{0:T(1024)S(1)} %eq.175, f32[2048]{0:T(1024)S(1)} %broadcast_in_dim.134, s32[2048]{0:T(1024)S(1)} %eq.171), kind=kLoop, calls=%fused_computation.15 | loop fusion | flops 3145728 | bytes 1081344 | tf_op jit(solution)/shard_map/convert_element_type | solution.py:143
  124.2 0.8 add_convert_fusion.3.rows_ref
  125.0 0.1 broadcast_subtract_fusion
  125.0 0.7 convolution_bitcast_fusion
  125.8 0.1 copy.37
  125.8 0.8 reshape.353.sec_ref
  126.7 3.9 %shard_map.133 = f32[768,256]{1,0:T(8,128)} custom-call(bf16[32,2048]{1,0:T(8,128)(2,1)} %add_convert_fusion.3.rows_ref, f32[24,2048]{1,0:T(8,128)} %reshape.353.sec_ref, bf16[2048,256]{1,0:T(8,128)(2,1)} %add_convert_fusion.1.cols_ref), custom_call_target="tpu_custom_call" | custom-call | flops 805306368 | bytes 2162688 | tf_op jit(solution)/shard_map/pallas_call | solution.py:287
  (39 shorter events, 0.4 us)
Async XLA Ops:
  0.0 40.5 %copy-start = (bf16[64,8192]{1,0:T(8,128)(2,1)S(1)}, bf16[64,8192]{1,0:T(8,128)(2,1)}, u32[]{:S(2)}) copy-start(bf16[64,8192]{1,0:T(8,128)(2,1)} %param.18) | copy-start | bytes 3145732
  36.3 1.8 %copy-start.8 = (s32[32]{0:T(128)S(1)}, s32[32]{0:T(128)}, u32[]{:S(2)}) copy-start(s32[32]{0:T(128)} %param.14) | copy-start | bytes 388
  36.3 1.8 %copy-start.10 = (s32[32]{0:T(128)S(1)}, s32[32]{0:T(128)}, u32[]{:S(2)}) copy-start(s32[32]{0:T(128)} %param.16) | copy-start | bytes 388
  38.2 2.3 %copy-start.1 = (bf16[32,16384]{1,0:T(8,128)(2,1)S(1)}, bf16[32,16384]{1,0:T(8,128)(2,1)}, u32[]{:S(2)}) copy-start(bf16[32,16384]{1,0:T(8,128)(2,1)} %param.13) | copy-start | bytes 3145732
  38.3 2.3 %copy-start.11 = (s32[32]{0:T(128)S(1)}, s32[32]{0:T(128)}, u32[]{:S(2)}) copy-start(s32[32]{0:T(128)} %param.15) | copy-start | bytes 388
  47.4 5.3 %copy-start.9 = (f32[3]{0:T(128)S(1)}, f32[3]{0:T(128)}, u32[]{:S(2)}) copy-start(f32[3]{0:T(128)} %constant.133.clone) | copy-start | bytes 40
  66.6 54.3 %copy-start.2 = (f32[32,64]{1,0:T(8,128)S(1)}, f32[32,64]{1,0:T(8,128)}, u32[]{:S(2)}) copy-start(f32[32,64]{1,0:T(8,128)} %param.22) | copy-start | bytes 24580
  66.6 54.3 %copy-start.3 = (s32[32,64]{1,0:T(8,128)S(1)}, s32[32,64]{1,0:T(8,128)}, u32[]{:S(2)}) copy-start(s32[32,64]{1,0:T(8,128)} %param.20) | copy-start | bytes 24580
  66.6 54.4 %copy-start.4 = (f32[32,64]{1,0:T(8,128)S(1)}, f32[32,64]{1,0:T(8,128)}, u32[]{:S(2)}) copy-start(f32[32,64]{1,0:T(8,128)} %param.21) | copy-start | bytes 24580
  66.6 54.5 %copy-start.5 = (s32[32,64]{1,0:T(8,128)S(1)}, s32[32,64]{1,0:T(8,128)}, u32[]{:S(2)}) copy-start(s32[32,64]{1,0:T(8,128)} %param.19) | copy-start | bytes 24580
  66.6 54.8 %copy-start.6 = (s32[32,128]{1,0:T(8,128)S(1)}, s32[32,128]{1,0:T(8,128)}, u32[]{:S(2)}) copy-start(s32[32,128]{1,0:T(8,128)} %param.23) | copy-start | bytes 49156
  69.5 55.4 %copy-start.7 = (f32[32,128]{1,0:T(8,128)S(1)}, f32[32,128]{1,0:T(8,128)}, u32[]{:S(2)}) copy-start(f32[32,128]{1,0:T(8,128)} %param.24) | copy-start | bytes 49156
  112.8 12.2 %collective-permute-start = (f32[32,3,1,64]{3,2,1,0:T(1,128)S(1)}, f32[32,3,1,64]{3,2,1,0:T(1,128)S(1)}, u32[]{:S(2)}, u32[]{:S(2)}) collective-permute-start(f32[32,3,1,64]{3,2,1,0:T(1,128)S(1)} %get-tuple-element.16), channel_id=1, source_target_pairs={{0,1},{1,2},{2,3},{3,4},{4,5},{5,6},{6,7},{7,8},{8,9},{9,10},{10,1... | collective-permute-start | bytes 73736 | tf_op jit(solution)/shard_map/ppermute | solution.py:227
  115.6 9.5 %collective-permute-start.1 = (f32[32,3,1,64]{3,2,1,0:T(1,128)S(1)}, f32[32,3,1,64]{3,2,1,0:T(1,128)S(1)}, u32[]{:S(2)}, u32[]{:S(2)}) collective-permute-start(f32[32,3,1,64]{3,2,1,0:T(1,128)S(1)} %get-tuple-element.17), channel_id=1, source_target_pairs={{1,0},{2,1},{3,2},{4,3},{5,4},{6,5},{7,6},{8,7},{9,8},{10,9},{11,1... | collective-permute-start | bytes 73736 | tf_op jit(solution)/shard_map/ppermute | solution.py:228

commit v5 on v4

--- a/solution.py
+++ b/solution.py
@@ -34,7 +34,7 @@
     return jnp.concatenate([cos_t, sin_t], axis=1).astype(jnp.bfloat16)
 
 
-def exchange_kernel(count, place, same, x_ref, out_ref, local_sem, send_sems, recv_sems):
+def exchange_kernel(count, place, pick, x_ref, out_ref, local_sem, send_sems, recv_sems):
     me, device = place()
     barrier = pltpu.get_barrier_semaphore()
     for k in range(1, count):
@@ -47,7 +47,7 @@
     pl.semaphore_wait(barrier, count - 1)
 
     def block(peer):
-        return x_ref.at[0] if same else x_ref.at[peer]
+        return pick(x_ref, peer)
 
     own = pltpu.make_async_copy(block(me), out_ref.at[me], local_sem)
     own.start()
@@ -85,10 +85,23 @@
     return group // 2, lambda peer: (2 * peer + lax.rem(group, 2), slab)
 
 
-def exchange(x, count, place, same, collective_id):
-    shape = (count,) + x.shape[1:]
+def whole(x_ref, peer):
+    return x_ref.at[0]
+
+
+def row_block(x_ref, peer):
+    return x_ref.at[peer]
+
+
+def lane_block(x_ref, peer):
+    width = x_ref.shape[1] // lax.axis_size("slab")
+    return x_ref.at[:, pl.ds(pl.multiple_of(peer * width, width), width)]
+
+
+def exchange(x, count, place, pick, collective_id, block_shape):
+    shape = (count,) + block_shape
     return pl.pallas_call(
-        functools.partial(exchange_kernel, count, place, same),
+        functools.partial(exchange_kernel, count, place, pick),
         out_shape=jax.ShapeDtypeStruct(shape, x.dtype),
         in_specs=[pl.BlockSpec(memory_space=pltpu.VMEM)],
         out_specs=pl.BlockSpec(memory_space=pltpu.VMEM),
@@ -101,12 +114,12 @@
     )(x)
 
 
-def align_frames(frames, ctf_rows, ref_rows, phase, score_scale):
+def align_frames(frames, ctf_rows, ref_re, ref_im, phase, score_scale):
     pixels = ctf_rows.shape[1]
     frame_re = frames[:, :pixels].astype(jnp.float32)
     frame_im = frames[:, pixels:].astype(jnp.float32)
-    ref_re = ref_rows[:, :pixels].astype(jnp.float32)
-    ref_im = ref_rows[:, pixels:].astype(jnp.float32)
+    ref_re = ref_re.astype(jnp.float32)
+    ref_im = ref_im.astype(jnp.float32)
     weight = ctf_rows.astype(jnp.float32)
     cross_terms = jnp.concatenate(
         [
@@ -183,11 +196,10 @@
     core = lax.rem(lax.axis_index("grp"), 2)
     ref_halves = references.reshape(2, -1, lanes)
     my_half = lax.dynamic_slice_in_dim(ref_halves, core, 1, 0)
-    half_refs = exchange(my_half, slab_count, slab_place, True, 0)
-    both_halves = exchange(half_refs.reshape(1, -1, lanes), 2, core_place, True, 1)
-    all_refs = both_halves.reshape(2, slab_count, pixels).transpose(1, 0, 2).reshape(
-        slab_count, 2 * pixels
-    )
+    half_refs = exchange(my_half, slab_count, slab_place, whole, 0, my_half.shape[1:])
+    both_halves = exchange(
+        half_refs.reshape(1, -1, lanes), 2, core_place, whole, 1, (slab_count * pixels // lanes, lanes)
+    ).reshape(2, slab_count, pixels)
     class_ids = jnp.arange(class_count, dtype=jnp.int32)
     owner_of = jnp.sum(
         jnp.where(image_class[:, None] == class_ids[None, :], class_owner[None, :], 0), axis=1
@@ -195,7 +207,10 @@
     pick_ref = (owner_of[:, None] == jnp.arange(slab_count, dtype=jnp.int32)[None, :]).astype(
         jnp.bfloat16
     )
-    ref_rows = jnp.dot(pick_ref, all_refs, preferred_element_type=jnp.float32).astype(
+    ref_re = jnp.dot(pick_ref, both_halves[0], preferred_element_type=jnp.float32).astype(
+        jnp.bfloat16
+    )
+    ref_im = jnp.dot(pick_ref, both_halves[1], preferred_element_type=jnp.float32).astype(
         jnp.bfloat16
     )
     pick_ctf = (image_ctf[:, None] == jnp.arange(groups_ctf, dtype=jnp.int32)[None, :]).astype(
@@ -204,24 +219,21 @@
     ctf_rows = jnp.dot(pick_ctf, ctf_table, preferred_element_type=jnp.float32).astype(
         jnp.bfloat16
     )
-    stacked = align_frames(images, ctf_rows, ref_rows, phase, score_scale)
+    stacked = align_frames(images, ctf_rows, ref_re, ref_im, phase, score_scale)
     member = (class_ids[:, None] == image_class[None, :]).astype(jnp.float32)
     partial = jnp.dot(
         member, stacked, precision=lax.Precision.HIGHEST, preferred_element_type=jnp.float32
     ).reshape(class_count, 3, pixels) * channel_scale[None, :, None]
-    by_half = partial.reshape(class_count, 3, slab_count, 2, band_pixels // 2).transpose(
-        3, 2, 0, 1, 4
-    ).reshape(2, -1, lanes)
-    paired = exchange(by_half, 2, core_place, False, 2)
-    pair_sum = (paired[0] + paired[1]).astype(jnp.bfloat16).reshape(slab_count, -1, lanes)
-    arrived = exchange(pair_sum, slab_count, slab_place, False, 3)
+    half_rows = class_count // 2 * 3
+    by_half = partial.reshape(2, half_rows, pixels)
+    paired = exchange(by_half, 2, core_place, row_block, 2, (half_rows, pixels))
+    pair_sum = (paired[0] + paired[1]).astype(jnp.bfloat16)
+    arrived = exchange(pair_sum, slab_count, slab_place, lane_block, 3, (half_rows, band_pixels))
     chip_band = jnp.sum(arrived.astype(jnp.float32), axis=0).astype(jnp.bfloat16)
-    chips = exchange(chip_band[None], group_count // 2, chip_place, True, 4)
+    chips = exchange(chip_band[None], group_count // 2, chip_place, whole, 4, chip_band.shape)
     half_band = jnp.sum(chips.astype(jnp.float32), axis=0)
-    full = exchange(half_band[None], 2, core_place, True, 5)
-    band = full.reshape(2, class_count, 3, band_pixels // 2).transpose(1, 2, 0, 3).reshape(
-        class_count, 3, band_rows, half_cols
-    )
+    full = exchange(half_band[None], 2, core_place, whole, 5, half_band.shape)
+    band = full.reshape(class_count, 3, band_rows, half_cols)
     up = [(i, i + 1) for i in range(slab_count - 1)]
     down = [(i + 1, i) for i in range(slab_count - 1)]
     from_below = lax.ppermute(band[:, :, band_rows - 1 :], "slab", up)

time: 131 us -> 125 us (0.954)
  local copies, waits for them, and re-layouts: 19.6 us -> 12 us
    mul x0 -> x1, other arithmetic: none -> 3.91 us  [local(): jnp.dot(member, stacked, precision=lax.Precision.HIGHEST, preferred_eleme...]
    reshape x4 -> x1, local copies, waits for them, and re-layouts: 4.62 us -> 1.02 us  [local(): band = full.reshape(class_count, 3, band_rows, half_cols)]
    transpose x1 -> x0, local copies, waits for them, and re-layouts: 2.43 us -> none  [local(): partial.reshape(class_count, 3, slab_count, 2, band_pixels // 2)]
    transpose x1 -> x0, other arithmetic: 2.4 us -> none  [local(): partial.reshape(class_count, 3, slab_count, 2, band_pixels // 2)]
    reshape x1, local copies, waits for them, and re-layouts: 5.27 us -> 3.44 us  [local(): partial = jnp.dot(member, stacked, precision=lax.Precision.HIGHEST, prefe...]
where the time goes in v5:
time: 125 us
  Pallas kernels  77.7 us (62%)
  other arithmetic  18.9 us (15%)
  local copies, waits for them, and re-layouts  12 us (10%)
  starting transfers between devices  7.95 us (6%)
  matrix products  7.74 us (6%)
    pallas_call x6, Pallas kernels, exchange(): pl.pallas_call(functools.partial(exchange_kernel, count, place, pick), ou...  73.8 us
    ppermute x1, starting transfers between devices, local(): from_above = lax.ppermute(band[:, :, :1], 'slab', down)  5.21 us
    mul x1, other arithmetic, local(): jnp.dot(member, stacked, precision=lax.Precision.HIGHEST, preferred_eleme...  3.91 us
    pallas_call x1, Pallas kernels, insert_planes(): pl.pallas_call(insert_kernel, out_shape=jax.ShapeDtypeStruct((planes * y_...  3.91 us
    reshape x1, local copies, waits for them, and re-layouts, local(): partial = jnp.dot(member, stacked, precision=lax.Precision.HIGHEST, prefe...  3.44 us
    dot_general x1, matrix products, local(): jnp.dot(member, stacked, precision=lax.Precision.HIGHEST, preferred_eleme...  3.25 us
    convert_element_type x1, other arithmetic, local(): pair_sum = (paired[0] + paired[1]).astype(jnp.bfloat16)  2.92 us
    ppermute x1, starting transfers between devices, local(): from_below = lax.ppermute(band[:, :, band_rows - 1:], 'slab', up)  2.74 us
  transfers between devices with their start and end apart: 2, of which 0 were waited for; matrix products, arithmetic and copies ran while one was open for 3% of the time, Pallas kernels for 0%

profile of v5, /device:TPU:8, one launch (start us, length us, event | category | flops | bytes accessed | tf_op | source)
XLA Modules:
  0.0 124.6 jit_solution(6237661014937832593)
XLA Ops:
  0.0 1.1 reduce.1
  1.1 0.6 constant_dynamic-slice_fusion.x_ref
  1.8 23.9 %shard_map.127 = bf16[32,64,128]{2,1,0:T(8,128)(2,1)} custom-call(bf16[1,64,128]{2,1,0:T(8,128)(2,1)} %constant_dynamic-slice_fusion.x_ref), custom_call_target="tpu_custom_call" | custom-call | tf_op jit(solution)/shard_map/pallas_call | solution.py:103
  25.6 4.1 %shard_map.128 = bf16[2,2048,128]{2,1,0:T(8,128)(2,1)} custom-call(bf16[1,2048,128]{2,1,0:T(8,128)(2,1)} %bitcast.29), custom_call_target="tpu_custom_call" | custom-call | tf_op jit(solution)/shard_map/pallas_call | solution.py:103
  29.8 1.3 %fusion.64 = (bf16[1,2048,128]{2,1,0:T(8,128)(2,1)S(1)}, bf16[1,2048,128]{2,1,0:T(8,128)(2,1)S(1)}) fusion(bf16[2,2048,128]{2,1,0:T(8,128)(2,1)} %shard_map.128), kind=kLoop, calls=%fused_computation.125 | loop fusion | bytes 2097152 | tf_op jit(solution)/shard_map/slice | solution.py:210
  31.0 0.2 squeeze.9
  31.3 0.2 squeeze.8
  31.5 0.2 select_reduce_fusion
  31.7 0.4 fusion
  32.1 0.3 fusion.1
  32.4 0.3 fusion.35
  32.7 0.3 fusion.33
  33.1 2.5 %add_convert_fusion = (bf16[128,64,128]{2,1,0:T(8,128)(2,1)S(1)}, bf16[128,64,128]{2,1,0:T(8,128)(2,1)S(1)}) fusion(f32[128,128]{1,0:T(8,128)S(1)} %get-tuple-element.21, f32[128,64]{1,0:T(8,128)S(1)} %get-tuple-element.23, f32[128,128]{1,0:T(8,128)S(1)} %get-tuple-element.20, f32[128,64]{1,0:T(8,128)S(1)} %get-tuple-element.22), kind=kLoop, calls=%fused_computation.6 | loop fusion | flops 8388608 | bytes 4390912 | tf_op jit(solution)/shard_map/convert.3
  35.6 1.7 %bitcast_dynamic-update-slice_fusion.1 = bf16[128,16384]{1,0:T(8,128)(2,1)S(1)} fusion(bf16[16,8,64,128]{3,2,1,0:T(8,128)(2,1)S(1)} %bitcast.28), kind=kLoop, calls=%fused_computation.15 | loop fusion | bytes 4194304
  37.4 1.7 %bitcast_dynamic-update-slice_fusion = bf16[128,16384]{1,0:T(8,128)(2,1)S(1)} fusion(bf16[128,16384]{1,0:T(8,128)(2,1)S(1)} %bitcast_dynamic-update-slice_fusion.1, bf16[16,8,64,128]{3,2,1,0:T(8,128)(2,1)S(1)} %bitcast.27), kind=kLoop, calls=%fused_computation.14 | loop fusion | bytes 4194304 | tf_op jit(solution)/shard_map/concatenate | solution.py:34
  39.1 0.7 fusion.11
  39.9 1.6 %fusion.66 = (f32[32]{0:T(128)S(1)}, f32[32,128]{1,0:T(8,128)S(1)}) fusion(bf16[128,16384]{1,0:T(8,128)(2,1)S(1)} %bitcast_dynamic-update-slice_fusion, bf16[32,8192]{1,0:T(8,128)(2,1)S(1)} %get-tuple-element.12, bf16[32,8192]{1,0:T(8,128)(2,1)S(1)} %get-tuple-element.11), kind=kOutput, calls=%fused_computation.127 | convolution fusion | flops 136323040 | bytes 5259392 | tf_op jit(solution)/shard_map/np,sp->ns/dot_general | solution.py:131
  41.5 0.2 fusion.44
  41.7 0.7 fusion.45
  42.4 0.4 fusion.16
  42.8 3.2 %fusion.3 = f32[32,24576]{1,0:T(8,128)} fusion(f32[32,8192]{1,0:T(8,128)S(1)} %get-tuple-element.13, f32[32,8192]{1,0:T(8,128)S(1)} %get-tuple-element.10, f32[32,8192]{1,0:T(8,128)S(1)} %get-tuple-element.9, s32[32]{0:T(128)S(1)} %copy-done.9), kind=kOutput, calls=%fused_computation.8 | convolution fusion | flops 303563776 | bytes 6291584 | tf_op jit(solution)/shard_map/dot_general | solution.py:224
  46.1 3.4 %reshape.339 = f32[2,48,8192]{2,1,0:T(8,128)} reshape(f32[32,24576]{1,0:T(8,128)} %fusion.3) | data formatting | bytes 6291456 | tf_op jit(solution)/shard_map/reshape | solution.py:226
  49.5 0.1 mul.303
  49.6 3.9 %broadcast_multiply_fusion.x_ref = f32[2,48,8192]{2,1,0:T(8,128)} fusion(f32[2,48,8192]{2,1,0:T(8,128)} %reshape.339, f32[48]{0:T(128)S(1)} %mul.303), kind=kLoop, calls=%fused_computation.28 | loop fusion | flops 786432 | bytes 6291648 | tf_op jit(solution)/shard_map/mul | solution.py:224
  53.5 7.3 %shard_map.129 = f32[2,48,8192]{2,1,0:T(8,128)} custom-call(f32[2,48,8192]{2,1,0:T(8,128)} %broadcast_multiply_fusion.x_ref), custom_call_target="tpu_custom_call" | custom-call | tf_op jit(solution)/shard_map/pallas_call | solution.py:103
  60.8 2.9 %fusion.22.x_ref = bf16[48,8192]{1,0:T(8,128)(2,1)} fusion(f32[2,48,8192]{2,1,0:T(8,128)} %shard_map.129), kind=kLoop, calls=%fused_computation.44 | loop fusion | flops 786432 | bytes 3932160 | tf_op jit(solution)/shard_map/convert_element_type | solution.py:230
  63.8 28.1 %shard_map.130 = bf16[32,48,256]{2,1,0:T(8,128)(2,1)} custom-call(bf16[48,8192]{1,0:T(8,128)(2,1)} %fusion.22.x_ref), custom_call_target="tpu_custom_call" | custom-call | tf_op jit(solution)/shard_map/pallas_call | solution.py:103
  91.9 1.9 %reduce_sum.41 = bf16[48,256]{1,0:T(8,128)(2,1)} reduce(bf16[32,48,256]{2,1,0:T(8,128)(2,1)} %shard_map.130, bf16[]{:T(256)} %constant.132.clone.1), dimensions={0}, to_apply=%region_3.4 | reduce | flops 380928 | bytes 811010 | tf_op jit(solution)/shard_map/reduce_sum | solution.py:232
  93.8 7.7 %shard_map.131 = bf16[4,48,256]{2,1,0:T(8,128)(2,1)} custom-call(bf16[1,48,256]{2,1,0:T(8,128)(2,1)} %bitcast.31), custom_call_target="tpu_custom_call" | custom-call | tf_op jit(solution)/shard_map/pallas_call | solution.py:103
  101.5 1.5 %convert_reduce_fusion = f32[48,256]{1,0:T(8,128)} fusion(bf16[4,48,256]{2,1,0:T(8,128)(2,1)} %shard_map.131), kind=kLoop, calls=%fused_computation.51 | loop fusion | flops 86016 | bytes 147456 | tf_op jit(solution)/shard_map/reduce_sum | solution.py:234
  103.0 2.7 %shard_map.132 = f32[2,48,256]{2,1,0:T(8,128)} custom-call(f32[1,48,256]{2,1,0:T(8,128)} %bitcast.30), custom_call_target="tpu_custom_call" | custom-call | tf_op jit(solution)/shard_map/pallas_call | solution.py:103
  105.8 1.0 reshape.340
  106.8 0.1 fusion.65
  106.9 2.7 %collective-permute-start = (f32[32,3,1,64]{3,2,1,0:T(1,128)S(1)}, f32[32,3,1,64]{3,2,1,0:T(1,128)S(1)}, u32[]{:S(2)}, u32[]{:S(2)}) collective-permute-start(f32[32,3,1,64]{3,2,1,0:T(1,128)S(1)} %get-tuple-element.18), channel_id=1, source_target_pairs={{0,1},{1,2},{2,3},{3,4},{4,5},{5,6},{6,7},{7,8},{8,9},{9,10},{10,1... | collective-permute-start | bytes 73736 | tf_op jit(solution)/shard_map/ppermute | solution.py:239
  109.6 5.2 %collective-permute-start.1 = (f32[32,3,1,64]{3,2,1,0:T(1,128)S(1)}, f32[32,3,1,64]{3,2,1,0:T(1,128)S(1)}, u32[]{:S(2)}, u32[]{:S(2)}) collective-permute-start(f32[32,3,1,64]{3,2,1,0:T(1,128)S(1)} %get-tuple-element.19), channel_id=1, source_target_pairs={{1,0},{2,1},{3,2},{4,3},{5,4},{6,5},{7,6},{8,7},{9,8},{10,9},{11,1... | collective-permute-start | bytes 73736 | tf_op jit(solution)/shard_map/ppermute | solution.py:240
  114.9 0.1 broadcast_in_dim.125
  115.0 0.1 eq.146
  115.1 0.1 broadcast_in_dim.137
  115.1 0.1 eq.171
  115.2 0.1 broadcast_in_dim.122
  115.5 0.1 broadcast_add_fusion
  115.6 2.6 %add_convert_fusion.1.cols_ref = bf16[2048,256]{1,0:T(8,128)(2,1)} fusion(f32[2048]{0:T(1024)S(1)} %broadcast_in_dim.137, s32[2048]{0:T(1024)S(1)} %eq.175, f32[2048]{0:T(1024)S(1)} %broadcast_in_dim.134, s32[2048]{0:T(1024)S(1)} %eq.171), kind=kLoop, calls=%fused_computation.16 | loop fusion | flops 3145728 | bytes 1081344 | tf_op jit(solution)/shard_map/convert_element_type | solution.py:156
  118.2 0.8 add_convert_fusion.3.rows_ref
  119.0 0.1 broadcast_subtract_fusion
  119.1 0.7 convolution_bitcast_fusion
  119.8 0.1 copy.16
  119.9 0.8 reshape.341.sec_ref
  120.7 3.9 %shard_map.133 = f32[768,256]{1,0:T(8,128)} custom-call(bf16[32,2048]{1,0:T(8,128)(2,1)} %add_convert_fusion.3.rows_ref, f32[24,2048]{1,0:T(8,128)} %reshape.341.sec_ref, bf16[2048,256]{1,0:T(8,128)(2,1)} %add_convert_fusion.1.cols_ref), custom_call_target="tpu_custom_call" | custom-call | flops 805306368 | bytes 2162688 | tf_op jit(solution)/shard_map/pallas_call | solution.py:299
  (39 shorter events, 0.3 us)
Async XLA Ops:
  0.0 39.1 %copy-start = (bf16[64,8192]{1,0:T(8,128)(2,1)S(1)}, bf16[64,8192]{1,0:T(8,128)(2,1)}, u32[]{:S(2)}) copy-start(bf16[64,8192]{1,0:T(8,128)(2,1)} %param.18) | copy-start | bytes 3145732
  1.8 29.7 %copy-start.9 = (s32[32]{0:T(128)S(1)}, s32[32]{0:T(128)}, u32[]{:S(2)}) copy-start(s32[32]{0:T(128)} %param.14) | copy-start | bytes 388
  1.8 29.8 %copy-start.11 = (s32[32]{0:T(128)S(1)}, s32[32]{0:T(128)}, u32[]{:S(2)}) copy-start(s32[32]{0:T(128)} %param.16) | copy-start | bytes 388
  37.3 1.8 %copy-start.1 = (bf16[32,16384]{1,0:T(8,128)(2,1)S(1)}, bf16[32,16384]{1,0:T(8,128)(2,1)}, u32[]{:S(2)}) copy-start(bf16[32,16384]{1,0:T(8,128)(2,1)} %param.13) | copy-start | bytes 3145732
  37.3 1.8 %copy-start.8 = (s32[32]{0:T(128)S(1)}, s32[32]{0:T(128)}, u32[]{:S(2)}) copy-start(s32[32]{0:T(128)} %param.15) | copy-start | bytes 388
  46.1 3.4 %copy-start.10 = (f32[3]{0:T(128)S(1)}, f32[3]{0:T(128)}, u32[]{:S(2)}) copy-start(f32[3]{0:T(128)} %constant.133.clone) | copy-start | bytes 40
  60.8 54.1 %copy-start.2 = (f32[32,64]{1,0:T(8,128)S(1)}, f32[32,64]{1,0:T(8,128)}, u32[]{:S(2)}) copy-start(f32[32,64]{1,0:T(8,128)} %param.22) | copy-start | bytes 24580
  60.8 54.2 %copy-start.3 = (s32[32,64]{1,0:T(8,128)S(1)}, s32[32,64]{1,0:T(8,128)}, u32[]{:S(2)}) copy-start(s32[32,64]{1,0:T(8,128)} %param.20) | copy-start | bytes 24580
  60.8 54.2 %copy-start.4 = (f32[32,64]{1,0:T(8,128)S(1)}, f32[32,64]{1,0:T(8,128)}, u32[]{:S(2)}) copy-start(f32[32,64]{1,0:T(8,128)} %param.21) | copy-start | bytes 24580
  60.8 54.3 %copy-start.5 = (s32[32,64]{1,0:T(8,128)S(1)}, s32[32,64]{1,0:T(8,128)}, u32[]{:S(2)}) copy-start(s32[32,64]{1,0:T(8,128)} %param.19) | copy-start | bytes 24580
  60.8 54.7 %copy-start.6 = (s32[32,128]{1,0:T(8,128)S(1)}, s32[32,128]{1,0:T(8,128)}, u32[]{:S(2)}) copy-start(s32[32,128]{1,0:T(8,128)} %param.23) | copy-start | bytes 49156
  63.8 55.2 %copy-start.7 = (f32[32,128]{1,0:T(8,128)S(1)}, f32[32,128]{1,0:T(8,128)}, u32[]{:S(2)}) copy-start(f32[32,128]{1,0:T(8,128)} %param.24) | copy-start | bytes 49156
  106.9 12.2 %collective-permute-start = (f32[32,3,1,64]{3,2,1,0:T(1,128)S(1)}, f32[32,3,1,64]{3,2,1,0:T(1,128)S(1)}, u32[]{:S(2)}, u32[]{:S(2)}) collective-permute-start(f32[32,3,1,64]{3,2,1,0:T(1,128)S(1)} %get-tuple-element.18), channel_id=1, source_target_pairs={{0,1},{1,2},{2,3},{3,4},{4,5},{5,6},{6,7},{7,8},{8,9},{9,10},{10,1... | collective-permute-start | bytes 73736 | tf_op jit(solution)/shard_map/ppermute | solution.py:239
  109.6 9.4 %collective-permute-start.1 = (f32[32,3,1,64]{3,2,1,0:T(1,128)S(1)}, f32[32,3,1,64]{3,2,1,0:T(1,128)S(1)}, u32[]{:S(2)}, u32[]{:S(2)}) collective-permute-start(f32[32,3,1,64]{3,2,1,0:T(1,128)S(1)} %get-tuple-element.19), channel_id=1, source_target_pairs={{1,0},{2,1},{3,2},{4,3},{5,4},{6,5},{7,6},{8,7},{9,8},{10,9},{11,1... | collective-permute-start | bytes 73736 | tf_op jit(solution)/shard_map/ppermute | solution.py:240

commit v6 on v5

--- a/solution.py
+++ b/solution.py
@@ -34,7 +34,10 @@
     return jnp.concatenate([cos_t, sin_t], axis=1).astype(jnp.bfloat16)
 
 
-def exchange_kernel(count, place, pick, x_ref, out_ref, local_sem, send_sems, recv_sems):
+def exchange_kernel(count, place, picks, *refs):
+    parts = len(picks)
+    x_refs, out_refs = refs[:parts], refs[parts : 2 * parts]
+    local_sems, send_sems, recv_sems = refs[2 * parts :]
     me, device = place()
     barrier = pltpu.get_barrier_semaphore()
     for k in range(1, count):
@@ -45,26 +48,25 @@
             device_id_type=pl.DeviceIdType.MESH,
         )
     pl.semaphore_wait(barrier, count - 1)
-
-    def block(peer):
-        return pick(x_ref, peer)
-
-    own = pltpu.make_async_copy(block(me), out_ref.at[me], local_sem)
-    own.start()
-    copies = []
-    for k in range(1, count):
-        peer = lax.rem(me + k, count)
-        copy = pltpu.make_async_remote_copy(
-            src_ref=block(peer),
-            dst_ref=out_ref.at[me],
-            send_sem=send_sems.at[k],
-            recv_sem=recv_sems.at[k],
-            device_id=device(peer),
-            device_id_type=pl.DeviceIdType.MESH,
-        )
-        copy.start()
-        copies.append(copy)
-    own.wait()
+    owns, copies = [], []
+    for part, (pick, x_ref, out_ref) in enumerate(zip(picks, x_refs, out_refs)):
+        own = pltpu.make_async_copy(pick(x_ref, me), out_ref.at[me], local_sems.at[part])
+        own.start()
+        owns.append(own)
+        for k in range(1, count):
+            peer = lax.rem(me + k, count)
+            copy = pltpu.make_async_remote_copy(
+                src_ref=pick(x_ref, peer),
+                dst_ref=out_ref.at[me],
+                send_sem=send_sems.at[part, k],
+                recv_sem=recv_sems.at[part, k],
+                device_id=device(peer),
+                device_id_type=pl.DeviceIdType.MESH,
+            )
+            copy.start()
+            copies.append(copy)
+    for own in owns:
+        own.wait()
     for copy in copies:
         copy.wait_send()
         copy.wait_recv()
@@ -80,9 +82,9 @@
     return lax.rem(group, 2), lambda peer: (group - lax.rem(group, 2) + peer, slab)
 
 
-def chip_place():
-    group, slab = lax.axis_index("grp"), lax.axis_index("slab")
-    return group // 2, lambda peer: (2 * peer + lax.rem(group, 2), slab)
+def group_place():
+    slab = lax.axis_index("slab")
+    return lax.axis_index("grp"), lambda peer: (peer, slab)
 
 
 def whole(x_ref, peer):
@@ -98,20 +100,26 @@
     return x_ref.at[:, pl.ds(pl.multiple_of(peer * width, width), width)]
 
 
+def exchange_many(xs, count, place, picks, collective_id, block_shapes):
+    parts = len(xs)
+    return pl.pallas_call(
+        functools.partial(exchange_kernel, count, place, tuple(picks)),
+        out_shape=[
+            jax.ShapeDtypeStruct((count,) + shape, x.dtype) for x, shape in zip(xs, block_shapes)
+        ],
+        in_specs=[pl.BlockSpec(memory_space=pltpu.VMEM)] * parts,
+        out_specs=[pl.BlockSpec(memory_space=pltpu.VMEM)] * parts,
+        scratch_shapes=[
+            pltpu.SemaphoreType.DMA((parts,)),
+            pltpu.SemaphoreType.DMA((parts, count)),
+            pltpu.SemaphoreType.DMA((parts, count)),
+        ],
+        compiler_params=pltpu.CompilerParams(collective_id=collective_id, has_side_effects=True),
+    )(*xs)
+
+
 def exchange(x, count, place, pick, collective_id, block_shape):
-    shape = (count,) + block_shape
-    return pl.pallas_call(
-        functools.partial(exchange_kernel, count, place, pick),
-        out_shape=jax.ShapeDtypeStruct(shape, x.dtype),
-        in_specs=[pl.BlockSpec(memory_space=pltpu.VMEM)],
-        out_specs=pl.BlockSpec(memory_space=pltpu.VMEM),
-        scratch_shapes=[
-            pltpu.SemaphoreType.DMA(()),
-            pltpu.SemaphoreType.DMA((count,)),
-            pltpu.SemaphoreType.DMA((count,)),
-        ],
-        compiler_params=pltpu.CompilerParams(collective_id=collective_id, has_side_effects=True),
-    )(x)
+    return exchange_many([x], count, place, [pick], collective_id, [block_shape])[0]
 
 
 def align_frames(frames, ctf_rows, ref_re, ref_im, phase, score_scale):
@@ -139,7 +147,6 @@
         [
             weight * (frame_re * mix_re + frame_im * mix_im),
             weight * (frame_im * mix_re - frame_re * mix_im),
-            weight * weight,
         ],
         axis=1,
     )
@@ -223,23 +230,64 @@
     member = (class_ids[:, None] == image_class[None, :]).astype(jnp.float32)
     partial = jnp.dot(
         member, stacked, precision=lax.Precision.HIGHEST, preferred_element_type=jnp.float32
-    ).reshape(class_count, 3, pixels) * channel_scale[None, :, None]
-    half_rows = class_count // 2 * 3
+    ) * channel_scale[0]
+    half_rows = class_count // 2 * 2
     by_half = partial.reshape(2, half_rows, pixels)
-    paired = exchange(by_half, 2, core_place, row_block, 2, (half_rows, pixels))
+    class_hits = (class_ids[:, None] == image_class[None, :]).astype(jnp.bfloat16)
+    ctf_hits = (image_ctf[:, None] == jnp.arange(groups_ctf, dtype=jnp.int32)[None, :]).astype(
+        jnp.bfloat16
+    )
+    counts = jnp.dot(class_hits, ctf_hits, preferred_element_type=jnp.float32)
+    paired, paired_counts = exchange_many(
+        [by_half, counts[None]],
+        2,
+        core_place,
+        [row_block, whole],
+        2,
+        [(half_rows, pixels), counts.shape],
+    )
     pair_sum = (paired[0] + paired[1]).astype(jnp.bfloat16)
-    arrived = exchange(pair_sum, slab_count, slab_place, lane_block, 3, (half_rows, band_pixels))
+    arrived, arrived_counts = exchange_many(
+        [pair_sum, jnp.sum(paired_counts, axis=0)[None]],
+        slab_count,
+        slab_place,
+        [lane_block, whole],
+        3,
+        [(half_rows, band_pixels), counts.shape],
+    )
     chip_band = jnp.sum(arrived.astype(jnp.float32), axis=0).astype(jnp.bfloat16)
-    chips = exchange(chip_band[None], group_count // 2, chip_place, whole, 4, chip_band.shape)
-    half_band = jnp.sum(chips.astype(jnp.float32), axis=0)
-    full = exchange(half_band[None], 2, core_place, whole, 5, half_band.shape)
-    band = full.reshape(class_count, 3, band_rows, half_cols)
+    groups, group_counts = exchange_many(
+        [chip_band[None], jnp.sum(arrived_counts, axis=0)[None]],
+        group_count,
+        group_place,
+        [whole, whole],
+        4,
+        [chip_band.shape, counts.shape],
+    )
+    band = jnp.sum(
+        groups.astype(jnp.float32).reshape(group_count // 2, 2, half_rows, band_pixels), axis=0
+    ).reshape(class_count, 2, band_rows, half_cols)
+    total_counts = jnp.sum(
+        group_counts.reshape(group_count // 2, 2, class_count, groups_ctf)[:, 0], axis=0
+    )
     up = [(i, i + 1) for i in range(slab_count - 1)]
     down = [(i + 1, i) for i in range(slab_count - 1)]
     from_below = lax.ppermute(band[:, :, band_rows - 1 :], "slab", up)
     from_above = lax.ppermute(band[:, :, :1], "slab", down)
-    class_bands = jnp.concatenate([from_below, band, from_above], axis=2)
+    data_bands = jnp.concatenate([from_below, band, from_above], axis=2)
     slab_index = lax.axis_index("slab")
+    ctf_sq = jnp.pad(
+        jnp.square(ctf_table.astype(jnp.float32)), ((0, 0), (half_cols, half_cols))
+    )
+    window = lax.dynamic_slice_in_dim(
+        ctf_sq, slab_index * band_pixels, band_pixels + 2 * half_cols, 1
+    )
+    weight_rows = jnp.dot(
+        total_counts, window, precision=lax.Precision.HIGHEST, preferred_element_type=jnp.float32
+    ) * channel_scale[2]
+    class_bands = jnp.concatenate(
+        [data_bands, weight_rows.reshape(class_count, 1, band_rows + 2, half_cols)], axis=1
+    )
     group_index = lax.axis_index("grp")
     offset_pad = jnp.pad(z_offset, ((0, 0), (1, 1)))
     frac_pad = jnp.pad(z_frac, ((0, 0), (1, 1)))

time: 125 us -> 124 us (level)
  the two profiles are of different devices: /device:TPU:8 before, /device:TPU:1 now
where the time goes in v6:
time: 124 us; the launch traced here: 121 us
  Pallas kernels  83.4 us (67%)
  other arithmetic  15.3 us (12%)
  local copies, waits for them, and re-layouts  10.5 us (8%)
  matrix products  7.4 us (6%)
  starting transfers between devices  4.39 us (4%)
    pallas_call x5, Pallas kernels, exchange_many(): pl.pallas_call(functools.partial(exchange_kernel, count, place, tuple(pic...  79.5 us
    pallas_call x1, Pallas kernels, insert_planes(): pl.pallas_call(insert_kernel, out_shape=jax.ShapeDtypeStruct((planes * y_...  3.91 us
    ppermute x1, starting transfers between devices, local(): from_below = lax.ppermute(band[:, :, band_rows - 1:], 'slab', up)  2.98 us
    convert_element_type x1, other arithmetic, stencil_weights(): return dense_weight.astype(jnp.bfloat16)  2.66 us
    unnamed x29, local copies, waits for them, and re-layouts  2.6 us
    another operation x1, other arithmetic  2.52 us
  transfers between devices with their start and end apart: 2, of which 0 were waited for; matrix products, arithmetic and copies ran while one was open for 4% of the time, Pallas kernels for 0%

profile of v6, /device:TPU:1, one launch (start us, length us, event | category | flops | bytes accessed | tf_op | source)
XLA Modules:
  0.0 121.5 jit_solution(10011319899544851162)
XLA Ops:
  0.0 0.8 copy-done
  0.8 0.2 reduce.2
  1.0 0.6 constant_dynamic-slice_fusion.refs_0_
  1.6 24.5 %shard_map.127 = bf16[32,64,128]{2,1,0:T(8,128)(2,1)} custom-call(bf16[1,64,128]{2,1,0:T(8,128)(2,1)} %constant_dynamic-slice_fusion.refs_0_), custom_call_target="tpu_custom_call" | custom-call | tf_op jit(solution)/shard_map/pallas_call | solution.py:105
  26.1 5.5 %shard_map.128 = bf16[2,2048,128]{2,1,0:T(8,128)(2,1)} custom-call(bf16[1,2048,128]{2,1,0:T(8,128)(2,1)} %bitcast.37), custom_call_target="tpu_custom_call" | custom-call | tf_op jit(solution)/shard_map/pallas_call | solution.py:105
  31.7 1.3 %fusion.67 = (bf16[1,2048,128]{2,1,0:T(8,128)(2,1)S(1)}, bf16[1,2048,128]{2,1,0:T(8,128)(2,1)S(1)}) fusion(bf16[2,2048,128]{2,1,0:T(8,128)(2,1)} %shard_map.128), kind=kLoop, calls=%fused_computation.133 | loop fusion | bytes 2097152 | tf_op jit(solution)/shard_map/slice | solution.py:217
  32.9 0.2 squeeze.16
  33.2 0.2 squeeze.15
  33.4 0.2 select_reduce_fusion
  33.6 0.3 fusion
  33.9 0.3 fusion.1
  34.3 0.3 fusion.34
  34.6 0.3 fusion.32
  35.0 2.5 %add_convert_fusion = (bf16[128,64,128]{2,1,0:T(8,128)(2,1)S(1)}, bf16[128,64,128]{2,1,0:T(8,128)(2,1)S(1)}) fusion(f32[128,128]{1,0:T(8,128)S(1)} %get-tuple-element.32, f32[128,64]{1,0:T(8,128)S(1)} %get-tuple-element.34, f32[128,128]{1,0:T(8,128)S(1)} %get-tuple-element.31, f32[128,64]{1,0:T(8,128)S(1)} %get-tuple-element.33), kind=kLoop, calls=%fused_computation.7 | loop fusion | flops 8388608 | bytes 4390912 | tf_op jit(solution)/shard_map/convert.4
  37.5 1.7 %bitcast_dynamic-update-slice_fusion.1 = bf16[128,16384]{1,0:T(8,128)(2,1)S(1)} fusion(bf16[16,8,64,128]{3,2,1,0:T(8,128)(2,1)S(1)} %bitcast.36), kind=kLoop, calls=%fused_computation.11 | loop fusion | bytes 4194304
  39.2 0.8 convolution_bitcast_fusion.1.refs_1_
  40.0 1.7 %bitcast_dynamic-update-slice_fusion = bf16[128,16384]{1,0:T(8,128)(2,1)S(1)} fusion(bf16[128,16384]{1,0:T(8,128)(2,1)S(1)} %bitcast_dynamic-update-slice_fusion.1, bf16[16,8,64,128]{3,2,1,0:T(8,128)(2,1)S(1)} %bitcast.35), kind=kLoop, calls=%fused_computation.10 | loop fusion | bytes 4194304 | tf_op jit(solution)/shard_map/concatenate | solution.py:34
  41.8 0.7 fusion.8
  42.5 1.6 %fusion.69 = (f32[32]{0:T(128)S(1)}, f32[32,128]{1,0:T(8,128)S(1)}) fusion(bf16[128,16384]{1,0:T(8,128)(2,1)S(1)} %bitcast_dynamic-update-slice_fusion, bf16[32,8192]{1,0:T(8,128)(2,1)S(1)} %get-tuple-element.24, bf16[32,8192]{1,0:T(8,128)(2,1)S(1)} %get-tuple-element.23), kind=kOutput, calls=%fused_computation.135 | convolution fusion | flops 136323040 | bytes 5259392 | tf_op jit(solution)/shard_map/np,sp->ns/dot_general | solution.py:139
  44.1 0.2 fusion.43
  44.3 0.7 fusion.44
  45.1 0.3 fusion.13
  45.4 1.1 convolution_multiply_fusion
  46.6 1.5 %reshape.346.refs_0_ = f32[2,32,8192]{2,1,0:T(8,128)} reshape(f32[32,16384]{1,0:T(8,128)S(1)} %convolution_multiply_fusion) | data formatting | bytes 4194304 | tf_op jit(solution)/shard_map/reshape | solution.py:235
  48.1 5.8 %shard_map.129 = (f32[2,32,8192]{2,1,0:T(8,128)}, f32[2,32,64]{2,1,0:T(8,128)}) custom-call(f32[2,32,8192]{2,1,0:T(8,128)} %reshape.346.refs_0_, f32[1,32,64]{2,1,0:T(8,128)} %convolution_bitcast_fusion.1.refs_1_), custom_call_target="tpu_custom_call" | custom-call | tf_op jit(solution)/shard_map/pallas_call | solution.py:105
  53.9 2.4 %fusion.19.refs_0_ = bf16[32,8192]{1,0:T(8,128)(2,1)} fusion(f32[2,32,8192]{2,1,0:T(8,128)} %get-tuple-element.11), kind=kLoop, calls=%fused_computation.45 | loop fusion | flops 524288 | bytes 2621440 | tf_op jit(solution)/shard_map/convert_element_type | solution.py:249
  56.3 0.6 reduce_sum.68
  56.9 33.5 %shard_map.130 = (bf16[32,32,256]{2,1,0:T(8,128)(2,1)}, f32[32,32,64]{2,1,0:T(8,128)}) custom-call(bf16[32,8192]{1,0:T(8,128)(2,1)} %fusion.19.refs_0_, f32[1,32,64]{2,1,0:T(8,128)} %bitcast.41), custom_call_target="tpu_custom_call" | custom-call | tf_op jit(solution)/shard_map/pallas_call | solution.py:105
  90.4 1.7 %reduce_sum.70 = f32[32,64]{1,0:T(8,128)} reduce(f32[32,32,64]{2,1,0:T(8,128)} %get-tuple-element.14, f32[]{:T(128)} %constant.114.clone.1), dimensions={0}, to_apply=%region_5.6 | reduce | flops 63488 | bytes 270340 | tf_op jit(solution)/shard_map/reduce_sum | solution.py:260
  92.2 1.8 %reduce_sum.69 = bf16[32,256]{1,0:T(8,128)(2,1)} reduce(bf16[32,32,256]{2,1,0:T(8,128)(2,1)} %get-tuple-element.13, bf16[]{:T(256)} %constant.134.clone.1), dimensions={0}, to_apply=%region_4.5 | reduce | flops 253952 | bytes 540674 | tf_op jit(solution)/shard_map/reduce_sum | solution.py:258
  93.9 10.3 %shard_map.131 = (bf16[8,32,256]{2,1,0:T(8,128)(2,1)}, f32[8,32,64]{2,1,0:T(8,128)}) custom-call(bf16[1,32,256]{2,1,0:T(8,128)(2,1)} %bitcast.43, f32[1,32,64]{2,1,0:T(8,128)} %bitcast.42), custom_call_target="tpu_custom_call" | custom-call | tf_op jit(solution)/shard_map/pallas_call | solution.py:105
  104.2 1.0 convert_reduce_fusion
  105.2 0.1 reshape.349
  105.3 0.7 fusion.68
  106.0 3.0 %collective-permute-start = (f32[32,2,1,64]{3,2,1,0:T(1,128)}, f32[32,2,1,64]{3,2,1,0:T(1,128)}, u32[]{:S(2)}, u32[]{:S(2)}) collective-permute-start(f32[32,2,1,64]{3,2,1,0:T(1,128)} %get-tuple-element.29), channel_id=1, source_target_pairs={{0,1},{1,2},{2,3},{3,4},{4,5},{5,6},{6,7},{7,8},{8,9},{9,10},{10,1... | collective-permute-start | bytes 49160 | tf_op jit(solution)/shard_map/ppermute | solution.py:275
  109.0 1.4 %collective-permute-start.1 = (f32[32,2,1,64]{3,2,1,0:T(1,128)}, f32[32,2,1,64]{3,2,1,0:T(1,128)}, u32[]{:S(2)}, u32[]{:S(2)}) collective-permute-start(f32[32,2,1,64]{3,2,1,0:T(1,128)} %get-tuple-element.30), channel_id=1, source_target_pairs={{1,0},{2,1},{3,2},{4,3},{5,4},{6,5},{7,6},{8,7},{9,8},{10,9},{11,1... | collective-permute-start | bytes 49160 | tf_op jit(solution)/shard_map/ppermute | solution.py:276
  110.4 0.1 convert_multiply_fusion
  110.8 0.1 eq.185
  111.2 0.3 convolution_multiply_fusion.1
  111.5 0.1 broadcast_add_fusion
  111.6 2.7 %add_convert_fusion.1.cols_ref = bf16[2048,256]{1,0:T(8,128)(2,1)} fusion(f32[2048]{0:T(1024)S(1)} %broadcast_in_dim.148, s32[2048]{0:T(1024)S(1)} %eq.189, f32[2048]{0:T(1024)S(1)} %broadcast_in_dim.145, s32[2048]{0:T(1024)S(1)} %eq.185), kind=kLoop, calls=%fused_computation.15 | loop fusion | flops 3145728 | bytes 1081344 | tf_op jit(solution)/shard_map/convert_element_type | solution.py:163
  114.2 0.8 add_convert_fusion.3.rows_ref
  115.0 0.1 broadcast_subtract_fusion
  115.1 0.1 reshape.351
  115.2 1.4 %convolution_bitcast_fusion = f32[3,8,32,64]{3,1,0,2:T(8,128)S(1)} fusion(f32[32,1,6,64]{3,2,1,0:T(8,128)S(1)} %bitcast.39, f32[32,2,1,64]{3,2,1,0:T(1,128)} %collective-permute-done.1, f32[32,2,4,64]{3,2,1,0:T(4,128)S(1)} %reshape.349, f32[32,2,1,64]{3,2,1,0:T(1,128)} %collective-permute-done, f32[32,6]{1,0:T(8,128)S(1)} %get-tuple-element.18, ...), kind=kOutput, calls=%fused_computation.27 | convolution fusion | flops 3657216 | bytes 347136 | tf_op jit(solution)/shard_map/ckra,crz->kzca/dot_general | solution.py:307
  116.6 0.1 copy.19
  116.7 0.8 reshape.352.sec_ref
  117.6 3.9 %shard_map.132 = f32[768,256]{1,0:T(8,128)} custom-call(bf16[32,2048]{1,0:T(8,128)(2,1)} %add_convert_fusion.3.rows_ref, f32[24,2048]{1,0:T(8,128)} %reshape.352.sec_ref, bf16[2048,256]{1,0:T(8,128)(2,1)} %add_convert_fusion.1.cols_ref), custom_call_target="tpu_custom_call" | custom-call | flops 805306368 | bytes 2162688 | tf_op jit(solution)/shard_map/pallas_call | solution.py:347
  (46 shorter events, 0.6 us)
Async XLA Ops:
  0.0 0.8 copy-start
  31.6 1.8 %copy-start.12 = (s32[32]{0:T(128)S(1)}, s32[32]{0:T(128)}, u32[]{:S(2)}) copy-start(s32[32]{0:T(128)} %param.14) | copy-start | bytes 388
  31.6 1.8 %copy-start.13 = (s32[32]{0:T(128)S(1)}, s32[32]{0:T(128)}, u32[]{:S(2)}) copy-start(s32[32]{0:T(128)} %param.16) | copy-start | bytes 388
  37.5 1.8 %copy-start.11 = (s32[32]{0:T(128)S(1)}, s32[32]{0:T(128)}, u32[]{:S(2)}) copy-start(s32[32]{0:T(128)} %param.15) | copy-start | bytes 388
  40.0 1.7 %copy-start.1 = (bf16[64,8192]{1,0:T(8,128)(2,1)S(1)}, bf16[64,8192]{1,0:T(8,128)(2,1)}, u32[]{:S(2)}) copy-start(bf16[64,8192]{1,0:T(8,128)(2,1)} %param.18) | copy-start | bytes 3145732
  40.0 1.8 %copy-start.2 = (bf16[32,16384]{1,0:T(8,128)(2,1)S(1)}, bf16[32,16384]{1,0:T(8,128)(2,1)}, u32[]{:S(2)}) copy-start(bf16[32,16384]{1,0:T(8,128)(2,1)} %param.13) | copy-start | bytes 3145732
  53.8 2.4 %copy-start.8 = (f32[2,32,64]{2,1,0:T(8,128)S(1)}, f32[2,32,64]{2,1,0:T(8,128)}, u32[]{:S(2)}) copy-start(f32[2,32,64]{2,1,0:T(8,128)} %get-tuple-element.12) | copy-start | bytes 49156
  92.1 18.4 %copy-start.3 = (f32[32,64]{1,0:T(8,128)S(1)}, f32[32,64]{1,0:T(8,128)}, u32[]{:S(2)}) copy-start(f32[32,64]{1,0:T(8,128)} %param.22) | copy-start | bytes 24580
  92.1 18.5 %copy-start.4 = (s32[32,64]{1,0:T(8,128)S(1)}, s32[32,64]{1,0:T(8,128)}, u32[]{:S(2)}) copy-start(s32[32,64]{1,0:T(8,128)} %param.20) | copy-start | bytes 24580
  92.2 18.6 %copy-start.5 = (f32[32,64]{1,0:T(8,128)S(1)}, f32[32,64]{1,0:T(8,128)}, u32[]{:S(2)}) copy-start(f32[32,64]{1,0:T(8,128)} %param.21) | copy-start | bytes 24580
  92.2 18.6 %copy-start.6 = (s32[32,64]{1,0:T(8,128)S(1)}, s32[32,64]{1,0:T(8,128)}, u32[]{:S(2)}) copy-start(s32[32,64]{1,0:T(8,128)} %param.19) | copy-start | bytes 24580
  104.2 6.7 %copy-start.7 = (f32[8,32,64]{2,1,0:T(8,128)S(1)}, f32[8,32,64]{2,1,0:T(8,128)}, u32[]{:S(2)}) copy-start(f32[8,32,64]{2,1,0:T(8,128)} %get-tuple-element.16) | copy-start | bytes 196612
  106.0 9.2 %collective-permute-start = (f32[32,2,1,64]{3,2,1,0:T(1,128)}, f32[32,2,1,64]{3,2,1,0:T(1,128)}, u32[]{:S(2)}, u32[]{:S(2)}) collective-permute-start(f32[32,2,1,64]{3,2,1,0:T(1,128)} %get-tuple-element.29), channel_id=1, source_target_pairs={{0,1},{1,2},{2,3},{3,4},{4,5},{5,6},{6,7},{7,8},{8,9},{9,10},{10,1... | collective-permute-start | bytes 49160 | tf_op jit(solution)/shard_map/ppermute | solution.py:275
  109.0 2.5 %copy-start.9 = (s32[32,128]{1,0:T(8,128)S(1)}, s32[32,128]{1,0:T(8,128)}, u32[]{:S(2)}) copy-start(s32[32,128]{1,0:T(8,128)} %param.23) | copy-start | bytes 49156
  109.0 6.2 %collective-permute-start.1 = (f32[32,2,1,64]{3,2,1,0:T(1,128)}, f32[32,2,1,64]{3,2,1,0:T(1,128)}, u32[]{:S(2)}, u32[]{:S(2)}) collective-permute-start(f32[32,2,1,64]{3,2,1,0:T(1,128)} %get-tuple-element.30), channel_id=1, source_target_pairs={{1,0},{2,1},{3,2},{4,3},{5,4},{6,5},{7,6},{8,7},{9,8},{10,9},{11,1... | collective-permute-start | bytes 49160 | tf_op jit(solution)/shard_map/ppermute | solution.py:276
  110.5 4.5 %copy-start.10 = (f32[32,128]{1,0:T(8,128)S(1)}, f32[32,128]{1,0:T(8,128)}, u32[]{:S(2)}) copy-start(f32[32,128]{1,0:T(8,128)} %param.24) | copy-start | bytes 49156

commit v7 on v6

--- a/solution.py
+++ b/solution.py
@@ -9,6 +9,7 @@
 from jax.sharding import PartitionSpec as P
 
 SHIFTS = 128
+Z_CHIPS = 8
 
 
 def phase_table(row_count, half_cols):
@@ -82,6 +83,18 @@
     return lax.rem(group, 2), lambda peer: (group - lax.rem(group, 2) + peer, slab)
 
 
+def z_place():
+    group, slab = lax.axis_index("grp"), lax.axis_index("slab")
+    z = lax.rem(slab, Z_CHIPS)
+    return z, lambda peer: (group, slab - z + peer)
+
+
+def y_place():
+    group, slab = lax.axis_index("grp"), lax.axis_index("slab")
+    z = lax.rem(slab, Z_CHIPS)
+    return slab // Z_CHIPS, lambda peer: (group, peer * Z_CHIPS + z)
+
+
 def group_place():
     slab = lax.axis_index("slab")
     return lax.axis_index("grp"), lambda peer: (peer, slab)
@@ -95,9 +108,12 @@
     return x_ref.at[peer]
 
 
-def lane_block(x_ref, peer):
-    width = x_ref.shape[1] // lax.axis_size("slab")
-    return x_ref.at[:, pl.ds(pl.multiple_of(peer * width, width), width)]
+def lane_blocks(count):
+    def pick(x_ref, peer):
+        width = x_ref.shape[1] // count
+        return x_ref.at[:, pl.ds(pl.multiple_of(peer * width, width), width)]
+
+    return pick
 
 
 def exchange_many(xs, count, place, picks, collective_id, block_shapes):
@@ -203,7 +219,11 @@
     core = lax.rem(lax.axis_index("grp"), 2)
     ref_halves = references.reshape(2, -1, lanes)
     my_half = lax.dynamic_slice_in_dim(ref_halves, core, 1, 0)
-    half_refs = exchange(my_half, slab_count, slab_place, whole, 0, my_half.shape[1:])
+    y_chips = slab_count // Z_CHIPS
+    row_refs = exchange(my_half, Z_CHIPS, z_place, whole, 0, my_half.shape[1:])
+    half_refs = exchange(
+        row_refs.reshape(1, -1, lanes), y_chips, y_place, whole, 6, (Z_CHIPS * pixels // lanes, lanes)
+    )
     both_halves = exchange(
         half_refs.reshape(1, -1, lanes), 2, core_place, whole, 1, (slab_count * pixels // lanes, lanes)
     ).reshape(2, slab_count, pixels)
@@ -232,44 +252,29 @@
         member, stacked, precision=lax.Precision.HIGHEST, preferred_element_type=jnp.float32
     ) * channel_scale[0]
     half_rows = class_count // 2 * 2
-    by_half = partial.reshape(2, half_rows, pixels)
     class_hits = (class_ids[:, None] == image_class[None, :]).astype(jnp.bfloat16)
     ctf_hits = (image_ctf[:, None] == jnp.arange(groups_ctf, dtype=jnp.int32)[None, :]).astype(
         jnp.bfloat16
     )
     counts = jnp.dot(class_hits, ctf_hits, preferred_element_type=jnp.float32)
-    paired, paired_counts = exchange_many(
-        [by_half, counts[None]],
-        2,
-        core_place,
-        [row_block, whole],
-        2,
-        [(half_rows, pixels), counts.shape],
-    )
+    count_rows = class_count * groups_ctf // band_pixels
+    tiled_counts = jnp.tile(counts.reshape(count_rows, band_pixels), (1, slab_count))
+    rows = half_rows + count_rows
+    by_half = jnp.concatenate(
+        [partial.reshape(2, half_rows, pixels), jnp.broadcast_to(tiled_counts, (2, count_rows, pixels))],
+        axis=1,
+    )
+    paired = exchange(by_half, 2, core_place, row_block, 2, (rows, pixels))
     pair_sum = (paired[0] + paired[1]).astype(jnp.bfloat16)
-    arrived, arrived_counts = exchange_many(
-        [pair_sum, jnp.sum(paired_counts, axis=0)[None]],
-        slab_count,
-        slab_place,
-        [lane_block, whole],
-        3,
-        [(half_rows, band_pixels), counts.shape],
-    )
+    y_chips = slab_count // Z_CHIPS
+    by_y = exchange(pair_sum, y_chips, y_place, lane_blocks(y_chips), 3, (rows, pixels // y_chips))
+    y_sum = jnp.sum(by_y.astype(jnp.float32), axis=0).astype(jnp.bfloat16)
+    arrived = exchange(y_sum, Z_CHIPS, z_place, lane_blocks(Z_CHIPS), 7, (rows, band_pixels))
     chip_band = jnp.sum(arrived.astype(jnp.float32), axis=0).astype(jnp.bfloat16)
-    groups, group_counts = exchange_many(
-        [chip_band[None], jnp.sum(arrived_counts, axis=0)[None]],
-        group_count,
-        group_place,
-        [whole, whole],
-        4,
-        [chip_band.shape, counts.shape],
-    )
-    band = jnp.sum(
-        groups.astype(jnp.float32).reshape(group_count // 2, 2, half_rows, band_pixels), axis=0
-    ).reshape(class_count, 2, band_rows, half_cols)
-    total_counts = jnp.sum(
-        group_counts.reshape(group_count // 2, 2, class_count, groups_ctf)[:, 0], axis=0
-    )
+    groups = exchange(chip_band[None], group_count, group_place, whole, 4, chip_band.shape)
+    groups = groups.astype(jnp.float32).reshape(group_count // 2, 2, rows, band_pixels)
+    band = jnp.sum(groups[:, :, :half_rows], axis=0).reshape(class_count, 2, band_rows, half_cols)
+    total_counts = jnp.sum(groups[:, 0, half_rows:], axis=0).reshape(class_count, groups_ctf)
     up = [(i, i + 1) for i in range(slab_count - 1)]
     down = [(i + 1, i) for i in range(slab_count - 1)]
     from_below = lax.ppermute(band[:, :, band_rows - 1 :], "slab", up)

time: 124 us -> 115 us (0.927)
  the two profiles are of different devices: /device:TPU:1 before, /device:TPU:24 now
where the time goes in v7:
time: 115 us; the launch traced here: 114 us
  Pallas kernels  70.9 us (62%)
  other arithmetic  16.6 us (14%)
  local copies, waits for them, and re-layouts  10.4 us (9%)
  matrix products  8.14 us (7%)
  starting transfers between devices  7.95 us (7%)
    pallas_call x7, Pallas kernels, exchange_many(): pl.pallas_call(functools.partial(exchange_kernel, count, place, tuple(pic...  67 us
    ppermute x1, starting transfers between devices, local(): from_above = lax.ppermute(band[:, :, :1], 'slab', down)  4.58 us
    pallas_call x1, Pallas kernels, insert_planes(): pl.pallas_call(insert_kernel, out_shape=jax.ShapeDtypeStruct((planes * y_...  3.91 us
    ppermute x1, starting transfers between devices, local(): from_below = lax.ppermute(band[:, :, band_rows - 1:], 'slab', up)  3.37 us
    convert_element_type x1, other arithmetic, local(): pair_sum = (paired[0] + paired[1]).astype(jnp.bfloat16)  2.67 us
    convert_element_type x1, other arithmetic, stencil_weights(): return dense_weight.astype(jnp.bfloat16)  2.64 us
    unnamed x25, local copies, waits for them, and re-layouts  2.6 us
    another operation x1, other arithmetic  2.52 us
  transfers between devices with their start and end apart: 2, of which 0 were waited for; matrix products, arithmetic and copies ran while one was open for 4% of the time, Pallas kernels for 0%

profile of v7, /device:TPU:24, one launch (start us, length us, event | category | flops | bytes accessed | tf_op | source)
XLA Modules:
  0.0 114.4 jit_solution(4782881237243055072)
XLA Ops:
  0.0 0.8 copy-done
  0.8 0.2 reduce.3
  1.0 0.6 constant_dynamic-slice_fusion.refs_0_
  1.6 13.4 %shard_map.127 = bf16[8,64,128]{2,1,0:T(8,128)(2,1)} custom-call(bf16[1,64,128]{2,1,0:T(8,128)(2,1)} %constant_dynamic-slice_fusion.refs_0_), custom_call_target="tpu_custom_call" | custom-call | tf_op jit(solution)/shard_map/pallas_call | solution.py:121
  15.0 10.2 %shard_map.128 = bf16[4,512,128]{2,1,0:T(8,128)(2,1)} custom-call(bf16[1,512,128]{2,1,0:T(8,128)(2,1)} %bitcast.37), custom_call_target="tpu_custom_call" | custom-call | tf_op jit(solution)/shard_map/pallas_call | solution.py:121
  25.3 4.1 %shard_map.129 = bf16[2,2048,128]{2,1,0:T(8,128)(2,1)} custom-call(bf16[1,2048,128]{2,1,0:T(8,128)(2,1)} %bitcast.35), custom_call_target="tpu_custom_call" | custom-call | tf_op jit(solution)/shard_map/pallas_call | solution.py:121
  29.4 1.3 %fusion.68 = (bf16[1,2048,128]{2,1,0:T(8,128)(2,1)S(1)}, bf16[1,2048,128]{2,1,0:T(8,128)(2,1)S(1)}) fusion(bf16[2,2048,128]{2,1,0:T(8,128)(2,1)} %shard_map.129), kind=kLoop, calls=%fused_computation.135 | loop fusion | bytes 2097152 | tf_op jit(solution)/shard_map/slice | solution.py:237
  30.7 0.2 squeeze.16
  30.9 0.2 squeeze.15
  31.2 0.2 select_reduce_fusion
  31.4 0.3 fusion
  31.7 0.4 fusion.1
  32.1 0.3 fusion.34
  32.4 0.3 fusion.32
  32.7 2.5 %add_convert_fusion = (bf16[128,64,128]{2,1,0:T(8,128)(2,1)S(1)}, bf16[128,64,128]{2,1,0:T(8,128)(2,1)S(1)}) fusion(f32[128,128]{1,0:T(8,128)S(1)} %get-tuple-element.20, f32[128,64]{1,0:T(8,128)S(1)} %get-tuple-element.22, f32[128,128]{1,0:T(8,128)S(1)} %get-tuple-element.19, f32[128,64]{1,0:T(8,128)S(1)} %get-tuple-element.21), kind=kLoop, calls=%fused_computation.7 | loop fusion | flops 8388608 | bytes 4390912 | tf_op jit(solution)/shard_map/convert.5
  35.3 1.7 %bitcast_dynamic-update-slice_fusion.1 = bf16[128,16384]{1,0:T(8,128)(2,1)S(1)} fusion(bf16[16,8,64,128]{3,2,1,0:T(8,128)(2,1)S(1)} %bitcast.34), kind=kLoop, calls=%fused_computation.12 | loop fusion | bytes 4194304
  37.0 0.2 fusion.43
  37.2 1.8 %bitcast_dynamic-update-slice_fusion = bf16[128,16384]{1,0:T(8,128)(2,1)S(1)} fusion(bf16[128,16384]{1,0:T(8,128)(2,1)S(1)} %bitcast_dynamic-update-slice_fusion.1, bf16[16,8,64,128]{3,2,1,0:T(8,128)(2,1)S(1)} %bitcast.33), kind=kLoop, calls=%fused_computation.11 | loop fusion | bytes 4194304 | tf_op jit(solution)/shard_map/concatenate | solution.py:35
  39.0 0.7 fusion.8
  39.7 1.6 %fusion.70 = (f32[32]{0:T(128)S(1)}, f32[32,128]{1,0:T(8,128)S(1)}) fusion(bf16[128,16384]{1,0:T(8,128)(2,1)S(1)} %bitcast_dynamic-update-slice_fusion, bf16[32,8192]{1,0:T(8,128)(2,1)S(1)} %get-tuple-element.12, bf16[32,8192]{1,0:T(8,128)(2,1)S(1)} %get-tuple-element.11), kind=kOutput, calls=%fused_computation.137 | convolution fusion | flops 136323040 | bytes 5259392 | tf_op jit(solution)/shard_map/np,sp->ns/dot_general | solution.py:155
  41.4 0.2 fusion.44
  41.5 0.7 fusion.45
  42.3 0.3 fusion.13
  42.7 2.5 %convolution_multiply_fusion = f32[32,16384]{1,0:T(8,128)} fusion(f32[32,8192]{1,0:T(8,128)S(1)} %get-tuple-element.10, f32[32,8192]{1,0:T(8,128)S(1)} %get-tuple-element.9, s32[32]{0:T(128)S(1)} %copy-done.10), kind=kOutput, calls=%fused_computation | convolution fusion | flops 202376192 | bytes 4194432 | tf_op jit(solution)/shard_map/dot_general | solution.py:251
  45.1 1.7 %reshape.354 = f32[2,32,8192]{2,1,0:T(8,128)S(1)} reshape(f32[32,16384]{1,0:T(8,128)} %convolution_multiply_fusion) | data formatting | bytes 4194304 | tf_op jit(solution)/shard_map/reshape | solution.py:264
  46.8 0.1 tile.10
  47.0 1.7 %pad_maximum_fusion.refs_0_ = f32[2,40,8192]{2,1,0:T(8,128)} fusion(f32[2,8,8192]{2,1,0:T(8,128)S(1)} %broadcast_in_dim.135, f32[2,32,8192]{2,1,0:T(8,128)S(1)} %reshape.354), kind=kLoop, calls=%fused_computation.9 | loop fusion | flops 655360 | bytes 5242880 | tf_op jit(solution)/shard_map/concatenate | solution.py:263
  48.7 6.4 %shard_map.130 = f32[2,40,8192]{2,1,0:T(8,128)} custom-call(f32[2,40,8192]{2,1,0:T(8,128)} %pad_maximum_fusion.refs_0_), custom_call_target="tpu_custom_call" | custom-call | tf_op jit(solution)/shard_map/pallas_call | solution.py:121
  55.1 2.7 %fusion.19.refs_0_ = bf16[40,8192]{1,0:T(8,128)(2,1)} fusion(f32[2,40,8192]{2,1,0:T(8,128)} %shard_map.130), kind=kLoop, calls=%fused_computation.45 | loop fusion | flops 655360 | bytes 3276800 | tf_op jit(solution)/shard_map/convert_element_type | solution.py:268
  57.8 13.3 %shard_map.131 = bf16[4,40,2048]{2,1,0:T(8,128)(2,1)} custom-call(bf16[40,8192]{1,0:T(8,128)(2,1)} %fusion.19.refs_0_), custom_call_target="tpu_custom_call" | custom-call | tf_op jit(solution)/shard_map/pallas_call | solution.py:121
  71.1 1.9 %reduce_sum.62.refs_0_ = bf16[40,2048]{1,0:T(8,128)(2,1)} reduce(bf16[4,40,2048]{2,1,0:T(8,128)(2,1)} %shard_map.131, bf16[]{:T(256)} %constant.135.clone.1), dimensions={0}, to_apply=%region_3.4 | reduce | flops 245760 | bytes 819202 | tf_op jit(solution)/shard_map/reduce_sum | solution.py:271
  72.9 11.3 %shard_map.132 = bf16[8,40,256]{2,1,0:T(8,128)(2,1)} custom-call(bf16[40,2048]{1,0:T(8,128)(2,1)} %reduce_sum.62.refs_0_), custom_call_target="tpu_custom_call" | custom-call | tf_op jit(solution)/shard_map/pallas_call | solution.py:121
  84.2 1.6 %reduce_sum.63 = bf16[40,256]{1,0:T(8,128)(2,1)} reduce(bf16[8,40,256]{2,1,0:T(8,128)(2,1)} %shard_map.132, bf16[]{:T(256)} %constant.135.clone.1), dimensions={0}, to_apply=%region_4.5 | reduce | flops 71680 | bytes 184322 | tf_op jit(solution)/shard_map/reduce_sum | solution.py:273
  85.8 8.3 %shard_map.133 = bf16[8,40,256]{2,1,0:T(8,128)(2,1)} custom-call(bf16[1,40,256]{2,1,0:T(8,128)(2,1)} %bitcast.39), custom_call_target="tpu_custom_call" | custom-call | tf_op jit(solution)/shard_map/pallas_call | solution.py:121
  94.1 0.9 bitcast_convert_fusion
  95.1 0.1 reshape.357
  95.3 3.4 %collective-permute-start = (f32[32,2,1,64]{3,2,1,0:T(1,128)S(1)}, f32[32,2,1,64]{3,2,1,0:T(1,128)S(1)}, u32[]{:S(2)}, u32[]{:S(2)}) collective-permute-start(f32[32,2,1,64]{3,2,1,0:T(1,128)S(1)} %get-tuple-element.17), channel_id=1, source_target_pairs={{0,1},{1,2},{2,3},{3,4},{4,5},{5,6},{6,7},{7,8},{8,9},{9,10},{10,1... | collective-permute-start | bytes 49160 | tf_op jit(solution)/shard_map/ppermute | solution.py:280
  98.7 4.6 %collective-permute-start.1 = (f32[32,2,1,64]{3,2,1,0:T(1,128)S(1)}, f32[32,2,1,64]{3,2,1,0:T(1,128)}, u32[]{:S(2)}, u32[]{:S(2)}) collective-permute-start(f32[32,2,1,64]{3,2,1,0:T(1,128)S(1)} %get-tuple-element.18), channel_id=1, source_target_pairs={{1,0},{2,1},{3,2},{4,3},{5,4},{6,5},{7,6},{8,7},{9,8},{10,9},{11,1... | collective-permute-start | bytes 49160 | tf_op jit(solution)/shard_map/ppermute | solution.py:281
  103.3 0.1 convert_multiply_fusion
  104.1 0.3 convolution_multiply_fusion.1
  104.4 0.1 broadcast_add_fusion
  104.5 2.6 %add_convert_fusion.1.cols_ref = bf16[2048,256]{1,0:T(8,128)(2,1)} fusion(f32[2048]{0:T(1024)S(1)} %broadcast_in_dim.140, s32[2048]{0:T(1024)S(1)} %eq.189, f32[2048]{0:T(1024)S(1)} %broadcast_in_dim.137, s32[2048]{0:T(1024)S(1)} %eq.185), kind=kLoop, calls=%fused_computation.16 | loop fusion | flops 3145728 | bytes 1081344 | tf_op jit(solution)/shard_map/convert_element_type | solution.py:179
  107.2 0.8 add_convert_fusion.3.rows_ref
  107.9 0.1 broadcast_subtract_fusion
  108.0 0.1 reshape.359
  108.1 1.4 %convolution_bitcast_fusion = f32[3,8,32,64]{3,1,0,2:T(8,128)S(1)} fusion(f32[32,1,6,64]{3,2,1,0:T(8,128)S(1)} %bitcast.38, f32[32,2,1,64]{3,2,1,0:T(1,128)} %collective-permute-done.1, f32[32,2,4,64]{3,2,1,0:T(4,128)S(1)} %reshape.357, f32[32,2,1,64]{3,2,1,0:T(1,128)S(1)} %collective-permute-done, f32[32,6]{1,0:T(8,128)S(1)} %get-tuple-element.6, ...), kind=kOutput, calls=%fused_computation.29 | convolution fusion | flops 3657216 | bytes 347136 | tf_op jit(solution)/shard_map/ckra,crz->kzca/dot_general | solution.py:312
  109.6 0.8 reshape.360.sec_ref
  110.5 3.9 %shard_map.134 = f32[768,256]{1,0:T(8,128)} custom-call(bf16[32,2048]{1,0:T(8,128)(2,1)} %add_convert_fusion.3.rows_ref, f32[24,2048]{1,0:T(8,128)} %reshape.360.sec_ref, bf16[2048,256]{1,0:T(8,128)(2,1)} %add_convert_fusion.1.cols_ref), custom_call_target="tpu_custom_call" | custom-call | flops 805306368 | bytes 2162688 | tf_op jit(solution)/shard_map/pallas_call | solution.py:352
  (49 shorter events, 1.0 us)
Async XLA Ops:
  0.0 0.8 copy-start
  29.4 1.8 %copy-start.10 = (s32[32]{0:T(128)S(1)}, s32[32]{0:T(128)}, u32[]{:S(2)}) copy-start(s32[32]{0:T(128)} %param.14) | copy-start | bytes 388
  29.4 1.8 %copy-start.11 = (s32[32]{0:T(128)S(1)}, s32[32]{0:T(128)}, u32[]{:S(2)}) copy-start(s32[32]{0:T(128)} %param.16) | copy-start | bytes 388
  35.2 1.8 %copy-start.9 = (s32[32]{0:T(128)S(1)}, s32[32]{0:T(128)}, u32[]{:S(2)}) copy-start(s32[32]{0:T(128)} %param.15) | copy-start | bytes 388
  37.2 1.8 %copy-start.1 = (bf16[64,8192]{1,0:T(8,128)(2,1)S(1)}, bf16[64,8192]{1,0:T(8,128)(2,1)}, u32[]{:S(2)}) copy-start(bf16[64,8192]{1,0:T(8,128)(2,1)} %param.18) | copy-start | bytes 3145732
  37.2 1.8 %copy-start.2 = (bf16[32,16384]{1,0:T(8,128)(2,1)S(1)}, bf16[32,16384]{1,0:T(8,128)(2,1)}, u32[]{:S(2)}) copy-start(bf16[32,16384]{1,0:T(8,128)(2,1)} %param.13) | copy-start | bytes 3145732
  94.1 9.4 %copy-start.3 = (f32[32,64]{1,0:T(8,128)S(1)}, f32[32,64]{1,0:T(8,128)}, u32[]{:S(2)}) copy-start(f32[32,64]{1,0:T(8,128)} %param.22) | copy-start | bytes 24580
  94.1 9.5 %copy-start.4 = (s32[32,64]{1,0:T(8,128)S(1)}, s32[32,64]{1,0:T(8,128)}, u32[]{:S(2)}) copy-start(s32[32,64]{1,0:T(8,128)} %param.20) | copy-start | bytes 24580
  95.1 8.6 %copy-start.5 = (f32[32,64]{1,0:T(8,128)S(1)}, f32[32,64]{1,0:T(8,128)}, u32[]{:S(2)}) copy-start(f32[32,64]{1,0:T(8,128)} %param.21) | copy-start | bytes 24580
  95.1 8.6 %copy-start.6 = (s32[32,64]{1,0:T(8,128)S(1)}, s32[32,64]{1,0:T(8,128)}, u32[]{:S(2)}) copy-start(s32[32,64]{1,0:T(8,128)} %param.19) | copy-start | bytes 24580
  95.3 12.8 %collective-permute-start = (f32[32,2,1,64]{3,2,1,0:T(1,128)S(1)}, f32[32,2,1,64]{3,2,1,0:T(1,128)S(1)}, u32[]{:S(2)}, u32[]{:S(2)}) collective-permute-start(f32[32,2,1,64]{3,2,1,0:T(1,128)S(1)} %get-tuple-element.17), channel_id=1, source_target_pairs={{0,1},{1,2},{2,3},{3,4},{4,5},{5,6},{6,7},{7,8},{8,9},{9,10},{10,1... | collective-permute-start | bytes 49160 | tf_op jit(solution)/shard_map/ppermute | solution.py:280
  98.7 9.4 %collective-permute-start.1 = (f32[32,2,1,64]{3,2,1,0:T(1,128)S(1)}, f32[32,2,1,64]{3,2,1,0:T(1,128)}, u32[]{:S(2)}, u32[]{:S(2)}) collective-permute-start(f32[32,2,1,64]{3,2,1,0:T(1,128)S(1)} %get-tuple-element.18), channel_id=1, source_target_pairs={{1,0},{2,1},{3,2},{4,3},{5,4},{6,5},{7,6},{8,7},{9,8},{10,9},{11,1... | collective-permute-start | bytes 49160 | tf_op jit(solution)/shard_map/ppermute | solution.py:281
  103.3 1.2 %copy-start.7 = (s32[32,128]{1,0:T(8,128)S(1)}, s32[32,128]{1,0:T(8,128)}, u32[]{:S(2)}) copy-start(s32[32,128]{1,0:T(8,128)} %param.23) | copy-start | bytes 49156
  103.4 4.5 %copy-start.8 = (f32[32,128]{1,0:T(8,128)S(1)}, f32[32,128]{1,0:T(8,128)}, u32[]{:S(2)}) copy-start(f32[32,128]{1,0:T(8,128)} %param.24) | copy-start | bytes 49156

commit v8 on v7

--- a/solution.py
+++ b/solution.py
@@ -104,6 +104,10 @@
     return x_ref.at[0]
 
 
+def entire(x_ref, peer):
+    return x_ref
+
+
 def row_block(x_ref, peer):
     return x_ref.at[peer]
 
@@ -136,6 +140,113 @@
 
 def exchange(x, count, place, pick, collective_id, block_shape):
     return exchange_many([x], count, place, [pick], collective_id, [block_shape])[0]
+
+
+def signal_all(devices):
+    barrier = pltpu.get_barrier_semaphore()
+    for device in devices:
+        pl.semaphore_signal(barrier, 1, device_id=device, device_id_type=pl.DeviceIdType.MESH)
+    pl.semaphore_wait(barrier, len(devices))
+
+
+def run_phase(count, place, pick, x_ref, out_ref, local_sem, send_sems, recv_sems):
+    me, device = place()
+    own = pltpu.make_async_copy(pick(x_ref, me), out_ref.at[me], local_sem)
+    own.start()
+    copies = []
+    for k in range(1, count):
+        peer = lax.rem(me + k, count)
+        copy = pltpu.make_async_remote_copy(
+            src_ref=pick(x_ref, peer),
+            dst_ref=out_ref.at[me],
+            send_sem=send_sems.at[k],
+            recv_sem=recv_sems.at[k],
+            device_id=device(peer),
+            device_id_type=pl.DeviceIdType.MESH,
+        )
+        copy.start()
+        copies.append(copy)
+    own.wait()
+    for copy in copies:
+        copy.wait_send()
+        copy.wait_recv()
+
+
+def peers(count, place):
+    me, device = place()
+    return [device(lax.rem(me + k, count)) for k in range(1, count)]
+
+
+def reduce_chain_kernel(y_chips, groups, x_ref, out_ref, core_buf, y_src, y_buf, z_src, z_buf, d_src,
+                        local_sems, send_sems, recv_sems):
+    signal_all(
+        peers(2, core_place)
+        + peers(y_chips, y_place)
+        + peers(Z_CHIPS, z_place)
+        + peers(groups, group_place)
+    )
+    run_phase(2, core_place, row_block, x_ref, core_buf, local_sems.at[0], send_sems.at[0], recv_sems.at[0])
+    y_src[...] = (core_buf[0] + core_buf[1]).astype(y_src.dtype)
+    run_phase(
+        y_chips, y_place, lane_blocks(y_chips), y_src, y_buf,
+        local_sems.at[1], send_sems.at[1], recv_sems.at[1],
+    )
+    z_src[...] = jnp.sum(y_buf[...].astype(jnp.float32), axis=0).astype(z_src.dtype)
+    run_phase(
+        Z_CHIPS, z_place, lane_blocks(Z_CHIPS), z_src, z_buf,
+        local_sems.at[2], send_sems.at[2], recv_sems.at[2],
+    )
+    d_src[0] = jnp.sum(z_buf[...].astype(jnp.float32), axis=0).astype(d_src.dtype)
+    run_phase(groups, group_place, whole, d_src, out_ref, local_sems.at[3], send_sems.at[3], recv_sems.at[3])
+
+
+def reduce_chain(x, y_chips, groups, collective_id):
+    _, rows, width = x.shape
+    band = width // (y_chips * Z_CHIPS)
+    wide = 8
+    return pl.pallas_call(
+        functools.partial(reduce_chain_kernel, y_chips, groups),
+        out_shape=jax.ShapeDtypeStruct((groups, rows, band), jnp.bfloat16),
+        in_specs=[pl.BlockSpec(memory_space=pltpu.VMEM)],
+        out_specs=pl.BlockSpec(memory_space=pltpu.VMEM),
+        scratch_shapes=[
+            pltpu.VMEM((2, rows, width), x.dtype),
+            pltpu.VMEM((rows, width), jnp.bfloat16),
+            pltpu.VMEM((y_chips, rows, width // y_chips), jnp.bfloat16),
+            pltpu.VMEM((rows, width // y_chips), jnp.bfloat16),
+            pltpu.VMEM((Z_CHIPS, rows, band), jnp.bfloat16),
+            pltpu.VMEM((1, rows, band), jnp.bfloat16),
+            pltpu.SemaphoreType.DMA((4,)),
+            pltpu.SemaphoreType.DMA((4, wide)),
+            pltpu.SemaphoreType.DMA((4, wide)),
+        ],
+        compiler_params=pltpu.CompilerParams(collective_id=collective_id, has_side_effects=True),
+    )(x)
+
+
+def gather_chain_kernel(y_chips, x_ref, out_ref, z_buf, y_buf, local_sems, send_sems, recv_sems):
+    signal_all(peers(Z_CHIPS, z_place) + peers(y_chips, y_place) + peers(2, core_place))
+    run_phase(Z_CHIPS, z_place, whole, x_ref, z_buf, local_sems.at[0], send_sems.at[0], recv_sems.at[0])
+    run_phase(y_chips, y_place, entire, z_buf, y_buf, local_sems.at[1], send_sems.at[1], recv_sems.at[1])
+    run_phase(2, core_place, entire, y_buf, out_ref, local_sems.at[2], send_sems.at[2], recv_sems.at[2])
+
+
+def gather_chain(x, y_chips, collective_id):
+    _, rows, lanes = x.shape
+    return pl.pallas_call(
+        functools.partial(gather_chain_kernel, y_chips),
+        out_shape=jax.ShapeDtypeStruct((2, y_chips, Z_CHIPS, rows, lanes), x.dtype),
+        in_specs=[pl.BlockSpec(memory_space=pltpu.VMEM)],
+        out_specs=pl.BlockSpec(memory_space=pltpu.VMEM),
+        scratch_shapes=[
+            pltpu.VMEM((Z_CHIPS, rows, lanes), x.dtype),
+            pltpu.VMEM((y_chips, Z_CHIPS, rows, lanes), x.dtype),
+            pltpu.SemaphoreType.DMA((3,)),
+            pltpu.SemaphoreType.DMA((3, Z_CHIPS)),
+            pltpu.SemaphoreType.DMA((3, Z_CHIPS)),
+        ],
+        compiler_params=pltpu.CompilerParams(collective_id=collective_id, has_side_effects=True),
+    )(x)
 
 
 def align_frames(frames, ctf_rows, ref_re, ref_im, phase, score_scale):
@@ -220,13 +331,7 @@
     ref_halves = references.reshape(2, -1, lanes)
     my_half = lax.dynamic_slice_in_dim(ref_halves, core, 1, 0)
     y_chips = slab_count // Z_CHIPS
-    row_refs = exchange(my_half, Z_CHIPS, z_place, whole, 0, my_half.shape[1:])
-    half_refs = exchange(
-        row_refs.reshape(1, -1, lanes), y_chips, y_place, whole, 6, (Z_CHIPS * pixels // lanes, lanes)
-    )
-    both_halves = exchange(
-        half_refs.reshape(1, -1, lanes), 2, core_place, whole, 1, (slab_count * pixels // lanes, lanes)
-    ).reshape(2, slab_count, pixels)
+    both_halves = gather_chain(my_half, y_chips, 0).reshape(2, slab_count, pixels)
     class_ids = jnp.arange(class_count, dtype=jnp.int32)
     owner_of = jnp.sum(
         jnp.where(image_class[:, None] == class_ids[None, :], class_owner[None, :], 0), axis=1
@@ -264,14 +369,7 @@
         [partial.reshape(2, half_rows, pixels), jnp.broadcast_to(tiled_counts, (2, count_rows, pixels))],
         axis=1,
     )
-    paired = exchange(by_half, 2, core_place, row_block, 2, (rows, pixels))
-    pair_sum = (paired[0] + paired[1]).astype(jnp.bfloat16)
-    y_chips = slab_count // Z_CHIPS
-    by_y = exchange(pair_sum, y_chips, y_place, lane_blocks(y_chips), 3, (rows, pixels // y_chips))
-    y_sum = jnp.sum(by_y.astype(jnp.float32), axis=0).astype(jnp.bfloat16)
-    arrived = exchange(y_sum, Z_CHIPS, z_place, lane_blocks(Z_CHIPS), 7, (rows, band_pixels))
-    chip_band = jnp.sum(arrived.astype(jnp.float32), axis=0).astype(jnp.bfloat16)
-    groups = exchange(chip_band[None], group_count, group_place, whole, 4, chip_band.shape)
+    groups = reduce_chain(by_half, slab_count // Z_CHIPS, group_count, 1)
     groups = groups.astype(jnp.float32).reshape(group_count // 2, 2, rows, band_pixels)
     band = jnp.sum(groups[:, :, :half_rows], axis=0).reshape(class_count, 2, band_rows, half_cols)
     total_counts = jnp.sum(groups[:, 0, half_rows:], axis=0).reshape(class_count, groups_ctf)

time: 115 us -> 95.5 us (0.83)
  the two profiles are of different devices: /device:TPU:24 before, /device:TPU:8 now
where the time goes in v8:
time: 95.5 us; the launch traced here: 95.1 us
  Pallas kernels  57.9 us (61%)
  other arithmetic  10.5 us (11%)
  local copies, waits for them, and re-layouts  9.9 us (10%)
  matrix products  8.31 us (9%)
  starting transfers between devices  8.13 us (9%)
    pallas_call x1, Pallas kernels, reduce_chain(): pl.pallas_call(functools.partial(reduce_chain_kernel, y_chips, groups), o...  31.6 us
    pallas_call x1, Pallas kernels, gather_chain(): pl.pallas_call(functools.partial(gather_chain_kernel, y_chips), out_shape...  22.3 us
    ppermute x1, starting transfers between devices, local(): from_above = lax.ppermute(band[:, :, :1], 'slab', down)  5.99 us
    pallas_call x1, Pallas kernels, insert_planes(): pl.pallas_call(insert_kernel, out_shape=jax.ShapeDtypeStruct((planes * y_...  3.91 us
    unnamed x26, local copies, waits for them, and re-layouts  3.88 us
    convert_element_type x1, other arithmetic, stencil_weights(): return dense_weight.astype(jnp.bfloat16)  2.65 us
    another operation x1, other arithmetic  2.52 us
    dot_general x1, matrix products, local(): jnp.dot(member, stacked, precision=lax.Precision.HIGHEST, preferred_eleme...  2.46 us
  transfers between devices with their start and end apart: 2, of which 0 were waited for; matrix products, arithmetic and copies ran while one was open for 5% of the time, Pallas kernels for 0%

profile of v8, /device:TPU:8, one launch (start us, length us, event | category | flops | bytes accessed | tf_op | source)
XLA Modules:
  0.0 95.1 jit_solution(3755679124631726165)
XLA Ops:
  0.1 0.8 copy-done
  0.8 0.2 reduce.1
  1.0 0.6 constant_dynamic-slice_fusion.x_ref
  1.6 22.3 %shard_map.127 = bf16[2,4,8,64,128]{4,3,2,1,0:T(8,128)(2,1)} custom-call(bf16[1,64,128]{2,1,0:T(8,128)(2,1)} %constant_dynamic-slice_fusion.x_ref), custom_call_target="tpu_custom_call" | custom-call | tf_op jit(solution)/shard_map/pallas_call | solution.py:236
  24.0 1.3 %slice_bitcast_fusion.1 = (bf16[4,8,64,128]{3,2,1,0:T(8,128)(2,1)S(1)}, bf16[4,8,64,128]{3,2,1,0:T(8,128)(2,1)S(1)}) fusion(bf16[2,4,8,64,128]{4,3,2,1,0:T(8,128)(2,1)} %shard_map.127), kind=kLoop, calls=%fused_computation.49 | loop fusion | bytes 2097152
  25.3 0.2 select_reduce_fusion
  25.5 0.4 fusion
  25.9 0.4 fusion.1
  26.4 0.3 fusion.37
  26.7 0.3 fusion.35
  27.0 2.5 %add_convert_fusion = (bf16[128,64,128]{2,1,0:T(8,128)(2,1)S(1)}, bf16[128,64,128]{2,1,0:T(8,128)(2,1)S(1)}) fusion(f32[128,128]{1,0:T(8,128)S(1)} %get-tuple-element.20, f32[128,64]{1,0:T(8,128)S(1)} %get-tuple-element.22, f32[128,128]{1,0:T(8,128)S(1)} %get-tuple-element.19, f32[128,64]{1,0:T(8,128)S(1)} %get-tuple-element.21), kind=kLoop, calls=%fused_computation.7 | loop fusion | flops 8388608 | bytes 4390912 | tf_op jit(solution)/shard_map/convert.3
  29.6 1.7 %bitcast_dynamic-update-slice_fusion.1 = bf16[128,16384]{1,0:T(8,128)(2,1)S(1)} fusion(bf16[16,8,64,128]{3,2,1,0:T(8,128)(2,1)S(1)} %bitcast.39), kind=kLoop, calls=%fused_computation.12 | loop fusion | bytes 4194304
  31.3 0.2 fusion.46
  31.5 1.8 %bitcast_dynamic-update-slice_fusion = bf16[128,16384]{1,0:T(8,128)(2,1)S(1)} fusion(bf16[128,16384]{1,0:T(8,128)(2,1)S(1)} %bitcast_dynamic-update-slice_fusion.1, bf16[16,8,64,128]{3,2,1,0:T(8,128)(2,1)S(1)} %bitcast.38), kind=kLoop, calls=%fused_computation.11 | loop fusion | bytes 4194304 | tf_op jit(solution)/shard_map/concatenate | solution.py:35
  33.3 0.7 fusion.8
  34.0 1.6 %fusion.72 = (f32[32]{0:T(128)S(1)}, f32[32,128]{1,0:T(8,128)S(1)}) fusion(bf16[128,16384]{1,0:T(8,128)(2,1)S(1)} %bitcast_dynamic-update-slice_fusion, bf16[32,8192]{1,0:T(8,128)(2,1)S(1)} %get-tuple-element.12, bf16[32,8192]{1,0:T(8,128)(2,1)S(1)} %get-tuple-element.11), kind=kOutput, calls=%fused_computation.140 | convolution fusion | flops 136323040 | bytes 5259392 | tf_op jit(solution)/shard_map/np,sp->ns/dot_general | solution.py:266
  35.6 0.2 fusion.47
  35.8 0.7 fusion.48
  36.6 0.3 fusion.13
  36.9 2.5 %convolution_multiply_fusion = f32[32,16384]{1,0:T(8,128)} fusion(f32[32,8192]{1,0:T(8,128)S(1)} %get-tuple-element.10, f32[32,8192]{1,0:T(8,128)S(1)} %get-tuple-element.9, s32[32]{0:T(128)S(1)} %copy-done.10), kind=kOutput, calls=%fused_computation | convolution fusion | flops 202376192 | bytes 4194432 | tf_op jit(solution)/shard_map/dot_general | solution.py:356
  39.4 1.7 %reshape.344 = f32[2,32,8192]{2,1,0:T(8,128)S(1)} reshape(f32[32,16384]{1,0:T(8,128)} %convolution_multiply_fusion) | data formatting | bytes 4194304 | tf_op jit(solution)/shard_map/reshape | solution.py:369
  41.1 0.1 tile.10
  41.3 1.7 %pad_maximum_fusion.x_ref = f32[2,40,8192]{2,1,0:T(8,128)} fusion(f32[2,8,8192]{2,1,0:T(8,128)S(1)} %broadcast_in_dim.132, f32[2,32,8192]{2,1,0:T(8,128)S(1)} %reshape.344), kind=kLoop, calls=%fused_computation.9 | loop fusion | flops 655360 | bytes 5242880 | tf_op jit(solution)/shard_map/concatenate | solution.py:368
  43.0 31.6 %shard_map.128 = bf16[8,40,256]{2,1,0:T(8,128)(2,1)} custom-call(f32[2,40,8192]{2,1,0:T(8,128)} %pad_maximum_fusion.x_ref), custom_call_target="tpu_custom_call" | custom-call | tf_op jit(solution)/shard_map/pallas_call | solution.py:207
  74.6 0.9 bitcast_convert_fusion
  75.6 0.1 reshape.347
  75.8 2.1 %collective-permute-start = (f32[32,2,1,64]{3,2,1,0:T(1,128)S(1)}, f32[32,2,1,64]{3,2,1,0:T(1,128)S(1)}, u32[]{:S(2)}, u32[]{:S(2)}) collective-permute-start(f32[32,2,1,64]{3,2,1,0:T(1,128)S(1)} %get-tuple-element.17), channel_id=1, source_target_pairs={{0,1},{1,2},{2,3},{3,4},{4,5},{5,6},{6,7},{7,8},{8,9},{9,10},{10,1... | collective-permute-start | bytes 49160 | tf_op jit(solution)/shard_map/ppermute | solution.py:378
  78.0 6.0 %collective-permute-start.1 = (f32[32,2,1,64]{3,2,1,0:T(1,128)S(1)}, f32[32,2,1,64]{3,2,1,0:T(1,128)}, u32[]{:S(2)}, u32[]{:S(2)}) collective-permute-start(f32[32,2,1,64]{3,2,1,0:T(1,128)S(1)} %get-tuple-element.18), channel_id=1, source_target_pairs={{1,0},{2,1},{3,2},{4,3},{5,4},{6,5},{7,6},{8,7},{9,8},{10,9},{11,1... | collective-permute-start | bytes 49160 | tf_op jit(solution)/shard_map/ppermute | solution.py:379
  84.0 0.1 convert_multiply_fusion
  84.2 0.1 broadcast_in_dim.125
  84.3 0.1 eq.76
  84.3 0.1 broadcast_in_dim.136
  84.4 0.1 eq.185
  84.5 0.1 reshape.348
  84.6 0.1 broadcast_in_dim.76
  84.6 0.1 eq.79
  84.7 0.1 broadcast_in_dim.133
  84.8 0.1 eq.189
  84.9 0.3 convolution_multiply_fusion.1
  85.2 0.1 broadcast_add_fusion
  85.2 2.6 %add_convert_fusion.1.cols_ref = bf16[2048,256]{1,0:T(8,128)(2,1)} fusion(f32[2048]{0:T(1024)S(1)} %broadcast_in_dim.136, s32[2048]{0:T(1024)S(1)} %eq.189, f32[2048]{0:T(1024)S(1)} %broadcast_in_dim.133, s32[2048]{0:T(1024)S(1)} %eq.185), kind=kLoop, calls=%fused_computation.16 | loop fusion | flops 3145728 | bytes 1081344 | tf_op jit(solution)/shard_map/convert_element_type | solution.py:290
  87.9 0.8 add_convert_fusion.2.rows_ref
  88.7 0.1 broadcast_subtract_fusion
  88.7 0.1 reshape.349
  88.8 1.4 %convolution_bitcast_fusion = f32[3,8,32,64]{3,1,0,2:T(8,128)S(1)} fusion(f32[32,1,6,64]{3,2,1,0:T(8,128)S(1)} %bitcast.41, f32[32,2,1,64]{3,2,1,0:T(1,128)} %collective-permute-done.1, f32[32,2,4,64]{3,2,1,0:T(4,128)S(1)} %reshape.347, f32[32,2,1,64]{3,2,1,0:T(1,128)S(1)} %collective-permute-done, f32[32,6]{1,0:T(8,128)S(1)} %get-tuple-element.6, ...), kind=kOutput, calls=%fused_computation.28 | convolution fusion | flops 3657216 | bytes 347136 | tf_op jit(solution)/shard_map/ckra,crz->kzca/dot_general | solution.py:410
  90.3 0.1 copy.19
  90.4 0.8 reshape.350.sec_ref
  91.2 3.9 %shard_map.129 = f32[768,256]{1,0:T(8,128)} custom-call(bf16[32,2048]{1,0:T(8,128)(2,1)} %add_convert_fusion.2.rows_ref, f32[24,2048]{1,0:T(8,128)} %reshape.350.sec_ref, bf16[2048,256]{1,0:T(8,128)(2,1)} %add_convert_fusion.1.cols_ref), custom_call_target="tpu_custom_call" | custom-call | flops 805306368 | bytes 2162688 | tf_op jit(solution)/shard_map/pallas_call | solution.py:450
  (39 shorter events, 0.2 us)
Async XLA Ops:
  0.0 0.8 copy-start
  0.0 25.3 %copy-start.10 = (s32[32]{0:T(128)S(1)}, s32[32]{0:T(128)}, u32[]{:S(2)}) copy-start(s32[32]{0:T(128)} %param.14) | copy-start | bytes 388
  0.0 25.3 %copy-start.11 = (s32[32]{0:T(128)S(1)}, s32[32]{0:T(128)}, u32[]{:S(2)}) copy-start(s32[32]{0:T(128)} %param.16) | copy-start | bytes 388
  29.5 1.8 %copy-start.9 = (s32[32]{0:T(128)S(1)}, s32[32]{0:T(128)}, u32[]{:S(2)}) copy-start(s32[32]{0:T(128)} %param.15) | copy-start | bytes 388
  31.5 1.8 %copy-start.1 = (bf16[64,8192]{1,0:T(8,128)(2,1)S(1)}, bf16[64,8192]{1,0:T(8,128)(2,1)}, u32[]{:S(2)}) copy-start(bf16[64,8192]{1,0:T(8,128)(2,1)} %param.18) | copy-start | bytes 3145732
  31.5 1.8 %copy-start.2 = (bf16[32,16384]{1,0:T(8,128)(2,1)S(1)}, bf16[32,16384]{1,0:T(8,128)(2,1)}, u32[]{:S(2)}) copy-start(bf16[32,16384]{1,0:T(8,128)(2,1)} %param.13) | copy-start | bytes 3145732
  74.6 9.6 %copy-start.3 = (f32[32,64]{1,0:T(8,128)S(1)}, f32[32,64]{1,0:T(8,128)}, u32[]{:S(2)}) copy-start(f32[32,64]{1,0:T(8,128)} %param.22) | copy-start | bytes 24580
  74.6 9.6 %copy-start.4 = (s32[32,64]{1,0:T(8,128)S(1)}, s32[32,64]{1,0:T(8,128)}, u32[]{:S(2)}) copy-start(s32[32,64]{1,0:T(8,128)} %param.20) | copy-start | bytes 24580
  75.6 8.7 %copy-start.5 = (f32[32,64]{1,0:T(8,128)S(1)}, f32[32,64]{1,0:T(8,128)}, u32[]{:S(2)}) copy-start(f32[32,64]{1,0:T(8,128)} %param.21) | copy-start | bytes 24580
  75.6 8.8 %copy-start.6 = (s32[32,64]{1,0:T(8,128)S(1)}, s32[32,64]{1,0:T(8,128)}, u32[]{:S(2)}) copy-start(s32[32,64]{1,0:T(8,128)} %param.19) | copy-start | bytes 24580
  75.8 13.0 %collective-permute-start = (f32[32,2,1,64]{3,2,1,0:T(1,128)S(1)}, f32[32,2,1,64]{3,2,1,0:T(1,128)S(1)}, u32[]{:S(2)}, u32[]{:S(2)}) collective-permute-start(f32[32,2,1,64]{3,2,1,0:T(1,128)S(1)} %get-tuple-element.17), channel_id=1, source_target_pairs={{0,1},{1,2},{2,3},{3,4},{4,5},{5,6},{6,7},{7,8},{8,9},{9,10},{10,1... | collective-permute-start | bytes 49160 | tf_op jit(solution)/shard_map/ppermute | solution.py:378
  78.0 10.9 %collective-permute-start.1 = (f32[32,2,1,64]{3,2,1,0:T(1,128)S(1)}, f32[32,2,1,64]{3,2,1,0:T(1,128)}, u32[]{:S(2)}, u32[]{:S(2)}) collective-permute-start(f32[32,2,1,64]{3,2,1,0:T(1,128)S(1)} %get-tuple-element.18), channel_id=1, source_target_pairs={{1,0},{2,1},{3,2},{4,3},{5,4},{6,5},{7,6},{8,7},{9,8},{10,9},{11,1... | collective-permute-start | bytes 49160 | tf_op jit(solution)/shard_map/ppermute | solution.py:379
  84.0 1.2 %copy-start.7 = (s32[32,128]{1,0:T(8,128)S(1)}, s32[32,128]{1,0:T(8,128)}, u32[]{:S(2)}) copy-start(s32[32,128]{1,0:T(8,128)} %param.23) | copy-start | bytes 49156
  84.1 4.5 %copy-start.8 = (f32[32,128]{1,0:T(8,128)S(1)}, f32[32,128]{1,0:T(8,128)}, u32[]{:S(2)}) copy-start(f32[32,128]{1,0:T(8,128)} %param.24) | copy-start | bytes 49156

commit v9 on v8

--- a/solution.py
+++ b/solution.py
@@ -12,7 +12,7 @@
 Z_CHIPS = 8
 
 
-def phase_table(row_count, half_cols):
+def phase_factors(row_count, half_cols):
     shift_ids = jnp.arange(SHIFTS)
     shift_rows = (shift_ids // 8 - SHIFTS // 16).astype(jnp.float32)
     shift_cols = (shift_ids % 8 - 4).astype(jnp.float32)
@@ -28,11 +28,7 @@
     lane_angle = (
         shift_rows[:, None] * lane_rows[None, :] + shift_cols[:, None] * lane_cols[None, :]
     ) * step
-    cos_b, sin_b = jnp.cos(block_angle)[:, :, None], jnp.sin(block_angle)[:, :, None]
-    cos_l, sin_l = jnp.cos(lane_angle)[:, None, :], jnp.sin(lane_angle)[:, None, :]
-    cos_t = (cos_b * cos_l - sin_b * sin_l).reshape(SHIFTS, row_count * half_cols)
-    sin_t = (sin_b * cos_l + cos_b * sin_l).reshape(SHIFTS, row_count * half_cols)
-    return jnp.concatenate([cos_t, sin_t], axis=1).astype(jnp.bfloat16)
+    return (jnp.cos(block_angle), jnp.sin(block_angle), jnp.cos(lane_angle), jnp.sin(lane_angle))
 
 
 def exchange_kernel(count, place, picks, *refs):
@@ -146,7 +142,7 @@
     barrier = pltpu.get_barrier_semaphore()
     for device in devices:
         pl.semaphore_signal(barrier, 1, device_id=device, device_id_type=pl.DeviceIdType.MESH)
-    pl.semaphore_wait(barrier, len(devices))
+    return lambda: pl.semaphore_wait(barrier, len(devices))
 
 
 def run_phase(count, place, pick, x_ref, out_ref, local_sem, send_sems, recv_sems):
@@ -177,14 +173,29 @@
     return [device(lax.rem(me + k, count)) for k in range(1, count)]
 
 
-def reduce_chain_kernel(y_chips, groups, x_ref, out_ref, core_buf, y_src, y_buf, z_src, z_buf, d_src,
+def stencil_kernel(ybase_ref, yfrac_ref, xbase_ref, xfrac_ref, rows_ref, cols_ref):
+    y_rows = rows_ref.shape[0]
+    y_ids = lax.axis_index("grp") * y_rows + lax.broadcasted_iota(jnp.int32, rows_ref.shape, 0)
+    y_base, y_frac = ybase_ref[...], yfrac_ref[...]
+    rows = jnp.where(y_ids == y_base, 1.0 - y_frac, 0.0) + jnp.where(y_ids == y_base + 1, y_frac, 0.0)
+    rows_ref[...] = rows.astype(rows_ref.dtype)
+    x_ids = lax.broadcasted_iota(jnp.int32, cols_ref.shape, 1)
+    x_base, x_frac = xbase_ref[...], xfrac_ref[...]
+    cols = jnp.where(x_ids == x_base, 1.0 - x_frac, 0.0) + jnp.where(x_ids == x_base + 1, x_frac, 0.0)
+    cols_ref[...] = cols.astype(cols_ref.dtype)
+
+
+def reduce_chain_kernel(y_chips, groups, x_ref, ybase_ref, yfrac_ref, xbase_ref, xfrac_ref,
+                        out_ref, rows_ref, cols_ref, core_buf, y_src, y_buf, z_src, z_buf, d_src,
                         local_sems, send_sems, recv_sems):
-    signal_all(
+    arrive = signal_all(
         peers(2, core_place)
         + peers(y_chips, y_place)
         + peers(Z_CHIPS, z_place)
         + peers(groups, group_place)
     )
+    stencil_kernel(ybase_ref, yfrac_ref, xbase_ref, xfrac_ref, rows_ref, cols_ref)
+    arrive()
     run_phase(2, core_place, row_block, x_ref, core_buf, local_sems.at[0], send_sems.at[0], recv_sems.at[0])
     y_src[...] = (core_buf[0] + core_buf[1]).astype(y_src.dtype)
     run_phase(
@@ -200,15 +211,20 @@
     run_phase(groups, group_place, whole, d_src, out_ref, local_sems.at[3], send_sems.at[3], recv_sems.at[3])
 
 
-def reduce_chain(x, y_chips, groups, collective_id):
+def reduce_chain(x, stencil, y_rows, side, y_chips, groups, collective_id):
     _, rows, width = x.shape
     band = width // (y_chips * Z_CHIPS)
     wide = 8
+    depth = stencil[0].shape[1]
     return pl.pallas_call(
         functools.partial(reduce_chain_kernel, y_chips, groups),
-        out_shape=jax.ShapeDtypeStruct((groups, rows, band), jnp.bfloat16),
-        in_specs=[pl.BlockSpec(memory_space=pltpu.VMEM)],
-        out_specs=pl.BlockSpec(memory_space=pltpu.VMEM),
+        out_shape=[
+            jax.ShapeDtypeStruct((groups, rows, band), jnp.bfloat16),
+            jax.ShapeDtypeStruct((y_rows, depth), jnp.bfloat16),
+            jax.ShapeDtypeStruct((depth, side), jnp.bfloat16),
+        ],
+        in_specs=[pl.BlockSpec(memory_space=pltpu.VMEM)] * 5,
+        out_specs=[pl.BlockSpec(memory_space=pltpu.VMEM)] * 3,
         scratch_shapes=[
             pltpu.VMEM((2, rows, width), x.dtype),
             pltpu.VMEM((rows, width), jnp.bfloat16),
@@ -221,23 +237,43 @@
             pltpu.SemaphoreType.DMA((4, wide)),
         ],
         compiler_params=pltpu.CompilerParams(collective_id=collective_id, has_side_effects=True),
-    )(x)
-
-
-def gather_chain_kernel(y_chips, x_ref, out_ref, z_buf, y_buf, local_sems, send_sems, recv_sems):
-    signal_all(peers(Z_CHIPS, z_place) + peers(y_chips, y_place) + peers(2, core_place))
+    )(x, *stencil)
+
+
+def phase_kernel(cos_b, sin_b, cos_l, sin_l, phase_ref):
+    half = phase_ref.shape[1] // 2
+    lanes = cos_l.shape[1]
+    c_l, s_l = cos_l[...], sin_l[...]
+    for q in range(cos_b.shape[1]):
+        c_b, s_b = cos_b[:, q : q + 1], sin_b[:, q : q + 1]
+        phase_ref[:, q * lanes : (q + 1) * lanes] = (c_b * c_l - s_b * s_l).astype(phase_ref.dtype)
+        phase_ref[:, half + q * lanes : half + (q + 1) * lanes] = (s_b * c_l + c_b * s_l).astype(
+            phase_ref.dtype
+        )
+
+
+def gather_chain_kernel(y_chips, x_ref, cos_b, sin_b, cos_l, sin_l, out_ref, phase_ref, z_buf, y_buf,
+                        local_sems, send_sems, recv_sems):
+    arrive = signal_all(peers(Z_CHIPS, z_place) + peers(y_chips, y_place) + peers(2, core_place))
+    phase_kernel(cos_b, sin_b, cos_l, sin_l, phase_ref)
+    arrive()
     run_phase(Z_CHIPS, z_place, whole, x_ref, z_buf, local_sems.at[0], send_sems.at[0], recv_sems.at[0])
     run_phase(y_chips, y_place, entire, z_buf, y_buf, local_sems.at[1], send_sems.at[1], recv_sems.at[1])
     run_phase(2, core_place, entire, y_buf, out_ref, local_sems.at[2], send_sems.at[2], recv_sems.at[2])
 
 
-def gather_chain(x, y_chips, collective_id):
+def gather_chain(x, trig, y_chips, collective_id):
     _, rows, lanes = x.shape
+    shifts = trig[0].shape[0]
+    table = 2 * trig[0].shape[1] * trig[2].shape[1]
     return pl.pallas_call(
         functools.partial(gather_chain_kernel, y_chips),
-        out_shape=jax.ShapeDtypeStruct((2, y_chips, Z_CHIPS, rows, lanes), x.dtype),
-        in_specs=[pl.BlockSpec(memory_space=pltpu.VMEM)],
-        out_specs=pl.BlockSpec(memory_space=pltpu.VMEM),
+        out_shape=[
+            jax.ShapeDtypeStruct((2, y_chips, Z_CHIPS, rows, lanes), x.dtype),
+            jax.ShapeDtypeStruct((shifts, table), jnp.bfloat16),
+        ],
+        in_specs=[pl.BlockSpec(memory_space=pltpu.VMEM)] * 5,
+        out_specs=[pl.BlockSpec(memory_space=pltpu.VMEM)] * 2,
         scratch_shapes=[
             pltpu.VMEM((Z_CHIPS, rows, lanes), x.dtype),
             pltpu.VMEM((y_chips, Z_CHIPS, rows, lanes), x.dtype),
@@ -246,7 +282,7 @@
             pltpu.SemaphoreType.DMA((3, Z_CHIPS)),
         ],
         compiler_params=pltpu.CompilerParams(collective_id=collective_id, has_side_effects=True),
-    )(x)
+    )(x, *trig)
 
 
 def align_frames(frames, ctf_rows, ref_re, ref_im, phase, score_scale):
@@ -316,7 +352,6 @@
     band_rows = row_count // slab_count
     band_pixels = band_rows * half_cols
     z_dev = 2 * band_rows
-    phase = phase_table(row_count, half_cols)
     score_scale = 2.0 / math.sqrt(2.0 * pixels)
     channel_scale = jnp.array(
         [
@@ -331,7 +366,8 @@
     ref_halves = references.reshape(2, -1, lanes)
     my_half = lax.dynamic_slice_in_dim(ref_halves, core, 1, 0)
     y_chips = slab_count // Z_CHIPS
-    both_halves = gather_chain(my_half, y_chips, 0).reshape(2, slab_count, pixels)
+    gathered, phase = gather_chain(my_half, phase_factors(row_count, half_cols), y_chips, 0)
+    both_halves = gathered.reshape(2, slab_count, pixels)
     class_ids = jnp.arange(class_count, dtype=jnp.int32)
     owner_of = jnp.sum(
         jnp.where(image_class[:, None] == class_ids[None, :], class_owner[None, :], 0), axis=1
@@ -369,7 +405,17 @@
         [partial.reshape(2, half_rows, pixels), jnp.broadcast_to(tiled_counts, (2, count_rows, pixels))],
         axis=1,
     )
-    groups = reduce_chain(by_half, slab_count // Z_CHIPS, group_count, 1)
+    y_rows = side_cells // group_count
+    flat = class_count * half_cols
+    stencil = (
+        y_base.reshape(1, flat),
+        y_frac.reshape(1, flat),
+        x_base.reshape(flat, 1),
+        x_frac.reshape(flat, 1),
+    )
+    groups, row_weights, col_weights = reduce_chain(
+        by_half, stencil, y_rows, side_cells, slab_count // Z_CHIPS, group_count, 1
+    )
     groups = groups.astype(jnp.float32).reshape(group_count // 2, 2, rows, band_pixels)
     band = jnp.sum(groups[:, :, :half_rows], axis=0).reshape(class_count, 2, band_rows, half_cols)
     total_counts = jnp.sum(groups[:, 0, half_rows:], axis=0).reshape(class_count, groups_ctf)
@@ -413,18 +459,6 @@
         depth_weight,
         precision=lax.Precision.HIGHEST,
     ).reshape(3 * z_dev, class_count * half_cols)
-    y_rows = side_cells // group_count
-    y_ids = group_index * y_rows + jnp.arange(y_rows, dtype=jnp.int32)
-    row_weights = jnp.where(
-        y_ids[:, None, None] == y_base[None, :, :], (1.0 - y_frac)[None, :, :], 0.0
-    )
-    row_weights = row_weights + jnp.where(
-        y_ids[:, None, None] == y_base[None, :, :] + 1, y_frac[None, :, :], 0.0
-    )
-    row_weights = row_weights.astype(jnp.bfloat16).reshape(y_rows, class_count * half_cols)
-    col_weights = stencil_weights(x_base, x_frac, side_cells).reshape(
-        class_count * half_cols, side_cells
-    )
     inserted = insert_planes(row_weights, sectioned, col_weights)
     return inserted.reshape(3, z_dev, y_rows, side_cells)
 

time: 95.5 us -> 96.2 us (level)
  the two profiles are of different devices: /device:TPU:8 before, /device:TPU:1 now
where the time goes in v9:
time: 96.2 us; the launch traced here: 95.6 us
  Pallas kernels  62.1 us (65%)
  local copies, waits for them, and re-layouts  13.2 us (14%)
  matrix products  7.5 us (8%)
  other arithmetic  5.86 us (6%)
  starting transfers between devices  4.26 us (4%)
  waiting for transfers between devices  2.41 us (3%)
    pallas_call x1, Pallas kernels, reduce_chain(): pl.pallas_call(functools.partial(reduce_chain_kernel, y_chips, groups), o...  30.8 us
    pallas_call x1, Pallas kernels, gather_chain(): pl.pallas_call(functools.partial(gather_chain_kernel, y_chips), out_shape...  27.4 us
    unnamed x27, local copies, waits for them, and re-layouts  4.07 us
    pallas_call x1, Pallas kernels, insert_planes(): pl.pallas_call(insert_kernel, out_shape=jax.ShapeDtypeStruct((planes * y_...  3.91 us
    ppermute x1, starting transfers between devices, local(): from_below = lax.ppermute(band[:, :, band_rows - 1:], 'slab', up)  2.97 us
    dot_general x1, matrix products, local(): jnp.dot(member, stacked, precision=lax.Precision.HIGHEST, preferred_eleme...  2.45 us
    ppermute x1, waiting for transfers between devices, local(): from_above = lax.ppermute(band[:, :, :1], 'slab', down)  2.41 us
    reshape x1, local copies, waits for them, and re-layouts, local(): x_frac.reshape(flat, 1)  2.01 us
  transfers between devices with their start and end apart: 2, of which 1 were waited for; matrix products, arithmetic and copies ran while one was open for 1% of the time, Pallas kernels for 0%

profile of v9, /device:TPU:1, one launch (start us, length us, event | category | flops | bytes accessed | tf_op | source)
XLA Modules:
  0.0 95.6 jit_solution(10501600932726791949)
XLA Ops:
  0.1 0.8 copy-done
  0.8 0.2 reduce.1
  1.0 0.6 constant_dynamic-slice_fusion.x_ref
  1.6 0.9 fusion.41
  2.6 1.0 %fusion.39 = (f32[128,128]{1,0:T(8,128)}, f32[128,128]{1,0:T(8,128)}) fusion(f32[128]{0:T(128)S(1)} %get-tuple-element.35, f32[128]{0:T(128)S(1)} %get-tuple-element.34, f32[128]{0:T(128)S(1)} %get-tuple-element.36, f32[128]{0:T(128)S(1)} %get-tuple-element.37), kind=kLoop, calls=%fused_computation.63 | loop fusion | flops 65536 | bytes 133120 | tf_op jit(solution)/shard_map/sin | solution.py:31
  3.6 27.4 %shard_map.127 = (bf16[2,4,8,64,128]{4,3,2,1,0:T(8,128)(2,1)}, bf16[128,16384]{1,0:T(8,128)(2,1)}) custom-call(bf16[1,64,128]{2,1,0:T(8,128)(2,1)} %constant_dynamic-slice_fusion.x_ref, f32[128,64]{1,0:T(8,128)} %get-tuple-element.30.cos_b, f32[128,64]{1,0:T(8,128)} %get-tuple-element.29.sin_b, f32[128,128]{1,0:T(8,128)} %get-tuple-element.28.cos_l, ...), custom_call_target="tpu_custom_call" | custom-call | tf_op jit(solution)/shard_map/pallas_call | solution.py:269
  31.0 1.3 %slice_bitcast_fusion.1 = (bf16[4,8,64,128]{3,2,1,0:T(8,128)(2,1)S(1)}, bf16[4,8,64,128]{3,2,1,0:T(8,128)(2,1)S(1)}) fusion(bf16[2,4,8,64,128]{4,3,2,1,0:T(8,128)(2,1)} %get-tuple-element.10), kind=kLoop, calls=%fused_computation.42 | loop fusion | bytes 2097152
  32.4 0.0 copy-start.10
  32.4 0.0 copy-start.3
  32.4 0.2 select_reduce_fusion
  32.6 0.4 fusion
  33.0 0.4 fusion.1
  33.5 0.2 fusion.46
  33.6 0.3 copy-done.3
  33.9 0.7 fusion.8
  34.6 1.5 %copy-done.1 = bf16[128,16384]{1,0:T(8,128)(2,1)S(1)} copy-done((bf16[128,16384]{1,0:T(8,128)(2,1)S(1)}, bf16[128,16384]{1,0:T(8,128)(2,1)}, u32[]{:S(2)}) %copy-start.1) | copy-done | bytes 4194328
  36.1 1.6 %fusion.72 = (f32[32]{0:T(128)S(1)}, f32[32,128]{1,0:T(8,128)S(1)}) fusion(bf16[128,16384]{1,0:T(8,128)(2,1)S(1)} %copy-done.1, bf16[32,8192]{1,0:T(8,128)(2,1)S(1)} %get-tuple-element.22, bf16[32,8192]{1,0:T(8,128)(2,1)S(1)} %get-tuple-element.21), kind=kOutput, calls=%fused_computation.127 | convolution fusion | flops 136323040 | bytes 5259392 | tf_op jit(solution)/shard_map/np,sp->ns/dot_general | solution.py:302
  37.7 0.2 fusion.47
  37.9 0.8 fusion.48
  38.7 0.4 fusion.13
  39.0 2.4 %convolution_multiply_fusion = f32[32,16384]{1,0:T(8,128)} fusion(f32[32,8192]{1,0:T(8,128)S(1)} %get-tuple-element.20, f32[32,8192]{1,0:T(8,128)S(1)} %get-tuple-element.19, s32[32]{0:T(128)S(1)} %copy-done.11), kind=kOutput, calls=%fused_computation | convolution fusion | flops 202376192 | bytes 4194432 | tf_op jit(solution)/shard_map/dot_general | solution.py:392
  41.5 1.8 %reshape.156 = f32[2,32,8192]{2,1,0:T(8,128)S(1)} reshape(f32[32,16384]{1,0:T(8,128)} %convolution_multiply_fusion) | data formatting | bytes 4194304 | tf_op jit(solution)/shard_map/reshape | solution.py:405
  43.3 0.0 copy-start.8
  43.3 0.0 copy-start.9
  43.3 0.1 tile.10
  43.4 2.0 %reshape.171.xbase_ref = s32[2048,1]{1,0:T(8,128)} reshape(s32[32,64]{1,0:T(8,128)S(1)} %copy-done.4) | data formatting | bytes 16384 | tf_op jit(solution)/shard_map/reshape | solution.py:413
  45.4 2.0 %reshape.172.xfrac_ref = f32[2048,1]{1,0:T(8,128)} reshape(f32[32,64]{1,0:T(8,128)S(1)} %copy-done.5) | data formatting | bytes 16384 | tf_op jit(solution)/shard_map/reshape | solution.py:414
  47.4 0.7 reshape.157.ybase_ref
  48.1 0.7 reshape.158.yfrac_ref
  48.8 1.7 %pad_maximum_fusion.x_ref = f32[2,40,8192]{2,1,0:T(8,128)} fusion(f32[2,8,8192]{2,1,0:T(8,128)S(1)} %broadcast_in_dim.30, f32[2,32,8192]{2,1,0:T(8,128)S(1)} %reshape.156), kind=kLoop, calls=%fused_computation.7 | loop fusion | flops 655360 | bytes 5242880 | tf_op jit(solution)/shard_map/concatenate | solution.py:404
  50.5 30.8 %shard_map.128 = (bf16[8,40,256]{2,1,0:T(8,128)(2,1)}, bf16[32,2048]{1,0:T(8,128)(2,1)}, bf16[2048,256]{1,0:T(8,128)(2,1)}) custom-call(f32[2,40,8192]{2,1,0:T(8,128)} %pad_maximum_fusion.x_ref, s32[1,2048]{1,0:T(1,128)} %reshape.157.ybase_ref, f32[1,2048]{1,0:T(1,128)} %reshape.158.yfrac_ref, s32[2048,1]{1,0:T(8,128)} %reshape.171.xbase_ref, ...), custom_call_target="tpu_custom_call" | custom-call | tf_op jit(solution)/shard_map/pallas_call | solution.py:219
  81.3 0.9 bitcast_convert_fusion
  82.3 0.1 reshape.163
  82.4 0.1 fusion.71
  82.4 3.0 %collective-permute-start = (f32[32,2,1,64]{3,2,1,0:T(1,128)S(1)}, f32[32,2,1,64]{3,2,1,0:T(1,128)S(1)}, u32[]{:S(2)}, u32[]{:S(2)}) collective-permute-start(f32[32,2,1,64]{3,2,1,0:T(1,128)S(1)} %get-tuple-element.25), channel_id=1, source_target_pairs={{0,1},{1,2},{2,3},{3,4},{4,5},{5,6},{6,7},{7,8},{8,9},{9,10},{10,1... | collective-permute-start | bytes 49160 | tf_op jit(solution)/shard_map/ppermute | solution.py:424
  85.4 1.3 %collective-permute-start.1 = (f32[32,2,1,64]{3,2,1,0:T(1,128)S(1)}, f32[32,2,1,64]{3,2,1,0:T(1,128)S(1)}, u32[]{:S(2)}, u32[]{:S(2)}) collective-permute-start(f32[32,2,1,64]{3,2,1,0:T(1,128)S(1)} %get-tuple-element.26), channel_id=1, source_target_pairs={{1,0},{2,1},{3,2},{4,3},{5,4},{6,5},{7,6},{8,7},{9,8},{10,9},{11,1... | collective-permute-start | bytes 49160 | tf_op jit(solution)/shard_map/ppermute | solution.py:425
  86.7 0.1 convert_multiply_fusion
  86.9 0.1 reshape.164
  87.0 0.3 convolution_multiply_fusion.1
  87.3 0.2 copy-done.6
  87.4 0.1 broadcast_add_fusion
  87.5 0.1 broadcast_subtract_fusion
  87.6 0.1 reshape.165
  87.7 2.4 %collective-permute-done.1 = f32[32,2,1,64]{3,2,1,0:T(1,128)S(1)} collective-permute-done((f32[32,2,1,64]{3,2,1,0:T(1,128)S(1)}, f32[32,2,1,64]{3,2,1,0:T(1,128)S(1)}, u32[]{:S(2)}, u32[]{:S(2)}) %collective-permute-start.1) | collective-permute-done | bytes 16416 | tf_op jit(solution)/shard_map/ppermute | solution.py:425
  90.1 0.7 convolution_bitcast_fusion
  90.8 0.1 copy.28
  90.9 0.8 reshape.166.sec_ref
  91.7 3.9 %shard_map.129 = f32[768,256]{1,0:T(8,128)} custom-call(bf16[32,2048]{1,0:T(8,128)(2,1)} %get-tuple-element.12.rows_ref, f32[24,2048]{1,0:T(8,128)} %reshape.166.sec_ref, bf16[2048,256]{1,0:T(8,128)(2,1)} %get-tuple-element.14.cols_ref), custom_call_target="tpu_custom_call" | custom-call | flops 805306368 | bytes 2162688 | tf_op jit(solution)/shard_map/pallas_call | solution.py:484
  (27 shorter events, 0.1 us)
Async XLA Ops:
  0.0 0.8 copy-start
  0.0 32.3 %copy-start.11 = (s32[32]{0:T(128)S(1)}, s32[32]{0:T(128)}, u32[]{:S(2)}) copy-start(s32[32]{0:T(128)} %param.14) | copy-start | bytes 388
  0.0 32.3 %copy-start.12 = (s32[32]{0:T(128)S(1)}, s32[32]{0:T(128)}, u32[]{:S(2)}) copy-start(s32[32]{0:T(128)} %param.16) | copy-start | bytes 388
  32.4 1.1 %copy-start.10 = (s32[32]{0:T(128)S(1)}, s32[32]{0:T(128)}, u32[]{:S(2)}) copy-start(s32[32]{0:T(128)} %param.15) | copy-start | bytes 388
  32.4 1.3 %copy-start.2 = (bf16[64,8192]{1,0:T(8,128)(2,1)S(1)}, bf16[64,8192]{1,0:T(8,128)(2,1)}, u32[]{:S(2)}) copy-start(bf16[64,8192]{1,0:T(8,128)(2,1)} %param.18) | copy-start | bytes 3145732
  32.4 1.5 %copy-start.3 = (bf16[32,16384]{1,0:T(8,128)(2,1)S(1)}, bf16[32,16384]{1,0:T(8,128)(2,1)}, u32[]{:S(2)}) copy-start(bf16[32,16384]{1,0:T(8,128)(2,1)} %param.13) | copy-start | bytes 3145732
  33.9 2.2 %copy-start.1 = (bf16[128,16384]{1,0:T(8,128)(2,1)S(1)}, bf16[128,16384]{1,0:T(8,128)(2,1)}, u32[]{:S(2)}) copy-start(bf16[128,16384]{1,0:T(8,128)(2,1)} %get-tuple-element.11) | copy-start | bytes 12582916
  41.5 1.9 %copy-start.4 = (s32[32,64]{1,0:T(8,128)S(1)}, s32[32,64]{1,0:T(8,128)}, u32[]{:S(2)}) copy-start(s32[32,64]{1,0:T(8,128)} %param.19) | copy-start | bytes 24580
  41.5 3.9 %copy-start.5 = (f32[32,64]{1,0:T(8,128)S(1)}, f32[32,64]{1,0:T(8,128)}, u32[]{:S(2)}) copy-start(f32[32,64]{1,0:T(8,128)} %param.21) | copy-start | bytes 24580
  43.3 4.1 %copy-start.8 = (s32[32,64]{1,0:T(8,128)S(1)}, s32[32,64]{1,0:T(8,128)}, u32[]{:S(2)}) copy-start(s32[32,64]{1,0:T(8,128)} %param.20) | copy-start | bytes 24580
  43.3 4.8 %copy-start.9 = (f32[32,64]{1,0:T(8,128)S(1)}, f32[32,64]{1,0:T(8,128)}, u32[]{:S(2)}) copy-start(f32[32,64]{1,0:T(8,128)} %param.22) | copy-start | bytes 24580
  82.4 5.3 %collective-permute-start = (f32[32,2,1,64]{3,2,1,0:T(1,128)S(1)}, f32[32,2,1,64]{3,2,1,0:T(1,128)S(1)}, u32[]{:S(2)}, u32[]{:S(2)}) collective-permute-start(f32[32,2,1,64]{3,2,1,0:T(1,128)S(1)} %get-tuple-element.25), channel_id=1, source_target_pairs={{0,1},{1,2},{2,3},{3,4},{4,5},{5,6},{6,7},{7,8},{8,9},{9,10},{10,1... | collective-permute-start | bytes 49160 | tf_op jit(solution)/shard_map/ppermute | solution.py:424
  85.4 4.7 %collective-permute-start.1 = (f32[32,2,1,64]{3,2,1,0:T(1,128)S(1)}, f32[32,2,1,64]{3,2,1,0:T(1,128)S(1)}, u32[]{:S(2)}, u32[]{:S(2)}) collective-permute-start(f32[32,2,1,64]{3,2,1,0:T(1,128)S(1)} %get-tuple-element.26), channel_id=1, source_target_pairs={{1,0},{2,1},{3,2},{4,3},{5,4},{6,5},{7,6},{8,7},{9,8},{10,9},{11,1... | collective-permute-start | bytes 49160 | tf_op jit(solution)/shard_map/ppermute | solution.py:425
  86.7 0.7 copy-start.6
  86.7 0.8 copy-start.7

commit v10 on v9

--- a/solution.py
+++ b/solution.py
@@ -173,28 +173,35 @@
     return [device(lax.rem(me + k, count)) for k in range(1, count)]
 
 
-def stencil_kernel(ybase_ref, yfrac_ref, xbase_ref, xfrac_ref, rows_ref, cols_ref):
+def stencil_kernel(base_ref, frac_ref, rows_ref, cols_ref):
     y_rows = rows_ref.shape[0]
     y_ids = lax.axis_index("grp") * y_rows + lax.broadcasted_iota(jnp.int32, rows_ref.shape, 0)
-    y_base, y_frac = ybase_ref[...], yfrac_ref[...]
+    y_base, y_frac = base_ref[0:1, :], frac_ref[0:1, :]
     rows = jnp.where(y_ids == y_base, 1.0 - y_frac, 0.0) + jnp.where(y_ids == y_base + 1, y_frac, 0.0)
     rows_ref[...] = rows.astype(rows_ref.dtype)
-    x_ids = lax.broadcasted_iota(jnp.int32, cols_ref.shape, 1)
-    x_base, x_frac = xbase_ref[...], xfrac_ref[...]
+    x_ids = lax.broadcasted_iota(jnp.int32, cols_ref.shape, 0)
+    x_base, x_frac = base_ref[1:2, :], frac_ref[1:2, :]
     cols = jnp.where(x_ids == x_base, 1.0 - x_frac, 0.0) + jnp.where(x_ids == x_base + 1, x_frac, 0.0)
     cols_ref[...] = cols.astype(cols_ref.dtype)
 
 
-def reduce_chain_kernel(y_chips, groups, x_ref, ybase_ref, yfrac_ref, xbase_ref, xfrac_ref,
-                        out_ref, rows_ref, cols_ref, core_buf, y_src, y_buf, z_src, z_buf, d_src,
-                        local_sems, send_sems, recv_sems):
+def neighbour_place():
+    group, slab = lax.axis_index("grp"), lax.axis_index("slab")
+    count = lax.axis_size("slab")
+    return [(group, lax.rem(slab + 1, count)), (group, lax.rem(slab + count - 1, count))]
+
+
+def reduce_chain_kernel(y_chips, groups, x_ref, base_ref, frac_ref,
+                        total_ref, halo_ref, rows_ref, cols_ref, core_buf, y_src, y_buf, z_src, z_buf,
+                        d_src, d_buf, local_sems, send_sems, recv_sems, halo_send, halo_recv):
     arrive = signal_all(
         peers(2, core_place)
         + peers(y_chips, y_place)
         + peers(Z_CHIPS, z_place)
         + peers(groups, group_place)
-    )
-    stencil_kernel(ybase_ref, yfrac_ref, xbase_ref, xfrac_ref, rows_ref, cols_ref)
+        + neighbour_place()
+    )
+    stencil_kernel(base_ref, frac_ref, rows_ref, cols_ref)
     arrive()
     run_phase(2, core_place, row_block, x_ref, core_buf, local_sems.at[0], send_sems.at[0], recv_sems.at[0])
     y_src[...] = (core_buf[0] + core_buf[1]).astype(y_src.dtype)
@@ -208,7 +215,26 @@
         local_sems.at[2], send_sems.at[2], recv_sems.at[2],
     )
     d_src[0] = jnp.sum(z_buf[...].astype(jnp.float32), axis=0).astype(d_src.dtype)
-    run_phase(groups, group_place, whole, d_src, out_ref, local_sems.at[3], send_sems.at[3], recv_sems.at[3])
+    run_phase(groups, group_place, whole, d_src, d_buf, local_sems.at[3], send_sems.at[3], recv_sems.at[3])
+    for half in range(2):
+        total_ref[half] = jnp.sum(
+            jnp.stack([d_buf[j].astype(jnp.float32) for j in range(half, groups, 2)]), axis=0
+        )
+    copies = []
+    for side, device in enumerate(neighbour_place()):
+        copy = pltpu.make_async_remote_copy(
+            src_ref=total_ref,
+            dst_ref=halo_ref.at[side],
+            send_sem=halo_send.at[side],
+            recv_sem=halo_recv.at[side],
+            device_id=device,
+            device_id_type=pl.DeviceIdType.MESH,
+        )
+        copy.start()
+        copies.append(copy)
+    for copy in copies:
+        copy.wait_send()
+        copy.wait_recv()
 
 
 def reduce_chain(x, stencil, y_rows, side, y_chips, groups, collective_id):
@@ -219,12 +245,13 @@
     return pl.pallas_call(
         functools.partial(reduce_chain_kernel, y_chips, groups),
         out_shape=[
-            jax.ShapeDtypeStruct((groups, rows, band), jnp.bfloat16),
+            jax.ShapeDtypeStruct((2, rows, band), jnp.float32),
+            jax.ShapeDtypeStruct((2, 2, rows, band), jnp.float32),
             jax.ShapeDtypeStruct((y_rows, depth), jnp.bfloat16),
-            jax.ShapeDtypeStruct((depth, side), jnp.bfloat16),
-        ],
-        in_specs=[pl.BlockSpec(memory_space=pltpu.VMEM)] * 5,
-        out_specs=[pl.BlockSpec(memory_space=pltpu.VMEM)] * 3,
+            jax.ShapeDtypeStruct((side, depth), jnp.bfloat16),
+        ],
+        in_specs=[pl.BlockSpec(memory_space=pltpu.VMEM)] * 3,
+        out_specs=[pl.BlockSpec(memory_space=pltpu.VMEM)] * 4,
         scratch_shapes=[
             pltpu.VMEM((2, rows, width), x.dtype),
             pltpu.VMEM((rows, width), jnp.bfloat16),
@@ -232,9 +259,12 @@
             pltpu.VMEM((rows, width // y_chips), jnp.bfloat16),
             pltpu.VMEM((Z_CHIPS, rows, band), jnp.bfloat16),
             pltpu.VMEM((1, rows, band), jnp.bfloat16),
+            pltpu.VMEM((groups, rows, band), jnp.bfloat16),
             pltpu.SemaphoreType.DMA((4,)),
             pltpu.SemaphoreType.DMA((4, wide)),
             pltpu.SemaphoreType.DMA((4, wide)),
+            pltpu.SemaphoreType.DMA((2,)),
+            pltpu.SemaphoreType.DMA((2,)),
         ],
         compiler_params=pltpu.CompilerParams(collective_id=collective_id, has_side_effects=True),
     )(x, *stencil)
@@ -408,21 +438,18 @@
     y_rows = side_cells // group_count
     flat = class_count * half_cols
     stencil = (
-        y_base.reshape(1, flat),
-        y_frac.reshape(1, flat),
-        x_base.reshape(flat, 1),
-        x_frac.reshape(flat, 1),
-    )
-    groups, row_weights, col_weights = reduce_chain(
+        jnp.stack([y_base.reshape(flat), x_base.reshape(flat)]),
+        jnp.stack([y_frac.reshape(flat), x_frac.reshape(flat)]),
+    )
+    total, halo, row_weights, col_weights = reduce_chain(
         by_half, stencil, y_rows, side_cells, slab_count // Z_CHIPS, group_count, 1
     )
-    groups = groups.astype(jnp.float32).reshape(group_count // 2, 2, rows, band_pixels)
-    band = jnp.sum(groups[:, :, :half_rows], axis=0).reshape(class_count, 2, band_rows, half_cols)
-    total_counts = jnp.sum(groups[:, 0, half_rows:], axis=0).reshape(class_count, groups_ctf)
-    up = [(i, i + 1) for i in range(slab_count - 1)]
-    down = [(i + 1, i) for i in range(slab_count - 1)]
-    from_below = lax.ppermute(band[:, :, band_rows - 1 :], "slab", up)
-    from_above = lax.ppermute(band[:, :, :1], "slab", down)
+    band = total[:, :half_rows].reshape(class_count, 2, band_rows, half_cols)
+    total_counts = total[0, half_rows:].reshape(class_count, groups_ctf)
+    halo = halo[:, :, :half_rows].reshape(2, class_count, 2, band_rows, half_cols)
+    slab_index = lax.axis_index("slab")
+    from_below = jnp.where(slab_index > 0, halo[0][:, :, band_rows - 1 :], 0.0)
+    from_above = jnp.where(slab_index < slab_count - 1, halo[1][:, :, :1], 0.0)
     data_bands = jnp.concatenate([from_below, band, from_above], axis=2)
     slab_index = lax.axis_index("slab")
     ctf_sq = jnp.pad(
@@ -474,13 +501,15 @@
         return carry
 
     lax.fori_loop(0, sec_ref.shape[0], body, 0)
-    out_ref[...] = jnp.dot(lifted_ref[...], cols_ref[...], preferred_element_type=jnp.float32)
+    out_ref[...] = lax.dot_general(
+        lifted_ref[...], cols_ref[...], (((1,), (1,)), ((), ())), preferred_element_type=jnp.float32
+    )
 
 
 def insert_planes(row_weights, sectioned, col_weights):
     planes = sectioned.shape[0]
     y_rows, depth = row_weights.shape
-    side = col_weights.shape[1]
+    side = col_weights.shape[0]
     return pl.pallas_call(
         insert_kernel,
         out_shape=jax.ShapeDtypeStruct((planes * y_rows, side), jnp.float32),

time: 96.2 us -> 90.5 us (0.941)
  Pallas kernels: 62.1 us -> 66.7 us
  starting transfers between devices: 4.26 us -> 0 us
  local copies, waits for them, and re-layouts: 13.2 us -> 9.37 us
  waiting for transfers between devices: 2.41 us -> 0 us
    reshape x6 -> x1, local copies, waits for them, and re-layouts: 5.54 us -> 0.11 us  [local(): band = total[:, :half_rows].reshape(class_count, 2, band_rows, half_cols)]
    pallas_call x1, Pallas kernels: 30.8 us -> 35.4 us  [reduce_chain(): pl.pallas_call(functools.partial(reduce_chain_kernel, y_chips, groups), o...]
    ppermute x2 -> x0, starting transfers between devices: 4.26 us -> none  [the longest x1 2.97 us: local(): from_below = lax.ppermute(band[:, :, band_rows - 1:], 'slab', up)]
    ppermute x2 -> x0, waiting for transfers between devices: 2.41 us -> none  [the longest x1 2.41 us: local(): from_above = lax.ppermute(band[:, :, :1], 'slab', down)]
    another operation x0 -> x2, other arithmetic: none -> 1.24 us  [the longest x1 0.62 us: local(): jnp.stack([y_base.reshape(flat), x_base.reshape(flat)])]
    unnamed x27 -> x31, local copies, waits for them, and re-layouts: 4.07 us -> 4.47 us
  transfers between devices with their start and end apart: 2 -> 0, of which waited for: 1 -> 0; matrix products, arithmetic and copies ran while one was open for 1% -> 0% of each run, Pallas kernels for 0% -> 0%
where the time goes in v10:
time: 90.5 us; the launch traced here: 90.1 us
  Pallas kernels  66.7 us (74%)
  local copies, waits for them, and re-layouts  9.37 us (10%)
  matrix products  7.52 us (8%)
  other arithmetic  6.21 us (7%)
    pallas_call x1, Pallas kernels, reduce_chain(): pl.pallas_call(functools.partial(reduce_chain_kernel, y_chips, groups), o...  35.4 us
    pallas_call x1, Pallas kernels, gather_chain(): pl.pallas_call(functools.partial(gather_chain_kernel, y_chips), out_shape...  27.4 us
    unnamed x31, local copies, waits for them, and re-layouts  4.47 us
    pallas_call x1, Pallas kernels, insert_planes(): pl.pallas_call(insert_kernel, out_shape=jax.ShapeDtypeStruct((planes * y_...  3.94 us
    dot_general x1, matrix products, local(): jnp.dot(member, stacked, precision=lax.Precision.HIGHEST, preferred_eleme...  2.46 us

profile of v10, /device:TPU:1, one launch (start us, length us, event | category | flops | bytes accessed | tf_op | source)
XLA Modules:
  0.0 90.1 jit_solution(16368712502050334914)
XLA Ops:
  0.0 0.8 copy-done
  0.8 0.2 reduce
  1.0 0.6 constant_dynamic-slice_fusion.x_ref
  1.6 1.0 %fusion.39 = (f32[128,128]{1,0:T(8,128)}, f32[128,128]{1,0:T(8,128)}) fusion(f32[128]{0:T(128)S(1)} %get-tuple-element.37, f32[128]{0:T(128)S(1)} %get-tuple-element.36, f32[128]{0:T(128)S(1)} %get-tuple-element.38, f32[128]{0:T(128)S(1)} %get-tuple-element.39), kind=kLoop, calls=%fused_computation.62 | loop fusion | flops 65536 | bytes 133120 | tf_op jit(solution)/shard_map/sin | solution.py:31
  2.6 1.0 %fusion.41 = (f32[128,64]{1,0:T(8,128)}, f32[128,64]{1,0:T(8,128)}) fusion(f32[128]{0:T(128)S(1)} %get-tuple-element.39, f32[64]{0:T(128)S(1)} %add_convert_fusion), kind=kLoop, calls=%fused_computation.65 | loop fusion | flops 16384 | bytes 66304 | tf_op jit(solution)/shard_map/sin | solution.py:31
  3.6 27.4 %shard_map.127 = (bf16[2,4,8,64,128]{4,3,2,1,0:T(8,128)(2,1)}, bf16[128,16384]{1,0:T(8,128)(2,1)}) custom-call(bf16[1,64,128]{2,1,0:T(8,128)(2,1)} %constant_dynamic-slice_fusion.x_ref, f32[128,64]{1,0:T(8,128)} %get-tuple-element.32.cos_b, f32[128,64]{1,0:T(8,128)} %get-tuple-element.31.sin_b, f32[128,128]{1,0:T(8,128)} %get-tuple-element.30.cos_l, ...), custom_call_target="tpu_custom_call" | custom-call | tf_op jit(solution)/shard_map/pallas_call | solution.py:299
  31.0 1.3 %slice_bitcast_fusion.1 = (bf16[4,8,64,128]{3,2,1,0:T(8,128)(2,1)S(1)}, bf16[4,8,64,128]{3,2,1,0:T(8,128)(2,1)S(1)}) fusion(bf16[2,4,8,64,128]{4,3,2,1,0:T(8,128)(2,1)} %get-tuple-element.11), kind=kLoop, calls=%fused_computation.42 | loop fusion | bytes 2097152
  32.4 0.0 copy-start.2
  32.4 0.2 select_reduce_fusion
  32.6 0.4 fusion
  33.0 0.4 fusion.1
  33.5 0.1 copy-done.2
  33.6 0.3 copy-done.3
  33.9 0.7 fusion.8
  34.6 1.5 %copy-done.1 = bf16[128,16384]{1,0:T(8,128)(2,1)S(1)} copy-done((bf16[128,16384]{1,0:T(8,128)(2,1)S(1)}, bf16[128,16384]{1,0:T(8,128)(2,1)}, u32[]{:S(2)}) %copy-start.1) | copy-done | bytes 4194328
  36.1 1.6 %fusion.72 = (f32[32]{0:T(128)S(1)}, f32[32,128]{1,0:T(8,128)S(1)}) fusion(bf16[128,16384]{1,0:T(8,128)(2,1)S(1)} %copy-done.1, bf16[32,8192]{1,0:T(8,128)(2,1)S(1)} %get-tuple-element.24, bf16[32,8192]{1,0:T(8,128)(2,1)S(1)} %get-tuple-element.23), kind=kOutput, calls=%fused_computation.128 | convolution fusion | flops 136323040 | bytes 5259392 | tf_op jit(solution)/shard_map/np,sp->ns/dot_general | solution.py:332
  37.7 0.2 fusion.47
  37.9 0.8 fusion.48
  38.7 0.4 fusion.13
  39.0 2.5 %convolution_multiply_fusion = f32[32,16384]{1,0:T(8,128)} fusion(f32[32,8192]{1,0:T(8,128)S(1)} %get-tuple-element.22, f32[32,8192]{1,0:T(8,128)S(1)} %get-tuple-element.21, s32[32]{0:T(128)S(1)} %copy-done.13), kind=kOutput, calls=%fused_computation | convolution fusion | flops 202376192 | bytes 4194432 | tf_op jit(solution)/shard_map/dot_general | solution.py:422
  41.5 1.7 %reshape.140 = f32[2,32,8192]{2,1,0:T(8,128)S(1)} reshape(f32[32,16384]{1,0:T(8,128)} %convolution_multiply_fusion) | data formatting | bytes 4194304 | tf_op jit(solution)/shard_map/reshape | solution.py:435
  43.2 0.2 fusion.46
  43.4 0.1 tile.10
  43.6 0.0 copy-start.8
  43.6 0.0 copy-start.11
  43.6 1.7 %pad_maximum_fusion.x_ref = f32[2,40,8192]{2,1,0:T(8,128)} fusion(f32[2,8,8192]{2,1,0:T(8,128)S(1)} %broadcast_in_dim.35, f32[2,32,8192]{2,1,0:T(8,128)S(1)} %reshape.140), kind=kLoop, calls=%fused_computation.7 | loop fusion | flops 655360 | bytes 5242880 | tf_op jit(solution)/shard_map/concatenate | solution.py:434
  45.3 0.1 stack_reshape.12
  45.4 0.1 stack_reshape.13
  45.5 0.6 pad_add_fusion.base_ref
  46.1 0.1 stack_reshape.14
  46.2 0.1 stack_reshape.15
  46.3 0.6 pad_maximum_fusion.1.frac_ref
  46.9 35.4 %shard_map.128 = (f32[2,40,256]{2,1,0:T(8,128)}, f32[2,2,40,256]{3,2,1,0:T(8,128)}, bf16[32,2048]{1,0:T(8,128)(2,1)}, bf16[256,2048]{1,0:T(8,128)(2,1)}) custom-call(f32[2,40,8192]{2,1,0:T(8,128)} %pad_maximum_fusion.x_ref, s32[2,2048]{1,0:T(2,128)} %pad_add_fusion.base_ref, f32[2,2048]{1,0:T(2,128)} %pad_maximum_fusion.1.frac_ref), custom_call_target="tpu_custom_call" | custom-call | tf_op jit(solution)/shard_map/pallas_call | solution.py:245
  82.2 0.7 slice.61
  82.9 0.1 reshape_squeeze.3
  83.0 0.1 convert_multiply_fusion
  83.2 0.3 convolution_multiply_fusion.1
  83.5 0.1 reshape.142
  83.6 0.4 copy-done.4
  84.0 0.1 squeeze.22
  84.1 0.1 squeeze.21
  84.3 0.1 reshape.141
  84.4 0.1 broadcast_add_fusion
  84.5 0.1 broadcast_subtract_fusion
  84.6 0.7 convolution_bitcast_fusion
  85.3 0.1 copy.22
  85.4 0.8 reshape.143.sec_ref
  86.2 3.9 %shard_map.129 = f32[768,256]{1,0:T(8,128)} custom-call(bf16[32,2048]{1,0:T(8,128)(2,1)} %get-tuple-element.13.rows_ref, f32[24,2048]{1,0:T(8,128)} %reshape.143.sec_ref, bf16[256,2048]{1,0:T(8,128)(2,1)} %get-tuple-element.16.cols_ref), custom_call_target="tpu_custom_call" | custom-call | flops 805306368 | bytes 2162688 | tf_op jit(solution)/shard_map/pallas_call | solution.py:513
  (32 shorter events, 0.2 us)
Async XLA Ops:
  0.0 0.8 copy-start
  0.0 32.4 %copy-start.13 = (s32[32]{0:T(128)S(1)}, s32[32]{0:T(128)}, u32[]{:S(2)}) copy-start(s32[32]{0:T(128)} %param.14) | copy-start | bytes 388
  0.0 32.4 %copy-start.14 = (s32[32]{0:T(128)S(1)}, s32[32]{0:T(128)}, u32[]{:S(2)}) copy-start(s32[32]{0:T(128)} %param.16) | copy-start | bytes 388
  32.4 1.2 %copy-start.2 = (bf16[64,8192]{1,0:T(8,128)(2,1)S(1)}, bf16[64,8192]{1,0:T(8,128)(2,1)}, u32[]{:S(2)}) copy-start(bf16[64,8192]{1,0:T(8,128)(2,1)} %param.18) | copy-start | bytes 3145732
  32.4 1.5 %copy-start.3 = (bf16[32,16384]{1,0:T(8,128)(2,1)S(1)}, bf16[32,16384]{1,0:T(8,128)(2,1)}, u32[]{:S(2)}) copy-start(bf16[32,16384]{1,0:T(8,128)(2,1)} %param.13) | copy-start | bytes 3145732
  32.4 1.5 %copy-start.12 = (s32[32]{0:T(128)S(1)}, s32[32]{0:T(128)}, u32[]{:S(2)}) copy-start(s32[32]{0:T(128)} %param.15) | copy-start | bytes 388
  33.9 2.2 %copy-start.1 = (bf16[128,16384]{1,0:T(8,128)(2,1)S(1)}, bf16[128,16384]{1,0:T(8,128)(2,1)}, u32[]{:S(2)}) copy-start(bf16[128,16384]{1,0:T(8,128)(2,1)} %get-tuple-element.12) | copy-start | bytes 12582916
  43.6 1.7 %copy-start.8 = (s32[32,64]{1,0:T(8,128)S(1)}, s32[32,64]{1,0:T(8,128)}, u32[]{:S(2)}) copy-start(s32[32,64]{1,0:T(8,128)} %param.20) | copy-start | bytes 24580
  43.6 1.8 %copy-start.9 = (s32[32,64]{1,0:T(8,128)S(1)}, s32[32,64]{1,0:T(8,128)}, u32[]{:S(2)}) copy-start(s32[32,64]{1,0:T(8,128)} %param.19) | copy-start | bytes 24580
  43.6 2.5 %copy-start.10 = (f32[32,64]{1,0:T(8,128)S(1)}, f32[32,64]{1,0:T(8,128)}, u32[]{:S(2)}) copy-start(f32[32,64]{1,0:T(8,128)} %param.22) | copy-start | bytes 24580
  43.6 2.6 %copy-start.11 = (f32[32,64]{1,0:T(8,128)S(1)}, f32[32,64]{1,0:T(8,128)}, u32[]{:S(2)}) copy-start(f32[32,64]{1,0:T(8,128)} %param.21) | copy-start | bytes 24580
  83.0 0.9 %copy-start.4 = (f32[2,2,40,256]{3,2,1,0:T(8,128)S(1)}, f32[2,2,40,256]{3,2,1,0:T(8,128)}, u32[]{:S(2)}) copy-start(f32[2,2,40,256]{3,2,1,0:T(8,128)} %get-tuple-element.14) | copy-start | bytes 491524
  83.2 1.1 %copy-start.5 = (f32[2,40,256]{2,1,0:T(8,128)S(1)}, f32[2,40,256]{2,1,0:T(8,128)}, u32[]{:S(2)}) copy-start(f32[2,40,256]{2,1,0:T(8,128)} %get-tuple-element.15) | copy-start | bytes 245764
  83.2 1.3 %copy-start.6 = (s32[32,128]{1,0:T(8,128)S(1)}, s32[32,128]{1,0:T(8,128)}, u32[]{:S(2)}) copy-start(s32[32,128]{1,0:T(8,128)} %param.23) | copy-start | bytes 49156
  83.2 1.3 %copy-start.7 = (f32[32,128]{1,0:T(8,128)S(1)}, f32[32,128]{1,0:T(8,128)}, u32[]{:S(2)}) copy-start(f32[32,128]{1,0:T(8,128)} %param.24) | copy-start | bytes 49156

commit v11 on v10

--- a/solution.py
+++ b/solution.py
@@ -204,7 +204,7 @@
     stencil_kernel(base_ref, frac_ref, rows_ref, cols_ref)
     arrive()
     run_phase(2, core_place, row_block, x_ref, core_buf, local_sems.at[0], send_sems.at[0], recv_sems.at[0])
-    y_src[...] = (core_buf[0] + core_buf[1]).astype(y_src.dtype)
+    y_src[...] = (core_buf[0].astype(jnp.float32) + core_buf[1].astype(jnp.float32)).astype(y_src.dtype)
     run_phase(
         y_chips, y_place, lane_blocks(y_chips), y_src, y_buf,
         local_sems.at[1], send_sems.at[1], recv_sems.at[1],
@@ -336,12 +336,9 @@
     shift_mix = jnp.dot(shift_probs, phase, preferred_element_type=jnp.float32)
     mix_re = shift_mix[:, :pixels]
     mix_im = shift_mix[:, pixels:]
-    return jnp.concatenate(
-        [
-            weight * (frame_re * mix_re + frame_im * mix_im),
-            weight * (frame_im * mix_re - frame_re * mix_im),
-        ],
-        axis=1,
+    return (
+        weight * (frame_re * mix_re + frame_im * mix_im),
+        weight * (frame_im * mix_re - frame_re * mix_im),
     )
 
 
@@ -419,10 +416,15 @@
     )
     stacked = align_frames(images, ctf_rows, ref_re, ref_im, phase, score_scale)
     member = (class_ids[:, None] == image_class[None, :]).astype(jnp.float32)
-    partial = jnp.dot(
-        member, stacked, precision=lax.Precision.HIGHEST, preferred_element_type=jnp.float32
-    ) * channel_scale[0]
-    half_rows = class_count // 2 * 2
+    aligned_re, aligned_im = stacked
+    partial_re, partial_im = (
+        jnp.dot(
+            member, part, precision=lax.Precision.HIGHEST, preferred_element_type=jnp.float32
+        ) * channel_scale[0]
+        for part in (aligned_re, aligned_im)
+    )
+    half_classes = class_count // 2
+    half_rows = half_classes * 2
     class_hits = (class_ids[:, None] == image_class[None, :]).astype(jnp.bfloat16)
     ctf_hits = (image_ctf[:, None] == jnp.arange(groups_ctf, dtype=jnp.int32)[None, :]).astype(
         jnp.bfloat16
@@ -431,10 +433,19 @@
     count_rows = class_count * groups_ctf // band_pixels
     tiled_counts = jnp.tile(counts.reshape(count_rows, band_pixels), (1, slab_count))
     rows = half_rows + count_rows
-    by_half = jnp.concatenate(
-        [partial.reshape(2, half_rows, pixels), jnp.broadcast_to(tiled_counts, (2, count_rows, pixels))],
-        axis=1,
-    )
+    by_half = jnp.stack(
+        [
+            jnp.concatenate(
+                [
+                    partial_re[h * half_classes : (h + 1) * half_classes],
+                    partial_im[h * half_classes : (h + 1) * half_classes],
+                    tiled_counts,
+                ],
+                axis=0,
+            )
+            for h in range(2)
+        ]
+    ).astype(jnp.bfloat16)
     y_rows = side_cells // group_count
     flat = class_count * half_cols
     stencil = (
@@ -444,9 +455,11 @@
     total, halo, row_weights, col_weights = reduce_chain(
         by_half, stencil, y_rows, side_cells, slab_count // Z_CHIPS, group_count, 1
     )
-    band = total[:, :half_rows].reshape(class_count, 2, band_rows, half_cols)
+    band = total[:, :half_rows].reshape(2, 2, half_classes, band_rows, half_cols)
+    band = band.transpose(0, 2, 1, 3, 4).reshape(class_count, 2, band_rows, half_cols)
     total_counts = total[0, half_rows:].reshape(class_count, groups_ctf)
-    halo = halo[:, :, :half_rows].reshape(2, class_count, 2, band_rows, half_cols)
+    halo = halo[:, :, :half_rows].reshape(2, 2, 2, half_classes, band_rows, half_cols)
+    halo = halo.transpose(0, 1, 3, 2, 4, 5).reshape(2, class_count, 2, band_rows, half_cols)
     slab_index = lax.axis_index("slab")
     from_below = jnp.where(slab_index > 0, halo[0][:, :, band_rows - 1 :], 0.0)
     from_above = jnp.where(slab_index < slab_count - 1, halo[1][:, :, :1], 0.0)

time: 90.5 us -> 86.3 us (0.954)
  local copies, waits for them, and re-layouts: 9.37 us -> 7.69 us
  Pallas kernels: 66.7 us -> 65.5 us
    concatenate x1 -> x0, other arithmetic: 1.68 us -> none  [local(): jnp.concatenate([partial.reshape(2, half_rows, pixels), jnp.broadcast_to(...]
    reshape x2, local copies, waits for them, and re-layouts: 1.85 us -> 0.27 us  [the longest x1 0.15 us: local(): halo[:, :, :half_rows].reshape(2, 2, 2, half_classes, band_rows, half_cols)]
    another operation x0 -> x2, other arithmetic: none -> 1.32 us  [local(): jnp.stack([jnp.concatenate([partial_re[h * half_classes:(h + 1) * half_cl...]
    pallas_call x1, Pallas kernels: 35.4 us -> 34.1 us  [reduce_chain(): pl.pallas_call(functools.partial(reduce_chain_kernel, y_chips, groups), o...]
    dot_general x1 -> x2, matrix products: 2.46 us -> 1.91 us  [local(): jnp.dot(member, part, precision=lax.Precision.HIGHEST, preferred_element_...]
where the time goes in v11:
time: 86.3 us; the launch traced here: 86 us
  Pallas kernels  65.5 us (76%)
  local copies, waits for them, and re-layouts  7.69 us (9%)
  matrix products  6.96 us (8%)
  other arithmetic  5.46 us (6%)
    pallas_call x1, Pallas kernels, reduce_chain(): pl.pallas_call(functools.partial(reduce_chain_kernel, y_chips, groups), o...  34.1 us
    pallas_call x1, Pallas kernels, gather_chain(): pl.pallas_call(functools.partial(gather_chain_kernel, y_chips), out_shape...  27.4 us
    unnamed x31, local copies, waits for them, and re-layouts  4.47 us
    pallas_call x1, Pallas kernels, insert_planes(): pl.pallas_call(insert_kernel, out_shape=jax.ShapeDtypeStruct((planes * y_...  3.95 us
    dot_general x2, matrix products, local(): jnp.dot(member, part, precision=lax.Precision.HIGHEST, preferred_element_...  1.91 us

profile of v11, /device:TPU:1, one launch (start us, length us, event | category | flops | bytes accessed | tf_op | source)
XLA Modules:
  0.0 86.0 jit_solution(7841987301317174212)
XLA Ops:
  0.0 0.8 copy-done
  0.8 0.2 reduce
  1.0 0.6 constant_dynamic-slice_fusion.x_ref
  1.6 1.0 %fusion.50 = (f32[128,128]{1,0:T(8,128)}, f32[128,128]{1,0:T(8,128)}) fusion(f32[128]{0:T(128)S(1)} %get-tuple-element.41, f32[128]{0:T(128)S(1)} %get-tuple-element.40, f32[128]{0:T(128)S(1)} %get-tuple-element.42, f32[128]{0:T(128)S(1)} %get-tuple-element.43), kind=kLoop, calls=%fused_computation.75 | loop fusion | flops 65536 | bytes 133120 | tf_op jit(solution)/shard_map/sin | solution.py:31
  2.6 1.0 %fusion.52 = (f32[128,64]{1,0:T(8,128)}, f32[128,64]{1,0:T(8,128)}) fusion(f32[128]{0:T(128)S(1)} %get-tuple-element.43, f32[64]{0:T(128)S(1)} %add_convert_fusion), kind=kLoop, calls=%fused_computation.78 | loop fusion | flops 16384 | bytes 66304 | tf_op jit(solution)/shard_map/sin | solution.py:31
  3.6 27.4 %shard_map.127 = (bf16[2,4,8,64,128]{4,3,2,1,0:T(8,128)(2,1)}, bf16[128,16384]{1,0:T(8,128)(2,1)}) custom-call(bf16[1,64,128]{2,1,0:T(8,128)(2,1)} %constant_dynamic-slice_fusion.x_ref, f32[128,64]{1,0:T(8,128)} %get-tuple-element.36.cos_b, f32[128,64]{1,0:T(8,128)} %get-tuple-element.35.sin_b, f32[128,128]{1,0:T(8,128)} %get-tuple-element.34.cos_l, ...), custom_call_target="tpu_custom_call" | custom-call | tf_op jit(solution)/shard_map/pallas_call | solution.py:299
  31.0 1.3 %slice_bitcast_fusion.1 = (bf16[4,8,64,128]{3,2,1,0:T(8,128)(2,1)S(1)}, bf16[4,8,64,128]{3,2,1,0:T(8,128)(2,1)S(1)}) fusion(bf16[2,4,8,64,128]{4,3,2,1,0:T(8,128)(2,1)} %get-tuple-element.11), kind=kLoop, calls=%fused_computation.51 | loop fusion | bytes 2097152
  32.4 0.0 copy-start.13
  32.4 0.2 select_reduce_fusion
  32.6 0.4 fusion.2
  33.0 0.4 fusion.3
  33.4 0.1 copy-done.2
  33.6 0.3 copy-done.3
  33.9 0.7 fusion.7
  34.6 1.5 %copy-done.1 = bf16[128,16384]{1,0:T(8,128)(2,1)S(1)} copy-done((bf16[128,16384]{1,0:T(8,128)(2,1)S(1)}, bf16[128,16384]{1,0:T(8,128)(2,1)}, u32[]{:S(2)}) %copy-start.1) | copy-done | bytes 4194328
  36.1 1.6 %fusion.84 = (f32[32]{0:T(128)S(1)}, f32[32,128]{1,0:T(8,128)S(1)}) fusion(bf16[128,16384]{1,0:T(8,128)(2,1)S(1)} %copy-done.1, bf16[32,8192]{1,0:T(8,128)(2,1)S(1)} %get-tuple-element.22, bf16[32,8192]{1,0:T(8,128)(2,1)S(1)} %get-tuple-element.21), kind=kOutput, calls=%fused_computation.142 | convolution fusion | flops 136323040 | bytes 5259392 | tf_op jit(solution)/shard_map/np,sp->ns/dot_general | solution.py:332
  37.7 0.2 fusion.57
  37.9 0.8 fusion.58
  38.6 1.0 %fusion = bf16[32,8192]{1,0:T(8,128)(2,1)S(1)} fusion(f32[32,8192]{1,0:T(8,128)S(1)} %get-tuple-element.37, f32[32,16384]{1,0:T(8,128)S(1)} %fusion.58, bf16[32,16384]{1,0:T(8,128)(2,1)S(1)} %copy-done.3, s32[32]{0:T(128)S(1)} %copy-done.12), kind=kOutput, calls=%fused_computation.2 | convolution fusion | flops 102761472 | bytes 4718720 | tf_op jit(solution)/shard_map/dot_general | solution.py:421
  39.6 1.0 %fusion.1 = bf16[32,8192]{1,0:T(8,128)(2,1)S(1)} fusion(f32[32,8192]{1,0:T(8,128)S(1)} %get-tuple-element.37, f32[32,16384]{1,0:T(8,128)S(1)} %fusion.58, bf16[32,16384]{1,0:T(8,128)(2,1)S(1)} %copy-done.3, s32[32]{0:T(128)S(1)} %copy-done.12), kind=kOutput, calls=%fused_computation.3 | convolution fusion | flops 102761472 | bytes 4718720 | tf_op jit(solution)/shard_map/dot_general | solution.py:421
  40.6 0.2 convolution_convert_fusion.3
  40.8 0.1 reshape.150
  41.0 0.0 copy-start.9
  41.0 0.0 copy-start.10
  41.0 0.1 fusion.24
  41.1 1.2 %pad_maximum_fusion.x_ref = bf16[2,40,8192]{2,1,0:T(8,128)(2,1)} fusion(bf16[1,40,8192]{2,1,0:T(8,128)(2,1)S(1)} %get-tuple-element.32, bf16[1,40,8192]{2,1,0:T(8,128)(2,1)S(1)} %get-tuple-element.31), kind=kLoop, calls=%fused_computation.20 | loop fusion | flops 655360 | bytes 2621440 | tf_op jit(solution)/shard_map/stack | solution.py:436
  42.3 0.1 stack_reshape.12
  42.4 0.1 stack_reshape.13
  42.5 0.6 pad_add_fusion.base_ref
  43.1 0.1 stack_reshape.14
  43.2 0.1 stack_reshape.15
  43.3 0.6 pad_maximum_fusion.3.frac_ref
  43.9 34.1 %shard_map.128 = (f32[2,40,256]{2,1,0:T(8,128)}, f32[2,2,40,256]{3,2,1,0:T(8,128)}, bf16[32,2048]{1,0:T(8,128)(2,1)}, bf16[256,2048]{1,0:T(8,128)(2,1)}) custom-call(bf16[2,40,8192]{2,1,0:T(8,128)(2,1)} %pad_maximum_fusion.x_ref, s32[2,2048]{1,0:T(2,128)} %pad_add_fusion.base_ref, f32[2,2048]{1,0:T(2,128)} %pad_maximum_fusion.3.frac_ref), custom_call_target="tpu_custom_call" | custom-call | tf_op jit(solution)/shard_map/pallas_call | solution.py:245
  78.0 0.7 slice.83
  78.7 0.1 reshape_squeeze.3
  78.8 0.1 convert_multiply_fusion
  79.0 0.0 copy-start.6
  79.0 0.3 convolution_multiply_fusion.2
  79.3 0.1 reshape.146
  79.4 0.4 copy-done.4
  79.7 0.2 reshape.143
  80.1 0.1 reshape.144
  80.3 0.1 broadcast_add_fusion
  80.4 0.1 broadcast_subtract_fusion
  80.4 0.7 convolution_bitcast_fusion
  81.1 0.1 copy.34
  81.2 0.8 reshape.147.sec_ref
  82.0 3.9 %shard_map.129 = f32[768,256]{1,0:T(8,128)} custom-call(bf16[32,2048]{1,0:T(8,128)(2,1)} %get-tuple-element.13.rows_ref, f32[24,2048]{1,0:T(8,128)} %reshape.147.sec_ref, bf16[256,2048]{1,0:T(8,128)(2,1)} %get-tuple-element.16.cols_ref), custom_call_target="tpu_custom_call" | custom-call | flops 805306368 | bytes 2162688 | tf_op jit(solution)/shard_map/pallas_call | solution.py:526
  (36 shorter events, 0.3 us)
Async XLA Ops:
  0.0 0.8 copy-start
  0.0 32.4 %copy-start.12 = (s32[32]{0:T(128)S(1)}, s32[32]{0:T(128)}, u32[]{:S(2)}) copy-start(s32[32]{0:T(128)} %param.14) | copy-start | bytes 388
  0.0 32.4 %copy-start.14 = (s32[32]{0:T(128)S(1)}, s32[32]{0:T(128)}, u32[]{:S(2)}) copy-start(s32[32]{0:T(128)} %param.16) | copy-start | bytes 388
  32.3 1.2 %copy-start.2 = (bf16[64,8192]{1,0:T(8,128)(2,1)S(1)}, bf16[64,8192]{1,0:T(8,128)(2,1)}, u32[]{:S(2)}) copy-start(bf16[64,8192]{1,0:T(8,128)(2,1)} %param.18) | copy-start | bytes 3145732
  32.3 1.5 %copy-start.3 = (bf16[32,16384]{1,0:T(8,128)(2,1)S(1)}, bf16[32,16384]{1,0:T(8,128)(2,1)}, u32[]{:S(2)}) copy-start(bf16[32,16384]{1,0:T(8,128)(2,1)} %param.13) | copy-start | bytes 3145732
  32.4 1.5 %copy-start.13 = (s32[32]{0:T(128)S(1)}, s32[32]{0:T(128)}, u32[]{:S(2)}) copy-start(s32[32]{0:T(128)} %param.15) | copy-start | bytes 388
  33.9 2.2 %copy-start.1 = (bf16[128,16384]{1,0:T(8,128)(2,1)S(1)}, bf16[128,16384]{1,0:T(8,128)(2,1)}, u32[]{:S(2)}) copy-start(bf16[128,16384]{1,0:T(8,128)(2,1)} %get-tuple-element.12) | copy-start | bytes 12582916
  40.9 1.4 %copy-start.8 = (s32[32,64]{1,0:T(8,128)S(1)}, s32[32,64]{1,0:T(8,128)}, u32[]{:S(2)}) copy-start(s32[32,64]{1,0:T(8,128)} %param.20) | copy-start | bytes 24580
  41.0 1.4 %copy-start.9 = (s32[32,64]{1,0:T(8,128)S(1)}, s32[32,64]{1,0:T(8,128)}, u32[]{:S(2)}) copy-start(s32[32,64]{1,0:T(8,128)} %param.19) | copy-start | bytes 24580
  41.0 2.1 %copy-start.10 = (f32[32,64]{1,0:T(8,128)S(1)}, f32[32,64]{1,0:T(8,128)}, u32[]{:S(2)}) copy-start(f32[32,64]{1,0:T(8,128)} %param.22) | copy-start | bytes 24580
  41.0 2.2 %copy-start.11 = (f32[32,64]{1,0:T(8,128)S(1)}, f32[32,64]{1,0:T(8,128)}, u32[]{:S(2)}) copy-start(f32[32,64]{1,0:T(8,128)} %param.21) | copy-start | bytes 24580
  78.8 0.9 %copy-start.4 = (f32[2,2,40,256]{3,2,1,0:T(8,128)S(1)}, f32[2,2,40,256]{3,2,1,0:T(8,128)}, u32[]{:S(2)}) copy-start(f32[2,2,40,256]{3,2,1,0:T(8,128)} %get-tuple-element.14) | copy-start | bytes 491524
  79.0 1.1 %copy-start.5 = (f32[2,40,256]{2,1,0:T(8,128)S(1)}, f32[2,40,256]{2,1,0:T(8,128)}, u32[]{:S(2)}) copy-start(f32[2,40,256]{2,1,0:T(8,128)} %get-tuple-element.15) | copy-start | bytes 245764
  79.0 1.3 %copy-start.6 = (s32[32,128]{1,0:T(8,128)S(1)}, s32[32,128]{1,0:T(8,128)}, u32[]{:S(2)}) copy-start(s32[32,128]{1,0:T(8,128)} %param.23) | copy-start | bytes 49156
  79.0 1.4 %copy-start.7 = (f32[32,128]{1,0:T(8,128)S(1)}, f32[32,128]{1,0:T(8,128)}, u32[]{:S(2)}) copy-start(f32[32,128]{1,0:T(8,128)} %param.24) | copy-start | bytes 49156

commit v12 on v11

--- a/solution.py
+++ b/solution.py
@@ -10,25 +10,6 @@
 
 SHIFTS = 128
 Z_CHIPS = 8
-
-
-def phase_factors(row_count, half_cols):
-    shift_ids = jnp.arange(SHIFTS)
-    shift_rows = (shift_ids // 8 - SHIFTS // 16).astype(jnp.float32)
-    shift_cols = (shift_ids % 8 - 4).astype(jnp.float32)
-    lanes = 128
-    per_lane_row = lanes // half_cols
-    blocks = row_count * half_cols // lanes
-    block_rows = (jnp.arange(blocks) * per_lane_row - row_count // 2).astype(jnp.float32)
-    lane_ids = jnp.arange(lanes)
-    lane_rows = (lane_ids // half_cols).astype(jnp.float32)
-    lane_cols = (lane_ids % half_cols).astype(jnp.float32)
-    step = 2.0 * math.pi / row_count
-    block_angle = shift_rows[:, None] * block_rows[None, :] * step
-    lane_angle = (
-        shift_rows[:, None] * lane_rows[None, :] + shift_cols[:, None] * lane_cols[None, :]
-    ) * step
-    return (jnp.cos(block_angle), jnp.sin(block_angle), jnp.cos(lane_angle), jnp.sin(lane_angle))
 
 
 def exchange_kernel(count, place, picks, *refs):
@@ -270,11 +251,28 @@
     )(x, *stencil)
 
 
-def phase_kernel(cos_b, sin_b, cos_l, sin_l, phase_ref):
+def phase_kernel(row_count, half_cols, phase_ref):
     half = phase_ref.shape[1] // 2
-    lanes = cos_l.shape[1]
-    c_l, s_l = cos_l[...], sin_l[...]
-    for q in range(cos_b.shape[1]):
+    lanes = 128
+    blocks = half // lanes
+    shifts = phase_ref.shape[0]
+    step = 2.0 * math.pi / row_count
+    t_b = lax.broadcasted_iota(jnp.int32, (shifts, blocks), 0)
+    q_b = lax.broadcasted_iota(jnp.int32, (shifts, blocks), 1)
+    shift_rows_b = (t_b // 8 - SHIFTS // 16).astype(jnp.float32)
+    block_rows = (q_b * (lanes // half_cols) - row_count // 2).astype(jnp.float32)
+    block_angle = shift_rows_b * block_rows * step
+    t_l = lax.broadcasted_iota(jnp.int32, (shifts, lanes), 0)
+    l_l = lax.broadcasted_iota(jnp.int32, (shifts, lanes), 1)
+    shift_rows_l = (t_l // 8 - SHIFTS // 16).astype(jnp.float32)
+    shift_cols_l = (t_l % 8 - 4).astype(jnp.float32)
+    lane_angle = (
+        shift_rows_l * (l_l // half_cols).astype(jnp.float32)
+        + shift_cols_l * (l_l % half_cols).astype(jnp.float32)
+    ) * step
+    cos_b, sin_b = jnp.cos(block_angle), jnp.sin(block_angle)
+    c_l, s_l = jnp.cos(lane_angle), jnp.sin(lane_angle)
+    for q in range(blocks):
         c_b, s_b = cos_b[:, q : q + 1], sin_b[:, q : q + 1]
         phase_ref[:, q * lanes : (q + 1) * lanes] = (c_b * c_l - s_b * s_l).astype(phase_ref.dtype)
         phase_ref[:, half + q * lanes : half + (q + 1) * lanes] = (s_b * c_l + c_b * s_l).astype(
@@ -282,27 +280,27 @@
         )
 
 
-def gather_chain_kernel(y_chips, x_ref, cos_b, sin_b, cos_l, sin_l, out_ref, phase_ref, z_buf, y_buf,
+def gather_chain_kernel(y_chips, row_count, half_cols, x_ref, out_ref, phase_ref, z_buf, y_buf,
                         local_sems, send_sems, recv_sems):
     arrive = signal_all(peers(Z_CHIPS, z_place) + peers(y_chips, y_place) + peers(2, core_place))
-    phase_kernel(cos_b, sin_b, cos_l, sin_l, phase_ref)
+    phase_kernel(row_count, half_cols, phase_ref)
     arrive()
     run_phase(Z_CHIPS, z_place, whole, x_ref, z_buf, local_sems.at[0], send_sems.at[0], recv_sems.at[0])
     run_phase(y_chips, y_place, entire, z_buf, y_buf, local_sems.at[1], send_sems.at[1], recv_sems.at[1])
     run_phase(2, core_place, entire, y_buf, out_ref, local_sems.at[2], send_sems.at[2], recv_sems.at[2])
 
 
-def gather_chain(x, trig, y_chips, collective_id):
+def gather_chain(x, row_count, half_cols, y_chips, collective_id):
     _, rows, lanes = x.shape
-    shifts = trig[0].shape[0]
-    table = 2 * trig[0].shape[1] * trig[2].shape[1]
+    shifts = SHIFTS
+    table = 2 * row_count * half_cols
     return pl.pallas_call(
-        functools.partial(gather_chain_kernel, y_chips),
+        functools.partial(gather_chain_kernel, y_chips, row_count, half_cols),
         out_shape=[
             jax.ShapeDtypeStruct((2, y_chips, Z_CHIPS, rows, lanes), x.dtype),
             jax.ShapeDtypeStruct((shifts, table), jnp.bfloat16),
         ],
-        in_specs=[pl.BlockSpec(memory_space=pltpu.VMEM)] * 5,
+        in_specs=[pl.BlockSpec(memory_space=pltpu.VMEM)],
         out_specs=[pl.BlockSpec(memory_space=pltpu.VMEM)] * 2,
         scratch_shapes=[
             pltpu.VMEM((Z_CHIPS, rows, lanes), x.dtype),
@@ -312,7 +310,7 @@
             pltpu.SemaphoreType.DMA((3, Z_CHIPS)),
         ],
         compiler_params=pltpu.CompilerParams(collective_id=collective_id, has_side_effects=True),
-    )(x, *trig)
+    )(x)
 
 
 def align_frames(frames, ctf_rows, ref_re, ref_im, phase, score_scale):
@@ -393,7 +391,7 @@
     ref_halves = references.reshape(2, -1, lanes)
     my_half = lax.dynamic_slice_in_dim(ref_halves, core, 1, 0)
     y_chips = slab_count // Z_CHIPS
-    gathered, phase = gather_chain(my_half, phase_factors(row_count, half_cols), y_chips, 0)
+    gathered, phase = gather_chain(my_half, row_count, half_cols, y_chips, 0)
     both_halves = gathered.reshape(2, slab_count, pixels)
     class_ids = jnp.arange(class_count, dtype=jnp.int32)
     owner_of = jnp.sum(

time: 86.3 us -> 83.9 us (0.972)
  other arithmetic: 5.46 us -> 3.48 us
    sin x2 -> x0, other arithmetic: 1.95 us -> none  [the longest x1 0.99 us: phase_factors(): jnp.sin(lane_angle)]
where the time goes in v12:
time: 83.9 us; the launch traced here: 83.6 us
  Pallas kernels  65.1 us (78%)
  local copies, waits for them, and re-layouts  7.71 us (9%)
  matrix products  6.95 us (8%)
  other arithmetic  3.48 us (4%)
    pallas_call x1, Pallas kernels, reduce_chain(): pl.pallas_call(functools.partial(reduce_chain_kernel, y_chips, groups), o...  33.6 us
    pallas_call x1, Pallas kernels, gather_chain(): pl.pallas_call(functools.partial(gather_chain_kernel, y_chips, row_count,...  27.6 us
    unnamed x31, local copies, waits for them, and re-layouts  4.47 us
    pallas_call x1, Pallas kernels, insert_planes(): pl.pallas_call(insert_kernel, out_shape=jax.ShapeDtypeStruct((planes * y_...  3.95 us
    dot_general x2, matrix products, local(): jnp.dot(member, part, precision=lax.Precision.HIGHEST, preferred_element_...  1.9 us

profile of v12, /device:TPU:1, one launch (start us, length us, event | category | flops | bytes accessed | tf_op | source)
XLA Modules:
  0.0 83.6 jit_solution(2022651115191738252)
XLA Ops:
  0.0 0.8 copy-done
  0.8 0.2 reduce
  1.0 0.6 constant_dynamic-slice_fusion.x_ref
  1.6 27.6 %shard_map.127 = (bf16[2,4,8,64,128]{4,3,2,1,0:T(8,128)(2,1)}, bf16[128,16384]{1,0:T(8,128)(2,1)}) custom-call(bf16[1,64,128]{2,1,0:T(8,128)(2,1)} %constant_dynamic-slice_fusion.x_ref), custom_call_target="tpu_custom_call" | custom-call | tf_op jit(solution)/shard_map/pallas_call | solution.py:297
  29.2 1.3 %slice_bitcast_fusion.1 = (bf16[4,8,64,128]{3,2,1,0:T(8,128)(2,1)S(1)}, bf16[4,8,64,128]{3,2,1,0:T(8,128)(2,1)S(1)}) fusion(bf16[2,4,8,64,128]{4,3,2,1,0:T(8,128)(2,1)} %get-tuple-element.11), kind=kLoop, calls=%fused_computation.51 | loop fusion | bytes 2097152
  30.5 0.0 copy-start.2
  30.5 0.0 copy-start.3
  30.6 0.2 select_reduce_fusion
  30.8 0.4 fusion.2
  31.2 0.4 fusion.3
  31.6 0.1 copy-done.2
  31.8 0.3 copy-done.3
  32.1 0.7 fusion.7
  32.8 1.5 %copy-done.1 = bf16[128,16384]{1,0:T(8,128)(2,1)S(1)} copy-done((bf16[128,16384]{1,0:T(8,128)(2,1)S(1)}, bf16[128,16384]{1,0:T(8,128)(2,1)}, u32[]{:S(2)}) %copy-start.1) | copy-done | bytes 4194328
  34.3 1.6 %fusion.74 = (f32[32]{0:T(128)S(1)}, f32[32,128]{1,0:T(8,128)S(1)}) fusion(bf16[128,16384]{1,0:T(8,128)(2,1)S(1)} %copy-done.1, bf16[32,8192]{1,0:T(8,128)(2,1)S(1)} %get-tuple-element.22, bf16[32,8192]{1,0:T(8,128)(2,1)S(1)} %get-tuple-element.21), kind=kOutput, calls=%fused_computation.120 | convolution fusion | flops 136323040 | bytes 5259392 | tf_op jit(solution)/shard_map/np,sp->ns/dot_general | solution.py:330
  35.9 0.2 fusion.53
  36.1 0.8 fusion.54
  36.8 1.0 %fusion.1 = bf16[32,8192]{1,0:T(8,128)(2,1)S(1)} fusion(f32[32,8192]{1,0:T(8,128)S(1)} %get-tuple-element.33, f32[32,16384]{1,0:T(8,128)S(1)} %fusion.54, bf16[32,16384]{1,0:T(8,128)(2,1)S(1)} %copy-done.3, s32[32]{0:T(128)S(1)} %copy-done.12), kind=kOutput, calls=%fused_computation.3 | convolution fusion | flops 102761472 | bytes 4718720 | tf_op jit(solution)/shard_map/dot_general | solution.py:419
  37.8 0.9 %fusion = bf16[32,8192]{1,0:T(8,128)(2,1)S(1)} fusion(f32[32,8192]{1,0:T(8,128)S(1)} %get-tuple-element.33, f32[32,16384]{1,0:T(8,128)S(1)} %fusion.54, bf16[32,16384]{1,0:T(8,128)(2,1)S(1)} %copy-done.3, s32[32]{0:T(128)S(1)} %copy-done.12), kind=kOutput, calls=%fused_computation.2 | convolution fusion | flops 102761472 | bytes 4718720 | tf_op jit(solution)/shard_map/dot_general | solution.py:419
  38.8 0.1 fusion.71
  38.8 0.2 convolution_convert_fusion.3
  39.0 0.1 reshape.92
  39.1 0.0 copy-start.9
  39.2 0.0 copy-start.10
  39.2 0.1 fusion.24
  39.3 1.2 %pad_maximum_fusion.x_ref = bf16[2,40,8192]{2,1,0:T(8,128)(2,1)} fusion(bf16[1,40,8192]{2,1,0:T(8,128)(2,1)S(1)} %get-tuple-element.32, bf16[1,40,8192]{2,1,0:T(8,128)(2,1)S(1)} %get-tuple-element.31), kind=kLoop, calls=%fused_computation.20 | loop fusion | flops 655360 | bytes 2621440 | tf_op jit(solution)/shard_map/stack | solution.py:434
  40.5 0.1 stack_reshape.12
  40.6 0.1 stack_reshape.13
  40.7 0.6 pad_add_fusion.base_ref
  41.3 0.1 stack_reshape.14
  41.4 0.1 stack_reshape.15
  41.4 0.6 pad_maximum_fusion.3.frac_ref
  42.1 33.6 %shard_map.128 = (f32[2,40,256]{2,1,0:T(8,128)}, f32[2,2,40,256]{3,2,1,0:T(8,128)}, bf16[32,2048]{1,0:T(8,128)(2,1)}, bf16[256,2048]{1,0:T(8,128)(2,1)}) custom-call(bf16[2,40,8192]{2,1,0:T(8,128)(2,1)} %pad_maximum_fusion.x_ref, s32[2,2048]{1,0:T(2,128)} %pad_add_fusion.base_ref, f32[2,2048]{1,0:T(2,128)} %pad_maximum_fusion.3.frac_ref), custom_call_target="tpu_custom_call" | custom-call | tf_op jit(solution)/shard_map/pallas_call | solution.py:226
  75.6 0.7 slice.83
  76.3 0.1 reshape_squeeze.3
  76.4 0.1 convert_multiply_fusion
  76.6 0.0 copy-start.7
  76.6 0.3 convolution_multiply_fusion.2
  76.9 0.1 reshape.88
  77.0 0.4 copy-done.4
  77.3 0.2 reshape.85
  77.7 0.1 reshape.86
  77.9 0.1 broadcast_add_fusion
  78.0 0.1 broadcast_subtract_fusion
  78.0 0.7 convolution_bitcast_fusion
  78.7 0.1 copy.28
  78.8 0.8 %reshape.89.sec_ref = f32[24,2048]{1,0:T(8,128)} reshape(f32[3,8,32,64]{3,2,1,0:T(8,128)S(1)} %copy.28) | data formatting | bytes 393216 | tf_op jit(solution)/shard_map/reshape | solution.py:499
  79.6 3.9 %shard_map.129 = f32[768,256]{1,0:T(8,128)} custom-call(bf16[32,2048]{1,0:T(8,128)(2,1)} %get-tuple-element.13.rows_ref, f32[24,2048]{1,0:T(8,128)} %reshape.89.sec_ref, bf16[256,2048]{1,0:T(8,128)(2,1)} %get-tuple-element.16.cols_ref), custom_call_target="tpu_custom_call" | custom-call | flops 805306368 | bytes 2162688 | tf_op jit(solution)/shard_map/pallas_call | solution.py:524
  (30 shorter events, 0.3 us)
Async XLA Ops:
  0.0 0.8 %copy-start = (bf16[1,16384]{1,0:T(2,128)(2,1)S(1)}, bf16[1,16384]{1,0:T(2,128)(2,1)}, u32[]{:S(2)}) copy-start(bf16[1,16384]{1,0:T(2,128)(2,1)} %param.17) | copy-start | bytes 98308
  0.0 30.6 %copy-start.12 = (s32[32]{0:T(128)S(1)}, s32[32]{0:T(128)}, u32[]{:S(2)}) copy-start(s32[32]{0:T(128)} %param.14) | copy-start | bytes 388
  0.0 30.6 %copy-start.14 = (s32[32]{0:T(128)S(1)}, s32[32]{0:T(128)}, u32[]{:S(2)}) copy-start(s32[32]{0:T(128)} %param.16) | copy-start | bytes 388
  30.5 1.2 %copy-start.2 = (bf16[64,8192]{1,0:T(8,128)(2,1)S(1)}, bf16[64,8192]{1,0:T(8,128)(2,1)}, u32[]{:S(2)}) copy-start(bf16[64,8192]{1,0:T(8,128)(2,1)} %param.18) | copy-start | bytes 3145732
  30.5 1.5 %copy-start.3 = (bf16[32,16384]{1,0:T(8,128)(2,1)S(1)}, bf16[32,16384]{1,0:T(8,128)(2,1)}, u32[]{:S(2)}) copy-start(bf16[32,16384]{1,0:T(8,128)(2,1)} %param.13) | copy-start | bytes 3145732
  30.6 1.5 %copy-start.13 = (s32[32]{0:T(128)S(1)}, s32[32]{0:T(128)}, u32[]{:S(2)}) copy-start(s32[32]{0:T(128)} %param.15) | copy-start | bytes 388
  32.1 2.2 %copy-start.1 = (bf16[128,16384]{1,0:T(8,128)(2,1)S(1)}, bf16[128,16384]{1,0:T(8,128)(2,1)}, u32[]{:S(2)}) copy-start(bf16[128,16384]{1,0:T(8,128)(2,1)} %get-tuple-element.12) | copy-start | bytes 12582916
  39.1 1.4 %copy-start.8 = (s32[32,64]{1,0:T(8,128)S(1)}, s32[32,64]{1,0:T(8,128)}, u32[]{:S(2)}) copy-start(s32[32,64]{1,0:T(8,128)} %param.20) | copy-start | bytes 24580
  39.1 1.4 %copy-start.9 = (s32[32,64]{1,0:T(8,128)S(1)}, s32[32,64]{1,0:T(8,128)}, u32[]{:S(2)}) copy-start(s32[32,64]{1,0:T(8,128)} %param.19) | copy-start | bytes 24580
  39.2 2.1 %copy-start.10 = (f32[32,64]{1,0:T(8,128)S(1)}, f32[32,64]{1,0:T(8,128)}, u32[]{:S(2)}) copy-start(f32[32,64]{1,0:T(8,128)} %param.22) | copy-start | bytes 24580
  39.2 2.2 %copy-start.11 = (f32[32,64]{1,0:T(8,128)S(1)}, f32[32,64]{1,0:T(8,128)}, u32[]{:S(2)}) copy-start(f32[32,64]{1,0:T(8,128)} %param.21) | copy-start | bytes 24580
  76.4 0.9 %copy-start.4 = (f32[2,2,40,256]{3,2,1,0:T(8,128)S(1)}, f32[2,2,40,256]{3,2,1,0:T(8,128)}, u32[]{:S(2)}) copy-start(f32[2,2,40,256]{3,2,1,0:T(8,128)} %get-tuple-element.14) | copy-start | bytes 491524
  76.5 1.1 %copy-start.5 = (f32[2,40,256]{2,1,0:T(8,128)S(1)}, f32[2,40,256]{2,1,0:T(8,128)}, u32[]{:S(2)}) copy-start(f32[2,40,256]{2,1,0:T(8,128)} %get-tuple-element.15) | copy-start | bytes 245764
  76.6 1.3 %copy-start.6 = (s32[32,128]{1,0:T(8,128)S(1)}, s32[32,128]{1,0:T(8,128)}, u32[]{:S(2)}) copy-start(s32[32,128]{1,0:T(8,128)} %param.23) | copy-start | bytes 49156
  76.6 1.4 %copy-start.7 = (f32[32,128]{1,0:T(8,128)S(1)}, f32[32,128]{1,0:T(8,128)}, u32[]{:S(2)}) copy-start(f32[32,128]{1,0:T(8,128)} %param.24) | copy-start | bytes 49156

commit v13 on v12

--- a/solution.py
+++ b/solution.py
@@ -126,7 +126,7 @@
     return lambda: pl.semaphore_wait(barrier, len(devices))
 
 
-def run_phase(count, place, pick, x_ref, out_ref, local_sem, send_sems, recv_sems):
+def run_phase(count, place, pick, x_ref, out_ref, local_sem, send_sems, recv_sems, cover=None):
     me, device = place()
     own = pltpu.make_async_copy(pick(x_ref, me), out_ref.at[me], local_sem)
     own.start()
@@ -143,6 +143,8 @@
         )
         copy.start()
         copies.append(copy)
+    if cover is not None:
+        cover()
     own.wait()
     for copy in copies:
         copy.wait_send()
@@ -182,9 +184,9 @@
         + peers(groups, group_place)
         + neighbour_place()
     )
-    stencil_kernel(base_ref, frac_ref, rows_ref, cols_ref)
     arrive()
-    run_phase(2, core_place, row_block, x_ref, core_buf, local_sems.at[0], send_sems.at[0], recv_sems.at[0])
+    run_phase(2, core_place, row_block, x_ref, core_buf, local_sems.at[0], send_sems.at[0], recv_sems.at[0],
+              lambda: stencil_kernel(base_ref, frac_ref, rows_ref, cols_ref))
     y_src[...] = (core_buf[0].astype(jnp.float32) + core_buf[1].astype(jnp.float32)).astype(y_src.dtype)
     run_phase(
         y_chips, y_place, lane_blocks(y_chips), y_src, y_buf,
@@ -251,7 +253,7 @@
     )(x, *stencil)
 
 
-def phase_kernel(row_count, half_cols, phase_ref):
+def phase_kernel(row_count, half_cols, phase_ref, parts):
     half = phase_ref.shape[1] // 2
     lanes = 128
     blocks = half // lanes
@@ -270,24 +272,37 @@
         shift_rows_l * (l_l // half_cols).astype(jnp.float32)
         + shift_cols_l * (l_l % half_cols).astype(jnp.float32)
     ) * step
-    cos_b, sin_b = jnp.cos(block_angle), jnp.sin(block_angle)
-    c_l, s_l = jnp.cos(lane_angle), jnp.sin(lane_angle)
-    for q in range(blocks):
-        c_b, s_b = cos_b[:, q : q + 1], sin_b[:, q : q + 1]
-        phase_ref[:, q * lanes : (q + 1) * lanes] = (c_b * c_l - s_b * s_l).astype(phase_ref.dtype)
-        phase_ref[:, half + q * lanes : half + (q + 1) * lanes] = (s_b * c_l + c_b * s_l).astype(
-            phase_ref.dtype
-        )
+
+    def part(first, last):
+        def fill():
+            cos_b, sin_b = jnp.cos(block_angle), jnp.sin(block_angle)
+            c_l, s_l = jnp.cos(lane_angle), jnp.sin(lane_angle)
+            for q in range(first, last):
+                c_b, s_b = cos_b[:, q : q + 1], sin_b[:, q : q + 1]
+                phase_ref[:, q * lanes : (q + 1) * lanes] = (c_b * c_l - s_b * s_l).astype(
+                    phase_ref.dtype
+                )
+                phase_ref[:, half + q * lanes : half + (q + 1) * lanes] = (
+                    s_b * c_l + c_b * s_l
+                ).astype(phase_ref.dtype)
+
+        return fill
+
+    edges = [blocks * i // parts for i in range(parts + 1)]
+    return [part(edges[i], edges[i + 1]) for i in range(parts)]
 
 
 def gather_chain_kernel(y_chips, row_count, half_cols, x_ref, out_ref, phase_ref, z_buf, y_buf,
                         local_sems, send_sems, recv_sems):
     arrive = signal_all(peers(Z_CHIPS, z_place) + peers(y_chips, y_place) + peers(2, core_place))
-    phase_kernel(row_count, half_cols, phase_ref)
+    fills = phase_kernel(row_count, half_cols, phase_ref, 3)
     arrive()
-    run_phase(Z_CHIPS, z_place, whole, x_ref, z_buf, local_sems.at[0], send_sems.at[0], recv_sems.at[0])
-    run_phase(y_chips, y_place, entire, z_buf, y_buf, local_sems.at[1], send_sems.at[1], recv_sems.at[1])
-    run_phase(2, core_place, entire, y_buf, out_ref, local_sems.at[2], send_sems.at[2], recv_sems.at[2])
+    run_phase(Z_CHIPS, z_place, whole, x_ref, z_buf, local_sems.at[0], send_sems.at[0], recv_sems.at[0],
+              fills[0])
+    run_phase(y_chips, y_place, entire, z_buf, y_buf, local_sems.at[1], send_sems.at[1], recv_sems.at[1],
+              fills[1])
+    run_phase(2, core_place, entire, y_buf, out_ref, local_sems.at[2], send_sems.at[2], recv_sems.at[2],
+              fills[2])
 
 
 def gather_chain(x, row_count, half_cols, y_chips, collective_id):

time: 83.9 us -> 85.2 us (1.015)
  Pallas kernels: 65.1 us -> 66.4 us
    pallas_call x1, Pallas kernels: 33.6 us -> 35.6 us  [reduce_chain(): pl.pallas_call(functools.partial(reduce_chain_kernel, y_chips, groups), o...]
where the time goes in v13:
time: 85.2 us; the launch traced here: 84.9 us
  Pallas kernels  66.4 us (78%)
  local copies, waits for them, and re-layouts  7.71 us (9%)
  matrix products  6.96 us (8%)
  other arithmetic  3.48 us (4%)
    pallas_call x1, Pallas kernels, reduce_chain(): pl.pallas_call(functools.partial(reduce_chain_kernel, y_chips, groups), o...  35.6 us
    pallas_call x1, Pallas kernels, gather_chain(): pl.pallas_call(functools.partial(gather_chain_kernel, y_chips, row_count,...  26.8 us
    unnamed x31, local copies, waits for them, and re-layouts  4.47 us
    pallas_call x1, Pallas kernels, insert_planes(): pl.pallas_call(insert_kernel, out_shape=jax.ShapeDtypeStruct((planes * y_...  3.94 us
    dot_general x2, matrix products, local(): jnp.dot(member, part, precision=lax.Precision.HIGHEST, preferred_element_...  1.9 us

profile of v13, /device:TPU:1, one launch (start us, length us, event | category | flops | bytes accessed | tf_op | source)
XLA Modules:
  0.0 84.9 jit_solution(39700212101797895)
XLA Ops:
  0.0 0.8 copy-done
  0.8 0.2 reduce
  1.0 0.6 constant_dynamic-slice_fusion.x_ref
  1.6 26.8 %shard_map.127 = (bf16[2,4,8,64,128]{4,3,2,1,0:T(8,128)(2,1)}, bf16[128,16384]{1,0:T(8,128)(2,1)}) custom-call(bf16[1,64,128]{2,1,0:T(8,128)(2,1)} %constant_dynamic-slice_fusion.x_ref), custom_call_target="tpu_custom_call" | custom-call | tf_op jit(solution)/shard_map/pallas_call | solution.py:312
  28.5 1.3 %slice_bitcast_fusion.1 = (bf16[4,8,64,128]{3,2,1,0:T(8,128)(2,1)S(1)}, bf16[4,8,64,128]{3,2,1,0:T(8,128)(2,1)S(1)}) fusion(bf16[2,4,8,64,128]{4,3,2,1,0:T(8,128)(2,1)} %get-tuple-element.11), kind=kLoop, calls=%fused_computation.51 | loop fusion | bytes 2097152
  29.8 0.0 copy-start.13
  29.9 0.2 select_reduce_fusion
  30.0 0.4 fusion.2
  30.5 0.4 fusion.3
  30.9 0.1 copy-done.2
  31.0 0.3 copy-done.3
  31.4 0.7 fusion.7
  32.1 1.5 %copy-done.1 = bf16[128,16384]{1,0:T(8,128)(2,1)S(1)} copy-done((bf16[128,16384]{1,0:T(8,128)(2,1)S(1)}, bf16[128,16384]{1,0:T(8,128)(2,1)}, u32[]{:S(2)}) %copy-start.1) | copy-done | bytes 4194328
  33.5 1.6 %fusion.74 = (f32[32]{0:T(128)S(1)}, f32[32,128]{1,0:T(8,128)S(1)}) fusion(bf16[128,16384]{1,0:T(8,128)(2,1)S(1)} %copy-done.1, bf16[32,8192]{1,0:T(8,128)(2,1)S(1)} %get-tuple-element.22, bf16[32,8192]{1,0:T(8,128)(2,1)S(1)} %get-tuple-element.21), kind=kOutput, calls=%fused_computation.120 | convolution fusion | flops 136323040 | bytes 5259392 | tf_op jit(solution)/shard_map/np,sp->ns/dot_general | solution.py:345
  35.2 0.2 fusion.53
  35.4 0.8 fusion.54
  36.1 1.0 %fusion.1 = bf16[32,8192]{1,0:T(8,128)(2,1)S(1)} fusion(f32[32,8192]{1,0:T(8,128)S(1)} %get-tuple-element.33, f32[32,16384]{1,0:T(8,128)S(1)} %fusion.54, bf16[32,16384]{1,0:T(8,128)(2,1)S(1)} %copy-done.3, s32[32]{0:T(128)S(1)} %copy-done.12), kind=kOutput, calls=%fused_computation.3 | convolution fusion | flops 102761472 | bytes 4718720 | tf_op jit(solution)/shard_map/dot_general | solution.py:434
  37.1 0.9 %fusion = bf16[32,8192]{1,0:T(8,128)(2,1)S(1)} fusion(f32[32,8192]{1,0:T(8,128)S(1)} %get-tuple-element.33, f32[32,16384]{1,0:T(8,128)S(1)} %fusion.54, bf16[32,16384]{1,0:T(8,128)(2,1)S(1)} %copy-done.3, s32[32]{0:T(128)S(1)} %copy-done.12), kind=kOutput, calls=%fused_computation.2 | convolution fusion | flops 102761472 | bytes 4718720 | tf_op jit(solution)/shard_map/dot_general | solution.py:434
  38.0 0.1 fusion.71
  38.1 0.2 convolution_convert_fusion.3
  38.3 0.1 reshape.92
  38.4 0.0 copy-start.9
  38.4 0.0 copy-start.10
  38.4 0.1 fusion.24
  38.6 1.2 %pad_maximum_fusion.x_ref = bf16[2,40,8192]{2,1,0:T(8,128)(2,1)} fusion(bf16[1,40,8192]{2,1,0:T(8,128)(2,1)S(1)} %get-tuple-element.32, bf16[1,40,8192]{2,1,0:T(8,128)(2,1)S(1)} %get-tuple-element.31), kind=kLoop, calls=%fused_computation.20 | loop fusion | flops 655360 | bytes 2621440 | tf_op jit(solution)/shard_map/stack | solution.py:449
  39.8 0.1 stack_reshape.12
  39.8 0.1 stack_reshape.13
  39.9 0.6 pad_add_fusion.base_ref
  40.5 0.1 stack_reshape.14
  40.6 0.1 stack_reshape.15
  40.7 0.6 pad_maximum_fusion.3.frac_ref
  41.3 35.6 %shard_map.128 = (f32[2,40,256]{2,1,0:T(8,128)}, f32[2,2,40,256]{3,2,1,0:T(8,128)}, bf16[32,2048]{1,0:T(8,128)(2,1)}, bf16[256,2048]{1,0:T(8,128)(2,1)}) custom-call(bf16[2,40,8192]{2,1,0:T(8,128)(2,1)} %pad_maximum_fusion.x_ref, s32[2,2048]{1,0:T(2,128)} %pad_add_fusion.base_ref, f32[2,2048]{1,0:T(2,128)} %pad_maximum_fusion.3.frac_ref), custom_call_target="tpu_custom_call" | custom-call | tf_op jit(solution)/shard_map/pallas_call | solution.py:228
  76.9 0.7 slice.83
  77.6 0.1 reshape_squeeze.3
  77.7 0.1 convert_multiply_fusion
  77.8 0.0 copy-start.6
  77.9 0.0 copy-start.7
  77.9 0.3 convolution_multiply_fusion.2
  78.2 0.1 reshape.88
  78.2 0.4 copy-done.4
  78.6 0.2 reshape.85
  79.0 0.1 reshape.86
  79.2 0.1 broadcast_add_fusion
  79.3 0.1 broadcast_subtract_fusion
  79.3 0.7 convolution_bitcast_fusion
  80.0 0.1 copy.28
  80.1 0.8 reshape.89.sec_ref
  80.9 3.9 %shard_map.129 = f32[768,256]{1,0:T(8,128)} custom-call(bf16[32,2048]{1,0:T(8,128)(2,1)} %get-tuple-element.13.rows_ref, f32[24,2048]{1,0:T(8,128)} %reshape.89.sec_ref, bf16[256,2048]{1,0:T(8,128)(2,1)} %get-tuple-element.16.cols_ref), custom_call_target="tpu_custom_call" | custom-call | flops 805306368 | bytes 2162688 | tf_op jit(solution)/shard_map/pallas_call | solution.py:539
  (30 shorter events, 0.3 us)
Async XLA Ops:
  0.0 0.8 copy-start
  0.0 29.8 %copy-start.12 = (s32[32]{0:T(128)S(1)}, s32[32]{0:T(128)}, u32[]{:S(2)}) copy-start(s32[32]{0:T(128)} %param.14) | copy-start | bytes 388
  0.0 29.8 %copy-start.14 = (s32[32]{0:T(128)S(1)}, s32[32]{0:T(128)}, u32[]{:S(2)}) copy-start(s32[32]{0:T(128)} %param.16) | copy-start | bytes 388
  29.8 1.2 %copy-start.2 = (bf16[64,8192]{1,0:T(8,128)(2,1)S(1)}, bf16[64,8192]{1,0:T(8,128)(2,1)}, u32[]{:S(2)}) copy-start(bf16[64,8192]{1,0:T(8,128)(2,1)} %param.18) | copy-start | bytes 3145732
  29.8 1.5 %copy-start.3 = (bf16[32,16384]{1,0:T(8,128)(2,1)S(1)}, bf16[32,16384]{1,0:T(8,128)(2,1)}, u32[]{:S(2)}) copy-start(bf16[32,16384]{1,0:T(8,128)(2,1)} %param.13) | copy-start | bytes 3145732
  29.8 1.5 %copy-start.13 = (s32[32]{0:T(128)S(1)}, s32[32]{0:T(128)}, u32[]{:S(2)}) copy-start(s32[32]{0:T(128)} %param.15) | copy-start | bytes 388
  31.4 2.2 %copy-start.1 = (bf16[128,16384]{1,0:T(8,128)(2,1)S(1)}, bf16[128,16384]{1,0:T(8,128)(2,1)}, u32[]{:S(2)}) copy-start(bf16[128,16384]{1,0:T(8,128)(2,1)} %get-tuple-element.12) | copy-start | bytes 12582916
  38.4 1.4 %copy-start.8 = (s32[32,64]{1,0:T(8,128)S(1)}, s32[32,64]{1,0:T(8,128)}, u32[]{:S(2)}) copy-start(s32[32,64]{1,0:T(8,128)} %param.20) | copy-start | bytes 24580
  38.4 1.4 %copy-start.9 = (s32[32,64]{1,0:T(8,128)S(1)}, s32[32,64]{1,0:T(8,128)}, u32[]{:S(2)}) copy-start(s32[32,64]{1,0:T(8,128)} %param.19) | copy-start | bytes 24580
  38.4 2.1 %copy-start.10 = (f32[32,64]{1,0:T(8,128)S(1)}, f32[32,64]{1,0:T(8,128)}, u32[]{:S(2)}) copy-start(f32[32,64]{1,0:T(8,128)} %param.22) | copy-start | bytes 24580
  38.4 2.2 %copy-start.11 = (f32[32,64]{1,0:T(8,128)S(1)}, f32[32,64]{1,0:T(8,128)}, u32[]{:S(2)}) copy-start(f32[32,64]{1,0:T(8,128)} %param.21) | copy-start | bytes 24580
  77.7 0.9 %copy-start.4 = (f32[2,2,40,256]{3,2,1,0:T(8,128)S(1)}, f32[2,2,40,256]{3,2,1,0:T(8,128)}, u32[]{:S(2)}) copy-start(f32[2,2,40,256]{3,2,1,0:T(8,128)} %get-tuple-element.14) | copy-start | bytes 491524
  77.8 1.1 %copy-start.5 = (f32[2,40,256]{2,1,0:T(8,128)S(1)}, f32[2,40,256]{2,1,0:T(8,128)}, u32[]{:S(2)}) copy-start(f32[2,40,256]{2,1,0:T(8,128)} %get-tuple-element.15) | copy-start | bytes 245764
  77.8 1.3 %copy-start.6 = (s32[32,128]{1,0:T(8,128)S(1)}, s32[32,128]{1,0:T(8,128)}, u32[]{:S(2)}) copy-start(s32[32,128]{1,0:T(8,128)} %param.23) | copy-start | bytes 49156
  77.9 1.4 %copy-start.7 = (f32[32,128]{1,0:T(8,128)S(1)}, f32[32,128]{1,0:T(8,128)}, u32[]{:S(2)}) copy-start(f32[32,128]{1,0:T(8,128)} %param.24) | copy-start | bytes 49156

commit v14 on v12

--- a/solution.py
+++ b/solution.py
@@ -166,21 +166,25 @@
     cols_ref[...] = cols.astype(cols_ref.dtype)
 
 
-def neighbour_place():
-    group, slab = lax.axis_index("grp"), lax.axis_index("slab")
+def neighbour_place(groups):
+    slab = lax.axis_index("slab")
     count = lax.axis_size("slab")
-    return [(group, lax.rem(slab + 1, count)), (group, lax.rem(slab + count - 1, count))]
+    return [
+        (peer, lax.rem(slab + step, count))
+        for step in (1, count - 1)
+        for peer in range(groups)
+    ]
 
 
 def reduce_chain_kernel(y_chips, groups, x_ref, base_ref, frac_ref,
                         total_ref, halo_ref, rows_ref, cols_ref, core_buf, y_src, y_buf, z_src, z_buf,
-                        d_src, d_buf, local_sems, send_sems, recv_sems, halo_send, halo_recv):
+                        d_src, d_buf, edge_buf, local_sems, send_sems, recv_sems, halo_send, halo_recv):
     arrive = signal_all(
         peers(2, core_place)
         + peers(y_chips, y_place)
         + peers(Z_CHIPS, z_place)
         + peers(groups, group_place)
-        + neighbour_place()
+        + neighbour_place(groups)
     )
     stencil_kernel(base_ref, frac_ref, rows_ref, cols_ref)
     arrive()
@@ -196,26 +200,43 @@
         local_sems.at[2], send_sems.at[2], recv_sems.at[2],
     )
     d_src[0] = jnp.sum(z_buf[...].astype(jnp.float32), axis=0).astype(d_src.dtype)
+    group = lax.axis_index("grp")
+    edge_copies = []
+    for index, device in enumerate(neighbour_place(groups)):
+        side, peer = divmod(index, groups)
+        copy = pltpu.make_async_remote_copy(
+            src_ref=d_src.at[0],
+            dst_ref=edge_buf.at[side, group],
+            send_sem=halo_send.at[side, peer],
+            recv_sem=halo_recv.at[side, group],
+            device_id=device,
+            device_id_type=pl.DeviceIdType.MESH,
+        )
+        copy.start()
+        edge_copies.append(copy)
     run_phase(groups, group_place, whole, d_src, d_buf, local_sems.at[3], send_sems.at[3], recv_sems.at[3])
+    for copy in edge_copies:
+        copy.wait_send()
+    slab, count = lax.axis_index("slab"), lax.axis_size("slab")
+    for side, step in enumerate((count - 1, 1)):
+        for peer in range(groups):
+            pltpu.make_async_remote_copy(
+                src_ref=d_src.at[0],
+                dst_ref=edge_buf.at[side, peer],
+                send_sem=halo_send.at[side, peer],
+                recv_sem=halo_recv.at[side, peer],
+                device_id=(peer, lax.rem(slab + step, count)),
+                device_id_type=pl.DeviceIdType.MESH,
+            ).wait_recv()
     for half in range(2):
         total_ref[half] = jnp.sum(
             jnp.stack([d_buf[j].astype(jnp.float32) for j in range(half, groups, 2)]), axis=0
         )
-    copies = []
-    for side, device in enumerate(neighbour_place()):
-        copy = pltpu.make_async_remote_copy(
-            src_ref=total_ref,
-            dst_ref=halo_ref.at[side],
-            send_sem=halo_send.at[side],
-            recv_sem=halo_recv.at[side],
-            device_id=device,
-            device_id_type=pl.DeviceIdType.MESH,
-        )
-        copy.start()
-        copies.append(copy)
-    for copy in copies:
-        copy.wait_send()
-        copy.wait_recv()
+        for side in range(2):
+            halo_ref[side, half] = jnp.sum(
+                jnp.stack([edge_buf[side, j].astype(jnp.float32) for j in range(half, groups, 2)]),
+                axis=0,
+            )
 
 
 def reduce_chain(x, stencil, y_rows, side, y_chips, groups, collective_id):
@@ -241,11 +262,12 @@
             pltpu.VMEM((Z_CHIPS, rows, band), jnp.bfloat16),
             pltpu.VMEM((1, rows, band), jnp.bfloat16),
             pltpu.VMEM((groups, rows, band), jnp.bfloat16),
+            pltpu.VMEM((2, groups, rows, band), jnp.bfloat16),
             pltpu.SemaphoreType.DMA((4,)),
             pltpu.SemaphoreType.DMA((4, wide)),
             pltpu.SemaphoreType.DMA((4, wide)),
-            pltpu.SemaphoreType.DMA((2,)),
-            pltpu.SemaphoreType.DMA((2,)),
+            pltpu.SemaphoreType.DMA((2, groups)),
+            pltpu.SemaphoreType.DMA((2, groups)),
         ],
         compiler_params=pltpu.CompilerParams(collective_id=collective_id, has_side_effects=True),
     )(x, *stencil)

time: 83.9 us -> 82.5 us (0.983)
  Pallas kernels: 65.1 us -> 63.6 us
    pallas_call x1, Pallas kernels: 33.6 us -> 32.1 us  [reduce_chain(): pl.pallas_call(functools.partial(reduce_chain_kernel, y_chips, groups), o...]
where the time goes in v14:
time: 82.5 us; the launch traced here: 82.1 us
  Pallas kernels  63.6 us (77%)
  local copies, waits for them, and re-layouts  7.71 us (9%)
  matrix products  6.96 us (8%)
  other arithmetic  3.48 us (4%)
    pallas_call x1, Pallas kernels, reduce_chain(): pl.pallas_call(functools.partial(reduce_chain_kernel, y_chips, groups), o...  32.1 us
    pallas_call x1, Pallas kernels, gather_chain(): pl.pallas_call(functools.partial(gather_chain_kernel, y_chips, row_count,...  27.6 us
    unnamed x31, local copies, waits for them, and re-layouts  4.47 us
    pallas_call x1, Pallas kernels, insert_planes(): pl.pallas_call(insert_kernel, out_shape=jax.ShapeDtypeStruct((planes * y_...  3.94 us
    dot_general x2, matrix products, local(): jnp.dot(member, part, precision=lax.Precision.HIGHEST, preferred_element_...  1.9 us

profile of v14, /device:TPU:1, one launch (start us, length us, event | category | flops | bytes accessed | tf_op | source)
XLA Modules:
  0.0 82.1 jit_solution(8565411589417371499)
XLA Ops:
  0.0 0.8 copy-done
  0.8 0.2 reduce
  1.0 0.6 constant_dynamic-slice_fusion.x_ref
  1.6 27.6 %shard_map.127 = (bf16[2,4,8,64,128]{4,3,2,1,0:T(8,128)(2,1)}, bf16[128,16384]{1,0:T(8,128)(2,1)}) custom-call(bf16[1,64,128]{2,1,0:T(8,128)(2,1)} %constant_dynamic-slice_fusion.x_ref), custom_call_target="tpu_custom_call" | custom-call | tf_op jit(solution)/shard_map/pallas_call | solution.py:319
  29.2 1.3 %slice_bitcast_fusion.1 = (bf16[4,8,64,128]{3,2,1,0:T(8,128)(2,1)S(1)}, bf16[4,8,64,128]{3,2,1,0:T(8,128)(2,1)S(1)}) fusion(bf16[2,4,8,64,128]{4,3,2,1,0:T(8,128)(2,1)} %get-tuple-element.11), kind=kLoop, calls=%fused_computation.51 | loop fusion | bytes 2097152
  30.5 0.0 copy-start.2
  30.5 0.0 copy-start.3
  30.6 0.0 copy-start.13
  30.6 0.2 select_reduce_fusion
  30.8 0.4 fusion.2
  31.2 0.4 fusion.3
  31.6 0.1 copy-done.2
  31.8 0.3 copy-done.3
  32.1 0.7 fusion.7
  32.8 1.5 %copy-done.1 = bf16[128,16384]{1,0:T(8,128)(2,1)S(1)} copy-done((bf16[128,16384]{1,0:T(8,128)(2,1)S(1)}, bf16[128,16384]{1,0:T(8,128)(2,1)}, u32[]{:S(2)}) %copy-start.1) | copy-done | bytes 4194328
  34.3 1.6 %fusion.74 = (f32[32]{0:T(128)S(1)}, f32[32,128]{1,0:T(8,128)S(1)}) fusion(bf16[128,16384]{1,0:T(8,128)(2,1)S(1)} %copy-done.1, bf16[32,8192]{1,0:T(8,128)(2,1)S(1)} %get-tuple-element.22, bf16[32,8192]{1,0:T(8,128)(2,1)S(1)} %get-tuple-element.21), kind=kOutput, calls=%fused_computation.120 | convolution fusion | flops 136323040 | bytes 5259392 | tf_op jit(solution)/shard_map/np,sp->ns/dot_general | solution.py:352
  35.9 0.2 fusion.53
  36.1 0.8 fusion.54
  36.8 1.0 %fusion.1 = bf16[32,8192]{1,0:T(8,128)(2,1)S(1)} fusion(f32[32,8192]{1,0:T(8,128)S(1)} %get-tuple-element.33, f32[32,16384]{1,0:T(8,128)S(1)} %fusion.54, bf16[32,16384]{1,0:T(8,128)(2,1)S(1)} %copy-done.3, s32[32]{0:T(128)S(1)} %copy-done.12), kind=kOutput, calls=%fused_computation.3 | convolution fusion | flops 102761472 | bytes 4718720 | tf_op jit(solution)/shard_map/dot_general | solution.py:441
  37.8 0.9 %fusion = bf16[32,8192]{1,0:T(8,128)(2,1)S(1)} fusion(f32[32,8192]{1,0:T(8,128)S(1)} %get-tuple-element.33, f32[32,16384]{1,0:T(8,128)S(1)} %fusion.54, bf16[32,16384]{1,0:T(8,128)(2,1)S(1)} %copy-done.3, s32[32]{0:T(128)S(1)} %copy-done.12), kind=kOutput, calls=%fused_computation.2 | convolution fusion | flops 102761472 | bytes 4718720 | tf_op jit(solution)/shard_map/dot_general | solution.py:441
  38.8 0.1 fusion.71
  38.8 0.2 convolution_convert_fusion.3
  39.0 0.1 reshape.92
  39.1 0.0 copy-start.9
  39.2 0.0 copy-start.10
  39.2 0.1 fusion.24
  39.3 1.2 %pad_maximum_fusion.x_ref = bf16[2,40,8192]{2,1,0:T(8,128)(2,1)} fusion(bf16[1,40,8192]{2,1,0:T(8,128)(2,1)S(1)} %get-tuple-element.32, bf16[1,40,8192]{2,1,0:T(8,128)(2,1)S(1)} %get-tuple-element.31), kind=kLoop, calls=%fused_computation.20 | loop fusion | flops 655360 | bytes 2621440 | tf_op jit(solution)/shard_map/stack | solution.py:456
  40.5 0.1 stack_reshape.12
  40.6 0.1 stack_reshape.13
  40.7 0.6 pad_add_fusion.base_ref
  41.3 0.1 stack_reshape.14
  41.4 0.1 stack_reshape.15
  41.4 0.6 pad_maximum_fusion.3.frac_ref
  42.1 32.1 %shard_map.128 = (f32[2,40,256]{2,1,0:T(8,128)}, f32[2,2,40,256]{3,2,1,0:T(8,128)}, bf16[32,2048]{1,0:T(8,128)(2,1)}, bf16[256,2048]{1,0:T(8,128)(2,1)}) custom-call(bf16[2,40,8192]{2,1,0:T(8,128)(2,1)} %pad_maximum_fusion.x_ref, s32[2,2048]{1,0:T(2,128)} %pad_add_fusion.base_ref, f32[2,2048]{1,0:T(2,128)} %pad_maximum_fusion.3.frac_ref), custom_call_target="tpu_custom_call" | custom-call | tf_op jit(solution)/shard_map/pallas_call | solution.py:247
  74.2 0.7 slice.83
  74.9 0.1 reshape_squeeze.3
  75.0 0.1 convert_multiply_fusion
  75.1 0.3 convolution_multiply_fusion.2
  75.4 0.1 reshape.88
  75.5 0.4 copy-done.4
  75.9 0.2 reshape.85
  76.3 0.1 reshape.86
  76.4 0.1 broadcast_add_fusion
  76.5 0.1 broadcast_subtract_fusion
  76.6 0.7 convolution_bitcast_fusion
  77.3 0.1 copy.28
  77.3 0.8 %reshape.89.sec_ref = f32[24,2048]{1,0:T(8,128)} reshape(f32[3,8,32,64]{3,2,1,0:T(8,128)S(1)} %copy.28) | data formatting | bytes 393216 | tf_op jit(solution)/shard_map/reshape | solution.py:521
  78.2 3.9 %shard_map.129 = f32[768,256]{1,0:T(8,128)} custom-call(bf16[32,2048]{1,0:T(8,128)(2,1)} %get-tuple-element.13.rows_ref, f32[24,2048]{1,0:T(8,128)} %reshape.89.sec_ref, bf16[256,2048]{1,0:T(8,128)(2,1)} %get-tuple-element.16.cols_ref), custom_call_target="tpu_custom_call" | custom-call | flops 805306368 | bytes 2162688 | tf_op jit(solution)/shard_map/pallas_call | solution.py:546
  (30 shorter events, 0.3 us)
Async XLA Ops:
  0.0 0.8 %copy-start = (bf16[1,16384]{1,0:T(2,128)(2,1)S(1)}, bf16[1,16384]{1,0:T(2,128)(2,1)}, u32[]{:S(2)}) copy-start(bf16[1,16384]{1,0:T(2,128)(2,1)} %param.17) | copy-start | bytes 98308
  0.0 30.6 %copy-start.12 = (s32[32]{0:T(128)S(1)}, s32[32]{0:T(128)}, u32[]{:S(2)}) copy-start(s32[32]{0:T(128)} %param.14) | copy-start | bytes 388
  0.0 30.6 %copy-start.14 = (s32[32]{0:T(128)S(1)}, s32[32]{0:T(128)}, u32[]{:S(2)}) copy-start(s32[32]{0:T(128)} %param.16) | copy-start | bytes 388
  30.5 1.2 %copy-start.2 = (bf16[64,8192]{1,0:T(8,128)(2,1)S(1)}, bf16[64,8192]{1,0:T(8,128)(2,1)}, u32[]{:S(2)}) copy-start(bf16[64,8192]{1,0:T(8,128)(2,1)} %param.18) | copy-start | bytes 3145732
  30.5 1.5 %copy-start.3 = (bf16[32,16384]{1,0:T(8,128)(2,1)S(1)}, bf16[32,16384]{1,0:T(8,128)(2,1)}, u32[]{:S(2)}) copy-start(bf16[32,16384]{1,0:T(8,128)(2,1)} %param.13) | copy-start | bytes 3145732
  30.6 1.5 %copy-start.13 = (s32[32]{0:T(128)S(1)}, s32[32]{0:T(128)}, u32[]{:S(2)}) copy-start(s32[32]{0:T(128)} %param.15) | copy-start | bytes 388
  32.1 2.2 %copy-start.1 = (bf16[128,16384]{1,0:T(8,128)(2,1)S(1)}, bf16[128,16384]{1,0:T(8,128)(2,1)}, u32[]{:S(2)}) copy-start(bf16[128,16384]{1,0:T(8,128)(2,1)} %get-tuple-element.12) | copy-start | bytes 12582916
  39.1 1.4 %copy-start.8 = (s32[32,64]{1,0:T(8,128)S(1)}, s32[32,64]{1,0:T(8,128)}, u32[]{:S(2)}) copy-start(s32[32,64]{1,0:T(8,128)} %param.20) | copy-start | bytes 24580
  39.1 1.4 %copy-start.9 = (s32[32,64]{1,0:T(8,128)S(1)}, s32[32,64]{1,0:T(8,128)}, u32[]{:S(2)}) copy-start(s32[32,64]{1,0:T(8,128)} %param.19) | copy-start | bytes 24580
  39.2 2.1 %copy-start.10 = (f32[32,64]{1,0:T(8,128)S(1)}, f32[32,64]{1,0:T(8,128)}, u32[]{:S(2)}) copy-start(f32[32,64]{1,0:T(8,128)} %param.22) | copy-start | bytes 24580
  39.2 2.2 %copy-start.11 = (f32[32,64]{1,0:T(8,128)S(1)}, f32[32,64]{1,0:T(8,128)}, u32[]{:S(2)}) copy-start(f32[32,64]{1,0:T(8,128)} %param.21) | copy-start | bytes 24580
  75.0 0.9 %copy-start.4 = (f32[2,2,40,256]{3,2,1,0:T(8,128)S(1)}, f32[2,2,40,256]{3,2,1,0:T(8,128)}, u32[]{:S(2)}) copy-start(f32[2,2,40,256]{3,2,1,0:T(8,128)} %get-tuple-element.14) | copy-start | bytes 491524
  75.1 1.1 %copy-start.5 = (f32[2,40,256]{2,1,0:T(8,128)S(1)}, f32[2,40,256]{2,1,0:T(8,128)}, u32[]{:S(2)}) copy-start(f32[2,40,256]{2,1,0:T(8,128)} %get-tuple-element.15) | copy-start | bytes 245764
  75.1 1.3 %copy-start.6 = (s32[32,128]{1,0:T(8,128)S(1)}, s32[32,128]{1,0:T(8,128)}, u32[]{:S(2)}) copy-start(s32[32,128]{1,0:T(8,128)} %param.23) | copy-start | bytes 49156
  75.1 1.4 %copy-start.7 = (f32[32,128]{1,0:T(8,128)S(1)}, f32[32,128]{1,0:T(8,128)}, u32[]{:S(2)}) copy-start(f32[32,128]{1,0:T(8,128)} %param.24) | copy-start | bytes 49156

commit v15 on v14

--- a/solution.py
+++ b/solution.py
@@ -70,6 +70,14 @@
     group, slab = lax.axis_index("grp"), lax.axis_index("slab")
     z = lax.rem(slab, Z_CHIPS)
     return slab // Z_CHIPS, lambda peer: (group, peer * Z_CHIPS + z)
+
+
+def column_place():
+    group, slab = lax.axis_index("grp"), lax.axis_index("slab")
+    core, z = lax.rem(group, 2), lax.rem(slab, Z_CHIPS)
+    me = core * (lax.axis_size("slab") // Z_CHIPS) + slab // Z_CHIPS
+    y_chips = lax.axis_size("slab") // Z_CHIPS
+    return me, lambda peer: (group - core + peer // y_chips, lax.rem(peer, y_chips) * Z_CHIPS + z)
 
 
 def group_place():
@@ -302,14 +310,14 @@
         )
 
 
-def gather_chain_kernel(y_chips, row_count, half_cols, x_ref, out_ref, phase_ref, z_buf, y_buf,
+def gather_chain_kernel(y_chips, row_count, half_cols, x_ref, out_ref, phase_ref, z_buf,
                         local_sems, send_sems, recv_sems):
-    arrive = signal_all(peers(Z_CHIPS, z_place) + peers(y_chips, y_place) + peers(2, core_place))
+    arrive = signal_all(peers(Z_CHIPS, z_place) + peers(2 * y_chips, column_place))
     phase_kernel(row_count, half_cols, phase_ref)
     arrive()
     run_phase(Z_CHIPS, z_place, whole, x_ref, z_buf, local_sems.at[0], send_sems.at[0], recv_sems.at[0])
-    run_phase(y_chips, y_place, entire, z_buf, y_buf, local_sems.at[1], send_sems.at[1], recv_sems.at[1])
-    run_phase(2, core_place, entire, y_buf, out_ref, local_sems.at[2], send_sems.at[2], recv_sems.at[2])
+    run_phase(2 * y_chips, column_place, entire, z_buf, out_ref,
+              local_sems.at[1], send_sems.at[1], recv_sems.at[1])
 
 
 def gather_chain(x, row_count, half_cols, y_chips, collective_id):
@@ -319,17 +327,16 @@
     return pl.pallas_call(
         functools.partial(gather_chain_kernel, y_chips, row_count, half_cols),
         out_shape=[
-            jax.ShapeDtypeStruct((2, y_chips, Z_CHIPS, rows, lanes), x.dtype),
+            jax.ShapeDtypeStruct((2 * y_chips, Z_CHIPS, rows, lanes), x.dtype),
             jax.ShapeDtypeStruct((shifts, table), jnp.bfloat16),
         ],
         in_specs=[pl.BlockSpec(memory_space=pltpu.VMEM)],
         out_specs=[pl.BlockSpec(memory_space=pltpu.VMEM)] * 2,
         scratch_shapes=[
             pltpu.VMEM((Z_CHIPS, rows, lanes), x.dtype),
-            pltpu.VMEM((y_chips, Z_CHIPS, rows, lanes), x.dtype),
-            pltpu.SemaphoreType.DMA((3,)),
-            pltpu.SemaphoreType.DMA((3, Z_CHIPS)),
-            pltpu.SemaphoreType.DMA((3, Z_CHIPS)),
+            pltpu.SemaphoreType.DMA((2,)),
+            pltpu.SemaphoreType.DMA((2, 2 * y_chips)),
+            pltpu.SemaphoreType.DMA((2, 2 * y_chips)),
         ],
         compiler_params=pltpu.CompilerParams(collective_id=collective_id, has_side_effects=True),
     )(x)

time: 82.5 us -> 86.4 us (1.047)
  Pallas kernels: 63.6 us -> 67.5 us
    pallas_call x1, Pallas kernels: 32.1 us -> 35 us  [reduce_chain(): pl.pallas_call(functools.partial(reduce_chain_kernel, y_chips, groups), o...]
    pallas_call x1, Pallas kernels: 27.6 us -> 28.6 us  [gather_chain(): pl.pallas_call(functools.partial(gather_chain_kernel, y_chips, row_count,...]
where the time goes in v15:
time: 86.4 us; the launch traced here: 86 us
  Pallas kernels  67.5 us (78%)
  local copies, waits for them, and re-layouts  7.71 us (9%)
  matrix products  6.95 us (8%)
  other arithmetic  3.48 us (4%)
    pallas_call x1, Pallas kernels, reduce_chain(): pl.pallas_call(functools.partial(reduce_chain_kernel, y_chips, groups), o...  35 us
    pallas_call x1, Pallas kernels, gather_chain(): pl.pallas_call(functools.partial(gather_chain_kernel, y_chips, row_count,...  28.6 us
    unnamed x31, local copies, waits for them, and re-layouts  4.47 us
    pallas_call x1, Pallas kernels, insert_planes(): pl.pallas_call(insert_kernel, out_shape=jax.ShapeDtypeStruct((planes * y_...  3.94 us
    dot_general x2, matrix products, local(): jnp.dot(member, part, precision=lax.Precision.HIGHEST, preferred_element_...  1.9 us

profile of v15, /device:TPU:1, one launch (start us, length us, event | category | flops | bytes accessed | tf_op | source)
XLA Modules:
  0.0 86.0 jit_solution(1402818585491950586)
XLA Ops:
  0.0 0.8 copy-done
  0.8 0.2 reduce
  1.0 0.6 constant_dynamic-slice_fusion.x_ref
  1.6 28.6 %shard_map.127 = (bf16[8,8,64,128]{3,2,1,0:T(8,128)(2,1)}, bf16[128,16384]{1,0:T(8,128)(2,1)}) custom-call(bf16[1,64,128]{2,1,0:T(8,128)(2,1)} %constant_dynamic-slice_fusion.x_ref), custom_call_target="tpu_custom_call" | custom-call | tf_op jit(solution)/shard_map/pallas_call | solution.py:327
  30.2 1.3 %slice_bitcast_fusion.1 = (bf16[4,8,64,128]{3,2,1,0:T(8,128)(2,1)S(1)}, bf16[4,8,64,128]{3,2,1,0:T(8,128)(2,1)S(1)}) fusion(bf16[8,8,64,128]{3,2,1,0:T(8,128)(2,1)} %get-tuple-element.11), kind=kLoop, calls=%fused_computation.51 | loop fusion | bytes 2097152
  31.5 0.0 copy-start.2
  31.5 0.0 copy-start.3
  31.6 0.2 select_reduce_fusion
  31.8 0.4 fusion.2
  32.2 0.4 fusion.3
  32.6 0.1 copy-done.2
  32.8 0.3 copy-done.3
  33.1 0.7 fusion.7
  33.8 1.5 %copy-done.1 = bf16[128,16384]{1,0:T(8,128)(2,1)S(1)} copy-done((bf16[128,16384]{1,0:T(8,128)(2,1)S(1)}, bf16[128,16384]{1,0:T(8,128)(2,1)}, u32[]{:S(2)}) %copy-start.1) | copy-done | bytes 4194328
  35.3 1.6 %fusion.74 = (f32[32]{0:T(128)S(1)}, f32[32,128]{1,0:T(8,128)S(1)}) fusion(bf16[128,16384]{1,0:T(8,128)(2,1)S(1)} %copy-done.1, bf16[32,8192]{1,0:T(8,128)(2,1)S(1)} %get-tuple-element.22, bf16[32,8192]{1,0:T(8,128)(2,1)S(1)} %get-tuple-element.21), kind=kOutput, calls=%fused_computation.120 | convolution fusion | flops 136323040 | bytes 5259392 | tf_op jit(solution)/shard_map/np,sp->ns/dot_general | solution.py:359
  36.9 0.2 fusion.53
  37.1 0.8 fusion.54
  37.8 1.0 %fusion.1 = bf16[32,8192]{1,0:T(8,128)(2,1)S(1)} fusion(f32[32,8192]{1,0:T(8,128)S(1)} %get-tuple-element.33, f32[32,16384]{1,0:T(8,128)S(1)} %fusion.54, bf16[32,16384]{1,0:T(8,128)(2,1)S(1)} %copy-done.3, s32[32]{0:T(128)S(1)} %copy-done.12), kind=kOutput, calls=%fused_computation.3 | convolution fusion | flops 102761472 | bytes 4718720 | tf_op jit(solution)/shard_map/dot_general | solution.py:448
  38.8 0.9 %fusion = bf16[32,8192]{1,0:T(8,128)(2,1)S(1)} fusion(f32[32,8192]{1,0:T(8,128)S(1)} %get-tuple-element.33, f32[32,16384]{1,0:T(8,128)S(1)} %fusion.54, bf16[32,16384]{1,0:T(8,128)(2,1)S(1)} %copy-done.3, s32[32]{0:T(128)S(1)} %copy-done.12), kind=kOutput, calls=%fused_computation.2 | convolution fusion | flops 102761472 | bytes 4718720 | tf_op jit(solution)/shard_map/dot_general | solution.py:448
  39.7 0.1 fusion.71
  39.8 0.2 convolution_convert_fusion.3
  40.0 0.1 reshape.92
  40.1 0.0 copy-start.8
  40.1 0.0 copy-start.9
  40.2 0.1 fusion.24
  40.3 1.2 %pad_maximum_fusion.x_ref = bf16[2,40,8192]{2,1,0:T(8,128)(2,1)} fusion(bf16[1,40,8192]{2,1,0:T(8,128)(2,1)S(1)} %get-tuple-element.32, bf16[1,40,8192]{2,1,0:T(8,128)(2,1)S(1)} %get-tuple-element.31), kind=kLoop, calls=%fused_computation.20 | loop fusion | flops 655360 | bytes 2621440 | tf_op jit(solution)/shard_map/stack | solution.py:463
  41.5 0.1 stack_reshape.12
  41.6 0.1 stack_reshape.13
  41.7 0.6 pad_add_fusion.base_ref
  42.3 0.1 stack_reshape.14
  42.4 0.1 stack_reshape.15
  42.4 0.6 pad_maximum_fusion.3.frac_ref
  43.1 35.0 %shard_map.128 = (f32[2,40,256]{2,1,0:T(8,128)}, f32[2,2,40,256]{3,2,1,0:T(8,128)}, bf16[32,2048]{1,0:T(8,128)(2,1)}, bf16[256,2048]{1,0:T(8,128)(2,1)}) custom-call(bf16[2,40,8192]{2,1,0:T(8,128)(2,1)} %pad_maximum_fusion.x_ref, s32[2,2048]{1,0:T(2,128)} %pad_add_fusion.base_ref, f32[2,2048]{1,0:T(2,128)} %pad_maximum_fusion.3.frac_ref), custom_call_target="tpu_custom_call" | custom-call | tf_op jit(solution)/shard_map/pallas_call | solution.py:255
  78.1 0.7 slice.83
  78.8 0.1 reshape_squeeze.3
  78.9 0.1 convert_multiply_fusion
  79.0 0.0 copy-start.7
  79.0 0.3 convolution_multiply_fusion.2
  79.3 0.1 reshape.88
  79.4 0.4 copy-done.4
  79.8 0.2 reshape.85
  80.2 0.1 reshape.86
  80.3 0.1 broadcast_add_fusion
  80.4 0.1 broadcast_subtract_fusion
  80.5 0.7 convolution_bitcast_fusion
  81.2 0.1 copy.28
  81.2 0.8 reshape.89.sec_ref
  82.1 3.9 %shard_map.129 = f32[768,256]{1,0:T(8,128)} custom-call(bf16[32,2048]{1,0:T(8,128)(2,1)} %get-tuple-element.13.rows_ref, f32[24,2048]{1,0:T(8,128)} %reshape.89.sec_ref, bf16[256,2048]{1,0:T(8,128)(2,1)} %get-tuple-element.16.cols_ref), custom_call_target="tpu_custom_call" | custom-call | flops 805306368 | bytes 2162688 | tf_op jit(solution)/shard_map/pallas_call | solution.py:553
  (30 shorter events, 0.3 us)
Async XLA Ops:
  0.0 0.8 copy-start
  0.0 31.6 %copy-start.12 = (s32[32]{0:T(128)S(1)}, s32[32]{0:T(128)}, u32[]{:S(2)}) copy-start(s32[32]{0:T(128)} %param.14) | copy-start | bytes 388
  0.0 31.6 %copy-start.14 = (s32[32]{0:T(128)S(1)}, s32[32]{0:T(128)}, u32[]{:S(2)}) copy-start(s32[32]{0:T(128)} %param.16) | copy-start | bytes 388
  31.5 1.2 %copy-start.2 = (bf16[64,8192]{1,0:T(8,128)(2,1)S(1)}, bf16[64,8192]{1,0:T(8,128)(2,1)}, u32[]{:S(2)}) copy-start(bf16[64,8192]{1,0:T(8,128)(2,1)} %param.18) | copy-start | bytes 3145732
  31.5 1.5 %copy-start.3 = (bf16[32,16384]{1,0:T(8,128)(2,1)S(1)}, bf16[32,16384]{1,0:T(8,128)(2,1)}, u32[]{:S(2)}) copy-start(bf16[32,16384]{1,0:T(8,128)(2,1)} %param.13) | copy-start | bytes 3145732
  31.6 1.5 %copy-start.13 = (s32[32]{0:T(128)S(1)}, s32[32]{0:T(128)}, u32[]{:S(2)}) copy-start(s32[32]{0:T(128)} %param.15) | copy-start | bytes 388
  33.1 2.2 %copy-start.1 = (bf16[128,16384]{1,0:T(8,128)(2,1)S(1)}, bf16[128,16384]{1,0:T(8,128)(2,1)}, u32[]{:S(2)}) copy-start(bf16[128,16384]{1,0:T(8,128)(2,1)} %get-tuple-element.12) | copy-start | bytes 12582916
  40.1 1.4 %copy-start.8 = (s32[32,64]{1,0:T(8,128)S(1)}, s32[32,64]{1,0:T(8,128)}, u32[]{:S(2)}) copy-start(s32[32,64]{1,0:T(8,128)} %param.20) | copy-start | bytes 24580
  40.1 1.4 %copy-start.9 = (s32[32,64]{1,0:T(8,128)S(1)}, s32[32,64]{1,0:T(8,128)}, u32[]{:S(2)}) copy-start(s32[32,64]{1,0:T(8,128)} %param.19) | copy-start | bytes 24580
  40.1 2.1 %copy-start.10 = (f32[32,64]{1,0:T(8,128)S(1)}, f32[32,64]{1,0:T(8,128)}, u32[]{:S(2)}) copy-start(f32[32,64]{1,0:T(8,128)} %param.22) | copy-start | bytes 24580
  40.2 2.2 %copy-start.11 = (f32[32,64]{1,0:T(8,128)S(1)}, f32[32,64]{1,0:T(8,128)}, u32[]{:S(2)}) copy-start(f32[32,64]{1,0:T(8,128)} %param.21) | copy-start | bytes 24580
  78.9 0.9 %copy-start.4 = (f32[2,2,40,256]{3,2,1,0:T(8,128)S(1)}, f32[2,2,40,256]{3,2,1,0:T(8,128)}, u32[]{:S(2)}) copy-start(f32[2,2,40,256]{3,2,1,0:T(8,128)} %get-tuple-element.14) | copy-start | bytes 491524
  79.0 1.1 %copy-start.5 = (f32[2,40,256]{2,1,0:T(8,128)S(1)}, f32[2,40,256]{2,1,0:T(8,128)}, u32[]{:S(2)}) copy-start(f32[2,40,256]{2,1,0:T(8,128)} %get-tuple-element.15) | copy-start | bytes 245764
  79.0 1.3 %copy-start.6 = (s32[32,128]{1,0:T(8,128)S(1)}, s32[32,128]{1,0:T(8,128)}, u32[]{:S(2)}) copy-start(s32[32,128]{1,0:T(8,128)} %param.23) | copy-start | bytes 49156
  79.0 1.4 %copy-start.7 = (f32[32,128]{1,0:T(8,128)S(1)}, f32[32,128]{1,0:T(8,128)}, u32[]{:S(2)}) copy-start(f32[32,128]{1,0:T(8,128)} %param.24) | copy-start | bytes 49156

commit v16 on v14

--- a/solution.py
+++ b/solution.py
@@ -178,7 +178,8 @@
 
 def reduce_chain_kernel(y_chips, groups, x_ref, base_ref, frac_ref,
                         total_ref, halo_ref, rows_ref, cols_ref, core_buf, y_src, y_buf, z_src, z_buf,
-                        d_src, d_buf, edge_buf, local_sems, send_sems, recv_sems, halo_send, halo_recv):
+                        d_src, d_buf, edge_buf, local_sems, send_sems, recv_sems, halo_send, halo_recv,
+                        core_local, core_send, core_recv):
     arrive = signal_all(
         peers(2, core_place)
         + peers(y_chips, y_place)
@@ -188,12 +189,58 @@
     )
     stencil_kernel(base_ref, frac_ref, rows_ref, cols_ref)
     arrive()
-    run_phase(2, core_place, row_block, x_ref, core_buf, local_sems.at[0], send_sems.at[0], recv_sems.at[0])
-    y_src[...] = (core_buf[0].astype(jnp.float32) + core_buf[1].astype(jnp.float32)).astype(y_src.dtype)
-    run_phase(
-        y_chips, y_place, lane_blocks(y_chips), y_src, y_buf,
-        local_sems.at[1], send_sems.at[1], recv_sems.at[1],
-    )
+    me_c, core_device = core_place()
+    sibling = 1 - me_c
+    me_y, y_device = y_place()
+    width = x_ref.shape[2] // y_chips
+
+    def window(w):
+        return pl.ds(pl.multiple_of(w * width, width), width)
+
+    def core_copies(w):
+        own = pltpu.make_async_copy(
+            x_ref.at[me_c, :, window(w)], core_buf.at[me_c, :, window(w)], core_local.at[w]
+        )
+        far = pltpu.make_async_remote_copy(
+            src_ref=x_ref.at[sibling, :, window(w)],
+            dst_ref=core_buf.at[me_c, :, window(w)],
+            send_sem=core_send.at[w],
+            recv_sem=core_recv.at[w],
+            device_id=core_device(sibling),
+            device_id_type=pl.DeviceIdType.MESH,
+        )
+        return own, far
+
+    for w in range(y_chips):
+        for copy in core_copies(w):
+            copy.start()
+    y_copies = []
+    for k in range(y_chips):
+        w = lax.rem(me_y + k, y_chips)
+        own, far = core_copies(w)
+        own.wait()
+        far.wait_send()
+        far.wait_recv()
+        y_src[:, window(w)] = (
+            core_buf[0, :, window(w)].astype(jnp.float32) + core_buf[1, :, window(w)].astype(jnp.float32)
+        ).astype(y_src.dtype)
+        if k == 0:
+            copy = pltpu.make_async_copy(y_src.at[:, window(w)], y_buf.at[me_y], local_sems.at[1])
+        else:
+            copy = pltpu.make_async_remote_copy(
+                src_ref=y_src.at[:, window(w)],
+                dst_ref=y_buf.at[me_y],
+                send_sem=send_sems.at[1, k],
+                recv_sem=recv_sems.at[1, k],
+                device_id=y_device(w),
+                device_id_type=pl.DeviceIdType.MESH,
+            )
+        copy.start()
+        y_copies.append(copy)
+    y_copies[0].wait()
+    for copy in y_copies[1:]:
+        copy.wait_send()
+        copy.wait_recv()
     z_src[...] = jnp.sum(y_buf[...].astype(jnp.float32), axis=0).astype(z_src.dtype)
     run_phase(
         Z_CHIPS, z_place, lane_blocks(Z_CHIPS), z_src, z_buf,
@@ -268,6 +315,9 @@
             pltpu.SemaphoreType.DMA((4, wide)),
             pltpu.SemaphoreType.DMA((2, groups)),
             pltpu.SemaphoreType.DMA((2, groups)),
+            pltpu.SemaphoreType.DMA((y_chips,)),
+            pltpu.SemaphoreType.DMA((y_chips,)),
+            pltpu.SemaphoreType.DMA((y_chips,)),
         ],
         compiler_params=pltpu.CompilerParams(collective_id=collective_id, has_side_effects=True),
     )(x, *stencil)

time: 82.5 us -> 82.3 us (level)
  no operation moved by 1% of the time
where the time goes in v16:
time: 82.3 us; the launch traced here: 81.9 us
  Pallas kernels  63.4 us (77%)
  local copies, waits for them, and re-layouts  7.71 us (9%)
  matrix products  6.95 us (8%)
  other arithmetic  3.48 us (4%)
    pallas_call x1, Pallas kernels, reduce_chain(): pl.pallas_call(functools.partial(reduce_chain_kernel, y_chips, groups), o...  31.9 us
    pallas_call x1, Pallas kernels, gather_chain(): pl.pallas_call(functools.partial(gather_chain_kernel, y_chips, row_count,...  27.6 us
    unnamed x31, local copies, waits for them, and re-layouts  4.47 us
    pallas_call x1, Pallas kernels, insert_planes(): pl.pallas_call(insert_kernel, out_shape=jax.ShapeDtypeStruct((planes * y_...  3.94 us
    dot_general x2, matrix products, local(): jnp.dot(member, part, precision=lax.Precision.HIGHEST, preferred_element_...  1.9 us

profile of v16, /device:TPU:1, one launch (start us, length us, event | category | flops | bytes accessed | tf_op | source)
XLA Modules:
  0.0 81.9 jit_solution(5059416598729823507)
XLA Ops:
  0.0 0.8 %copy-done = bf16[1,16384]{1,0:T(2,128)(2,1)S(1)} copy-done((bf16[1,16384]{1,0:T(2,128)(2,1)S(1)}, bf16[1,16384]{1,0:T(2,128)(2,1)}, u32[]{:S(2)}) %copy-start) | copy-done | bytes 32792
  0.8 0.2 reduce
  1.0 0.6 constant_dynamic-slice_fusion.x_ref
  1.6 27.6 %shard_map.127 = (bf16[2,4,8,64,128]{4,3,2,1,0:T(8,128)(2,1)}, bf16[128,16384]{1,0:T(8,128)(2,1)}) custom-call(bf16[1,64,128]{2,1,0:T(8,128)(2,1)} %constant_dynamic-slice_fusion.x_ref), custom_call_target="tpu_custom_call" | custom-call | tf_op jit(solution)/shard_map/pallas_call | solution.py:369
  29.2 1.3 %slice_bitcast_fusion.1 = (bf16[4,8,64,128]{3,2,1,0:T(8,128)(2,1)S(1)}, bf16[4,8,64,128]{3,2,1,0:T(8,128)(2,1)S(1)}) fusion(bf16[2,4,8,64,128]{4,3,2,1,0:T(8,128)(2,1)} %get-tuple-element.11), kind=kLoop, calls=%fused_computation.51 | loop fusion | bytes 2097152
  30.5 0.0 copy-start.2
  30.5 0.0 copy-start.3
  30.6 0.0 copy-start.13
  30.6 0.2 select_reduce_fusion
  30.8 0.4 fusion.2
  31.2 0.4 fusion.3
  31.6 0.1 copy-done.2
  31.8 0.3 copy-done.3
  32.1 0.7 fusion.7
  32.8 1.5 %copy-done.1 = bf16[128,16384]{1,0:T(8,128)(2,1)S(1)} copy-done((bf16[128,16384]{1,0:T(8,128)(2,1)S(1)}, bf16[128,16384]{1,0:T(8,128)(2,1)}, u32[]{:S(2)}) %copy-start.1) | copy-done | bytes 4194328
  34.3 1.6 %fusion.74 = (f32[32]{0:T(128)S(1)}, f32[32,128]{1,0:T(8,128)S(1)}) fusion(bf16[128,16384]{1,0:T(8,128)(2,1)S(1)} %copy-done.1, bf16[32,8192]{1,0:T(8,128)(2,1)S(1)} %get-tuple-element.22, bf16[32,8192]{1,0:T(8,128)(2,1)S(1)} %get-tuple-element.21), kind=kOutput, calls=%fused_computation.120 | convolution fusion | flops 136323040 | bytes 5259392 | tf_op jit(solution)/shard_map/np,sp->ns/dot_general | solution.py:402
  35.9 0.2 fusion.53
  36.1 0.8 fusion.54
  36.8 1.0 %fusion.1 = bf16[32,8192]{1,0:T(8,128)(2,1)S(1)} fusion(f32[32,8192]{1,0:T(8,128)S(1)} %get-tuple-element.33, f32[32,16384]{1,0:T(8,128)S(1)} %fusion.54, bf16[32,16384]{1,0:T(8,128)(2,1)S(1)} %copy-done.3, s32[32]{0:T(128)S(1)} %copy-done.12), kind=kOutput, calls=%fused_computation.3 | convolution fusion | flops 102761472 | bytes 4718720 | tf_op jit(solution)/shard_map/dot_general | solution.py:491
  37.8 0.9 %fusion = bf16[32,8192]{1,0:T(8,128)(2,1)S(1)} fusion(f32[32,8192]{1,0:T(8,128)S(1)} %get-tuple-element.33, f32[32,16384]{1,0:T(8,128)S(1)} %fusion.54, bf16[32,16384]{1,0:T(8,128)(2,1)S(1)} %copy-done.3, s32[32]{0:T(128)S(1)} %copy-done.12), kind=kOutput, calls=%fused_computation.2 | convolution fusion | flops 102761472 | bytes 4718720 | tf_op jit(solution)/shard_map/dot_general | solution.py:491
  38.8 0.1 fusion.71
  38.8 0.2 convolution_convert_fusion.3
  39.0 0.1 reshape.92
  39.1 0.0 copy-start.9
  39.2 0.0 copy-start.10
  39.2 0.1 fusion.24
  39.3 1.2 %pad_maximum_fusion.x_ref = bf16[2,40,8192]{2,1,0:T(8,128)(2,1)} fusion(bf16[1,40,8192]{2,1,0:T(8,128)(2,1)S(1)} %get-tuple-element.32, bf16[1,40,8192]{2,1,0:T(8,128)(2,1)S(1)} %get-tuple-element.31), kind=kLoop, calls=%fused_computation.20 | loop fusion | flops 655360 | bytes 2621440 | tf_op jit(solution)/shard_map/stack | solution.py:506
  40.5 0.1 stack_reshape.12
  40.6 0.1 stack_reshape.13
  40.7 0.6 pad_add_fusion.base_ref
  41.3 0.1 stack_reshape.14
  41.4 0.1 stack_reshape.15
  41.4 0.6 pad_maximum_fusion.3.frac_ref
  42.1 31.9 %shard_map.128 = (f32[2,40,256]{2,1,0:T(8,128)}, f32[2,2,40,256]{3,2,1,0:T(8,128)}, bf16[32,2048]{1,0:T(8,128)(2,1)}, bf16[256,2048]{1,0:T(8,128)(2,1)}) custom-call(bf16[2,40,8192]{2,1,0:T(8,128)(2,1)} %pad_maximum_fusion.x_ref, s32[2,2048]{1,0:T(2,128)} %pad_add_fusion.base_ref, f32[2,2048]{1,0:T(2,128)} %pad_maximum_fusion.3.frac_ref), custom_call_target="tpu_custom_call" | custom-call | tf_op jit(solution)/shard_map/pallas_call | solution.py:294
  73.9 0.7 slice.83
  74.6 0.1 reshape_squeeze.3
  74.7 0.1 convert_multiply_fusion
  74.9 0.3 convolution_multiply_fusion.2
  75.2 0.1 reshape.88
  75.3 0.4 copy-done.4
  75.6 0.2 reshape.85
  76.0 0.1 reshape.86
  76.2 0.1 broadcast_add_fusion
  76.3 0.1 broadcast_subtract_fusion
  76.4 0.7 convolution_bitcast_fusion
  77.0 0.1 copy.28
  77.1 0.8 %reshape.89.sec_ref = f32[24,2048]{1,0:T(8,128)} reshape(f32[3,8,32,64]{3,2,1,0:T(8,128)S(1)} %copy.28) | data formatting | bytes 393216 | tf_op jit(solution)/shard_map/reshape | solution.py:571
  77.9 3.9 %shard_map.129 = f32[768,256]{1,0:T(8,128)} custom-call(bf16[32,2048]{1,0:T(8,128)(2,1)} %get-tuple-element.13.rows_ref, f32[24,2048]{1,0:T(8,128)} %reshape.89.sec_ref, bf16[256,2048]{1,0:T(8,128)(2,1)} %get-tuple-element.16.cols_ref), custom_call_target="tpu_custom_call" | custom-call | flops 805306368 | bytes 2162688 | tf_op jit(solution)/shard_map/pallas_call | solution.py:596
  (30 shorter events, 0.3 us)
Async XLA Ops:
  0.0 0.8 %copy-start = (bf16[1,16384]{1,0:T(2,128)(2,1)S(1)}, bf16[1,16384]{1,0:T(2,128)(2,1)}, u32[]{:S(2)}) copy-start(bf16[1,16384]{1,0:T(2,128)(2,1)} %param.17) | copy-start | bytes 98308
  0.0 30.6 %copy-start.12 = (s32[32]{0:T(128)S(1)}, s32[32]{0:T(128)}, u32[]{:S(2)}) copy-start(s32[32]{0:T(128)} %param.14) | copy-start | bytes 388
  0.0 30.6 %copy-start.14 = (s32[32]{0:T(128)S(1)}, s32[32]{0:T(128)}, u32[]{:S(2)}) copy-start(s32[32]{0:T(128)} %param.16) | copy-start | bytes 388
  30.5 1.2 %copy-start.2 = (bf16[64,8192]{1,0:T(8,128)(2,1)S(1)}, bf16[64,8192]{1,0:T(8,128)(2,1)}, u32[]{:S(2)}) copy-start(bf16[64,8192]{1,0:T(8,128)(2,1)} %param.18) | copy-start | bytes 3145732
  30.5 1.5 %copy-start.3 = (bf16[32,16384]{1,0:T(8,128)(2,1)S(1)}, bf16[32,16384]{1,0:T(8,128)(2,1)}, u32[]{:S(2)}) copy-start(bf16[32,16384]{1,0:T(8,128)(2,1)} %param.13) | copy-start | bytes 3145732
  30.6 1.5 %copy-start.13 = (s32[32]{0:T(128)S(1)}, s32[32]{0:T(128)}, u32[]{:S(2)}) copy-start(s32[32]{0:T(128)} %param.15) | copy-start | bytes 388
  32.1 2.2 %copy-start.1 = (bf16[128,16384]{1,0:T(8,128)(2,1)S(1)}, bf16[128,16384]{1,0:T(8,128)(2,1)}, u32[]{:S(2)}) copy-start(bf16[128,16384]{1,0:T(8,128)(2,1)} %get-tuple-element.12) | copy-start | bytes 12582916
  39.1 1.4 %copy-start.8 = (s32[32,64]{1,0:T(8,128)S(1)}, s32[32,64]{1,0:T(8,128)}, u32[]{:S(2)}) copy-start(s32[32,64]{1,0:T(8,128)} %param.20) | copy-start | bytes 24580
  39.1 1.4 %copy-start.9 = (s32[32,64]{1,0:T(8,128)S(1)}, s32[32,64]{1,0:T(8,128)}, u32[]{:S(2)}) copy-start(s32[32,64]{1,0:T(8,128)} %param.19) | copy-start | bytes 24580
  39.2 2.1 %copy-start.10 = (f32[32,64]{1,0:T(8,128)S(1)}, f32[32,64]{1,0:T(8,128)}, u32[]{:S(2)}) copy-start(f32[32,64]{1,0:T(8,128)} %param.22) | copy-start | bytes 24580
  39.2 2.2 %copy-start.11 = (f32[32,64]{1,0:T(8,128)S(1)}, f32[32,64]{1,0:T(8,128)}, u32[]{:S(2)}) copy-start(f32[32,64]{1,0:T(8,128)} %param.21) | copy-start | bytes 24580
  74.7 0.9 %copy-start.4 = (f32[2,2,40,256]{3,2,1,0:T(8,128)S(1)}, f32[2,2,40,256]{3,2,1,0:T(8,128)}, u32[]{:S(2)}) copy-start(f32[2,2,40,256]{3,2,1,0:T(8,128)} %get-tuple-element.14) | copy-start | bytes 491524
  74.9 1.1 %copy-start.5 = (f32[2,40,256]{2,1,0:T(8,128)S(1)}, f32[2,40,256]{2,1,0:T(8,128)}, u32[]{:S(2)}) copy-start(f32[2,40,256]{2,1,0:T(8,128)} %get-tuple-element.15) | copy-start | bytes 245764
  74.9 1.3 %copy-start.6 = (s32[32,128]{1,0:T(8,128)S(1)}, s32[32,128]{1,0:T(8,128)}, u32[]{:S(2)}) copy-start(s32[32,128]{1,0:T(8,128)} %param.23) | copy-start | bytes 49156
  74.9 1.4 %copy-start.7 = (f32[32,128]{1,0:T(8,128)S(1)}, f32[32,128]{1,0:T(8,128)}, u32[]{:S(2)}) copy-start(f32[32,128]{1,0:T(8,128)} %param.24) | copy-start | bytes 49156

commit v17 on v16

--- a/solution.py
+++ b/solution.py
@@ -352,14 +352,70 @@
         )
 
 
-def gather_chain_kernel(y_chips, row_count, half_cols, x_ref, out_ref, phase_ref, z_buf, y_buf,
-                        local_sems, send_sems, recv_sems):
+def gather_chain_kernel(y_chips, row_count, half_cols, x_ref, out_ref, phase_ref, z_buf,
+                        local_sems, send_sems, recv_sems, core_send, core_recv):
     arrive = signal_all(peers(Z_CHIPS, z_place) + peers(y_chips, y_place) + peers(2, core_place))
     phase_kernel(row_count, half_cols, phase_ref)
     arrive()
     run_phase(Z_CHIPS, z_place, whole, x_ref, z_buf, local_sems.at[0], send_sems.at[0], recv_sems.at[0])
-    run_phase(y_chips, y_place, entire, z_buf, y_buf, local_sems.at[1], send_sems.at[1], recv_sems.at[1])
-    run_phase(2, core_place, entire, y_buf, out_ref, local_sems.at[2], send_sems.at[2], recv_sems.at[2])
+    me_c, core_device = core_place()
+    me_y, y_device = y_place()
+    sibling = core_device(1 - me_c)
+
+    def forward(block, source):
+        return pltpu.make_async_remote_copy(
+            src_ref=source,
+            dst_ref=out_ref.at[me_c, block],
+            send_sem=core_send.at[block],
+            recv_sem=core_recv.at[block],
+            device_id=sibling,
+            device_id_type=pl.DeviceIdType.MESH,
+        )
+
+    own = pltpu.make_async_copy(z_buf, out_ref.at[me_c, me_y], local_sems.at[1])
+    own.start()
+    sent = [forward(me_y, z_buf)]
+    sent[0].start()
+    y_copies = []
+    for k in range(1, y_chips):
+        copy = pltpu.make_async_remote_copy(
+            src_ref=z_buf,
+            dst_ref=out_ref.at[me_c, me_y],
+            send_sem=send_sems.at[1, k],
+            recv_sem=recv_sems.at[1, k],
+            device_id=y_device(lax.rem(me_y + k, y_chips)),
+            device_id_type=pl.DeviceIdType.MESH,
+        )
+        copy.start()
+        y_copies.append(copy)
+    for k in range(1, y_chips):
+        block = lax.rem(me_y + y_chips - k, y_chips)
+        pltpu.make_async_remote_copy(
+            src_ref=z_buf,
+            dst_ref=out_ref.at[me_c, block],
+            send_sem=send_sems.at[1, k],
+            recv_sem=recv_sems.at[1, k],
+            device_id=y_device(block),
+            device_id_type=pl.DeviceIdType.MESH,
+        ).wait_recv()
+        copy = forward(block, out_ref.at[me_c, block])
+        copy.start()
+        sent.append(copy)
+    own.wait()
+    for copy in y_copies:
+        copy.wait_send()
+    for copy in sent:
+        copy.wait_send()
+    for k in range(y_chips):
+        block = lax.rem(me_y + k, y_chips)
+        pltpu.make_async_remote_copy(
+            src_ref=z_buf,
+            dst_ref=out_ref.at[1 - me_c, block],
+            send_sem=core_send.at[block],
+            recv_sem=core_recv.at[block],
+            device_id=sibling,
+            device_id_type=pl.DeviceIdType.MESH,
+        ).wait_recv()
 
 
 def gather_chain(x, row_count, half_cols, y_chips, collective_id):
@@ -376,10 +432,11 @@
         out_specs=[pl.BlockSpec(memory_space=pltpu.VMEM)] * 2,
         scratch_shapes=[
             pltpu.VMEM((Z_CHIPS, rows, lanes), x.dtype),
-            pltpu.VMEM((y_chips, Z_CHIPS, rows, lanes), x.dtype),
-            pltpu.SemaphoreType.DMA((3,)),
-            pltpu.SemaphoreType.DMA((3, Z_CHIPS)),
-            pltpu.SemaphoreType.DMA((3, Z_CHIPS)),
+            pltpu.SemaphoreType.DMA((2,)),
+            pltpu.SemaphoreType.DMA((2, Z_CHIPS)),
+            pltpu.SemaphoreType.DMA((2, Z_CHIPS)),
+            pltpu.SemaphoreType.DMA((y_chips,)),
+            pltpu.SemaphoreType.DMA((y_chips,)),
         ],
         compiler_params=pltpu.CompilerParams(collective_id=collective_id, has_side_effects=True),
     )(x)

time: 82.3 us -> 81.6 us (level)
  no operation moved by 1% of the time
where the time goes in v17:
time: 81.6 us; the launch traced here: 81.3 us
  Pallas kernels  62.8 us (77%)
  local copies, waits for them, and re-layouts  7.71 us (9%)
  matrix products  6.95 us (9%)
  other arithmetic  3.48 us (4%)
    pallas_call x1, Pallas kernels, reduce_chain(): pl.pallas_call(functools.partial(reduce_chain_kernel, y_chips, groups), o...  31.7 us
    pallas_call x1, Pallas kernels, gather_chain(): pl.pallas_call(functools.partial(gather_chain_kernel, y_chips, row_count,...  27.1 us
    unnamed x31, local copies, waits for them, and re-layouts  4.47 us
    pallas_call x1, Pallas kernels, insert_planes(): pl.pallas_call(insert_kernel, out_shape=jax.ShapeDtypeStruct((planes * y_...  3.94 us
    dot_general x2, matrix products, local(): jnp.dot(member, part, precision=lax.Precision.HIGHEST, preferred_element_...  1.9 us

profile of v17, /device:TPU:1, one launch (start us, length us, event | category | flops | bytes accessed | tf_op | source)
XLA Modules:
  0.0 81.3 jit_solution(16243294311111499556)
XLA Ops:
  0.0 0.8 %copy-done = bf16[1,16384]{1,0:T(2,128)(2,1)S(1)} copy-done((bf16[1,16384]{1,0:T(2,128)(2,1)S(1)}, bf16[1,16384]{1,0:T(2,128)(2,1)}, u32[]{:S(2)}) %copy-start) | copy-done | bytes 32792
  0.8 0.2 reduce
  1.0 0.6 constant_dynamic-slice_fusion.x_ref
  1.6 27.1 %shard_map.127 = (bf16[2,4,8,64,128]{4,3,2,1,0:T(8,128)(2,1)}, bf16[128,16384]{1,0:T(8,128)(2,1)}) custom-call(bf16[1,64,128]{2,1,0:T(8,128)(2,1)} %constant_dynamic-slice_fusion.x_ref), custom_call_target="tpu_custom_call" | custom-call | tf_op jit(solution)/shard_map/pallas_call | solution.py:425
  28.7 1.3 %slice_bitcast_fusion.1 = (bf16[4,8,64,128]{3,2,1,0:T(8,128)(2,1)S(1)}, bf16[4,8,64,128]{3,2,1,0:T(8,128)(2,1)S(1)}) fusion(bf16[2,4,8,64,128]{4,3,2,1,0:T(8,128)(2,1)} %get-tuple-element.11), kind=kLoop, calls=%fused_computation.51 | loop fusion | bytes 2097152
  30.1 0.0 copy-start.2
  30.1 0.0 copy-start.3
  30.1 0.2 select_reduce_fusion
  30.3 0.4 fusion.2
  30.7 0.4 fusion.3
  31.2 0.1 copy-done.2
  31.3 0.3 copy-done.3
  31.6 0.7 fusion.7
  32.3 1.5 %copy-done.1 = bf16[128,16384]{1,0:T(8,128)(2,1)S(1)} copy-done((bf16[128,16384]{1,0:T(8,128)(2,1)S(1)}, bf16[128,16384]{1,0:T(8,128)(2,1)}, u32[]{:S(2)}) %copy-start.1) | copy-done | bytes 4194328
  33.8 1.6 %fusion.74 = (f32[32]{0:T(128)S(1)}, f32[32,128]{1,0:T(8,128)S(1)}) fusion(bf16[128,16384]{1,0:T(8,128)(2,1)S(1)} %copy-done.1, bf16[32,8192]{1,0:T(8,128)(2,1)S(1)} %get-tuple-element.22, bf16[32,8192]{1,0:T(8,128)(2,1)S(1)} %get-tuple-element.21), kind=kOutput, calls=%fused_computation.120 | convolution fusion | flops 136323040 | bytes 5259392 | tf_op jit(solution)/shard_map/np,sp->ns/dot_general | solution.py:459
  35.4 0.2 fusion.53
  35.6 0.7 fusion.54
  36.4 1.0 %fusion.1 = bf16[32,8192]{1,0:T(8,128)(2,1)S(1)} fusion(f32[32,8192]{1,0:T(8,128)S(1)} %get-tuple-element.33, f32[32,16384]{1,0:T(8,128)S(1)} %fusion.54, bf16[32,16384]{1,0:T(8,128)(2,1)S(1)} %copy-done.3, s32[32]{0:T(128)S(1)} %copy-done.12), kind=kOutput, calls=%fused_computation.3 | convolution fusion | flops 102761472 | bytes 4718720 | tf_op jit(solution)/shard_map/dot_general | solution.py:548
  37.3 1.0 %fusion = bf16[32,8192]{1,0:T(8,128)(2,1)S(1)} fusion(f32[32,8192]{1,0:T(8,128)S(1)} %get-tuple-element.33, f32[32,16384]{1,0:T(8,128)S(1)} %fusion.54, bf16[32,16384]{1,0:T(8,128)(2,1)S(1)} %copy-done.3, s32[32]{0:T(128)S(1)} %copy-done.12), kind=kOutput, calls=%fused_computation.2 | convolution fusion | flops 102761472 | bytes 4718720 | tf_op jit(solution)/shard_map/dot_general | solution.py:548
  38.3 0.1 fusion.71
  38.4 0.2 convolution_convert_fusion.3
  38.5 0.1 reshape.92
  38.7 0.0 copy-start.9
  38.7 0.0 copy-start.10
  38.7 0.1 fusion.24
  38.8 1.2 %pad_maximum_fusion.x_ref = bf16[2,40,8192]{2,1,0:T(8,128)(2,1)} fusion(bf16[1,40,8192]{2,1,0:T(8,128)(2,1)S(1)} %get-tuple-element.32, bf16[1,40,8192]{2,1,0:T(8,128)(2,1)S(1)} %get-tuple-element.31), kind=kLoop, calls=%fused_computation.20 | loop fusion | flops 655360 | bytes 2621440 | tf_op jit(solution)/shard_map/stack | solution.py:563
  40.0 0.1 stack_reshape.12
  40.1 0.1 stack_reshape.13
  40.2 0.6 pad_add_fusion.base_ref
  40.8 0.1 stack_reshape.14
  40.9 0.1 stack_reshape.15
  41.0 0.6 pad_maximum_fusion.3.frac_ref
  41.6 31.7 %shard_map.128 = (f32[2,40,256]{2,1,0:T(8,128)}, f32[2,2,40,256]{3,2,1,0:T(8,128)}, bf16[32,2048]{1,0:T(8,128)(2,1)}, bf16[256,2048]{1,0:T(8,128)(2,1)}) custom-call(bf16[2,40,8192]{2,1,0:T(8,128)(2,1)} %pad_maximum_fusion.x_ref, s32[2,2048]{1,0:T(2,128)} %pad_add_fusion.base_ref, f32[2,2048]{1,0:T(2,128)} %pad_maximum_fusion.3.frac_ref), custom_call_target="tpu_custom_call" | custom-call | tf_op jit(solution)/shard_map/pallas_call | solution.py:294
  73.3 0.7 slice.83
  74.0 0.1 reshape_squeeze.3
  74.1 0.1 convert_multiply_fusion
  74.3 0.0 copy-start.6
  74.3 0.3 convolution_multiply_fusion.2
  74.6 0.1 reshape.88
  74.6 0.4 copy-done.4
  75.0 0.2 reshape.85
  75.4 0.1 reshape.86
  75.6 0.1 broadcast_add_fusion
  75.7 0.1 broadcast_subtract_fusion
  75.7 0.7 convolution_bitcast_fusion
  76.4 0.1 copy.28
  76.5 0.8 %reshape.89.sec_ref = f32[24,2048]{1,0:T(8,128)} reshape(f32[3,8,32,64]{3,2,1,0:T(8,128)S(1)} %copy.28) | data formatting | bytes 393216 | tf_op jit(solution)/shard_map/reshape | solution.py:628
  77.3 3.9 %shard_map.129 = f32[768,256]{1,0:T(8,128)} custom-call(bf16[32,2048]{1,0:T(8,128)(2,1)} %get-tuple-element.13.rows_ref, f32[24,2048]{1,0:T(8,128)} %reshape.89.sec_ref, bf16[256,2048]{1,0:T(8,128)(2,1)} %get-tuple-element.16.cols_ref), custom_call_target="tpu_custom_call" | custom-call | flops 805306368 | bytes 2162688 | tf_op jit(solution)/shard_map/pallas_call | solution.py:653
  (30 shorter events, 0.3 us)
Async XLA Ops:
  0.0 0.8 %copy-start = (bf16[1,16384]{1,0:T(2,128)(2,1)S(1)}, bf16[1,16384]{1,0:T(2,128)(2,1)}, u32[]{:S(2)}) copy-start(bf16[1,16384]{1,0:T(2,128)(2,1)} %param.17) | copy-start | bytes 98308
  0.0 30.1 %copy-start.12 = (s32[32]{0:T(128)S(1)}, s32[32]{0:T(128)}, u32[]{:S(2)}) copy-start(s32[32]{0:T(128)} %param.14) | copy-start | bytes 388
  0.0 30.1 %copy-start.14 = (s32[32]{0:T(128)S(1)}, s32[32]{0:T(128)}, u32[]{:S(2)}) copy-start(s32[32]{0:T(128)} %param.16) | copy-start | bytes 388
  30.1 1.2 %copy-start.2 = (bf16[64,8192]{1,0:T(8,128)(2,1)S(1)}, bf16[64,8192]{1,0:T(8,128)(2,1)}, u32[]{:S(2)}) copy-start(bf16[64,8192]{1,0:T(8,128)(2,1)} %param.18) | copy-start | bytes 3145732
  30.1 1.5 %copy-start.3 = (bf16[32,16384]{1,0:T(8,128)(2,1)S(1)}, bf16[32,16384]{1,0:T(8,128)(2,1)}, u32[]{:S(2)}) copy-start(bf16[32,16384]{1,0:T(8,128)(2,1)} %param.13) | copy-start | bytes 3145732
  30.1 1.5 %copy-start.13 = (s32[32]{0:T(128)S(1)}, s32[32]{0:T(128)}, u32[]{:S(2)}) copy-start(s32[32]{0:T(128)} %param.15) | copy-start | bytes 388
  31.6 2.2 %copy-start.1 = (bf16[128,16384]{1,0:T(8,128)(2,1)S(1)}, bf16[128,16384]{1,0:T(8,128)(2,1)}, u32[]{:S(2)}) copy-start(bf16[128,16384]{1,0:T(8,128)(2,1)} %get-tuple-element.12) | copy-start | bytes 12582916
  38.7 1.4 %copy-start.8 = (s32[32,64]{1,0:T(8,128)S(1)}, s32[32,64]{1,0:T(8,128)}, u32[]{:S(2)}) copy-start(s32[32,64]{1,0:T(8,128)} %param.20) | copy-start | bytes 24580
  38.7 1.4 %copy-start.9 = (s32[32,64]{1,0:T(8,128)S(1)}, s32[32,64]{1,0:T(8,128)}, u32[]{:S(2)}) copy-start(s32[32,64]{1,0:T(8,128)} %param.19) | copy-start | bytes 24580
  38.7 2.1 %copy-start.10 = (f32[32,64]{1,0:T(8,128)S(1)}, f32[32,64]{1,0:T(8,128)}, u32[]{:S(2)}) copy-start(f32[32,64]{1,0:T(8,128)} %param.22) | copy-start | bytes 24580
  38.7 2.2 %copy-start.11 = (f32[32,64]{1,0:T(8,128)S(1)}, f32[32,64]{1,0:T(8,128)}, u32[]{:S(2)}) copy-start(f32[32,64]{1,0:T(8,128)} %param.21) | copy-start | bytes 24580
  74.1 0.9 %copy-start.4 = (f32[2,2,40,256]{3,2,1,0:T(8,128)S(1)}, f32[2,2,40,256]{3,2,1,0:T(8,128)}, u32[]{:S(2)}) copy-start(f32[2,2,40,256]{3,2,1,0:T(8,128)} %get-tuple-element.14) | copy-start | bytes 491524
  74.2 1.1 %copy-start.5 = (f32[2,40,256]{2,1,0:T(8,128)S(1)}, f32[2,40,256]{2,1,0:T(8,128)}, u32[]{:S(2)}) copy-start(f32[2,40,256]{2,1,0:T(8,128)} %get-tuple-element.15) | copy-start | bytes 245764
  74.3 1.3 %copy-start.6 = (s32[32,128]{1,0:T(8,128)S(1)}, s32[32,128]{1,0:T(8,128)}, u32[]{:S(2)}) copy-start(s32[32,128]{1,0:T(8,128)} %param.23) | copy-start | bytes 49156
  74.3 1.4 %copy-start.7 = (f32[32,128]{1,0:T(8,128)S(1)}, f32[32,128]{1,0:T(8,128)}, u32[]{:S(2)}) copy-start(f32[32,128]{1,0:T(8,128)} %param.24) | copy-start | bytes 49156

commit v18 on v16

--- a/solution.py
+++ b/solution.py
@@ -583,7 +583,7 @@
         ).astype(jnp.bfloat16)
         return carry
 
-    lax.fori_loop(0, sec_ref.shape[0], body, 0)
+    lax.fori_loop(0, sec_ref.shape[0], body, 0, unroll=True)
     out_ref[...] = lax.dot_general(
         lifted_ref[...], cols_ref[...], (((1,), (1,)), ((), ())), preferred_element_type=jnp.float32
     )

time: 82.3 us -> 81.6 us (level)
  no operation moved by 1% of the time
where the time goes in v18:
time: 81.6 us; the launch traced here: 81.2 us
  Pallas kernels  62.8 us (77%)
  local copies, waits for them, and re-layouts  7.71 us (9%)
  matrix products  6.95 us (9%)
  other arithmetic  3.48 us (4%)
    pallas_call x1, Pallas kernels, reduce_chain(): pl.pallas_call(functools.partial(reduce_chain_kernel, y_chips, groups), o...  31.9 us
    pallas_call x1, Pallas kernels, gather_chain(): pl.pallas_call(functools.partial(gather_chain_kernel, y_chips, row_count,...  27.6 us
    unnamed x31, local copies, waits for them, and re-layouts  4.47 us
    pallas_call x1, Pallas kernels, insert_planes(): pl.pallas_call(insert_kernel, out_shape=jax.ShapeDtypeStruct((planes * y_...  3.3 us
    dot_general x2, matrix products, local(): jnp.dot(member, part, precision=lax.Precision.HIGHEST, preferred_element_...  1.9 us

profile of v18, /device:TPU:1, one launch (start us, length us, event | category | flops | bytes accessed | tf_op | source)
XLA Modules:
  0.0 81.2 jit_solution(13979157877476950513)
XLA Ops:
  0.0 0.8 %copy-done = bf16[1,16384]{1,0:T(2,128)(2,1)S(1)} copy-done((bf16[1,16384]{1,0:T(2,128)(2,1)S(1)}, bf16[1,16384]{1,0:T(2,128)(2,1)}, u32[]{:S(2)}) %copy-start) | copy-done | bytes 32792
  0.8 0.2 reduce
  1.0 0.6 constant_dynamic-slice_fusion.x_ref
  1.6 27.6 %shard_map.127 = (bf16[2,4,8,64,128]{4,3,2,1,0:T(8,128)(2,1)}, bf16[128,16384]{1,0:T(8,128)(2,1)}) custom-call(bf16[1,64,128]{2,1,0:T(8,128)(2,1)} %constant_dynamic-slice_fusion.x_ref), custom_call_target="tpu_custom_call" | custom-call | tf_op jit(solution)/shard_map/pallas_call | solution.py:369
  29.2 1.3 %slice_bitcast_fusion.1 = (bf16[4,8,64,128]{3,2,1,0:T(8,128)(2,1)S(1)}, bf16[4,8,64,128]{3,2,1,0:T(8,128)(2,1)S(1)}) fusion(bf16[2,4,8,64,128]{4,3,2,1,0:T(8,128)(2,1)} %get-tuple-element.11), kind=kLoop, calls=%fused_computation.51 | loop fusion | bytes 2097152
  30.5 0.0 copy-start.2
  30.5 0.0 copy-start.3
  30.6 0.0 copy-start.13
  30.6 0.2 select_reduce_fusion
  30.8 0.4 fusion.2
  31.2 0.4 fusion.3
  31.6 0.1 copy-done.2
  31.8 0.3 copy-done.3
  32.1 0.7 fusion.7
  32.8 1.5 %copy-done.1 = bf16[128,16384]{1,0:T(8,128)(2,1)S(1)} copy-done((bf16[128,16384]{1,0:T(8,128)(2,1)S(1)}, bf16[128,16384]{1,0:T(8,128)(2,1)}, u32[]{:S(2)}) %copy-start.1) | copy-done | bytes 4194328
  34.3 1.6 %fusion.74 = (f32[32]{0:T(128)S(1)}, f32[32,128]{1,0:T(8,128)S(1)}) fusion(bf16[128,16384]{1,0:T(8,128)(2,1)S(1)} %copy-done.1, bf16[32,8192]{1,0:T(8,128)(2,1)S(1)} %get-tuple-element.22, bf16[32,8192]{1,0:T(8,128)(2,1)S(1)} %get-tuple-element.21), kind=kOutput, calls=%fused_computation.120 | convolution fusion | flops 136323040 | bytes 5259392 | tf_op jit(solution)/shard_map/np,sp->ns/dot_general | solution.py:402
  35.9 0.2 fusion.53
  36.1 0.8 fusion.54
  36.8 1.0 %fusion.1 = bf16[32,8192]{1,0:T(8,128)(2,1)S(1)} fusion(f32[32,8192]{1,0:T(8,128)S(1)} %get-tuple-element.33, f32[32,16384]{1,0:T(8,128)S(1)} %fusion.54, bf16[32,16384]{1,0:T(8,128)(2,1)S(1)} %copy-done.3, s32[32]{0:T(128)S(1)} %copy-done.12), kind=kOutput, calls=%fused_computation.3 | convolution fusion | flops 102761472 | bytes 4718720 | tf_op jit(solution)/shard_map/dot_general | solution.py:491
  37.8 0.9 %fusion = bf16[32,8192]{1,0:T(8,128)(2,1)S(1)} fusion(f32[32,8192]{1,0:T(8,128)S(1)} %get-tuple-element.33, f32[32,16384]{1,0:T(8,128)S(1)} %fusion.54, bf16[32,16384]{1,0:T(8,128)(2,1)S(1)} %copy-done.3, s32[32]{0:T(128)S(1)} %copy-done.12), kind=kOutput, calls=%fused_computation.2 | convolution fusion | flops 102761472 | bytes 4718720 | tf_op jit(solution)/shard_map/dot_general | solution.py:491
  38.8 0.1 fusion.71
  38.8 0.2 convolution_convert_fusion.3
  39.0 0.1 reshape.92
  39.1 0.0 copy-start.9
  39.2 0.0 copy-start.10
  39.2 0.1 fusion.24
  39.3 1.2 %pad_maximum_fusion.x_ref = bf16[2,40,8192]{2,1,0:T(8,128)(2,1)} fusion(bf16[1,40,8192]{2,1,0:T(8,128)(2,1)S(1)} %get-tuple-element.32, bf16[1,40,8192]{2,1,0:T(8,128)(2,1)S(1)} %get-tuple-element.31), kind=kLoop, calls=%fused_computation.20 | loop fusion | flops 655360 | bytes 2621440 | tf_op jit(solution)/shard_map/stack | solution.py:506
  40.5 0.1 stack_reshape.12
  40.6 0.1 stack_reshape.13
  40.7 0.6 pad_add_fusion.base_ref
  41.3 0.1 stack_reshape.14
  41.4 0.1 stack_reshape.15
  41.4 0.6 pad_maximum_fusion.3.frac_ref
  42.1 31.9 %shard_map.128 = (f32[2,40,256]{2,1,0:T(8,128)}, f32[2,2,40,256]{3,2,1,0:T(8,128)}, bf16[32,2048]{1,0:T(8,128)(2,1)}, bf16[256,2048]{1,0:T(8,128)(2,1)}) custom-call(bf16[2,40,8192]{2,1,0:T(8,128)(2,1)} %pad_maximum_fusion.x_ref, s32[2,2048]{1,0:T(2,128)} %pad_add_fusion.base_ref, f32[2,2048]{1,0:T(2,128)} %pad_maximum_fusion.3.frac_ref), custom_call_target="tpu_custom_call" | custom-call | tf_op jit(solution)/shard_map/pallas_call | solution.py:294
  73.9 0.7 slice.83
  74.6 0.1 reshape_squeeze.3
  74.7 0.1 convert_multiply_fusion
  74.9 0.3 convolution_multiply_fusion.2
  75.2 0.1 reshape.88
  75.3 0.4 copy-done.4
  75.6 0.2 reshape.85
  76.0 0.1 reshape.86
  76.2 0.1 broadcast_add_fusion
  76.3 0.1 broadcast_subtract_fusion
  76.4 0.7 convolution_bitcast_fusion
  77.0 0.1 copy.28
  77.1 0.8 %reshape.89.sec_ref = f32[24,2048]{1,0:T(8,128)} reshape(f32[3,8,32,64]{3,2,1,0:T(8,128)S(1)} %copy.28) | data formatting | bytes 393216 | tf_op jit(solution)/shard_map/reshape | solution.py:571
  77.9 3.3 %shard_map.129 = f32[768,256]{1,0:T(8,128)} custom-call(bf16[32,2048]{1,0:T(8,128)(2,1)} %get-tuple-element.13.rows_ref, f32[24,2048]{1,0:T(8,128)} %reshape.89.sec_ref, bf16[256,2048]{1,0:T(8,128)(2,1)} %get-tuple-element.16.cols_ref), custom_call_target="tpu_custom_call" | custom-call | flops 805306368 | bytes 2162688 | tf_op jit(solution)/shard_map/pallas_call | solution.py:596
  (30 shorter events, 0.3 us)
Async XLA Ops:
  0.0 0.8 %copy-start = (bf16[1,16384]{1,0:T(2,128)(2,1)S(1)}, bf16[1,16384]{1,0:T(2,128)(2,1)}, u32[]{:S(2)}) copy-start(bf16[1,16384]{1,0:T(2,128)(2,1)} %param.17) | copy-start | bytes 98308
  0.0 30.6 %copy-start.12 = (s32[32]{0:T(128)S(1)}, s32[32]{0:T(128)}, u32[]{:S(2)}) copy-start(s32[32]{0:T(128)} %param.14) | copy-start | bytes 388
  0.0 30.6 %copy-start.14 = (s32[32]{0:T(128)S(1)}, s32[32]{0:T(128)}, u32[]{:S(2)}) copy-start(s32[32]{0:T(128)} %param.16) | copy-start | bytes 388
  30.5 1.2 %copy-start.2 = (bf16[64,8192]{1,0:T(8,128)(2,1)S(1)}, bf16[64,8192]{1,0:T(8,128)(2,1)}, u32[]{:S(2)}) copy-start(bf16[64,8192]{1,0:T(8,128)(2,1)} %param.18) | copy-start | bytes 3145732
  30.5 1.5 %copy-start.3 = (bf16[32,16384]{1,0:T(8,128)(2,1)S(1)}, bf16[32,16384]{1,0:T(8,128)(2,1)}, u32[]{:S(2)}) copy-start(bf16[32,16384]{1,0:T(8,128)(2,1)} %param.13) | copy-start | bytes 3145732
  30.6 1.5 %copy-start.13 = (s32[32]{0:T(128)S(1)}, s32[32]{0:T(128)}, u32[]{:S(2)}) copy-start(s32[32]{0:T(128)} %param.15) | copy-start | bytes 388
  32.1 2.2 %copy-start.1 = (bf16[128,16384]{1,0:T(8,128)(2,1)S(1)}, bf16[128,16384]{1,0:T(8,128)(2,1)}, u32[]{:S(2)}) copy-start(bf16[128,16384]{1,0:T(8,128)(2,1)} %get-tuple-element.12) | copy-start | bytes 12582916
  39.1 1.4 %copy-start.8 = (s32[32,64]{1,0:T(8,128)S(1)}, s32[32,64]{1,0:T(8,128)}, u32[]{:S(2)}) copy-start(s32[32,64]{1,0:T(8,128)} %param.20) | copy-start | bytes 24580
  39.1 1.4 %copy-start.9 = (s32[32,64]{1,0:T(8,128)S(1)}, s32[32,64]{1,0:T(8,128)}, u32[]{:S(2)}) copy-start(s32[32,64]{1,0:T(8,128)} %param.19) | copy-start | bytes 24580
  39.2 2.1 %copy-start.10 = (f32[32,64]{1,0:T(8,128)S(1)}, f32[32,64]{1,0:T(8,128)}, u32[]{:S(2)}) copy-start(f32[32,64]{1,0:T(8,128)} %param.22) | copy-start | bytes 24580
  39.2 2.2 %copy-start.11 = (f32[32,64]{1,0:T(8,128)S(1)}, f32[32,64]{1,0:T(8,128)}, u32[]{:S(2)}) copy-start(f32[32,64]{1,0:T(8,128)} %param.21) | copy-start | bytes 24580
  74.7 0.9 %copy-start.4 = (f32[2,2,40,256]{3,2,1,0:T(8,128)S(1)}, f32[2,2,40,256]{3,2,1,0:T(8,128)}, u32[]{:S(2)}) copy-start(f32[2,2,40,256]{3,2,1,0:T(8,128)} %get-tuple-element.14) | copy-start | bytes 491524
  74.9 1.1 %copy-start.5 = (f32[2,40,256]{2,1,0:T(8,128)S(1)}, f32[2,40,256]{2,1,0:T(8,128)}, u32[]{:S(2)}) copy-start(f32[2,40,256]{2,1,0:T(8,128)} %get-tuple-element.15) | copy-start | bytes 245764
  74.9 1.3 %copy-start.6 = (s32[32,128]{1,0:T(8,128)S(1)}, s32[32,128]{1,0:T(8,128)}, u32[]{:S(2)}) copy-start(s32[32,128]{1,0:T(8,128)} %param.23) | copy-start | bytes 49156
  74.9 1.4 %copy-start.7 = (f32[32,128]{1,0:T(8,128)S(1)}, f32[32,128]{1,0:T(8,128)}, u32[]{:S(2)}) copy-start(f32[32,128]{1,0:T(8,128)} %param.24) | copy-start | bytes 49156

commit v19 on v18

--- a/solution.py
+++ b/solution.py
@@ -154,14 +154,16 @@
     return [device(lax.rem(me + k, count)) for k in range(1, count)]
 
 
-def stencil_kernel(base_ref, frac_ref, rows_ref, cols_ref):
+def stencil_kernel(table_ref, rows_ref, cols_ref):
     y_rows = rows_ref.shape[0]
-    y_ids = lax.axis_index("grp") * y_rows + lax.broadcasted_iota(jnp.int32, rows_ref.shape, 0)
-    y_base, y_frac = base_ref[0:1, :], frac_ref[0:1, :]
+    y_ids = (
+        lax.axis_index("grp") * y_rows + lax.broadcasted_iota(jnp.int32, rows_ref.shape, 0)
+    ).astype(jnp.float32)
+    y_base, y_frac = table_ref[0:1, :], table_ref[1:2, :]
     rows = jnp.where(y_ids == y_base, 1.0 - y_frac, 0.0) + jnp.where(y_ids == y_base + 1, y_frac, 0.0)
     rows_ref[...] = rows.astype(rows_ref.dtype)
-    x_ids = lax.broadcasted_iota(jnp.int32, cols_ref.shape, 0)
-    x_base, x_frac = base_ref[1:2, :], frac_ref[1:2, :]
+    x_ids = lax.broadcasted_iota(jnp.int32, cols_ref.shape, 0).astype(jnp.float32)
+    x_base, x_frac = table_ref[2:3, :], table_ref[3:4, :]
     cols = jnp.where(x_ids == x_base, 1.0 - x_frac, 0.0) + jnp.where(x_ids == x_base + 1, x_frac, 0.0)
     cols_ref[...] = cols.astype(cols_ref.dtype)
 
@@ -176,7 +178,7 @@
     ]
 
 
-def reduce_chain_kernel(y_chips, groups, x_ref, base_ref, frac_ref,
+def reduce_chain_kernel(y_chips, groups, x_ref, table_ref,
                         total_ref, halo_ref, rows_ref, cols_ref, core_buf, y_src, y_buf, z_src, z_buf,
                         d_src, d_buf, edge_buf, local_sems, send_sems, recv_sems, halo_send, halo_recv,
                         core_local, core_send, core_recv):
@@ -187,7 +189,7 @@
         + peers(groups, group_place)
         + neighbour_place(groups)
     )
-    stencil_kernel(base_ref, frac_ref, rows_ref, cols_ref)
+    stencil_kernel(table_ref, rows_ref, cols_ref)
     arrive()
     me_c, core_device = core_place()
     sibling = 1 - me_c
@@ -299,7 +301,7 @@
             jax.ShapeDtypeStruct((y_rows, depth), jnp.bfloat16),
             jax.ShapeDtypeStruct((side, depth), jnp.bfloat16),
         ],
-        in_specs=[pl.BlockSpec(memory_space=pltpu.VMEM)] * 3,
+        in_specs=[pl.BlockSpec(memory_space=pltpu.VMEM)] * 2,
         out_specs=[pl.BlockSpec(memory_space=pltpu.VMEM)] * 4,
         scratch_shapes=[
             pltpu.VMEM((2, rows, width), x.dtype),
@@ -519,8 +521,14 @@
     y_rows = side_cells // group_count
     flat = class_count * half_cols
     stencil = (
-        jnp.stack([y_base.reshape(flat), x_base.reshape(flat)]),
-        jnp.stack([y_frac.reshape(flat), x_frac.reshape(flat)]),
+        jnp.stack(
+            [
+                y_base.reshape(flat).astype(jnp.float32),
+                y_frac.reshape(flat),
+                x_base.reshape(flat).astype(jnp.float32),
+                x_frac.reshape(flat),
+            ]
+        ),
     )
     total, halo, row_weights, col_weights = reduce_chain(
         by_half, stencil, y_rows, side_cells, slab_count // Z_CHIPS, group_count, 1

time: 81.6 us -> 81 us (level)
  no operation moved by 1% of the time
where the time goes in v19:
time: 81 us; the launch traced here: 80.7 us
  Pallas kernels  62.7 us (77%)
  local copies, waits for them, and re-layouts  7.72 us (10%)
  matrix products  6.95 us (9%)
  other arithmetic  2.9 us (4%)
    pallas_call x1, Pallas kernels, reduce_chain(): pl.pallas_call(functools.partial(reduce_chain_kernel, y_chips, groups), o...  31.8 us
    pallas_call x1, Pallas kernels, gather_chain(): pl.pallas_call(functools.partial(gather_chain_kernel, y_chips, row_count,...  27.6 us
    unnamed x31, local copies, waits for them, and re-layouts  4.47 us
    pallas_call x1, Pallas kernels, insert_planes(): pl.pallas_call(insert_kernel, out_shape=jax.ShapeDtypeStruct((planes * y_...  3.3 us
    dot_general x2, matrix products, local(): jnp.dot(member, part, precision=lax.Precision.HIGHEST, preferred_element_...  1.9 us

profile of v19, /device:TPU:1, one launch (start us, length us, event | category | flops | bytes accessed | tf_op | source)
XLA Modules:
  0.0 80.7 jit_solution(8815304435924725978)
XLA Ops:
  0.0 0.8 %copy-done = bf16[1,16384]{1,0:T(2,128)(2,1)S(1)} copy-done((bf16[1,16384]{1,0:T(2,128)(2,1)S(1)}, bf16[1,16384]{1,0:T(2,128)(2,1)}, u32[]{:S(2)}) %copy-start) | copy-done | bytes 32792
  0.8 0.2 reduce
  1.0 0.6 constant_dynamic-slice_fusion.x_ref
  1.6 27.6 %shard_map.127 = (bf16[2,4,8,64,128]{4,3,2,1,0:T(8,128)(2,1)}, bf16[128,16384]{1,0:T(8,128)(2,1)}) custom-call(bf16[1,64,128]{2,1,0:T(8,128)(2,1)} %constant_dynamic-slice_fusion.x_ref), custom_call_target="tpu_custom_call" | custom-call | tf_op jit(solution)/shard_map/pallas_call | solution.py:371
  29.2 1.3 %slice_bitcast_fusion.1 = (bf16[4,8,64,128]{3,2,1,0:T(8,128)(2,1)S(1)}, bf16[4,8,64,128]{3,2,1,0:T(8,128)(2,1)S(1)}) fusion(bf16[2,4,8,64,128]{4,3,2,1,0:T(8,128)(2,1)} %get-tuple-element.11), kind=kLoop, calls=%fused_computation.51 | loop fusion | bytes 2097152
  30.5 0.0 copy-start.2
  30.5 0.0 copy-start.3
  30.6 0.0 copy-start.13
  30.6 0.2 select_reduce_fusion
  30.8 0.4 fusion.2
  31.2 0.4 fusion.3
  31.6 0.1 copy-done.2
  31.8 0.3 copy-done.3
  32.1 0.7 fusion.7
  32.8 1.5 %copy-done.1 = bf16[128,16384]{1,0:T(8,128)(2,1)S(1)} copy-done((bf16[128,16384]{1,0:T(8,128)(2,1)S(1)}, bf16[128,16384]{1,0:T(8,128)(2,1)}, u32[]{:S(2)}) %copy-start.1) | copy-done | bytes 4194328
  34.3 1.6 %fusion.74 = (f32[32]{0:T(128)S(1)}, f32[32,128]{1,0:T(8,128)S(1)}) fusion(bf16[128,16384]{1,0:T(8,128)(2,1)S(1)} %copy-done.1, bf16[32,8192]{1,0:T(8,128)(2,1)S(1)} %get-tuple-element.22, bf16[32,8192]{1,0:T(8,128)(2,1)S(1)} %get-tuple-element.21), kind=kOutput, calls=%fused_computation.119 | convolution fusion | flops 136323040 | bytes 5259392 | tf_op jit(solution)/shard_map/np,sp->ns/dot_general | solution.py:404
  35.9 0.2 fusion.53
  36.1 0.8 fusion.54
  36.8 1.0 %fusion.1 = bf16[32,8192]{1,0:T(8,128)(2,1)S(1)} fusion(f32[32,8192]{1,0:T(8,128)S(1)} %get-tuple-element.33, f32[32,16384]{1,0:T(8,128)S(1)} %fusion.54, bf16[32,16384]{1,0:T(8,128)(2,1)S(1)} %copy-done.3, s32[32]{0:T(128)S(1)} %copy-done.12), kind=kOutput, calls=%fused_computation.3 | convolution fusion | flops 102761472 | bytes 4718720 | tf_op jit(solution)/shard_map/dot_general | solution.py:493
  37.8 0.9 %fusion = bf16[32,8192]{1,0:T(8,128)(2,1)S(1)} fusion(f32[32,8192]{1,0:T(8,128)S(1)} %get-tuple-element.33, f32[32,16384]{1,0:T(8,128)S(1)} %fusion.54, bf16[32,16384]{1,0:T(8,128)(2,1)S(1)} %copy-done.3, s32[32]{0:T(128)S(1)} %copy-done.12), kind=kOutput, calls=%fused_computation.2 | convolution fusion | flops 102761472 | bytes 4718720 | tf_op jit(solution)/shard_map/dot_general | solution.py:493
  38.8 0.1 fusion.71
  38.8 0.2 convolution_convert_fusion.3
  39.0 0.1 reshape.116
  39.1 0.0 copy-start.11
  39.2 0.0 copy-start.8
  39.2 0.1 fusion.24
  39.3 1.2 %pad_maximum_fusion.x_ref = bf16[2,40,8192]{2,1,0:T(8,128)(2,1)} fusion(bf16[1,40,8192]{2,1,0:T(8,128)(2,1)S(1)} %get-tuple-element.32, bf16[1,40,8192]{2,1,0:T(8,128)(2,1)S(1)} %get-tuple-element.31), kind=kLoop, calls=%fused_computation.20 | loop fusion | flops 655360 | bytes 2621440 | tf_op jit(solution)/shard_map/stack | solution.py:508
  40.5 0.1 convert_element_type.77
  40.6 0.1 convert_element_type.79
  40.7 0.1 stack_reshape.6
  40.8 0.1 stack_reshape.7
  40.8 0.7 pad_maximum_fusion.3.table_ref
  41.5 31.8 %shard_map.128 = (f32[2,40,256]{2,1,0:T(8,128)}, f32[2,2,40,256]{3,2,1,0:T(8,128)}, bf16[32,2048]{1,0:T(8,128)(2,1)}, bf16[256,2048]{1,0:T(8,128)(2,1)}) custom-call(bf16[2,40,8192]{2,1,0:T(8,128)(2,1)} %pad_maximum_fusion.x_ref, f32[4,2048]{1,0:T(4,128)} %pad_maximum_fusion.3.table_ref), custom_call_target="tpu_custom_call" | custom-call | tf_op jit(solution)/shard_map/pallas_call | solution.py:296
  73.4 0.7 slice.83
  74.1 0.1 reshape_squeeze.3
  74.1 0.1 convert_multiply_fusion
  74.3 0.0 copy-start.6
  74.3 0.3 convolution_multiply_fusion.2
  74.6 0.1 reshape.112
  74.7 0.4 copy-done.4
  75.1 0.2 reshape.109
  75.4 0.1 reshape.110
  75.6 0.1 broadcast_add_fusion
  75.7 0.1 broadcast_subtract_fusion
  75.8 0.7 convolution_bitcast_fusion
  76.4 0.1 copy.28
  76.5 0.8 %reshape.113.sec_ref = f32[24,2048]{1,0:T(8,128)} reshape(f32[3,8,32,64]{3,2,1,0:T(8,128)S(1)} %copy.28) | data formatting | bytes 393216 | tf_op jit(solution)/shard_map/reshape | solution.py:579
  77.4 3.3 %shard_map.129 = f32[768,256]{1,0:T(8,128)} custom-call(bf16[32,2048]{1,0:T(8,128)(2,1)} %get-tuple-element.13.rows_ref, f32[24,2048]{1,0:T(8,128)} %reshape.113.sec_ref, bf16[256,2048]{1,0:T(8,128)(2,1)} %get-tuple-element.16.cols_ref), custom_call_target="tpu_custom_call" | custom-call | flops 805306368 | bytes 2162688 | tf_op jit(solution)/shard_map/pallas_call | solution.py:604
  (31 shorter events, 0.3 us)
Async XLA Ops:
  0.0 0.8 %copy-start = (bf16[1,16384]{1,0:T(2,128)(2,1)S(1)}, bf16[1,16384]{1,0:T(2,128)(2,1)}, u32[]{:S(2)}) copy-start(bf16[1,16384]{1,0:T(2,128)(2,1)} %param.17) | copy-start | bytes 98308
  0.0 30.6 %copy-start.12 = (s32[32]{0:T(128)S(1)}, s32[32]{0:T(128)}, u32[]{:S(2)}) copy-start(s32[32]{0:T(128)} %param.14) | copy-start | bytes 388
  0.0 30.6 %copy-start.14 = (s32[32]{0:T(128)S(1)}, s32[32]{0:T(128)}, u32[]{:S(2)}) copy-start(s32[32]{0:T(128)} %param.16) | copy-start | bytes 388
  30.5 1.2 %copy-start.2 = (bf16[64,8192]{1,0:T(8,128)(2,1)S(1)}, bf16[64,8192]{1,0:T(8,128)(2,1)}, u32[]{:S(2)}) copy-start(bf16[64,8192]{1,0:T(8,128)(2,1)} %param.18) | copy-start | bytes 3145732
  30.5 1.5 %copy-start.3 = (bf16[32,16384]{1,0:T(8,128)(2,1)S(1)}, bf16[32,16384]{1,0:T(8,128)(2,1)}, u32[]{:S(2)}) copy-start(bf16[32,16384]{1,0:T(8,128)(2,1)} %param.13) | copy-start | bytes 3145732
  30.6 1.5 %copy-start.13 = (s32[32]{0:T(128)S(1)}, s32[32]{0:T(128)}, u32[]{:S(2)}) copy-start(s32[32]{0:T(128)} %param.15) | copy-start | bytes 388
  32.1 2.2 %copy-start.1 = (bf16[128,16384]{1,0:T(8,128)(2,1)S(1)}, bf16[128,16384]{1,0:T(8,128)(2,1)}, u32[]{:S(2)}) copy-start(bf16[128,16384]{1,0:T(8,128)(2,1)} %get-tuple-element.12) | copy-start | bytes 12582916
  39.1 1.4 %copy-start.10 = (s32[32,64]{1,0:T(8,128)S(1)}, s32[32,64]{1,0:T(8,128)}, u32[]{:S(2)}) copy-start(s32[32,64]{1,0:T(8,128)} %param.20) | copy-start | bytes 24580
  39.1 1.4 %copy-start.11 = (s32[32,64]{1,0:T(8,128)S(1)}, s32[32,64]{1,0:T(8,128)}, u32[]{:S(2)}) copy-start(s32[32,64]{1,0:T(8,128)} %param.19) | copy-start | bytes 24580
  39.2 1.5 %copy-start.8 = (f32[32,64]{1,0:T(8,128)S(1)}, f32[32,64]{1,0:T(8,128)}, u32[]{:S(2)}) copy-start(f32[32,64]{1,0:T(8,128)} %param.22) | copy-start | bytes 24580
  39.2 1.6 %copy-start.9 = (f32[32,64]{1,0:T(8,128)S(1)}, f32[32,64]{1,0:T(8,128)}, u32[]{:S(2)}) copy-start(f32[32,64]{1,0:T(8,128)} %param.21) | copy-start | bytes 24580
  74.1 0.9 %copy-start.4 = (f32[2,2,40,256]{3,2,1,0:T(8,128)S(1)}, f32[2,2,40,256]{3,2,1,0:T(8,128)}, u32[]{:S(2)}) copy-start(f32[2,2,40,256]{3,2,1,0:T(8,128)} %get-tuple-element.14) | copy-start | bytes 491524
  74.3 1.1 %copy-start.5 = (f32[2,40,256]{2,1,0:T(8,128)S(1)}, f32[2,40,256]{2,1,0:T(8,128)}, u32[]{:S(2)}) copy-start(f32[2,40,256]{2,1,0:T(8,128)} %get-tuple-element.15) | copy-start | bytes 245764
  74.3 1.3 %copy-start.6 = (s32[32,128]{1,0:T(8,128)S(1)}, s32[32,128]{1,0:T(8,128)}, u32[]{:S(2)}) copy-start(s32[32,128]{1,0:T(8,128)} %param.23) | copy-start | bytes 49156
  74.3 1.4 %copy-start.7 = (f32[32,128]{1,0:T(8,128)S(1)}, f32[32,128]{1,0:T(8,128)}, u32[]{:S(2)}) copy-start(f32[32,128]{1,0:T(8,128)} %param.24) | copy-start | bytes 49156

commit v20 on v19

--- a/solution.py
+++ b/solution.py
@@ -254,7 +254,7 @@
     for index, device in enumerate(neighbour_place(groups)):
         side, peer = divmod(index, groups)
         copy = pltpu.make_async_remote_copy(
-            src_ref=d_src.at[0],
+            src_ref=d_src.at[0, : edge_buf.shape[2]],
             dst_ref=edge_buf.at[side, group],
             send_sem=halo_send.at[side, peer],
             recv_sem=halo_recv.at[side, group],
@@ -270,7 +270,7 @@
     for side, step in enumerate((count - 1, 1)):
         for peer in range(groups):
             pltpu.make_async_remote_copy(
-                src_ref=d_src.at[0],
+                src_ref=d_src.at[0, : edge_buf.shape[2]],
                 dst_ref=edge_buf.at[side, peer],
                 send_sem=halo_send.at[side, peer],
                 recv_sem=halo_recv.at[side, peer],
@@ -293,11 +293,12 @@
     band = width // (y_chips * Z_CHIPS)
     wide = 8
     depth = stencil[0].shape[1]
+    data_rows = rows - 8
     return pl.pallas_call(
         functools.partial(reduce_chain_kernel, y_chips, groups),
         out_shape=[
             jax.ShapeDtypeStruct((2, rows, band), jnp.float32),
-            jax.ShapeDtypeStruct((2, 2, rows, band), jnp.float32),
+            jax.ShapeDtypeStruct((2, 2, data_rows, band), jnp.float32),
             jax.ShapeDtypeStruct((y_rows, depth), jnp.bfloat16),
             jax.ShapeDtypeStruct((side, depth), jnp.bfloat16),
         ],
@@ -311,7 +312,7 @@
             pltpu.VMEM((Z_CHIPS, rows, band), jnp.bfloat16),
             pltpu.VMEM((1, rows, band), jnp.bfloat16),
             pltpu.VMEM((groups, rows, band), jnp.bfloat16),
-            pltpu.VMEM((2, groups, rows, band), jnp.bfloat16),
+            pltpu.VMEM((2, groups, data_rows, band), jnp.bfloat16),
             pltpu.SemaphoreType.DMA((4,)),
             pltpu.SemaphoreType.DMA((4, wide)),
             pltpu.SemaphoreType.DMA((4, wide)),

time: 81 us -> 80.5 us (level)
  no operation moved by 1% of the time
where the time goes in v20:
time: 80.5 us; the launch traced here: 80.1 us
  Pallas kernels  62.2 us (77%)
  local copies, waits for them, and re-layouts  7.69 us (10%)
  matrix products  6.95 us (9%)
  other arithmetic  2.9 us (4%)
    pallas_call x1, Pallas kernels, reduce_chain(): pl.pallas_call(functools.partial(reduce_chain_kernel, y_chips, groups), o...  31.3 us
    pallas_call x1, Pallas kernels, gather_chain(): pl.pallas_call(functools.partial(gather_chain_kernel, y_chips, row_count,...  27.6 us
    unnamed x31, local copies, waits for them, and re-layouts  4.46 us
    pallas_call x1, Pallas kernels, insert_planes(): pl.pallas_call(insert_kernel, out_shape=jax.ShapeDtypeStruct((planes * y_...  3.29 us
    dot_general x2, matrix products, local(): jnp.dot(member, part, precision=lax.Precision.HIGHEST, preferred_element_...  1.9 us
    dot_general x1, matrix products, align_frames(): jnp.einsum('np,sp->ns', cross_terms, phase, preferred_element_type=jnp.fl...  1.61 us

profile of v20, /device:TPU:1, one launch (start us, length us, event | category | flops | bytes accessed | tf_op | source)
XLA Modules:
  0.0 80.1 jit_solution(10162579177923431246)
XLA Ops:
  0.0 0.8 %copy-done = bf16[1,16384]{1,0:T(2,128)(2,1)S(1)} copy-done((bf16[1,16384]{1,0:T(2,128)(2,1)S(1)}, bf16[1,16384]{1,0:T(2,128)(2,1)}, u32[]{:S(2)}) %copy-start) | copy-done | bytes 32792
  0.8 0.2 reduce
  1.0 0.6 constant_dynamic-slice_fusion.x_ref
  1.6 27.6 %shard_map.127 = (bf16[2,4,8,64,128]{4,3,2,1,0:T(8,128)(2,1)}, bf16[128,16384]{1,0:T(8,128)(2,1)}) custom-call(bf16[1,64,128]{2,1,0:T(8,128)(2,1)} %constant_dynamic-slice_fusion.x_ref), custom_call_target="tpu_custom_call" | custom-call | tf_op jit(solution)/shard_map/pallas_call | solution.py:372
  29.2 1.3 %slice_bitcast_fusion.1 = (bf16[4,8,64,128]{3,2,1,0:T(8,128)(2,1)S(1)}, bf16[4,8,64,128]{3,2,1,0:T(8,128)(2,1)S(1)}) fusion(bf16[2,4,8,64,128]{4,3,2,1,0:T(8,128)(2,1)} %get-tuple-element.11), kind=kLoop, calls=%fused_computation.51 | loop fusion | bytes 2097152
  30.5 0.0 copy-start.2
  30.5 0.0 copy-start.3
  30.6 0.0 copy-start.13
  30.6 0.2 select_reduce_fusion
  30.8 0.4 fusion.2
  31.2 0.4 fusion.3
  31.6 0.1 copy-done.2
  31.8 0.3 copy-done.3
  32.1 0.7 fusion.7
  32.8 1.5 %copy-done.1 = bf16[128,16384]{1,0:T(8,128)(2,1)S(1)} copy-done((bf16[128,16384]{1,0:T(8,128)(2,1)S(1)}, bf16[128,16384]{1,0:T(8,128)(2,1)}, u32[]{:S(2)}) %copy-start.1) | copy-done | bytes 4194328
  34.3 1.6 %fusion.74 = (f32[32]{0:T(128)S(1)}, f32[32,128]{1,0:T(8,128)S(1)}) fusion(bf16[128,16384]{1,0:T(8,128)(2,1)S(1)} %copy-done.1, bf16[32,8192]{1,0:T(8,128)(2,1)S(1)} %get-tuple-element.22, bf16[32,8192]{1,0:T(8,128)(2,1)S(1)} %get-tuple-element.21), kind=kOutput, calls=%fused_computation.119 | convolution fusion | flops 136323040 | bytes 5259392 | tf_op jit(solution)/shard_map/np,sp->ns/dot_general | solution.py:405
  35.9 0.2 fusion.53
  36.1 0.8 fusion.54
  36.8 1.0 %fusion.1 = bf16[32,8192]{1,0:T(8,128)(2,1)S(1)} fusion(f32[32,8192]{1,0:T(8,128)S(1)} %get-tuple-element.33, f32[32,16384]{1,0:T(8,128)S(1)} %fusion.54, bf16[32,16384]{1,0:T(8,128)(2,1)S(1)} %copy-done.3, s32[32]{0:T(128)S(1)} %copy-done.12), kind=kOutput, calls=%fused_computation.3 | convolution fusion | flops 102761472 | bytes 4718720 | tf_op jit(solution)/shard_map/dot_general | solution.py:494
  37.8 0.9 %fusion = bf16[32,8192]{1,0:T(8,128)(2,1)S(1)} fusion(f32[32,8192]{1,0:T(8,128)S(1)} %get-tuple-element.33, f32[32,16384]{1,0:T(8,128)S(1)} %fusion.54, bf16[32,16384]{1,0:T(8,128)(2,1)S(1)} %copy-done.3, s32[32]{0:T(128)S(1)} %copy-done.12), kind=kOutput, calls=%fused_computation.2 | convolution fusion | flops 102761472 | bytes 4718720 | tf_op jit(solution)/shard_map/dot_general | solution.py:494
  38.8 0.1 fusion.71
  38.8 0.2 convolution_convert_fusion.3
  39.0 0.1 reshape.116
  39.1 0.0 copy-start.10
  39.2 0.0 copy-start.9
  39.2 0.1 fusion.24
  39.3 1.2 %pad_maximum_fusion.x_ref = bf16[2,40,8192]{2,1,0:T(8,128)(2,1)} fusion(bf16[1,40,8192]{2,1,0:T(8,128)(2,1)S(1)} %get-tuple-element.32, bf16[1,40,8192]{2,1,0:T(8,128)(2,1)S(1)} %get-tuple-element.31), kind=kLoop, calls=%fused_computation.20 | loop fusion | flops 655360 | bytes 2621440 | tf_op jit(solution)/shard_map/stack | solution.py:509
  40.5 0.1 convert_element_type.77
  40.6 0.1 convert_element_type.79
  40.7 0.1 stack_reshape.6
  40.8 0.1 stack_reshape.7
  40.8 0.7 pad_maximum_fusion.3.table_ref
  41.5 31.3 %shard_map.128 = (f32[2,40,256]{2,1,0:T(8,128)}, f32[2,2,32,256]{3,2,1,0:T(8,128)}, bf16[32,2048]{1,0:T(8,128)(2,1)}, bf16[256,2048]{1,0:T(8,128)(2,1)}) custom-call(bf16[2,40,8192]{2,1,0:T(8,128)(2,1)} %pad_maximum_fusion.x_ref, f32[4,2048]{1,0:T(4,128)} %pad_maximum_fusion.3.table_ref), custom_call_target="tpu_custom_call" | custom-call | tf_op jit(solution)/shard_map/pallas_call | solution.py:297
  72.8 0.7 slice.79
  73.5 0.1 reshape_squeeze.3
  73.6 0.1 convert_multiply_fusion
  73.8 0.0 copy-start.7
  73.8 0.3 convolution_multiply_fusion.2
  74.1 0.1 reshape.112
  74.2 0.3 copy-done.4
  74.5 0.2 reshape.109
  74.9 0.1 reshape.110
  75.0 0.1 broadcast_add_fusion
  75.1 0.1 broadcast_subtract_fusion
  75.2 0.7 convolution_bitcast_fusion
  75.9 0.1 copy.28
  76.0 0.8 %reshape.113.sec_ref = f32[24,2048]{1,0:T(8,128)} reshape(f32[3,8,32,64]{3,2,1,0:T(8,128)S(1)} %copy.28) | data formatting | bytes 393216 | tf_op jit(solution)/shard_map/reshape | solution.py:580
  76.8 3.3 %shard_map.129 = f32[768,256]{1,0:T(8,128)} custom-call(bf16[32,2048]{1,0:T(8,128)(2,1)} %get-tuple-element.13.rows_ref, f32[24,2048]{1,0:T(8,128)} %reshape.113.sec_ref, bf16[256,2048]{1,0:T(8,128)(2,1)} %get-tuple-element.16.cols_ref), custom_call_target="tpu_custom_call" | custom-call | flops 805306368 | bytes 2162688 | tf_op jit(solution)/shard_map/pallas_call | solution.py:605
  (30 shorter events, 0.2 us)
Async XLA Ops:
  0.0 0.8 %copy-start = (bf16[1,16384]{1,0:T(2,128)(2,1)S(1)}, bf16[1,16384]{1,0:T(2,128)(2,1)}, u32[]{:S(2)}) copy-start(bf16[1,16384]{1,0:T(2,128)(2,1)} %param.17) | copy-start | bytes 98308
  0.0 30.6 %copy-start.12 = (s32[32]{0:T(128)S(1)}, s32[32]{0:T(128)}, u32[]{:S(2)}) copy-start(s32[32]{0:T(128)} %param.14) | copy-start | bytes 388
  0.0 30.6 %copy-start.14 = (s32[32]{0:T(128)S(1)}, s32[32]{0:T(128)}, u32[]{:S(2)}) copy-start(s32[32]{0:T(128)} %param.16) | copy-start | bytes 388
  30.5 1.2 %copy-start.2 = (bf16[64,8192]{1,0:T(8,128)(2,1)S(1)}, bf16[64,8192]{1,0:T(8,128)(2,1)}, u32[]{:S(2)}) copy-start(bf16[64,8192]{1,0:T(8,128)(2,1)} %param.18) | copy-start | bytes 3145732
  30.5 1.5 %copy-start.3 = (bf16[32,16384]{1,0:T(8,128)(2,1)S(1)}, bf16[32,16384]{1,0:T(8,128)(2,1)}, u32[]{:S(2)}) copy-start(bf16[32,16384]{1,0:T(8,128)(2,1)} %param.13) | copy-start | bytes 3145732
  30.6 1.5 %copy-start.13 = (s32[32]{0:T(128)S(1)}, s32[32]{0:T(128)}, u32[]{:S(2)}) copy-start(s32[32]{0:T(128)} %param.15) | copy-start | bytes 388
  32.1 2.2 %copy-start.1 = (bf16[128,16384]{1,0:T(8,128)(2,1)S(1)}, bf16[128,16384]{1,0:T(8,128)(2,1)}, u32[]{:S(2)}) copy-start(bf16[128,16384]{1,0:T(8,128)(2,1)} %get-tuple-element.12) | copy-start | bytes 12582916
  39.1 1.4 %copy-start.10 = (s32[32,64]{1,0:T(8,128)S(1)}, s32[32,64]{1,0:T(8,128)}, u32[]{:S(2)}) copy-start(s32[32,64]{1,0:T(8,128)} %param.20) | copy-start | bytes 24580
  39.1 1.4 %copy-start.11 = (s32[32,64]{1,0:T(8,128)S(1)}, s32[32,64]{1,0:T(8,128)}, u32[]{:S(2)}) copy-start(s32[32,64]{1,0:T(8,128)} %param.19) | copy-start | bytes 24580
  39.2 1.5 %copy-start.8 = (f32[32,64]{1,0:T(8,128)S(1)}, f32[32,64]{1,0:T(8,128)}, u32[]{:S(2)}) copy-start(f32[32,64]{1,0:T(8,128)} %param.22) | copy-start | bytes 24580
  39.2 1.6 %copy-start.9 = (f32[32,64]{1,0:T(8,128)S(1)}, f32[32,64]{1,0:T(8,128)}, u32[]{:S(2)}) copy-start(f32[32,64]{1,0:T(8,128)} %param.21) | copy-start | bytes 24580
  73.6 0.9 %copy-start.4 = (f32[2,2,32,256]{3,2,1,0:T(8,128)S(1)}, f32[2,2,32,256]{3,2,1,0:T(8,128)}, u32[]{:S(2)}) copy-start(f32[2,2,32,256]{3,2,1,0:T(8,128)} %get-tuple-element.14) | copy-start | bytes 393220
  73.7 1.1 %copy-start.5 = (f32[2,40,256]{2,1,0:T(8,128)S(1)}, f32[2,40,256]{2,1,0:T(8,128)}, u32[]{:S(2)}) copy-start(f32[2,40,256]{2,1,0:T(8,128)} %get-tuple-element.15) | copy-start | bytes 245764
  73.8 1.3 %copy-start.6 = (s32[32,128]{1,0:T(8,128)S(1)}, s32[32,128]{1,0:T(8,128)}, u32[]{:S(2)}) copy-start(s32[32,128]{1,0:T(8,128)} %param.23) | copy-start | bytes 49156
  73.8 1.4 %copy-start.7 = (f32[32,128]{1,0:T(8,128)S(1)}, f32[32,128]{1,0:T(8,128)}, u32[]{:S(2)}) copy-start(f32[32,128]{1,0:T(8,128)} %param.24) | copy-start | bytes 49156
